TPU v7x, 32 devices: a whole 2x2x4 slice. The times are simulated.
32 devices in a mesh: expert: 8 (over z, x), tensor: 4 (over y, core).
Axes of the slice: x: 2, y: 2, z: 4, core: 2. Of those that a mesh axis runs over, the one named last changes fastest.
Arguments:
- tokens: bfloat16 [2048, 1280], P('expert'), may hold values from -6 to 6
- segment_ids: int32 [2048], replicated, may hold values from 0 to 3, never falling along the last dimension, each value on 1 to 1024 neighbouring positions
- expert_ids: int32 [2048, 7], P('expert'), may hold values from 0 to 15, all different within a row; in each aligned block of 256 rows (0 to 255, 256 to 511, ...) at most 224 rows name the same one
- gate_values: float32 [2048, 7], P('expert'), may hold values from 0.1 to 0.3
- expert_slot: int32 [16], replicated, may hold values from 0 to 15, each once
- first_gain: float32 [1280], replicated, may hold values from 0.1 to 1.9
- second_gain: float32 [1280], replicated, may hold values from 0.1 to 1.9
- query_weight: bfloat16 [10, 2, 64, 1280], P(None, None, 'tensor'), may hold values from -0.15625 to 0.15625
- key_weight: bfloat16 [10, 2, 64, 1280], P(None, None, 'tensor'), may hold values from -0.15625 to 0.15625
- value_weight: bfloat16 [10, 2, 64, 1280], P(None, None, 'tensor'), may hold values from -0.15625 to 0.15625
- output_weight: bfloat16 [10, 2, 64, 1280], P(None, None, 'tensor'), may hold values from -2.5 to 2.5
- shared_gate: bfloat16 [896, 1280], P('tensor'), may hold values from -0.15625 to 0.15625
- shared_up: bfloat16 [896, 1280], P('tensor'), may hold values from -0.15625 to 0.15625
- shared_down: bfloat16 [896, 1280], P('tensor'), may hold values from -0.1875 to 0.1875
- routed_gate: bfloat16 [16, 896, 1280], P('expert', 'tensor'), may hold values from -0.15625 to 0.15625
- routed_up: bfloat16 [16, 896, 1280], P('expert', 'tensor'), may hold values from -0.15625 to 0.15625
- routed_down: bfloat16 [16, 896, 1280], P('expert', 'tensor'), may hold values from -0.1875 to 0.1875
- cotangent: bfloat16 [2048, 1280], P('expert'), may hold values from -6 to 6
Outputs:
- output: bfloat16 [2048, 1280], P('expert')
- input_grad: bfloat16 [2048, 1280], P('expert')
- gate_grad: float32 [2048, 7], P('expert')
- first_gain_grad: float32 [1280], P('expert')
- second_gain_grad: float32 [1280], P('expert')
- query_grad: float32 [10, 2, 64, 1280], P(None, None, 'tensor', 'expert')
- key_grad: float32 [10, 2, 64, 1280], P(None, None, 'tensor', 'expert')
- value_grad: float32 [10, 2, 64, 1280], P(None, None, 'tensor', 'expert')
- output_weight_grad: float32 [10, 2, 64, 1280], P(None, None, 'tensor', 'expert')
- shared_gate_grad: float32 [896, 1280], P('tensor', 'expert')
- shared_up_grad: float32 [896, 1280], P('tensor', 'expert')
- shared_down_grad: float32 [896, 1280], P('tensor', 'expert')
- routed_gate_grad: float32 [16, 896, 1280], P('expert', 'tensor')
- routed_up_grad: float32 [16, 896, 1280], P('expert', 'tensor')
- routed_down_grad: float32 [16, 896, 1280], P('expert', 'tensor')
Inputs may be any that keep to these rules, and one draw needn't show every extreme that they name: `segment_ids`: segment ids never fall along the stream; every document has at most 1024 tokens and one has exactly 1024. `expert_ids`: A token's 7 experts are different. Within the 256 tokens of one index of expert no expert is named more than 224 times, a bound that some block reaches there. Each slot once: expert e uses the weights of slot expert_slot[e], which index expert_slot[e] // 2 of the expert axis holds.
All inputs are finite; a program needn't handle non-finite values.
Results may differ from a plain program's by a relative error of at most 0.014.
Values may be sent and summed in bfloat16 or wider, within the bound.
No kernel may reach another device: no remote copies, remote signals or barrier semaphores. Data moves between devices by JAX's collectives and lax.ppermute only.
A program may use at most 256 MiB of HBM per device.

v0:
```python
import jax
import jax.numpy as jnp
from jax import lax
from jax.sharding import PartitionSpec as P

HD = 128
REACH = 4


EPSILON = 1e-06
MASKED = -1e30


def passed_along(x, axis, by):
    devices = lax.axis_size(axis)
    pairs = [(i, i + by) for i in range(devices) if 0 <= i + by < devices]
    return lax.ppermute(x, axis, pairs)


def rms_scale(values):
    return lax.rsqrt(jnp.mean(values * values, axis=-1, keepdims=True) + EPSILON)


def norm_backward(grad_out, values, inverse_rms, gain_vector):
    weighted = grad_out * gain_vector
    normal = values * inverse_rms
    gain_grad = jnp.sum(grad_out * normal, axis=0)
    grad_in = inverse_rms * (
        weighted - normal * jnp.mean(normal * weighted, axis=-1, keepdims=True)
    )
    return (grad_in, gain_grad)


def rotate(vectors, cosine, sine_table):
    first_half = vectors[:, :, 0]
    second_half = vectors[:, :, 1]
    return jnp.stack(
        (
            first_half * cosine - second_half * sine_table,
            second_half * cosine + first_half * sine_table,
        ),
        axis=2,
    )


def rotate_back(gradient, cosine, sine_table):
    first_half = gradient[:, :, 0]
    second_half = gradient[:, :, 1]
    return jnp.stack(
        (
            first_half * cosine + second_half * sine_table,
            second_half * cosine - first_half * sine_table,
        ),
        axis=2,
    )


def swish_grads(grad_act, gate_pre, up_pre):
    sigmoid_value = jax.nn.sigmoid(gate_pre)
    swish_value = gate_pre * sigmoid_value
    grad_gate = (
        grad_act * up_pre * sigmoid_value * (1.0 + gate_pre * (1.0 - sigmoid_value))
    ).astype(jnp.bfloat16)
    grad_up = (grad_act * swish_value).astype(jnp.bfloat16)
    return (grad_gate, grad_up)


def contract(left_side, right_side, left_axis, right_axis):
    return lax.dot_general(
        left_side,
        right_side,
        (((left_axis,), (right_axis,)), ((), ())),
        preferred_element_type=jnp.float32,
    )


def on_device(
    tokens,
    segment_ids,
    expert_ids,
    gate_values,
    expert_slot,
    first_gain,
    second_gain,
    query_weight,
    key_weight,
    value_weight,
    output_weight,
    shared_gate,
    shared_up,
    shared_down,
    routed_gate,
    routed_up,
    routed_down,
    cotangent,
):
    local_rows, model_width = tokens.shape
    top_count = expert_ids.shape[1]
    experts_total = expert_slot.shape[0]
    slots_local = routed_gate.shape[0]
    expert_count = lax.axis_size("expert")
    expert_rank = lax.axis_index("expert")
    tensor_rank = lax.axis_index("tensor")
    head_count = query_weight.shape[0]
    pair_width = query_weight.shape[2]
    local_width = head_count * 2 * pair_width
    capacity = (2 * top_count * local_rows + experts_total - 1) // experts_total
    score_scale = HD ** (-0.5)
    stream_length = segment_ids.shape[0]
    places = jnp.arange(stream_length, dtype=jnp.int32)
    is_first = jnp.concatenate([jnp.ones((1,), jnp.bool_), segment_ids[1:] != segment_ids[:-1]])
    doc_start = lax.cummax(jnp.where(is_first, places, 0), axis=0)
    positions = lax.dynamic_slice_in_dim(places - doc_start, expert_rank * local_rows, local_rows)
    freq_index = tensor_rank * pair_width + jnp.arange(pair_width, dtype=jnp.int32)
    inverse_freq = 10000.0 ** (-2.0 * freq_index.astype(jnp.float32) / HD)
    angles = positions.astype(jnp.float32)[:, None] * inverse_freq[None, :]
    cosine = jnp.cos(angles)[:, None, :]
    sine_table = jnp.sin(angles)[:, None, :]
    inputs = tokens.astype(jnp.float32)
    first_scale = rms_scale(inputs)
    normed_one = (inputs * first_scale * first_gain).astype(jnp.bfloat16)
    query_mat = query_weight.reshape(local_width, model_width)
    key_mat = key_weight.reshape(local_width, model_width)
    value_mat = value_weight.reshape(local_width, model_width)
    output_mat = output_weight.reshape(local_width, model_width)
    head_shape = (local_rows, head_count, 2, pair_width)
    query_rot = rotate(
        contract(normed_one, query_mat, 1, 1).reshape(head_shape), cosine, sine_table
    ).astype(jnp.bfloat16)
    key_rot = rotate(
        contract(normed_one, key_mat, 1, 1).reshape(head_shape), cosine, sine_table
    ).astype(jnp.bfloat16)
    value_low = contract(normed_one, value_mat, 1, 1).reshape(head_shape).astype(jnp.bfloat16)
    query_full, key_full, value_full = (query_rot, key_rot, value_low)
    key_list = [key_full]
    value_list = [value_full]
    for distance in range(1, REACH + 1):
        moved_key, moved_value = passed_along((key_full, value_full), "expert", distance)
        key_list.append(moved_key)
        value_list.append(moved_value)
    key_stack = jnp.stack(key_list)
    value_stack = jnp.stack(value_list)
    seg_padded = jnp.concatenate([jnp.full((REACH * local_rows,), -1, jnp.int32), segment_ids])
    row_range = jnp.arange(local_rows, dtype=jnp.int32)
    seg_list = []
    place_list = []
    for distance in range(REACH + 1):
        source = expert_rank - distance
        seg_list.append(
            lax.dynamic_slice_in_dim(seg_padded, (source + REACH) * local_rows, local_rows)
        )
        place_list.append(source * local_rows + row_range)
    key_seg = jnp.stack(seg_list)
    key_place = jnp.stack(place_list)
    allowed = (
        (key_seg[:, None, :] == seg_list[0][None, :, None])
        & (key_place[:, None, :] <= place_list[0][None, :, None])
        & (key_place[:, None, :] >= 0)
    )
    partial_scores = jnp.einsum(
        "thcm,jshcm->jhts", query_full, key_stack, preferred_element_type=jnp.float32
    )
    scores = lax.psum(partial_scores, "tensor") * score_scale
    scores = jnp.where(allowed[:, None], scores, MASKED)
    row_max = jnp.max(scores, axis=(0, 3), keepdims=True)
    log_total = row_max + jnp.log(jnp.sum(jnp.exp(scores - row_max), axis=(0, 3), keepdims=True))
    probs_low = jnp.exp(scores - log_total).astype(jnp.bfloat16)
    attended = jnp.einsum(
        "jhts,jshcm->thcm", probs_low, value_stack, preferred_element_type=jnp.float32
    )
    attended_low = attended.reshape(local_rows, local_width).astype(jnp.bfloat16)
    attn_part = jnp.dot(attended_low, output_mat, preferred_element_type=jnp.float32)
    hidden_state = inputs + lax.psum(attn_part, "tensor")
    second_scale = rms_scale(hidden_state)
    normed_two = (hidden_state * second_scale * second_gain).astype(jnp.bfloat16)
    shared_gate_pre = contract(normed_two, shared_gate, 1, 1)
    shared_up_pre = contract(normed_two, shared_up, 1, 1)
    shared_act = (jax.nn.silu(shared_gate_pre) * shared_up_pre).astype(jnp.bfloat16)
    shared_part = jnp.dot(shared_act, shared_down, preferred_element_type=jnp.float32)
    flat_ids = expert_ids.reshape(-1)
    onehot = (flat_ids[:, None] == jnp.arange(experts_total, dtype=jnp.int32)[None, :]).astype(
        jnp.int32
    )
    slot_of_row = jnp.sum(onehot * expert_slot[None, :], axis=1)
    rank_of_row = jnp.sum((jnp.cumsum(onehot, axis=0) - 1) * onehot, axis=1)
    target = slot_of_row * capacity + rank_of_row
    row_tokens = jnp.repeat(normed_two, top_count, axis=0)
    send_rows = (
        jnp.zeros((experts_total * capacity, model_width), jnp.bfloat16).at[target].set(row_tokens)
    )
    send_rows = send_rows.reshape(expert_count, slots_local, capacity, model_width)
    arrived_rows = lax.all_to_all(send_rows, "expert", split_axis=0, concat_axis=0, tiled=True)
    gate_pre = jnp.einsum(
        "nlcd,lfd->nlcf", arrived_rows, routed_gate, preferred_element_type=jnp.float32
    )
    up_pre = jnp.einsum(
        "nlcd,lfd->nlcf", arrived_rows, routed_up, preferred_element_type=jnp.float32
    )
    active = (jax.nn.silu(gate_pre) * up_pre).astype(jnp.bfloat16)
    partial_out = jnp.einsum(
        "nlcf,lfd->nlcd", active, routed_down, preferred_element_type=jnp.float32
    )
    column_width = partial_out.shape[3]
    returned = lax.all_to_all(partial_out, "expert", split_axis=0, concat_axis=0, tiled=True)
    back_rows = returned.reshape(experts_total * capacity, column_width)[target].reshape(
        local_rows, top_count, column_width
    )
    routed_sum = jnp.einsum("tk,tkd->td", gate_values, back_rows)
    ffn_part = shared_part + routed_sum
    ffn_full = lax.psum(ffn_part.astype(jnp.bfloat16), "tensor").astype(jnp.float32)
    output = (hidden_state + ffn_full).astype(jnp.bfloat16)
    grad_full = cotangent.astype(jnp.float32)
    gate_grad_part = jnp.einsum("tkd,td->tk", back_rows, grad_full)
    grad_rows = (
        (gate_values[:, :, None] * grad_full[:, None, :])
        .astype(jnp.bfloat16)
        .reshape(local_rows * top_count, model_width)
    )
    send_grads = (
        jnp.zeros((experts_total * capacity, model_width), jnp.bfloat16).at[target].set(grad_rows)
    )
    send_grads = send_grads.reshape(expert_count, slots_local, capacity, model_width)
    grad_arrived = lax.all_to_all(send_grads, "expert", split_axis=0, concat_axis=0, tiled=True)
    grad_active = jnp.einsum(
        "nlcd,lfd->nlcf", grad_arrived, routed_down, preferred_element_type=jnp.float32
    )
    active_again = (jax.nn.silu(gate_pre) * up_pre).astype(jnp.bfloat16)
    routed_down_grad = jnp.einsum(
        "nlcf,nlcd->lfd", active_again, grad_arrived, preferred_element_type=jnp.float32
    )
    grad_gate_pre, grad_up_pre = swish_grads(grad_active, gate_pre, up_pre)
    routed_gate_grad = jnp.einsum(
        "nlcf,nlcd->lfd", grad_gate_pre, arrived_rows, preferred_element_type=jnp.float32
    )
    routed_up_grad = jnp.einsum(
        "nlcf,nlcd->lfd", grad_up_pre, arrived_rows, preferred_element_type=jnp.float32
    )
    grad_arrived_rows = jnp.einsum(
        "nlcf,lfd->nlcd", grad_gate_pre, routed_gate, preferred_element_type=jnp.float32
    ) + jnp.einsum("nlcf,lfd->nlcd", grad_up_pre, routed_up, preferred_element_type=jnp.float32)
    grad_home = lax.all_to_all(grad_arrived_rows, "expert", split_axis=0, concat_axis=0, tiled=True)
    grad_routed = jnp.sum(
        grad_home.reshape(experts_total * capacity, model_width)[target].reshape(
            local_rows, top_count, model_width
        ),
        axis=1,
    )
    shared_down_grad = contract(shared_act, cotangent, 0, 0)
    grad_shared_act = contract(cotangent, shared_down, 1, 1)
    grad_shared_gate, grad_shared_up = swish_grads(grad_shared_act, shared_gate_pre, shared_up_pre)
    shared_gate_grad = contract(grad_shared_gate, normed_two, 0, 0)
    shared_up_grad = contract(grad_shared_up, normed_two, 0, 0)
    grad_norm_two_part = (
        grad_routed
        + jnp.dot(grad_shared_gate, shared_gate, preferred_element_type=jnp.float32)
        + jnp.dot(grad_shared_up, shared_up, preferred_element_type=jnp.float32)
    )
    grad_norm_two, gate_grad = lax.psum((grad_norm_two_part, gate_grad_part), "tensor")
    grad_second, second_gain_local = norm_backward(
        grad_norm_two, hidden_state, second_scale, second_gain
    )
    grad_hidden = grad_full + grad_second
    grad_attn = grad_hidden.astype(jnp.bfloat16)
    output_weight_local = contract(attended_low, grad_attn, 0, 0)
    grad_attended = contract(grad_attn, output_mat, 1, 1).astype(jnp.bfloat16).reshape(head_shape)
    grad_probs_part = jnp.einsum(
        "thcm,jshcm->jhts", grad_attended, value_stack, preferred_element_type=jnp.float32
    )
    grad_probs = lax.psum(grad_probs_part, "tensor")
    probs_again = jnp.exp(scores - log_total)
    grad_values = jnp.einsum(
        "jhts,thcm->jshcm",
        probs_again.astype(jnp.bfloat16),
        grad_attended,
        preferred_element_type=jnp.float32,
    )
    inner_sum = jnp.sum(probs_again * grad_probs, axis=(0, 3), keepdims=True)
    grad_scores = (probs_again * (grad_probs - inner_sum)).astype(jnp.bfloat16)
    grad_query_rot = (
        jnp.einsum("jhts,jshcm->thcm", grad_scores, key_stack, preferred_element_type=jnp.float32)
        * score_scale
    )
    grad_keys = (
        jnp.einsum("jhts,thcm->jshcm", grad_scores, query_full, preferred_element_type=jnp.float32)
        * score_scale
    )
    key_total = grad_keys[0]
    value_total = grad_values[0]
    for distance in range(1, REACH + 1):
        back_key, back_value = passed_along(
            (grad_keys[distance], grad_values[distance]), "expert", -distance
        )
        key_total = key_total + back_key
        value_total = value_total + back_value
    grad_query = (
        rotate_back(grad_query_rot, cosine, sine_table)
        .astype(jnp.bfloat16)
        .reshape(local_rows, local_width)
    )
    grad_key = (
        rotate_back(key_total, cosine, sine_table)
        .astype(jnp.bfloat16)
        .reshape(local_rows, local_width)
    )
    grad_value = value_total.astype(jnp.bfloat16).reshape(local_rows, local_width)
    query_local = contract(grad_query, normed_one, 0, 0)
    key_local = contract(grad_key, normed_one, 0, 0)
    value_local = contract(grad_value, normed_one, 0, 0)
    grad_norm_one_part = (
        jnp.dot(grad_query, query_mat, preferred_element_type=jnp.float32)
        + jnp.dot(grad_key, key_mat, preferred_element_type=jnp.float32)
        + jnp.dot(grad_value, value_mat, preferred_element_type=jnp.float32)
    )
    grad_norm_one = lax.psum(grad_norm_one_part, "tensor")
    grad_first, first_gain_local = norm_backward(grad_norm_one, inputs, first_scale, first_gain)
    input_grad = (grad_hidden + grad_first).astype(jnp.bfloat16)
    weight_shape = query_weight.shape
    summed = (
        lax.psum_scatter(
            query_local.reshape(weight_shape), "expert", scatter_dimension=3, tiled=True
        ),
        lax.psum_scatter(
            key_local.reshape(weight_shape), "expert", scatter_dimension=3, tiled=True
        ),
        lax.psum_scatter(
            value_local.reshape(weight_shape), "expert", scatter_dimension=3, tiled=True
        ),
        lax.psum_scatter(
            output_weight_local.reshape(weight_shape), "expert", scatter_dimension=3, tiled=True
        ),
        lax.psum_scatter(shared_gate_grad, "expert", scatter_dimension=1, tiled=True),
        lax.psum_scatter(shared_up_grad, "expert", scatter_dimension=1, tiled=True),
        lax.psum_scatter(shared_down_grad, "expert", scatter_dimension=1, tiled=True),
        lax.psum_scatter(first_gain_local, "expert", scatter_dimension=0, tiled=True),
        lax.psum_scatter(second_gain_local, "expert", scatter_dimension=0, tiled=True),
    )
    (
        query_grad,
        key_grad,
        value_grad,
        output_weight_grad,
        shared_gate_sum,
        shared_up_sum,
        shared_down_sum,
        first_gain_grad,
        second_gain_grad,
    ) = summed
    return (
        output,
        input_grad,
        gate_grad,
        first_gain_grad,
        second_gain_grad,
        query_grad,
        key_grad,
        value_grad,
        output_weight_grad,
        shared_gate_sum,
        shared_up_sum,
        shared_down_sum,
        routed_gate_grad,
        routed_up_grad,
        routed_down_grad,
    )


def solution(mesh):
    placed = (
        P("expert", None),
        P(),
        P("expert", None),
        P("expert", None),
        P(),
        P(),
        P(),
        P(None, None, "tensor", None),
        P(None, None, "tensor", None),
        P(None, None, "tensor", None),
        P(None, None, "tensor", None),
        P("tensor", None),
        P("tensor", None),
        P("tensor", None),
        P("expert", "tensor", None),
        P("expert", "tensor", None),
        P("expert", "tensor", None),
        P("expert", None),
    )
    return jax.shard_map(
        on_device,
        mesh=mesh,
        in_specs=placed,
        out_specs=(
            P("expert", None),
            P("expert", None),
            P("expert", None),
            P("expert"),
            P("expert"),
            P(None, None, "tensor", "expert"),
            P(None, None, "tensor", "expert"),
            P(None, None, "tensor", "expert"),
            P(None, None, "tensor", "expert"),
            P("tensor", "expert"),
            P("tensor", "expert"),
            P("tensor", "expert"),
            P("expert", "tensor", None),
            P("expert", "tensor", None),
            P("expert", "tensor", None),
        ),
        check_vma=False,
    )
```

profile of v0, /device:TPU:0, one launch (start us, length us, event | category | flops | bytes accessed | tf_op | source)
XLA Modules:
  0.0 2302.5 jit_solution(11879512822494382175)
XLA Ops:
  71.9 206.3 %all-reduce.11.cloned.1.call-done = f32[5,10,256,256]{2,3,0,1:T(8,128)} async-done(((f32[5,10,256,256]{2,3,0,1:T(8,128)}), f32[5,10,256,256]{2,3,0,1:T(8,128)}) %all-reduce.11.cloned.1.call-update) | async-done | bytes 13107216 | tf_op jit(solution)/shard_map/psum | solution.py:163
  296.6 38.6 %all-reduce.13.cloned.1.call-done = f32[256,1280]{1,0:T(8,128)} async-done(((f32[256,1280]{1,0:T(8,128)}), f32[256,1280]{1,0:T(8,128)}) %all-reduce.13.cloned.1.call-update) | async-done | bytes 1310736 | tf_op jit(solution)/shard_map/psum | solution.py:173
  348.8 16.9 scatter_custom_fusion
  386.8 24.3 %scatter_custom_fusion.1 = bf16[3584,1280]{1,0:T(8,128)(2,1)} fusion(s32[1792]{0:T(1024)S(1)} %fusion.123, f32[1792,1280]{1,0:T(8,128)} %mul.436, f32[1792]{0:T(1024)S(1)} %mul.433, bf16[]{:T(256)} %constant.92.clone.1), kind=kCustom, calls=%fused_computation.37 | custom fusion | flops 4587520 | bytes 18358274 | tf_op jit(solution)/shard_map/scatter | solution.py:220
  411.1 160.5 %all-to-all-done = bf16[8,2,224,1280]{3,2,1,0:T(8,128)(2,1)} async-done(((bf16[8,2,224,1280]{3,2,1,0:T(8,128)(2,1)}), bf16[8,2,224,1280]{3,2,1,0:T(8,128)(2,1)}, u32[]{:S(2)}, u32[]{:S(2)}) %all-to-all-start) | async-done | bytes 9175072 | tf_op jit(solution)/shard_map/all_to_all | solution.py:192
  593.1 182.6 %all-to-all-done.2 = bf16[8,2,224,1280]{3,2,1,0:T(8,128)(2,1)} async-done(((bf16[8,2,224,1280]{3,2,1,0:T(8,128)(2,1)}), bf16[8,2,224,1280]{3,2,1,0:T(8,128)(2,1)}, u32[]{:S(2)}, u32[]{:S(2)}) %all-to-all-start.2) | async-done | bytes 9175072 | tf_op jit(solution)/shard_map/all_to_all | solution.py:223
  819.1 15.0 add_bitcast_fusion
  846.6 160.9 %all-to-all-done.1 = bf16[8,2,224,1280]{3,2,1,0:T(8,128)(2,1)} async-done(((bf16[8,2,224,1280]{3,2,1,0:T(8,128)(2,1)}), bf16[8,2,224,1280]{3,2,1,0:T(8,128)(2,1)}, u32[]{:S(2)}, u32[]{:S(2)}) %all-to-all-start.1) | async-done | bytes 9175072 | tf_op jit(solution)/shard_map/all_to_all | solution.py:204
  1015.4 15.4 gather_fusion
  1038.3 369.9 %all-to-all-done.3 = f32[8,2,224,1280]{3,2,1,0:T(8,128)} async-done(((f32[8,2,224,1280]{3,2,1,0:T(8,128)}), f32[8,2,224,1280]{3,2,1,0:T(8,128)}, u32[]{:S(2)}, u32[]{:S(2)}) %all-to-all-start.3) | async-done | bytes 18350112 | tf_op jit(solution)/shard_map/all_to_all | solution.py:241
  1408.2 16.4 gather_fusion.1
  1448.9 33.1 %all-reduce.17.cloned.1.call-done = f32[256,1280]{1,0:T(8,128)} async-done(((f32[256,1280]{1,0:T(8,128)}), f32[256,1280]{1,0:T(8,128)}) %all-reduce.17.cloned.1.call-update) | async-done | bytes 1310736 | tf_op jit(solution)/shard_map/psum | solution.py:258
  1483.8 35.1 %all-reduce.15.cloned.1.call-done = bf16[256,1280]{1,0:T(8,128)(2,1)} async-done(((bf16[256,1280]{1,0:T(8,128)(2,1)}), bf16[256,1280]{1,0:T(8,128)(2,1)}) %all-reduce.15.cloned.1.call-update) | async-done | bytes 655376 | tf_op jit(solution)/shard_map/psum | solution.py:210
  1532.4 15.0 copy.229
  1588.0 23.3 %collective-permute-done.15 = f32[256,10,2,16]{0,3,2,1:T(8,128)S(1)} collective-permute-done((f32[256,10,2,16]{0,3,2,1:T(8,128)S(1)}, f32[256,10,2,16]{0,3,2,1:T(8,128)S(1)}, u32[]{:S(2)}, u32[]{:S(2)}) %collective-permute-start.15) | collective-permute-done | bytes 327712 | tf_op jit(solution)/shard_map/ppermute | solution.py:17
  1613.2 15.0 copy.227
  1642.2 117.0 %all-reduce.19.cloned.1.call-done = f32[5,10,256,256]{2,3,0,1:T(8,128)} async-done(((f32[5,10,256,256]{2,3,0,1:T(8,128)}), f32[5,10,256,256]{2,3,0,1:T(8,128)}) %all-reduce.19.cloned.1.call-update) | async-done | bytes 13107216 | tf_op jit(solution)/shard_map/psum | solution.py:269
  1801.3 19.4 collective-permute-done.11
  1952.8 42.7 %all-reduce.3 = (f32[1280]{0:T(1024)S(1)}, f32[1280]{0:T(1024)S(1)}) all-reduce(f32[1280]{0:T(1024)S(1)} %get-tuple-element.17, f32[1280]{0:T(1024)S(1)} %get-tuple-element.15), channel_id=2, replica_groups=mesh['expert'=8,'tensor'=4] {'expert'}, use_global_device_ids=true, to_apply=%region_24.25.clone | all-reduce | flops 2560 | bytes 20480
  1999.3 23.0 %reduce-scatter.22.cloned.1.call-done = f32[160,320]{1,0:T(8,128)} async-done(((f32[1280,320]{1,0:T(8,128)}), f32[160,320]{1,0:T(8,128)}) %reduce-scatter.22.cloned.1.call-update) | async-done | bytes 204816
  2027.0 65.1 %reduce-scatter.24.cloned.1.call-done = f32[160,320]{1,0:T(8,128)} async-done(((f32[1280,320]{1,0:T(8,128)}), f32[160,320]{1,0:T(8,128)}) %reduce-scatter.24.cloned.1.call-update) | async-done | bytes 204816
  2096.9 63.1 %reduce-scatter.18.cloned.1.call-done = f32[224,160]{0,1:T(8,128)} async-done(((f32[224,1280]{0,1:T(8,128)}), f32[224,160]{0,1:T(8,128)}) %reduce-scatter.18.cloned.1.call-update) | async-done | bytes 143376 | tf_op jit(solution)/shard_map/reduce_scatter | solution.py:332
  2160.0 67.8 %reduce-scatter.16.cloned.1.call-done = f32[224,160]{0,1:T(8,128)} async-done(((f32[224,1280]{0,1:T(8,128)}), f32[224,160]{0,1:T(8,128)}) %reduce-scatter.16.cloned.1.call-update) | async-done | bytes 143376 | tf_op jit(solution)/shard_map/reduce_scatter | solution.py:331
  2227.8 68.0 %reduce-scatter.20.cloned.1.call-done = f32[224,160]{0,1:T(8,128)} async-done(((f32[224,1280]{0,1:T(8,128)}), f32[224,160]{0,1:T(8,128)}) %reduce-scatter.20.cloned.1.call-update) | async-done | bytes 143376 | tf_op jit(solution)/shard_map/reduce_scatter | solution.py:333
  (340 shorter events, 491.7 us)
Async XLA Ops:
  7.2 270.9 %all-reduce.11.cloned.1.call-start = ((), (), s32[]{:S(2)}) async-start(), calls=%async_computation.11 | async-start | bytes 26214400 | tf_op jit(solution)/shard_map/psum | solution.py:163
  38.5 296.7 %all-reduce.13.cloned.1.call-start = ((), (), s32[]{:S(2)}) async-start(), calls=%async_computation.12 | async-start | bytes 2621440 | tf_op jit(solution)/shard_map/psum | solution.py:173
  40.3 30.7 %collective-permute-start.2 = (bf16[256,10,2,16]{0,3,2,1:T(8,128)(2,1)S(1)}, bf16[256,10,2,16]{0,3,2,1:T(8,128)(2,1)S(1)}, u32[]{:S(2)}, u32[]{:S(2)}) collective-permute-start(bf16[256,10,2,16]{0,3,2,1:T(8,128)(2,1)S(1)} %get-tuple-element.58), channel_id=1, source_target_pairs={{0,12},{4,16},{8,20},{12,24},{16,28},{1,13},{5,17},{9,21},{13,25},... | collective-permute-start | bytes 491528 | tf_op jit(solution)/shard_map/ppermute | solution.py:17
  365.7 205.9 %all-to-all-start = ((bf16[8,2,224,1280]{3,2,1,0:T(8,128)(2,1)}), bf16[8,2,224,1280]{3,2,1,0:T(8,128)(2,1)}, u32[]{:S(2)}, u32[]{:S(2)}) async-start(bf16[8,2,224,1280]{3,2,1,0:T(8,128)(2,1)} %bitcast.380), calls=%async_computation | async-start | bytes 18350080 | tf_op jit(solution)/shard_map/all_to_all | solution.py:192
  571.6 204.1 %all-to-all-start.2 = ((bf16[8,2,224,1280]{3,2,1,0:T(8,128)(2,1)}), bf16[8,2,224,1280]{3,2,1,0:T(8,128)(2,1)}, u32[]{:S(2)}, u32[]{:S(2)}) async-start(bf16[8,2,224,1280]{3,2,1,0:T(8,128)(2,1)} %bitcast.379), calls=%async_computation.2 | async-start | bytes 18350080 | tf_op jit(solution)/shard_map/all_to_all | solution.py:223
  803.2 204.3 %all-to-all-start.1 = ((bf16[8,2,224,1280]{3,2,1,0:T(8,128)(2,1)}), bf16[8,2,224,1280]{3,2,1,0:T(8,128)(2,1)}, u32[]{:S(2)}, u32[]{:S(2)}) async-start(bf16[8,2,224,1280]{3,2,1,0:T(8,128)(2,1)} %copy.153), calls=%async_computation.1 | async-start | bytes 18350080 | tf_op jit(solution)/shard_map/all_to_all | solution.py:204
  1007.5 400.7 %all-to-all-start.3 = ((f32[8,2,224,1280]{3,2,1,0:T(8,128)}), f32[8,2,224,1280]{3,2,1,0:T(8,128)}, u32[]{:S(2)}, u32[]{:S(2)}) async-start(f32[8,2,224,1280]{3,2,1,0:T(8,128)} %copy.156), calls=%async_computation.3 | async-start | bytes 36700160 | tf_op jit(solution)/shard_map/all_to_all | solution.py:241
  1013.3 468.7 %all-reduce.17.cloned.1.call-start = ((), (), s32[]{:S(2)}) async-start(), calls=%async_computation.14 | async-start | bytes 2621440 | tf_op jit(solution)/shard_map/psum | solution.py:258
  1443.5 75.4 %all-reduce.15.cloned.1.call-start = ((), (), s32[]{:S(2)}) async-start(), calls=%async_computation.13 | async-start | bytes 1310720 | tf_op jit(solution)/shard_map/psum | solution.py:210
  1448.9 310.4 %all-reduce.19.cloned.1.call-start = ((), (), s32[]{:S(2)}) async-start(), calls=%async_computation.15 | async-start | bytes 26214400 | tf_op jit(solution)/shard_map/psum | solution.py:269
  1530.0 397.4 %reduce-scatter.28.cloned.1.call-start = ((), (), s32[]{:S(2)}) async-start(), calls=%async_computation.23 | async-start | bytes 2211840
  1561.2 373.0 %reduce-scatter.26.cloned.1.call-start = ((), (), s32[]{:S(2)}) async-start(), calls=%async_computation.22 | async-start | bytes 2211840
  1571.5 39.8 %collective-permute-start.15 = (f32[256,10,2,16]{0,3,2,1:T(8,128)S(1)}, f32[256,10,2,16]{0,3,2,1:T(8,128)S(1)}, u32[]{:S(2)}, u32[]{:S(2)}) collective-permute-start(f32[256,10,2,16]{0,3,2,1:T(8,128)S(1)} %get-tuple-element.30), channel_id=1, source_target_pairs={{16,0},{20,4},{24,8},{28,12},{17,1},{21,5},{25,9},{29,13},{18,2},{... | collective-permute-start | bytes 983048 | tf_op jit(solution)/shard_map/ppermute | solution.py:17
  1572.8 38.5 %collective-permute-start.14 = (f32[256,10,2,16]{0,3,2,1:T(8,128)S(1)}, f32[256,10,2,16]{0,3,2,1:T(8,128)S(1)}, u32[]{:S(2)}, u32[]{:S(2)}) collective-permute-start(f32[256,10,2,16]{0,3,2,1:T(8,128)S(1)} %get-tuple-element.31), channel_id=1, source_target_pairs={{12,0},{16,4},{20,8},{24,12},{28,16},{13,1},{17,5},{21,9},{25,13},... | collective-permute-start | bytes 983048 | tf_op jit(solution)/shard_map/ppermute | solution.py:17
  1641.9 309.0 %all-reduce.21.cloned.1.call-start = ((), (), s32[]{:S(2)}) async-start(), calls=%async_computation.16 | async-start | bytes 2621440 | tf_op jit(solution)/shard_map/psum | solution.py:314
  1781.2 20.1 collective-permute-start.8
  1782.6 38.1 %collective-permute-start.11 = (f32[256,10,2,16]{0,3,1,2:T(8,128)S(1)}, f32[256,10,2,16]{0,3,1,2:T(8,128)S(1)}, u32[]{:S(2)}, u32[]{:S(2)}) collective-permute-start(f32[256,10,2,16]{0,3,1,2:T(8,128)S(1)} %get-tuple-element.33), channel_id=1, source_target_pairs={{16,0},{20,4},{24,8},{28,12},{17,1},{21,5},{25,9},{29,13},{18,2},{... | collective-permute-start | bytes 983048 | tf_op jit(solution)/shard_map/ppermute | solution.py:17
  1783.9 36.8 %collective-permute-start.10 = (f32[256,10,2,16]{0,3,1,2:T(8,128)S(1)}, f32[256,10,2,16]{0,3,1,2:T(8,128)S(1)}, u32[]{:S(2)}, u32[]{:S(2)}) collective-permute-start(f32[256,10,2,16]{0,3,1,2:T(8,128)S(1)} %get-tuple-element.34), channel_id=1, source_target_pairs={{12,0},{16,4},{20,8},{24,12},{28,16},{13,1},{17,5},{21,9},{25,13},... | collective-permute-start | bytes 983048 | tf_op jit(solution)/shard_map/ppermute | solution.py:17
  1785.2 35.5 %collective-permute-start.9 = (f32[256,10,2,16]{0,3,1,2:T(8,128)S(1)}, f32[256,10,2,16]{0,3,1,2:T(8,128)S(1)}, u32[]{:S(2)}, u32[]{:S(2)}) collective-permute-start(f32[256,10,2,16]{0,3,1,2:T(8,128)S(1)} %get-tuple-element.35), channel_id=1, source_target_pairs={{8,0},{12,4},{16,8},{20,12},{24,16},{28,20},{9,1},{13,5},{17,9},{2... | collective-permute-start | bytes 983048 | tf_op jit(solution)/shard_map/ppermute | solution.py:17
  1825.1 197.3 %reduce-scatter.22.cloned.1.call-start = ((), (), s32[]{:S(2)}) async-start(), calls=%async_computation.20 | async-start | bytes 2211840
  1855.4 236.8 %reduce-scatter.24.cloned.1.call-start = ((), (), s32[]{:S(2)}) async-start(), calls=%async_computation.21 | async-start | bytes 2211840
  1886.6 273.4 %reduce-scatter.18.cloned.1.call-start = ((), (), s32[]{:S(2)}) async-start(), calls=%async_computation.18 | async-start | bytes 1474560 | tf_op jit(solution)/shard_map/reduce_scatter | solution.py:332
  1888.1 339.7 %reduce-scatter.16.cloned.1.call-start = ((), (), s32[]{:S(2)}) async-start(), calls=%async_computation.17 | async-start | bytes 1474560 | tf_op jit(solution)/shard_map/reduce_scatter | solution.py:331
  1889.7 406.1 %reduce-scatter.20.cloned.1.call-start = ((), (), s32[]{:S(2)}) async-start(), calls=%async_computation.19 | async-start | bytes 1474560 | tf_op jit(solution)/shard_map/reduce_scatter | solution.py:333
  (80 other events, 2547.2 us)
Sparse Core Ops, SparseCore 0:
  38.6 239.4 all-reduce.10
  295.8 39.3 all-reduce.12
  1443.6 38.4 all-reduce.16
  1484.8 34.0 all-reduce.14
  1530.1 229.1 all-reduce.18
  1762.6 78.7 reduce-scatter.27
  1844.8 65.5 reduce-scatter.25
  1912.8 38.0 all-reduce.20
  1954.5 67.8 reduce-scatter.21
  2025.7 66.4 reduce-scatter.23
  2096.2 63.7 reduce-scatter.17
  2163.8 63.9 reduce-scatter.15
  2231.8 63.9 reduce-scatter.19
where the time goes:
time: 2310 us; the launch traced here: 2300 us
  waiting for transfers between devices  1670 us (72%)
  local copies, waits for them, and re-layouts  267 us (12%)
  matrix products  143 us (6%)
  other arithmetic  81.3 us (4%)
  starting transfers between devices  70.9 us (3%)
  blocking collectives  50.5 us (2%)
    all_to_all x1, waiting for transfers between devices, on_device(): lax.all_to_all(grad_arrived_rows, 'expert', split_axis=0, concat_axis=0,...  370 us
    psum x1, waiting for transfers between devices, on_device(): scores = lax.psum(partial_scores, 'tensor') * score_scale  206 us
    all_to_all x1, waiting for transfers between devices, on_device(): lax.all_to_all(send_grads, 'expert', split_axis=0, concat_axis=0, tiled=T...  183 us
    all_to_all x1, waiting for transfers between devices, on_device(): lax.all_to_all(partial_out, 'expert', split_axis=0, concat_axis=0, tiled=...  161 us
    all_to_all x1, waiting for transfers between devices, on_device(): lax.all_to_all(send_rows, 'expert', split_axis=0, concat_axis=0, tiled=True)  161 us
    unnamed x170, local copies, waits for them, and re-layouts  153 us
    psum x1, waiting for transfers between devices, on_device(): grad_probs = lax.psum(grad_probs_part, 'tensor')  117 us
    unnamed x17, waiting for transfers between devices  88.4 us
  transfers between devices with their start and end apart: 33, of which 21 were waited for; matrix products, arithmetic and copies ran while one was open for 15% of the time, Pallas kernels for 0%

commit v1 on v0

v1 whole, which is shorter than its diff:
```python
import jax
import jax.numpy as jnp
from jax import lax
from jax.experimental import pallas as pl
from jax.experimental.pallas import tpu as pltpu
from jax.sharding import PartitionSpec as P

HD = 128
REACH = 4
EPSILON = 1e-06
MASKED = -1e30
BF = jnp.bfloat16
F32 = jnp.float32
BOTH = ("expert", "tensor")
VMEM_LIMIT = 60 * 1024 * 1024


def dot(a, b, ca, cb):
    return lax.dot_general(a, b, (((ca,), (cb,)), ((), ())), preferred_element_type=F32)


def whole(shape):
    zeros = (0,) * len(shape)
    return pl.BlockSpec(shape, lambda *_: zeros)


def query_groups(blocks, groups):
    cost = [min(b, REACH) + 1 for b in range(blocks)]
    most = max(cost)
    while True:
        starts, load = [0], 0
        for b in range(blocks):
            if load + cost[b] > most:
                starts.append(b)
                load = 0
            load += cost[b]
        if len(starts) <= groups:
            break
        most += 1
    return starts + [blocks] * (groups + 2 - len(starts))


def rms_scale(values):
    return lax.rsqrt(jnp.mean(values * values, axis=-1, keepdims=True) + EPSILON)


def norm_backward(grad_out, values, inverse_rms, gain_vector):
    weighted = grad_out * gain_vector
    normal = values * inverse_rms
    gain_grad = jnp.sum(grad_out * normal, axis=0)
    grad_in = inverse_rms * (
        weighted - normal * jnp.mean(normal * weighted, axis=-1, keepdims=True)
    )
    return grad_in, gain_grad


def project(tokens, gain, wq, wk, wv, cosine, sine, units, groups):
    rows, width = tokens.shape
    heads = wq.shape[0]
    hw = wq.shape[1] * wq.shape[2]
    pw = wq.shape[2]

    def body(tok, gain_ref, q_ref, k_ref, v_ref, cos_ref, sin_ref, norm_ref, send_ref):
        x = tok[...].astype(F32)
        normed = (x * rms_scale(x) * gain_ref[...]).astype(BF)
        norm_ref[...] = normed
        cos = cos_ref[...]
        sin = sin_ref[...]
        for part, w_ref in enumerate((q_ref, k_ref, v_ref)):
            pre = dot(w_ref[...], normed, 1, 1)
            for h in range(heads):
                a = pre[h * hw : h * hw + pw]
                b = pre[h * hw + pw : (h + 1) * hw]
                if part < 2:
                    a, b = a * cos - b * sin, b * cos + a * sin
                chunk = jnp.concatenate([a, b], axis=0).astype(BF)
                for unit in range(h, units, heads):
                    send_ref[unit, part * hw : (part + 1) * hw] = chunk

    flat = (heads * hw, width)
    return pl.pallas_call(
        body,
        out_shape=(
            jax.ShapeDtypeStruct((rows, width), BF),
            jax.ShapeDtypeStruct((units, 3 * hw, rows), BF),
        ),
        compiler_params=pltpu.CompilerParams(vmem_limit_bytes=VMEM_LIMIT),
        name="project",
    )(tokens, gain[None], wq.reshape(flat), wk.reshape(flat), wv.reshape(flat), cosine, sine)


def allowed_pairs(seg_col, seg_row, query_block, key_block, rows):
    wide = jnp.concatenate([seg_col] * (rows // seg_col.shape[1]), axis=1)
    same = wide == seg_row
    ahead = lax.broadcasted_iota(jnp.int32, (rows, rows), 0) - lax.broadcasted_iota(
        jnp.int32, (rows, rows), 1
    )
    return same & (ahead + (query_block - key_block) * rows >= 0)


def attend(bounds, arrived, seg_col, seg_row, most):
    blocks, quarters, chunk, rows = arrived.shape
    hw = chunk // 3
    hd = quarters * hw
    scale = HD ** (-0.5)

    def part(ref, block, which):
        return ref[block, :, which * hw : (which + 1) * hw, :].reshape(hd, rows)

    def body(bounds_ref, arr_ref, col_ref, row_ref, out_ref, lse_ref, score_ref):
        query_block = bounds_ref[0] + pl.program_id(0)

        @pl.when(query_block < bounds_ref[1])
        def _():
            query = part(arr_ref, query_block, 0)
            col = col_ref[query_block]
            low = jnp.maximum(query_block - REACH, 0)

            def first(kb, best):
                s = dot(query, part(arr_ref, kb, 1), 0, 0) * scale
                s = jnp.where(allowed_pairs(col, row_ref[kb], query_block, kb, rows), s, MASKED)
                score_ref[kb - low] = s
                return jnp.maximum(best, jnp.max(s, axis=1, keepdims=True))

            best = lax.fori_loop(low, query_block + 1, first, jnp.full((rows, 1), MASKED, F32))

            def second(kb, carry):
                total, out = carry
                p = jnp.exp(score_ref[kb - low] - best)
                total = total + jnp.sum(p, axis=1, keepdims=True)
                return total, out + dot(p.astype(BF), part(arr_ref, kb, 2), 1, 1)

            total, out = lax.fori_loop(
                low, query_block + 1, second, (jnp.zeros((rows, 1), F32), jnp.zeros((rows, hd), F32))
            )
            out_ref[query_block] = (out / total).astype(BF)
            lse_ref[query_block] = jnp.broadcast_to(best + jnp.log(total), (rows, 128))

    grid_spec = pltpu.PrefetchScalarGridSpec(
        num_scalar_prefetch=1,
        grid=(most,),
        in_specs=[whole(arrived.shape), whole(seg_col.shape), whole(seg_row.shape)],
        out_specs=[whole((blocks, rows, hd)), whole((blocks, rows, 128))],
        scratch_shapes=[pltpu.VMEM((REACH + 1, rows, rows), F32)],
    )
    return pl.pallas_call(
        body,
        grid_spec=grid_spec,
        out_shape=(
            jax.ShapeDtypeStruct((blocks, rows, hd), BF),
            jax.ShapeDtypeStruct((blocks, rows, 128), F32),
        ),
        compiler_params=pltpu.CompilerParams(vmem_limit_bytes=VMEM_LIMIT),
        name="attend",
    )(bounds, arrived, seg_col, seg_row)


def attend_back(bounds, arrived, seg_col, seg_row, lse, grad_out, most):
    blocks, quarters, chunk, rows = arrived.shape
    hw = chunk // 3
    hd = quarters * hw
    scale = HD ** (-0.5)

    def part(ref, block, which):
        return ref[block, :, which * hw : (which + 1) * hw, :].reshape(hd, rows)

    def body(bounds_ref, arr_ref, col_ref, row_ref, lse_ref, do_ref, res_ref, prob_ref, dp_ref, dk_ref, dv_ref):
        step = pl.program_id(0)
        query_block = bounds_ref[0] + step

        @pl.when(step == 0)
        def _():
            res_ref[...] = jnp.zeros(res_ref.shape, BF)
            dk_ref[...] = jnp.zeros(dk_ref.shape, F32)
            dv_ref[...] = jnp.zeros(dv_ref.shape, F32)

        @pl.when(query_block < bounds_ref[1])
        def _():
            query = part(arr_ref, query_block, 0)
            col = col_ref[query_block]
            lse_now = jnp.concatenate([lse_ref[query_block]] * (rows // 128), axis=1)
            do = do_ref[query_block]
            low = jnp.maximum(query_block - REACH, 0)

            def first(kb, inner):
                s = dot(query, part(arr_ref, kb, 1), 0, 0) * scale
                ok = allowed_pairs(col, row_ref[kb], query_block, kb, rows)
                p = jnp.where(ok, jnp.exp(jnp.where(ok, s - lse_now, 0.0)), 0.0)
                dp = dot(do, part(arr_ref, kb, 2), 1, 0)
                prob_ref[kb - low] = p
                dp_ref[kb - low] = dp
                dv_ref[kb] += dot(do, p.astype(BF), 0, 0)
                return inner + jnp.sum(p * dp, axis=1, keepdims=True)

            inner = lax.fori_loop(low, query_block + 1, first, jnp.zeros((rows, 1), F32))

            def second(kb, dq):
                ds = (prob_ref[kb - low] * (dp_ref[kb - low] - inner)).astype(BF)
                dk_ref[kb] += dot(query, ds, 1, 0)
                return dq + dot(part(arr_ref, kb, 1), ds, 1, 1)

            dq = lax.fori_loop(low, query_block + 1, second, jnp.zeros((hd, rows), F32))
            res_ref[query_block, :, 0:hw, :] = (dq * scale).astype(BF).reshape(quarters, hw, rows)

        @pl.when(step == pl.num_programs(0) - 1)
        def _():
            for b in range(blocks):
                res_ref[b, :, hw : 2 * hw, :] = (dk_ref[b] * scale).astype(BF).reshape(quarters, hw, rows)
                res_ref[b, :, 2 * hw : 3 * hw, :] = dv_ref[b].astype(BF).reshape(quarters, hw, rows)

    grid_spec = pltpu.PrefetchScalarGridSpec(
        num_scalar_prefetch=1,
        grid=(most,),
        in_specs=[
            whole(arrived.shape),
            whole(seg_col.shape),
            whole(seg_row.shape),
            whole(lse.shape),
            whole(grad_out.shape),
        ],
        out_specs=whole(arrived.shape),
        scratch_shapes=[
            pltpu.VMEM((REACH + 1, rows, rows), F32),
            pltpu.VMEM((REACH + 1, rows, rows), F32),
            pltpu.VMEM((blocks, hd, rows), F32),
            pltpu.VMEM((blocks, hd, rows), F32),
        ],
    )
    return pl.pallas_call(
        body,
        grid_spec=grid_spec,
        out_shape=jax.ShapeDtypeStruct(arrived.shape, BF),
        compiler_params=pltpu.CompilerParams(vmem_limit_bytes=VMEM_LIMIT),
        name="attend_back",
    )(bounds, arrived, seg_col, seg_row, lse, grad_out)


def weight_specs(parts, hidden, width, mats):
    return [pl.BlockSpec((1, hidden, width), lambda s, *_: (s, 0, 0))] * (parts * mats)


def down_products(grads_in, downs):
    count, width = grads_in.shape
    parts = len(downs)
    slots, hidden, _ = downs[0].shape

    def body(dy_ref, *refs):
        for k in range(parts):
            refs[parts][0, k] = dot(dy_ref[...], refs[k][0], 1, 1)

    return pl.pallas_call(
        body,
        grid=(slots,),
        in_specs=[whole(grads_in.shape)] + weight_specs(parts, hidden, width, 1),
        out_specs=pl.BlockSpec((1, parts, count, hidden), lambda s: (s, 0, 0, 0)),
        out_shape=jax.ShapeDtypeStruct((slots, parts, count, hidden), F32),
        compiler_params=pltpu.CompilerParams(vmem_limit_bytes=VMEM_LIMIT),
        name="down_products",
    )(grads_in, *downs)


def swish_parts(g, u, da):
    sig = jax.nn.sigmoid(g)
    swish = g * sig
    return swish * u, da * u * (sig * (1.0 + g * (1.0 - sig))), da * swish


def experts_first(rows_in, down_prod, gates, gate_ws, up_ws):
    count, width = rows_in.shape
    parts = len(gate_ws)
    slots, hidden, _ = gate_ws[0].shape

    def body(x_ref, da_ref, gate_ref, *refs):
        gate_w, up_w = refs[:parts], refs[parts : 2 * parts]
        act_ref, dg_ref, du_ref, gg_ref, dx_ref, acc_ref = refs[2 * parts :]
        s = pl.program_id(0)
        x = x_ref[...]
        lane = lax.broadcasted_iota(jnp.int32, (count, 128), 1)
        gate = jnp.sum(jnp.where(lane == s, gate_ref[...], 0.0), axis=1, keepdims=True)
        total = jnp.zeros((count, 1), F32)

        @pl.when(s == 0)
        def _():
            acc_ref[...] = jnp.zeros(acc_ref.shape, F32)
            gg_ref[...] = jnp.zeros(gg_ref.shape, F32)

        for k in range(parts):
            g = dot(x, gate_w[k][0], 1, 1)
            u = dot(x, up_w[k][0], 1, 1)
            da = da_ref[0, k]
            act, dg, du = swish_parts(g, u, da * gate)
            total = total + jnp.sum(act * da, axis=1, keepdims=True)
            act_ref[0, k] = (act * gate).astype(BF)
            dg_ref[0, k] = dg.astype(BF)
            du_ref[0, k] = du.astype(BF)
            acc_ref[...] += dot(dg_ref[0, k], gate_w[k][0], 1, 0) + dot(du_ref[0, k], up_w[k][0], 1, 0)

        gg_ref[...] += jnp.where(lane == s, total, 0.0)

        @pl.when(s == slots - 1)
        def _():
            dx_ref[...] = acc_ref[...].astype(BF)

    hid = jax.ShapeDtypeStruct((slots, parts, count, hidden), BF)
    hid_spec = pl.BlockSpec((1, parts, count, hidden), lambda s: (s, 0, 0, 0))
    return pl.pallas_call(
        body,
        grid=(slots,),
        in_specs=[whole(rows_in.shape), hid_spec, whole(gates.shape)]
        + weight_specs(parts, hidden, width, 2),
        out_specs=[hid_spec, hid_spec, hid_spec, whole((count, 128)), whole((count, width))],
        out_shape=(
            hid,
            hid,
            hid,
            jax.ShapeDtypeStruct((count, 128), F32),
            jax.ShapeDtypeStruct((count, width), BF),
        ),
        scratch_shapes=[pltpu.VMEM((count, width), F32)],
        compiler_params=pltpu.CompilerParams(vmem_limit_bytes=VMEM_LIMIT),
        name="experts_first",
    )(rows_in, down_prod, gates, *gate_ws, *up_ws)


def experts_second(rows_in, grads_in, act, dgate, dup, downs):
    count, width = rows_in.shape
    parts = len(downs)
    slots, hidden, _ = downs[0].shape

    def body(x_ref, dy_ref, act_ref, dg_ref, du_ref, *refs):
        down_w = refs[:parts]
        out_ref = refs[parts]
        grads = refs[parts + 1 : 4 * parts + 1]
        acc_ref = refs[4 * parts + 1]
        s = pl.program_id(0)

        @pl.when(s == 0)
        def _():
            acc_ref[...] = jnp.zeros(acc_ref.shape, F32)

        for k in range(parts):
            acc_ref[...] += dot(act_ref[0, k], down_w[k][0], 1, 0)
            grads[3 * k][0] = dot(dg_ref[0, k], x_ref[...], 0, 0).astype(BF)
            grads[3 * k + 1][0] = dot(du_ref[0, k], x_ref[...], 0, 0).astype(BF)
            grads[3 * k + 2][0] = dot(act_ref[0, k], dy_ref[...], 0, 0).astype(BF)

        @pl.when(s == slots - 1)
        def _():
            out_ref[...] = acc_ref[...].astype(BF)

    hid_spec = pl.BlockSpec((1, parts, count, hidden), lambda s: (s, 0, 0, 0))
    grad_spec = pl.BlockSpec((1, hidden, width), lambda s: (s, 0, 0))
    grad_shape = jax.ShapeDtypeStruct((slots, hidden, width), BF)
    return pl.pallas_call(
        body,
        grid=(slots,),
        in_specs=[whole(rows_in.shape), whole(grads_in.shape), hid_spec, hid_spec, hid_spec]
        + weight_specs(parts, hidden, width, 1),
        out_specs=[whole((count, width))] + [grad_spec] * (3 * parts),
        out_shape=(jax.ShapeDtypeStruct((count, width), BF),) + (grad_shape,) * (3 * parts),
        scratch_shapes=[pltpu.VMEM((count, width), F32)],
        compiler_params=pltpu.CompilerParams(vmem_limit_bytes=VMEM_LIMIT),
        name="experts_second",
    )(rows_in, grads_in, act, dgate, dup, *downs)


def shared_own(rows, grads, gate_ws, up_ws, down_ws):
    parts = len(gate_ws)

    def body(x_ref, dy_ref, *refs):
        out_ref, dx_ref = refs[3 * parts :]
        for k in range(parts):
            gw, uw, dw = refs[k], refs[parts + k], refs[2 * parts + k]
            act, dg, du = swish_parts(
                dot(x_ref[...], gw[...], 1, 1),
                dot(x_ref[...], uw[...], 1, 1),
                dot(dy_ref[...], dw[...], 1, 1),
            )
            out = dot(act.astype(BF), dw[...], 1, 0)
            dx = dot(dg.astype(BF), gw[...], 1, 0) + dot(du.astype(BF), uw[...], 1, 0)
            if k == 0:
                out_ref[...] = out
                dx_ref[...] = dx
            else:
                out_ref[...] += out
                dx_ref[...] += dx

    shape = jax.ShapeDtypeStruct(rows.shape, F32)
    return pl.pallas_call(
        body,
        out_shape=(shape, shape),
        compiler_params=pltpu.CompilerParams(vmem_limit_bytes=VMEM_LIMIT),
        name="shared_own",
    )(rows, grads, *gate_ws, *up_ws, *down_ws)


def shared_grads(rows_in, grads_in, rows_cut, grads_cut, gate_ws, up_ws, down_ws):
    parts = len(gate_ws)
    hidden = gate_ws[0].shape[0]
    cut = rows_cut.shape[1]

    def body(x_ref, dy_ref, xc_ref, dyc_ref, *refs):
        out_ref = refs[3 * parts]
        for k in range(parts):
            act, dg, du = swish_parts(
                dot(x_ref[...], refs[k][...], 1, 1),
                dot(x_ref[...], refs[parts + k][...], 1, 1),
                dot(dy_ref[...], refs[2 * parts + k][...], 1, 1),
            )
            out_ref[k, 0] = dot(dg.astype(BF), xc_ref[...], 0, 0).astype(BF)
            out_ref[k, 1] = dot(du.astype(BF), xc_ref[...], 0, 0).astype(BF)
            out_ref[k, 2] = dot(act.astype(BF), dyc_ref[...], 0, 0).astype(BF)

    return pl.pallas_call(
        body,
        out_shape=jax.ShapeDtypeStruct((parts, 3, hidden, cut), BF),
        compiler_params=pltpu.CompilerParams(vmem_limit_bytes=VMEM_LIMIT),
        name="shared_grads",
    )(rows_in, grads_in, rows_cut, grads_cut, *gate_ws, *up_ws, *down_ws)


def project_back(back, cosine, sine, normed, wq, wk, wv, groups):
    heads = wq.shape[0]
    pw = wq.shape[2]
    hw = 2 * pw
    rows, width = normed.shape
    span = heads * hw

    def body(back_ref, cos_ref, sin_ref, norm_ref, q_ref, k_ref, v_ref, wt_ref, dx_ref, grad_ref):
        cos = cos_ref[...]
        sin = sin_ref[...]
        for h in range(heads):
            total = back_ref[h].astype(F32)
            for r in range(1, groups):
                total = total + back_ref[r * heads + h].astype(F32)
            for part in range(3):
                a = total[part * hw : part * hw + pw]
                b = total[part * hw + pw : (part + 1) * hw]
                if part < 2:
                    a, b = a * cos + b * sin, b * cos - a * sin
                at = part * span + h * hw
                grad_ref[at : at + hw] = jnp.concatenate([a, b], axis=0).astype(BF)
        wt_ref[...] = dot(norm_ref[...], grad_ref[...], 0, 1).astype(BF)
        dx = dot(grad_ref[0:span], q_ref[...], 0, 0)
        dx = dx + dot(grad_ref[span : 2 * span], k_ref[...], 0, 0)
        dx_ref[...] = (dx + dot(grad_ref[2 * span :], v_ref[...], 0, 0)).astype(BF)

    flat = (span, width)
    return pl.pallas_call(
        body,
        out_shape=(
            jax.ShapeDtypeStruct((width, 3 * span), BF),
            jax.ShapeDtypeStruct((rows, width), BF),
        ),
        scratch_shapes=[pltpu.VMEM((3 * span, rows), BF)],
        compiler_params=pltpu.CompilerParams(vmem_limit_bytes=VMEM_LIMIT),
        name="project_back",
    )(back, cosine, sine, normed, wq.reshape(flat), wk.reshape(flat), wv.reshape(flat))


def after(x, *others):
    return lax.optimization_barrier((x,) + others)[0]


def added(parts):
    total = parts[0].astype(F32)
    for p in parts[1:]:
        total = total + p.astype(F32)
    return total


def swapped(x, by, size):
    return lax.ppermute(x, "tensor", [(i, i ^ by) for i in range(size)])


def exchange(x, axis):
    return lax.all_to_all(x, axis, 0, 0, tiled=True)


def spread(x, axis):
    size = lax.axis_size(axis)
    return lax.all_to_all(
        jnp.broadcast_to(x[None], (size,) + x.shape), axis, 0, 0, tiled=True
    )


def on_device(
    tokens,
    segment_ids,
    expert_ids,
    gate_values,
    expert_slot,
    first_gain,
    second_gain,
    query_weight,
    key_weight,
    value_weight,
    output_weight,
    shared_gate,
    shared_up,
    shared_down,
    routed_gate,
    routed_up,
    routed_down,
    cotangent,
):
    rows, width = tokens.shape
    top = expert_ids.shape[1]
    experts_total = expert_slot.shape[0]
    slots_local = routed_gate.shape[0]
    blocks = lax.axis_size("expert")
    quarters = lax.axis_size("tensor")
    rank = lax.axis_index("expert")
    quarter = lax.axis_index("tensor")
    heads = query_weight.shape[0]
    pair_width = query_weight.shape[2]
    hw = 2 * pair_width
    hd = quarters * hw
    units = blocks * quarters
    groups = units // heads
    own = rows // quarters
    cut = width // blocks
    starts = query_groups(blocks, groups)
    most = max(starts[i + 1] - starts[i] for i in range(groups))
    unit_group = [min(j // heads, groups) for j in range(units)]
    unit = rank * quarters + quarter
    low_table = jnp.array([starts[g] for g in unit_group], jnp.int32)
    high_table = jnp.array([starts[g + 1] if g < groups else starts[g] for g in unit_group], jnp.int32)
    bounds = jnp.stack([low_table[unit], high_table[unit]])
    block_group = jnp.array(
        [max(g for g in range(groups) if starts[g] <= b) for b in range(blocks)], jnp.int32
    )[rank]

    seg_mine = lax.dynamic_slice_in_dim(segment_ids, rank * rows, rows)
    doc_start = jnp.sum((segment_ids[:, None] < seg_mine[None, :]).astype(jnp.int32), axis=0)
    positions = rank * rows + jnp.arange(rows, dtype=jnp.int32) - doc_start
    freq_index = quarter * pair_width + jnp.arange(pair_width, dtype=jnp.int32)
    inverse_freq = 10000.0 ** (-2.0 * freq_index.astype(F32) / HD)
    angles = inverse_freq[:, None] * positions.astype(F32)[None, :]
    cosine = jnp.cos(angles)
    sine = jnp.sin(angles)
    seg_row = segment_ids.reshape(blocks, 1, rows)
    seg_col = jnp.broadcast_to(segment_ids.reshape(blocks, rows, 1), (blocks, rows, 128))

    normed_one, send = project(
        tokens, first_gain, query_weight, key_weight, value_weight, cosine, sine, units, groups
    )
    arrived = exchange(send, BOTH).reshape(blocks, quarters, 3 * hw, rows)

    def across(x):
        return swapped(x, 2, quarters)

    def beside(x):
        return swapped(x, 1, quarters)

    out_mine = output_weight.reshape(heads, hw, width)
    out_far = across(after(out_mine, normed_one))
    gate_far = across(after(routed_gate, normed_one))
    up_far = across(after(routed_up, normed_one))
    down_far = across(after(routed_down, out_far, arrived))
    out_ws = (out_mine, beside(after(out_mine, normed_one)), out_far, beside(out_far))
    gate_ws = (routed_gate, beside(after(routed_gate, normed_one)), gate_far, beside(gate_far))
    up_ws = (routed_up, beside(after(routed_up, normed_one)), up_far, beside(up_far))
    down_ws = (routed_down, beside(after(routed_down, arrived)), down_far, beside(down_far))
    out_full = jnp.zeros((heads, quarters, hw, width), BF)
    for k in range(quarters):
        out_full = lax.dynamic_update_slice(out_full, out_ws[k][:, None], (0, quarter ^ k, 0, 0))
    out_full = out_full.reshape(heads * hd, width)

    own_tokens = lax.dynamic_slice_in_dim(tokens, quarter * own, own).astype(F32)
    own_grads = lax.dynamic_slice_in_dim(cotangent, quarter * own, own)
    own_ids = lax.dynamic_slice_in_dim(expert_ids, quarter * own, own)
    own_gates = lax.dynamic_slice_in_dim(gate_values, quarter * own, own)
    onehot = own_ids[:, :, None] == jnp.arange(experts_total, dtype=jnp.int32)
    own_slots = jnp.sum(jnp.where(onehot, expert_slot[None, None, :], 0), axis=2)
    slot_hot = own_slots[:, :, None] == jnp.arange(experts_total, dtype=jnp.int32)
    dense_gates = jnp.sum(jnp.where(slot_hot, own_gates[:, :, None], 0.0), axis=1)
    gate_send = after(dense_gates, normed_one).T.reshape(blocks, slots_local, own)
    gates_in = exchange(gate_send, "expert").transpose(0, 2, 1).reshape(blocks * own, slots_local)
    gates_in = jnp.concatenate(
        [gates_in, jnp.zeros((blocks * own, 128 - slots_local), F32)], axis=1
    )
    grads_in = spread(after(own_grads, arrived), "expert").reshape(blocks * own, width)

    attended_units, lse = attend(bounds, arrived, seg_col, seg_row, most)
    back = exchange(attended_units.reshape(units, own, hd), BOTH)
    attended_heads = lax.dynamic_slice_in_dim(back, block_group * heads, heads)
    attended = attended_heads.transpose(1, 0, 2).reshape(own, heads * hd)
    hidden_state = own_tokens + jnp.dot(attended, out_full, preferred_element_type=F32)
    second_scale = rms_scale(hidden_state)
    normed_two = (hidden_state * second_scale * second_gain).astype(BF)

    rows_in = spread(normed_two, "expert").reshape(blocks * own, width)
    shared_mine = [after(w, rows_in, down_far) for w in (shared_gate, shared_up, shared_down)]
    shared_ws = []
    for w in shared_mine:
        far = across(w)
        shared_ws.append((w, beside(w), far, beside(far)))

    total_rows = blocks * own
    step = min(total_rows, 512)
    spans = [slice(c, c + step) for c in range(0, total_rows, step)]
    firsts = []
    for c in spans:
        prod = down_products(grads_in[c], down_ws)
        firsts.append(experts_first(rows_in[c], prod, gates_in[c], gate_ws, up_ws))
    grad_rows = jnp.concatenate([f[4] for f in firsts], axis=0)
    gate_sums = jnp.concatenate([f[3] for f in firsts], axis=0)
    grad_home = exchange(grad_rows.reshape(blocks, own, width), "expert")

    rows_cut = lax.dynamic_slice_in_dim(rows_in, rank * cut, cut, axis=1)
    grads_cut = lax.dynamic_slice_in_dim(grads_in, rank * cut, cut, axis=1)
    seconds = [
        experts_second(rows_in[c], grads_in[c], f[0], f[1], f[2], down_ws)
        for c, f in zip(spans, firsts)
    ]
    out_part = jnp.concatenate([s[0] for s in seconds], axis=0)
    if len(seconds) == 1:
        parts = seconds[0][1:]
    else:
        parts = [added([s[1 + i] for s in seconds]).astype(BF) for i in range(3 * quarters)]
    grad_parts = [[parts[3 * k + m] for k in range(quarters)] for m in range(3)]
    shared_out, shared_dx = shared_own(normed_two, own_grads, *shared_ws)
    shared_parts = [
        shared_grads(rows_in[c], grads_in[c], rows_cut[c], grads_cut[c], *shared_ws) for c in spans
    ]
    shared_parts = shared_parts[0] if len(spans) == 1 else added(shared_parts).astype(BF)

    grad_home = after(grad_home, out_part, shared_dx, shared_parts)
    grad_norm_two = jnp.sum(grad_home.astype(F32), axis=0) + shared_dx
    grad_full = own_grads.astype(F32)
    grad_second, second_gain_local = norm_backward(
        grad_norm_two, hidden_state, second_scale, second_gain
    )
    grad_hidden = grad_full + grad_second
    grad_attn = grad_hidden.astype(BF)
    grad_attended = jnp.einsum(
        "td,hcd->htc", grad_attn, out_full.reshape(heads, hd, width), preferred_element_type=F32
    ).astype(BF)
    do_send = jnp.concatenate([grad_attended] * groups + [grad_attended[: units - groups * heads]], axis=0)
    do_units = exchange(do_send, BOTH).reshape(blocks, rows, hd)
    out_home = exchange(after(out_part, grad_home).reshape(blocks, own, width), "expert")

    routed = []
    for m in range(3):
        g = grad_parts[m]
        to_far = (g[2].astype(F32) + beside(g[3]).astype(F32)).astype(BF)
        routed.append(added([g[0], beside(g[1]), across(to_far)]))
    shared = added([shared_parts[0]] + [swapped(shared_parts[k], k, quarters) for k in range(1, quarters)])

    grad_units = attend_back(bounds, arrived, seg_col, seg_row, lse, do_units, most)
    back_grads = exchange(grad_units.reshape(units, 3 * hw, rows), BOTH)

    att_t = after(attended, do_units).T.reshape(heads, quarters, hw, own).transpose(1, 0, 2, 3)
    att_t = exchange(att_t, "tensor")
    attn_all = spread(after(grad_attn, do_units), "tensor").reshape(quarters, own, width)
    attn_all, att_t = lax.optimization_barrier((attn_all, att_t, grad_units))[:2]
    out_grad_t = jnp.einsum(
        "qtd,qhct->dhc", attn_all, att_t.reshape(quarters, heads, hw, own), preferred_element_type=F32
    ).astype(BF)
    out_grad = exchange(out_grad_t.reshape(blocks, cut, heads * hw), "expert")

    qkv_grad_t, grad_one_part = project_back(
        back_grads, cosine, sine, normed_one, query_weight, key_weight, value_weight, groups
    )
    grad_one = jnp.sum(
        exchange(grad_one_part.reshape(quarters, own, width), "tensor").astype(F32), axis=0
    )
    qkv_grad = exchange(qkv_grad_t.reshape(blocks, cut, 3 * heads * hw), "expert")
    first_scale = rms_scale(own_tokens)
    grad_first, first_gain_local = norm_backward(grad_one, own_tokens, first_scale, first_gain)
    input_grad = spread((grad_hidden + grad_first).astype(BF), "tensor").reshape(rows, width)

    out_home = jnp.sum(after(out_home, qkv_grad_t).astype(F32), axis=0) + shared_out
    output = spread((hidden_state + out_home).astype(BF), "tensor").reshape(rows, width)
    gate_back = exchange(
        after(gate_sums, do_units)[:, :slots_local].reshape(blocks, own, slots_local).transpose(0, 2, 1),
        "expert",
    ).reshape(experts_total, own)
    gate_grad = jnp.sum(jnp.where(slot_hot, after(gate_back, grad_units).T[:, None, :], 0.0), axis=2)
    gate_grad = spread(gate_grad, "tensor").reshape(rows, top)

    gains = jnp.stack([first_gain_local, second_gain_local]).reshape(2, blocks, cut).transpose(1, 0, 2)
    gains = jnp.broadcast_to(gains[:, None], (blocks, quarters, 2, cut)).reshape(units, 2, cut)
    gains = jnp.sum(exchange(gains, BOTH), axis=0)

    out_grad = jnp.sum(out_grad.astype(F32), axis=0)
    qkv_grad = jnp.sum(qkv_grad.astype(F32), axis=0)
    weight_shape = (heads, 2, pair_width, cut)
    qkv_rows = qkv_grad.T.reshape(3, *weight_shape)
    return (
        output,
        input_grad,
        gate_grad,
        gains[0],
        gains[1],
        qkv_rows[0],
        qkv_rows[1],
        qkv_rows[2],
        out_grad.T.reshape(weight_shape),
        shared[0],
        shared[1],
        shared[2],
        routed[0],
        routed[1],
        routed[2],
    )


def solution(mesh):
    placed = (
        P("expert", None),
        P(),
        P("expert", None),
        P("expert", None),
        P(),
        P(),
        P(),
        P(None, None, "tensor", None),
        P(None, None, "tensor", None),
        P(None, None, "tensor", None),
        P(None, None, "tensor", None),
        P("tensor", None),
        P("tensor", None),
        P("tensor", None),
        P("expert", "tensor", None),
        P("expert", "tensor", None),
        P("expert", "tensor", None),
        P("expert", None),
    )
    return jax.shard_map(
        on_device,
        mesh=mesh,
        in_specs=placed,
        out_specs=(
            P("expert", None),
            P("expert", None),
            P("expert", None),
            P("expert"),
            P("expert"),
            P(None, None, "tensor", "expert"),
            P(None, None, "tensor", "expert"),
            P(None, None, "tensor", "expert"),
            P(None, None, "tensor", "expert"),
            P("tensor", "expert"),
            P("tensor", "expert"),
            P("tensor", "expert"),
            P("expert", "tensor", None),
            P("expert", "tensor", None),
            P("expert", "tensor", None),
        ),
        check_vma=False,
    )
```

time: 2310 us -> 637 us (0.28)
  waiting for transfers between devices: 1670 us -> 301 us
  local copies, waits for them, and re-layouts: 267 us -> 48.8 us
  matrix products: 143 us -> 5.28 us
  Pallas kernels: 0 us -> 95.7 us
  other arithmetic: 81.3 us -> 33.7 us
    all_to_all x4 -> x17, waiting for transfers between devices: 874 us -> 156 us  [the longest x11 102 us: exchange(): return lax.all_to_all(x, axis, 0, 0, tiled=True)]
    psum x6 -> x0, waiting for transfers between devices: 440 us -> none  [the longest x1 206 us: on_device(): scores = lax.psum(partial_scores, 'tensor') * score_scale]
    reduce_scatter x3 -> x0, waiting for transfers between devices: 199 us -> none  [the longest x1 68 us: on_device(): lax.psum_scatter(shared_down_grad, 'expert', scatter_dimension=1, tiled=T...]
    unnamed x170 -> x93, local copies, waits for them, and re-layouts: 153 us -> 10 us
    dot_general x38 -> x3, matrix products: 143 us -> 5.28 us  [the longest x1 2.33 us: on_device(): jnp.einsum('qtd,qhct->dhc', attn_all, att_t.reshape(quarters, heads, hw,...]
    pallas_call x0 -> x9, Pallas kernels: none -> 95.7 us  [the longest x1 20.4 us: experts_first(): pl.pallas_call(body, grid=(slots,), in_specs=[whole(rows_in.shape), hid_s...]
    unnamed x17 -> x0, waiting for transfers between devices: 88.4 us -> none
    ppermute x16 -> x33, waiting for transfers between devices: 73 us -> 145 us  [swapped(): return lax.ppermute(x, 'tensor', [(i, i ^ by) for i in range(size)])]
  transfers between devices with their start and end apart: 33 -> 50, of which waited for: 21 -> 19; matrix products, arithmetic and copies ran while one was open for 15% -> 11% of each run, Pallas kernels for 0% -> 11%
where the time goes in v1:
time: 637 us; the launch traced here: 630 us
  waiting for transfers between devices  301 us (47%)
  Pallas kernels  95.7 us (15%)
  starting transfers between devices  86.2 us (14%)
  blocking collectives  57.1 us (9%)
  local copies, waits for them, and re-layouts  48.8 us (8%)
  other arithmetic  33.7 us (5%)
    ppermute x33, waiting for transfers between devices, swapped(): return lax.ppermute(x, 'tensor', [(i, i ^ by) for i in range(size)])  145 us
    all_to_all x11, waiting for transfers between devices, exchange(): return lax.all_to_all(x, axis, 0, 0, tiled=True)  102 us
    all_to_all x2, blocking collectives, exchange(): return lax.all_to_all(x, axis, 0, 0, tiled=True)  57.1 us
    all_to_all x6, waiting for transfers between devices, spread(): lax.all_to_all(jnp.broadcast_to(x[None], (size,) + x.shape), axis, 0, 0,...  54 us
    all_to_all x11, starting transfers between devices, exchange(): return lax.all_to_all(x, axis, 0, 0, tiled=True)  46.2 us
    all_to_all x6, starting transfers between devices, spread(): lax.all_to_all(jnp.broadcast_to(x[None], (size,) + x.shape), axis, 0, 0,...  23.8 us
    pallas_call x1, Pallas kernels, experts_first(): pl.pallas_call(body, grid=(slots,), in_specs=[whole(rows_in.shape), hid_s...  20.4 us
    pallas_call x1, Pallas kernels, experts_second(): pl.pallas_call(body, grid=(slots,), in_specs=[whole(rows_in.shape), whole...  18.3 us
  transfers between devices with their start and end apart: 50, of which 19 were waited for; matrix products, arithmetic and copies ran while one was open for 11% of the time, Pallas kernels for 11%

profile of v1, /device:TPU:0, one launch (start us, length us, event | category | flops | bytes accessed | tf_op | source)
XLA Modules:
  0.0 630.0 jit_solution(3411600219657545654)
XLA Ops:
  8.6 7.3 %all-to-all-start = ((bf16[32,96,256]{2,1,0:T(8,128)(2,1)}), bf16[32,96,256]{2,1,0:T(8,128)(2,1)S(1)}, u32[]{:S(2)}, u32[]{:S(2)}) async-start(bf16[32,96,256]{2,1,0:T(8,128)(2,1)} %get-tuple-element.60), calls=%async_computation | async-start | bytes 3145728 | tf_op jit(solution)/shard_map/all_to_all | solution.py:477
  18.1 35.3 %all-to-all-done = bf16[32,96,256]{2,1,0:T(8,128)(2,1)S(1)} async-done(((bf16[32,96,256]{2,1,0:T(8,128)(2,1)}), bf16[32,96,256]{2,1,0:T(8,128)(2,1)S(1)}, u32[]{:S(2)}, u32[]{:S(2)}) %all-to-all-start) | async-done | bytes 1572896 | tf_op jit(solution)/shard_map/all_to_all | solution.py:477
  60.3 9.3 %attend.1 = (bf16[8,256,128]{2,1,0:T(8,128)(2,1)}, f32[8,256,128]{2,1,0:T(8,128)}) custom-call(s32[2]{0:T(128)} %pad_add_fusion.bounds_ref, bf16[8,4,96,256]{3,2,1,0:T(8,128)(2,1)} %bitcast.119, s32[8,256,128]{2,1,0:T(8,128)} %broadcast_in_dim.60.col_ref, s32[8,1,256]{2,1,0:T(1,128)} %bitcast.144), custom_call_target="tpu_custom_call" | custom-call | tf_op jit(solution)/shard_map/attend/pallas_call | solution.py:146
  82.2 19.0 %collective-permute-done.1 = bf16[10,32,1280]{2,1,0:T(8,128)(2,1)} collective-permute-done((bf16[10,32,1280]{2,1,0:T(8,128)(2,1)}, bf16[10,32,1280]{2,1,0:T(8,128)(2,1)}, u32[]{:S(2)}, u32[]{:S(2)}) %collective-permute-start.1) | collective-permute-done | bytes 819232 | tf_op jit(solution)/shard_map/ppermute | solution.py:473
  114.3 25.3 %all-to-all-done.3 = bf16[8,64,1280]{2,1,0:T(8,128)(2,1)} async-done(((bf16[8,64,1280]{2,1,0:T(8,128)(2,1)}), bf16[8,64,1280]{2,1,0:T(8,128)(2,1)}, u32[]{:S(2)}, u32[]{:S(2)}) %all-to-all-start.3) | async-done | bytes 1310752 | tf_op jit(solution)/shard_map/all_to_all | solution.py:482
  145.7 28.7 %collective-permute-done.4.refs_2_ = bf16[2,224,1280]{2,1,0:T(8,128)(2,1)} collective-permute-done((bf16[2,224,1280]{2,1,0:T(8,128)(2,1)}, bf16[2,224,1280]{2,1,0:T(8,128)(2,1)}, u32[]{:S(2)}, u32[]{:S(2)}) %collective-permute-start.4) | collective-permute-done | bytes 1146912 | tf_op jit(solution)/shard_map/ppermute | solution.py:473
  184.4 20.4 %experts_first.1 = (bf16[2,4,512,224]{3,2,1,0:T(8,128)(2,1)}, bf16[2,4,512,224]{3,2,1,0:T(8,128)(2,1)}, bf16[2,4,512,224]{3,2,1,0:T(8,128)(2,1)}, f32[512,128]{1,0:T(8,128)}, bf16[512,1280]{1,0:T(8,128)(2,1)}) custom-call(bf16[512,1280]{1,0:T(8,128)(2,1)} %bitcast.18.x_ref, f32[2,4,512,224]{3,2,1,0:T(8,128)} %down_products.1.da_ref, ...), custom_call_target="tpu_custom_call" | custom-call | tf_op jit(solution)/shard_map/experts_first/pallas_call | solution.py:306
  213.6 13.2 %collective-permute-done.13.refs_2_ = bf16[224,1280]{1,0:T(8,128)(2,1)} collective-permute-done((bf16[224,1280]{1,0:T(8,128)(2,1)}, bf16[224,1280]{1,0:T(8,128)(2,1)}, u32[]{:S(2)}, u32[]{:S(2)}) %collective-permute-start.13) | collective-permute-done | bytes 573472 | tf_op jit(solution)/shard_map/ppermute | solution.py:473
  226.8 12.3 %collective-permute-done.16.refs_6_ = bf16[224,1280]{1,0:T(8,128)(2,1)} collective-permute-done((bf16[224,1280]{1,0:T(8,128)(2,1)}, bf16[224,1280]{1,0:T(8,128)(2,1)}, u32[]{:S(2)}, u32[]{:S(2)}) %collective-permute-start.16) | collective-permute-done | bytes 573472 | tf_op jit(solution)/shard_map/ppermute | solution.py:473
  239.1 11.1 %collective-permute-done.19.refs_10_ = bf16[224,1280]{1,0:T(8,128)(2,1)} collective-permute-done((bf16[224,1280]{1,0:T(8,128)(2,1)}, bf16[224,1280]{1,0:T(8,128)(2,1)}, u32[]{:S(2)}, u32[]{:S(2)}) %collective-permute-start.19) | collective-permute-done | bytes 573472 | tf_op jit(solution)/shard_map/ppermute | solution.py:473
  252.6 18.3 %experts_second.1 = (bf16[512,1280]{1,0:T(8,128)(2,1)}, bf16[2,224,1280]{2,1,0:T(8,128)(2,1)}, bf16[2,224,1280]{2,1,0:T(8,128)(2,1)}, bf16[2,224,1280]{2,1,0:T(8...) custom-call(bf16[512,1280]{1,0:T(8,128)(2,1)} %bitcast.18.x_ref, ...), custom_call_target="tpu_custom_call" | custom-call | tf_op jit(solution)/shard_map/experts_second/pallas_call | solution.py:354
  272.8 7.9 %shared_own.1 = (f32[64,1280]{1,0:T(8,128)}, f32[64,1280]{1,0:T(8,128)}) custom-call(bf16[64,1280]{1,0:T(8,128)(2,1)} %copy-done.11, bf16[64,1280]{1,0:T(8,128)(2,1)} %copy-done.12, bf16[224,1280]{1,0:T(8,128)(2,1)} %refs_0_.7, bf16[224,1280]{1,0:T(8,128)(2,1)} %collective-permute-done.12.refs_1_, bf16[224,1280]{1,0:T(8,128)(2,1)} %collective-permute-done.13.refs_2_, ...), custom_call_target="tpu_custom_call" | custom-call | tf_op jit(solution)/shard_map/shared_own/pallas_call | solution.py:389
  280.6 12.4 %shared_grads.1 = bf16[4,3,224,160]{3,2,1,0:T(8,128)(2,1)} custom-call(bf16[512,1280]{1,0:T(8,128)(2,1)} %bitcast.18.x_ref, bf16[512,1280]{1,0:T(8,128)(2,1)} %bitcast.19.dy_ref, bf16[512,160]{1,0:T(8,128)(2,1)} %constant_dynamic-slice_fusion.1.xc_ref, bf16[512,160]{1,0:T(8,128)(2,1)} %constant_dynamic-slice_fusion.dyc_ref, bf16[224,1280]{1,0:T(8,128)(2,1)} %refs_0_.7, ...), custom_call_target="tpu_custom_call" | custom-call | tf_op jit(solution)/shard_map/shared_grads/pallas_call | solution.py:414
  298.0 20.2 %all_to_all.95 = bf16[32,64,128]{2,1,0:T(8,128)(2,1)} all-to-all(bf16[32,64,128]{2,1,0:T(8,128)(2,1)S(1)} %pad_maximum_fusion), channel_id=1, replica_groups=mesh['expert'=8,'tensor'=4] {'expert','tensor'}, dimensions={0} | all-to-all | bytes 1048576 | tf_op jit(solution)/shard_map/all_to_all | solution.py:477
  322.4 11.4 %attend_back.1 = bf16[8,4,96,256]{3,2,1,0:T(8,128)(2,1)} custom-call(s32[2]{0:T(128)} %pad_add_fusion.bounds_ref, bf16[8,4,96,256]{3,2,1,0:T(8,128)(2,1)} %bitcast.120, s32[8,256,128]{2,1,0:T(8,128)} %broadcast_in_dim.60.col_ref, s32[8,1,256]{2,1,0:T(1,128)} %bitcast.145, f32[8,256,128]{2,1,0:T(8,128)} %get-tuple-element.81.lse_ref, ...), custom_call_target="tpu_custom_call" | custom-call | tf_op jit(solution)/shard_map/attend_back/pallas_call | solution.py:229
  354.9 10.2 %all-to-all-done.16 = bf16[4,64,1280]{2,1,0:T(8,128)(2,1)S(1)} async-done(((bf16[4,64,1280]{2,1,0:T(8,128)(2,1)}), bf16[4,64,1280]{2,1,0:T(8,128)(2,1)S(1)}, u32[]{:S(2)}, u32[]{:S(2)}) %all-to-all-start.16) | async-done | bytes 655392 | tf_op jit(solution)/shard_map/all_to_all | solution.py:482
  365.1 36.9 %all_to_all.96 = bf16[8,64,1280]{2,1,0:T(8,128)(2,1)S(1)} all-to-all(bf16[8,64,1280]{2,1,0:T(8,128)(2,1)S(1)} %bitcast.132), channel_id=1, replica_groups=mesh['expert'=8,'tensor'=4] {'expert'}, dimensions={0} | all-to-all | bytes 2621440 | tf_op jit(solution)/shard_map/all_to_all | solution.py:477
  415.3 27.2 %all-to-all-done.8.back_ref = bf16[32,96,256]{2,1,0:T(8,128)(2,1)S(1)} async-done(((bf16[32,96,256]{2,1,0:T(8,128)(2,1)}), bf16[32,96,256]{2,1,0:T(8,128)(2,1)S(1)}, u32[]{:S(2)}, u32[]{:S(2)}) %all-to-all-start.8) | async-done | bytes 1572896 | tf_op jit(solution)/shard_map/all_to_all | solution.py:477
  454.0 17.1 %all-to-all-done.18 = bf16[8,160,320]{2,1,0:T(8,128)(2,1)} async-done(((bf16[8,160,320]{2,1,0:T(8,128)(2,1)}), bf16[8,160,320]{2,1,0:T(8,128)(2,1)}, u32[]{:S(2)}, u32[]{:S(2)}) %all-to-all-start.18) | async-done | bytes 819232 | tf_op jit(solution)/shard_map/all_to_all | solution.py:477
  474.6 10.1 %all-to-all-done.10 = bf16[4,64,1280]{2,1,0:T(8,128)(2,1)S(1)} async-done(((bf16[4,64,1280]{2,1,0:T(8,128)(2,1)}), bf16[4,64,1280]{2,1,0:T(8,128)(2,1)S(1)}, u32[]{:S(2)}, u32[]{:S(2)}) %all-to-all-start.10) | async-done | bytes 655392 | tf_op jit(solution)/shard_map/all_to_all | solution.py:477
  489.7 9.7 %all-to-all-done.9 = bf16[4,64,1280]{2,1,0:T(8,128)(2,1)S(1)} async-done(((bf16[4,64,1280]{2,1,0:T(8,128)(2,1)}), bf16[4,64,1280]{2,1,0:T(8,128)(2,1)S(1)}, u32[]{:S(2)}, u32[]{:S(2)}) %all-to-all-start.9) | async-done | bytes 655392 | tf_op jit(solution)/shard_map/all_to_all | solution.py:482
  540.1 24.5 %collective-permute-done.23 = bf16[3,224,160]{2,1,0:T(8,128)(2,1)S(1)} collective-permute-done((bf16[3,224,160]{2,1,0:T(8,128)(2,1)S(1)}, bf16[3,224,160]{2,1,0:T(8,128)(2,1)S(1)}, u32[]{:S(2)}, u32[]{:S(2)}) %collective-permute-start.23) | collective-permute-done | bytes 215072 | tf_op jit(solution)/shard_map/ppermute | solution.py:473
  576.7 15.4 %collective-permute-done.29 = bf16[2,224,1280]{2,1,0:T(8,128)(2,1)} collective-permute-done((bf16[2,224,1280]{2,1,0:T(8,128)(2,1)}, bf16[2,224,1280]{2,1,0:T(8,128)(2,1)}, u32[]{:S(2)}, u32[]{:S(2)}) %collective-permute-start.29) | collective-permute-done | bytes 1146912 | tf_op jit(solution)/shard_map/ppermute | solution.py:473
  595.6 21.0 %collective-permute-done.26 = bf16[2,224,1280]{2,1,0:T(8,128)(2,1)S(1)} collective-permute-done((bf16[2,224,1280]{2,1,0:T(8,128)(2,1)}, bf16[2,224,1280]{2,1,0:T(8,128)(2,1)S(1)}, u32[]{:S(2)}, u32[]{:S(2)}) %collective-permute-start.26) | collective-permute-done | bytes 1146912 | tf_op jit(solution)/shard_map/ppermute | solution.py:473
  (266 shorter events, 203.6 us)
Async XLA Ops:
  8.6 44.8 %all-to-all-start = ((bf16[32,96,256]{2,1,0:T(8,128)(2,1)}), bf16[32,96,256]{2,1,0:T(8,128)(2,1)S(1)}, u32[]{:S(2)}, u32[]{:S(2)}) async-start(bf16[32,96,256]{2,1,0:T(8,128)(2,1)} %get-tuple-element.60), calls=%async_computation | async-start | bytes 3145728 | tf_op jit(solution)/shard_map/all_to_all | solution.py:477
  69.6 31.6 %all-to-all-start.1 = ((bf16[32,64,128]{2,1,0:T(8,128)(2,1)}), bf16[32,64,128]{2,1,0:T(8,128)(2,1)}, u32[]{:S(2)}, u32[]{:S(2)}) async-start(bf16[32,64,128]{2,1,0:T(8,128)(2,1)} %bitcast.138), calls=%async_computation.1 | async-start | bytes 1048576 | tf_op jit(solution)/shard_map/all_to_all | solution.py:477
  76.4 98.0 %collective-permute-start.10 = (bf16[2,224,1280]{2,1,0:T(8,128)(2,1)}, bf16[2,224,1280]{2,1,0:T(8,128)(2,1)}, u32[]{:S(2)}, u32[]{:S(2)}) collective-permute-start(bf16[2,224,1280]{2,1,0:T(8,128)(2,1)} %refs_4_.1), channel_id=1, source_target_pairs={{0,2},{1,3},{2,0},{3,1},{4,6},{5,7},{6,4},{7,5},{8,10},{9,11},{10,... | collective-permute-start | bytes 3440648 | tf_op jit(solution)/shard_map/ppermute | solution.py:473
  76.7 98.1 %collective-permute-start.7 = (bf16[2,224,1280]{2,1,0:T(8,128)(2,1)}, bf16[2,224,1280]{2,1,0:T(8,128)(2,1)}, u32[]{:S(2)}, u32[]{:S(2)}) collective-permute-start(bf16[2,224,1280]{2,1,0:T(8,128)(2,1)} %refs_0_.4), channel_id=1, source_target_pairs={{0,2},{1,3},{2,0},{3,1},{4,6},{5,7},{6,4},{7,5},{8,10},{9,11},{10,... | collective-permute-start | bytes 3440648 | tf_op jit(solution)/shard_map/ppermute | solution.py:473
  102.3 37.3 %all-to-all-start.3 = ((bf16[8,64,1280]{2,1,0:T(8,128)(2,1)}), bf16[8,64,1280]{2,1,0:T(8,128)(2,1)}, u32[]{:S(2)}, u32[]{:S(2)}) async-start(bf16[8,64,1280]{2,1,0:T(8,128)(2,1)} %broadcast_in_dim.66), calls=%async_computation.3 | async-start | bytes 2621440 | tf_op jit(solution)/shard_map/all_to_all | solution.py:482
  111.1 63.2 %collective-permute-start.4 = (bf16[2,224,1280]{2,1,0:T(8,128)(2,1)}, bf16[2,224,1280]{2,1,0:T(8,128)(2,1)}, u32[]{:S(2)}, u32[]{:S(2)}) collective-permute-start(bf16[2,224,1280]{2,1,0:T(8,128)(2,1)} %refs_0_.5), channel_id=1, source_target_pairs={{0,2},{1,3},{2,0},{3,1},{4,6},{5,7},{6,4},{7,5},{8,10},{9,11},{10,... | collective-permute-start | bytes 3440648 | tf_op jit(solution)/shard_map/ppermute | solution.py:473
  111.6 63.3 %collective-permute-start.3 = (bf16[2,224,1280]{2,1,0:T(8,128)(2,1)}, bf16[2,224,1280]{2,1,0:T(8,128)(2,1)}, u32[]{:S(2)}, u32[]{:S(2)}) collective-permute-start(bf16[2,224,1280]{2,1,0:T(8,128)(2,1)} %refs_0_.5), channel_id=1, source_target_pairs={{0,1},{1,0},{2,3},{3,2},{4,5},{5,4},{6,7},{7,6},{8,9},{9,8},{10,11... | collective-permute-start | bytes 3440648 | tf_op jit(solution)/shard_map/ppermute | solution.py:473
  140.8 43.6 %all-to-all-start.2 = ((bf16[8,64,1280]{2,1,0:T(8,128)(2,1)}), bf16[8,64,1280]{2,1,0:T(8,128)(2,1)}, u32[]{:S(2)}, u32[]{:S(2)}) async-start(bf16[8,64,1280]{2,1,0:T(8,128)(2,1)} %broadcast_in_dim.65), calls=%async_computation.2 | async-start | bytes 2621440 | tf_op jit(solution)/shard_map/all_to_all | solution.py:482
  145.6 38.7 %collective-permute-start.6 = (bf16[2,224,1280]{2,1,0:T(8,128)(2,1)}, bf16[2,224,1280]{2,1,0:T(8,128)(2,1)}, u32[]{:S(2)}, u32[]{:S(2)}) collective-permute-start(bf16[2,224,1280]{2,1,0:T(8,128)(2,1)} %refs_0_.4), channel_id=1, source_target_pairs={{0,1},{1,0},{2,3},{3,2},{4,5},{5,4},{6,7},{7,6},{8,9},{9,8},{10,11... | collective-permute-start | bytes 3440648 | tf_op jit(solution)/shard_map/ppermute | solution.py:473
  204.8 88.3 %all-to-all-start.5 = ((bf16[8,64,1280]{2,1,0:T(8,128)(2,1)}), bf16[8,64,1280]{2,1,0:T(8,128)(2,1)}, u32[]{:S(2)}, u32[]{:S(2)}) async-start(bf16[8,64,1280]{2,1,0:T(8,128)(2,1)} %bitcast.133), calls=%async_computation.5 | async-start | bytes 2621440 | tf_op jit(solution)/shard_map/all_to_all | solution.py:477
  212.6 37.6 %collective-permute-start.19 = (bf16[224,1280]{1,0:T(8,128)(2,1)}, bf16[224,1280]{1,0:T(8,128)(2,1)}, u32[]{:S(2)}, u32[]{:S(2)}) collective-permute-start(bf16[224,1280]{1,0:T(8,128)(2,1)} %refs_8_.1), channel_id=1, source_target_pairs={{0,2},{1,3},{2,0},{3,1},{4,6},{5,7},{6,4},{7,5},{8,10},{9,11},{10,... | collective-permute-start | bytes 1720328 | tf_op jit(solution)/shard_map/ppermute | solution.py:473
  213.1 37.1 %collective-permute-start.12 = (bf16[224,1280]{1,0:T(8,128)(2,1)}, bf16[224,1280]{1,0:T(8,128)(2,1)}, u32[]{:S(2)}, u32[]{:S(2)}) collective-permute-start(bf16[224,1280]{1,0:T(8,128)(2,1)} %refs_0_.7), channel_id=1, source_target_pairs={{0,1},{1,0},{2,3},{3,2},{4,5},{5,4},{6,7},{7,6},{8,9},{9,8},{10,11... | collective-permute-start | bytes 1720328 | tf_op jit(solution)/shard_map/ppermute | solution.py:473
  213.1 59.7 %collective-permute-start.15 = (bf16[224,1280]{1,0:T(8,128)(2,1)}, bf16[224,1280]{1,0:T(8,128)(2,1)}, u32[]{:S(2)}, u32[]{:S(2)}) collective-permute-start(bf16[224,1280]{1,0:T(8,128)(2,1)} %refs_4_.3), channel_id=1, source_target_pairs={{0,1},{1,0},{2,3},{3,2},{4,5},{5,4},{6,7},{7,6},{8,9},{9,8},{10,11... | collective-permute-start | bytes 1720328 | tf_op jit(solution)/shard_map/ppermute | solution.py:473
  226.8 46.0 %collective-permute-start.18 = (bf16[224,1280]{1,0:T(8,128)(2,1)}, bf16[224,1280]{1,0:T(8,128)(2,1)}, u32[]{:S(2)}, u32[]{:S(2)}) collective-permute-start(bf16[224,1280]{1,0:T(8,128)(2,1)} %refs_8_.1), channel_id=1, source_target_pairs={{0,1},{1,0},{2,3},{3,2},{4,5},{5,4},{6,7},{7,6},{8,9},{9,8},{10,11... | collective-permute-start | bytes 1720328 | tf_op jit(solution)/shard_map/ppermute | solution.py:473
  239.1 33.7 %collective-permute-start.14 = (bf16[224,1280]{1,0:T(8,128)(2,1)}, bf16[224,1280]{1,0:T(8,128)(2,1)}, u32[]{:S(2)}, u32[]{:S(2)}) collective-permute-start(bf16[224,1280]{1,0:T(8,128)(2,1)} %collective-permute-done.13.refs_2_), channel_id=1, source_target_pairs={{0,1},{1,0},{2,3},{3,2},{4,5},{5,4},{6,7},{7,6},{8,9},{9,8},{10,11... | collective-permute-start | bytes 1720328 | tf_op jit(solution)/shard_map/ppermute | solution.py:473
  402.0 40.5 %all-to-all-start.8 = ((bf16[32,96,256]{2,1,0:T(8,128)(2,1)}), bf16[32,96,256]{2,1,0:T(8,128)(2,1)S(1)}, u32[]{:S(2)}, u32[]{:S(2)}) async-start(bf16[32,96,256]{2,1,0:T(8,128)(2,1)} %bitcast.30), calls=%async_computation.8 | async-start | bytes 3145728 | tf_op jit(solution)/shard_map/all_to_all | solution.py:477
  447.4 69.7 %collective-permute-start.31 = (bf16[2,224,1280]{2,1,0:T(8,128)(2,1)}, bf16[2,224,1280]{2,1,0:T(8,128)(2,1)}, u32[]{:S(2)}, u32[]{:S(2)}) collective-permute-start(bf16[2,224,1280]{2,1,0:T(8,128)(2,1)} %get-tuple-element.104), channel_id=1, source_target_pairs={{0,1},{1,0},{2,3},{3,2},{4,5},{5,4},{6,7},{7,6},{8,9},{9,8},{10,11... | collective-permute-start | bytes 3440648 | tf_op jit(solution)/shard_map/ppermute | solution.py:473
  447.4 85.1 %collective-permute-start.28 = (bf16[2,224,1280]{2,1,0:T(8,128)(2,1)}, bf16[2,224,1280]{2,1,0:T(8,128)(2,1)}, u32[]{:S(2)}, u32[]{:S(2)}) collective-permute-start(bf16[2,224,1280]{2,1,0:T(8,128)(2,1)} %get-tuple-element.100), channel_id=1, source_target_pairs={{0,1},{1,0},{2,3},{3,2},{4,5},{5,4},{6,7},{7,6},{8,9},{9,8},{10,11... | collective-permute-start | bytes 3440648 | tf_op jit(solution)/shard_map/ppermute | solution.py:473
  515.2 57.0 %collective-permute-start.30 = (bf16[2,224,1280]{2,1,0:T(8,128)(2,1)}, bf16[2,224,1280]{2,1,0:T(8,128)(2,1)}, u32[]{:S(2)}, u32[]{:S(2)}) collective-permute-start(bf16[2,224,1280]{2,1,0:T(8,128)(2,1)} %get-tuple-element.102), channel_id=1, source_target_pairs={{0,1},{1,0},{2,3},{3,2},{4,5},{5,4},{6,7},{7,6},{8,9},{9,8},{10,11... | collective-permute-start | bytes 3440648 | tf_op jit(solution)/shard_map/ppermute | solution.py:473
  525.9 98.9 %all-to-all-start.15 = ((bf16[8,160,960]{2,1,0:T(8,128)(2,1)}), bf16[8,160,960]{2,1,0:T(8,128)(2,1)S(1)}, u32[]{:S(2)}, u32[]{:S(2)}) async-start(bf16[8,160,960]{2,1,0:T(8,128)(2,1)} %bitcast.128), calls=%async_computation.15 | async-start | bytes 5242880 | tf_op jit(solution)/shard_map/all_to_all | solution.py:477
  532.5 40.4 %collective-permute-start.32 = (bf16[2,224,1280]{2,1,0:T(8,128)(2,1)}, bf16[2,224,1280]{2,1,0:T(8,128)(2,1)}, u32[]{:S(2)}, u32[]{:S(2)}) collective-permute-start(bf16[2,224,1280]{2,1,0:T(8,128)(2,1)} %add_convert_fusion), channel_id=1, source_target_pairs={{0,2},{1,3},{2,0},{3,1},{4,6},{5,7},{6,4},{7,5},{8,10},{9,11},{10,... | collective-permute-start | bytes 3440648 | tf_op jit(solution)/shard_map/ppermute | solution.py:473
  538.2 38.6 %collective-permute-start.27 = (bf16[2,224,1280]{2,1,0:T(8,128)(2,1)}, bf16[2,224,1280]{2,1,0:T(8,128)(2,1)}, u32[]{:S(2)}, u32[]{:S(2)}) collective-permute-start(bf16[2,224,1280]{2,1,0:T(8,128)(2,1)} %get-tuple-element.98), channel_id=1, source_target_pairs={{0,1},{1,0},{2,3},{3,2},{4,5},{5,4},{6,7},{7,6},{8,9},{9,8},{10,11... | collective-permute-start | bytes 3440648 | tf_op jit(solution)/shard_map/ppermute | solution.py:473
  540.0 55.6 %collective-permute-start.24 = (bf16[2,224,1280]{2,1,0:T(8,128)(2,1)}, bf16[2,224,1280]{2,1,0:T(8,128)(2,1)}, u32[]{:S(2)}, u32[]{:S(2)}) collective-permute-start(bf16[2,224,1280]{2,1,0:T(8,128)(2,1)} %get-tuple-element.94), channel_id=1, source_target_pairs={{0,1},{1,0},{2,3},{3,2},{4,5},{5,4},{6,7},{7,6},{8,9},{9,8},{10,11... | collective-permute-start | bytes 3440648 | tf_op jit(solution)/shard_map/ppermute | solution.py:473
  572.2 44.4 %collective-permute-start.26 = (bf16[2,224,1280]{2,1,0:T(8,128)(2,1)}, bf16[2,224,1280]{2,1,0:T(8,128)(2,1)S(1)}, u32[]{:S(2)}, u32[]{:S(2)}) collective-permute-start(bf16[2,224,1280]{2,1,0:T(8,128)(2,1)} %add_convert_fusion.2), channel_id=1, source_target_pairs={{0,2},{1,3},{2,0},{3,1},{4,6},{5,7},{6,4},{7,5},{8,10},{9,11},{10,... | collective-permute-start | bytes 3440648 | tf_op jit(solution)/shard_map/ppermute | solution.py:473
  (66 other events, 1066.8 us)

commit v2 on v1

--- a/solution.py
+++ b/solution.py
@@ -265,14 +265,15 @@
     return swish * u, da * u * (sig * (1.0 + g * (1.0 - sig))), da * swish
 
 
-def experts_first(rows_in, down_prod, gates, gate_ws, up_ws):
+def experts_first(rows_in, down_prod, gates, gate_ws, up_ws, own):
     count, width = rows_in.shape
     parts = len(gate_ws)
     slots, hidden, _ = gate_ws[0].shape
 
     def body(x_ref, da_ref, gate_ref, *refs):
         gate_w, up_w = refs[:parts], refs[parts : 2 * parts]
-        act_ref, dg_ref, du_ref, gg_ref, dx_ref, acc_ref = refs[2 * parts :]
+        act_ref, dg_ref, du_ref, gg_ref = refs[2 * parts : 2 * parts + 4]
+        dx_refs, acc_ref = refs[2 * parts + 4 : -1], refs[-1]
         s = pl.program_id(0)
         x = x_ref[...]
         lane = lax.broadcasted_iota(jnp.int32, (count, 128), 1)
@@ -299,7 +300,8 @@
 
         @pl.when(s == slots - 1)
         def _():
-            dx_ref[...] = acc_ref[...].astype(BF)
+            for b, dx_ref in enumerate(dx_refs):
+                dx_ref[...] = acc_ref[b * own : (b + 1) * own].astype(BF)
 
     hid = jax.ShapeDtypeStruct((slots, parts, count, hidden), BF)
     hid_spec = pl.BlockSpec((1, parts, count, hidden), lambda s: (s, 0, 0, 0))
@@ -308,30 +310,32 @@
         grid=(slots,),
         in_specs=[whole(rows_in.shape), hid_spec, whole(gates.shape)]
         + weight_specs(parts, hidden, width, 2),
-        out_specs=[hid_spec, hid_spec, hid_spec, whole((count, 128)), whole((count, width))],
+        out_specs=[hid_spec, hid_spec, hid_spec, whole((count, 128))]
+        + [whole((own, width))] * (count // own),
         out_shape=(
             hid,
             hid,
             hid,
             jax.ShapeDtypeStruct((count, 128), F32),
-            jax.ShapeDtypeStruct((count, width), BF),
-        ),
+        )
+        + (jax.ShapeDtypeStruct((own, width), BF),) * (count // own),
         scratch_shapes=[pltpu.VMEM((count, width), F32)],
         compiler_params=pltpu.CompilerParams(vmem_limit_bytes=VMEM_LIMIT),
         name="experts_first",
     )(rows_in, down_prod, gates, *gate_ws, *up_ws)
 
 
-def experts_second(rows_in, grads_in, act, dgate, dup, downs):
+def experts_second(rows_in, grads_in, act, dgate, dup, downs, own):
     count, width = rows_in.shape
     parts = len(downs)
     slots, hidden, _ = downs[0].shape
+    outs = count // own
 
     def body(x_ref, dy_ref, act_ref, dg_ref, du_ref, *refs):
         down_w = refs[:parts]
-        out_ref = refs[parts]
-        grads = refs[parts + 1 : 4 * parts + 1]
-        acc_ref = refs[4 * parts + 1]
+        out_refs = refs[parts : parts + outs]
+        grads = refs[parts + outs : -1]
+        acc_ref = refs[-1]
         s = pl.program_id(0)
 
         @pl.when(s == 0)
@@ -346,7 +350,8 @@
 
         @pl.when(s == slots - 1)
         def _():
-            out_ref[...] = acc_ref[...].astype(BF)
+            for b, out_ref in enumerate(out_refs):
+                out_ref[...] = acc_ref[b * own : (b + 1) * own].astype(BF)
 
     hid_spec = pl.BlockSpec((1, parts, count, hidden), lambda s: (s, 0, 0, 0))
     grad_spec = pl.BlockSpec((1, hidden, width), lambda s: (s, 0, 0))
@@ -356,8 +361,8 @@
         grid=(slots,),
         in_specs=[whole(rows_in.shape), whole(grads_in.shape), hid_spec, hid_spec, hid_spec]
         + weight_specs(parts, hidden, width, 1),
-        out_specs=[whole((count, width))] + [grad_spec] * (3 * parts),
-        out_shape=(jax.ShapeDtypeStruct((count, width), BF),) + (grad_shape,) * (3 * parts),
+        out_specs=[whole((own, width))] * outs + [grad_spec] * (3 * parts),
+        out_shape=(jax.ShapeDtypeStruct((own, width), BF),) * outs + (grad_shape,) * (3 * parts),
         scratch_shapes=[pltpu.VMEM((count, width), F32)],
         compiler_params=pltpu.CompilerParams(vmem_limit_bytes=VMEM_LIMIT),
         name="experts_second",
@@ -419,14 +424,62 @@
     )(rows_in, grads_in, rows_cut, grads_cut, *gate_ws, *up_ws, *down_ws)
 
 
-def project_back(back, cosine, sine, normed, wq, wk, wv, groups):
+def store_chunks(place_ref, value, low_ref, high_ref):
+    half, cut, _ = low_ref.shape
+    for c in range(half):
+        first = value[2 * c * cut : (2 * c + 1) * cut]
+        second = value[(2 * c + 1) * cut : (2 * c + 2) * cut]
+        at = place_ref[0] ^ c
+        even = place_ref[1] == 0
+        low_ref[at] = jnp.where(even, first, second).astype(BF)
+        high_ref[at] = jnp.where(even, second, first).astype(BF)
+
+
+def output_grads(place, attn_parts, att_parts, heads, hw, blocks):
+    parts = len(attn_parts)
+    own, width = attn_parts[0].shape
+    span = heads * hw
+    full = att_parts[0].shape[1]
+    hd = full // heads
+
+    def body(place_ref, *refs):
+        low_ref, high_ref = refs[2 * parts :]
+        attn = jnp.concatenate([r[...] for r in refs[:parts]], axis=0)
+        att = jnp.concatenate([r[...] for r in refs[parts : 2 * parts]], axis=0)
+        row = lax.broadcasted_iota(jnp.int32, (full, span), 0)
+        col = lax.broadcasted_iota(jnp.int32, (full, span), 1)
+        source = (col // hw) * hd + place_ref[2] * hw + col % hw
+        pick = jnp.where(row == source, 1.0, 0.0).astype(BF)
+        mine = dot(att, pick, 1, 0).astype(BF)
+        store_chunks(place_ref, dot(attn, mine, 0, 0), low_ref, high_ref)
+
+    shape = (blocks // 2, width // blocks, span)
+    return pl.pallas_call(
+        body,
+        grid_spec=pltpu.PrefetchScalarGridSpec(
+            num_scalar_prefetch=1,
+            grid=(1,),
+            in_specs=[whole((own, width))] * parts + [whole((own, full))] * parts,
+            out_specs=[whole(shape)] * 2,
+        ),
+        out_shape=(jax.ShapeDtypeStruct(shape, BF),) * 2,
+        compiler_params=pltpu.CompilerParams(vmem_limit_bytes=VMEM_LIMIT),
+        name="output_grads",
+    )(place, *attn_parts, *att_parts)
+
+
+def project_back(place, back, cosine, sine, normed, wq, wk, wv, groups, blocks, quarters):
     heads = wq.shape[0]
     pw = wq.shape[2]
     hw = 2 * pw
     rows, width = normed.shape
+    own = rows // quarters
     span = heads * hw
 
-    def body(back_ref, cos_ref, sin_ref, norm_ref, q_ref, k_ref, v_ref, wt_ref, dx_ref, grad_ref):
+    def body(place_ref, back_ref, cos_ref, sin_ref, norm_ref, q_ref, k_ref, v_ref, *refs):
+        dx_ref = refs[0]
+        chunk_refs = refs[1:-1]
+        grad_ref = refs[-1]
         cos = cos_ref[...]
         sin = sin_ref[...]
         for h in range(heads):
@@ -440,22 +493,39 @@
                     a, b = a * cos + b * sin, b * cos - a * sin
                 at = part * span + h * hw
                 grad_ref[at : at + hw] = jnp.concatenate([a, b], axis=0).astype(BF)
-        wt_ref[...] = dot(norm_ref[...], grad_ref[...], 0, 1).astype(BF)
+        for part in range(3):
+            value = dot(norm_ref[...], grad_ref[part * span : (part + 1) * span], 0, 1)
+            store_chunks(place_ref, value, chunk_refs[2 * part], chunk_refs[2 * part + 1])
         dx = dot(grad_ref[0:span], q_ref[...], 0, 0)
         dx = dx + dot(grad_ref[span : 2 * span], k_ref[...], 0, 0)
-        dx_ref[...] = (dx + dot(grad_ref[2 * span :], v_ref[...], 0, 0)).astype(BF)
+        dx = dx + dot(grad_ref[2 * span :], v_ref[...], 0, 0)
+        for j in range(quarters):
+            dx_ref[place_ref[2] ^ j] = dx[j * own : (j + 1) * own].astype(BF)
 
     flat = (span, width)
-    return pl.pallas_call(
-        body,
-        out_shape=(
-            jax.ShapeDtypeStruct((width, 3 * span), BF),
-            jax.ShapeDtypeStruct((rows, width), BF),
+    chunk = (blocks // 2, width // blocks, span)
+    return pl.pallas_call(
+        body,
+        grid_spec=pltpu.PrefetchScalarGridSpec(
+            num_scalar_prefetch=1,
+            grid=(1,),
+            in_specs=[
+                whole(back.shape),
+                whole(cosine.shape),
+                whole(sine.shape),
+                whole(normed.shape),
+                whole(flat),
+                whole(flat),
+                whole(flat),
+            ],
+            out_specs=[whole((quarters, own, width))] + [whole(chunk)] * 6,
+            scratch_shapes=[pltpu.VMEM((3 * span, rows), BF)],
         ),
-        scratch_shapes=[pltpu.VMEM((3 * span, rows), BF)],
+        out_shape=(jax.ShapeDtypeStruct((quarters, own, width), BF),)
+        + (jax.ShapeDtypeStruct(chunk, BF),) * 6,
         compiler_params=pltpu.CompilerParams(vmem_limit_bytes=VMEM_LIMIT),
         name="project_back",
-    )(back, cosine, sine, normed, wq.reshape(flat), wk.reshape(flat), wv.reshape(flat))
+    )(place, back, cosine, sine, normed, wq.reshape(flat), wk.reshape(flat), wv.reshape(flat))
 
 
 def after(x, *others):
@@ -469,19 +539,44 @@
     return total
 
 
-def swapped(x, by, size):
-    return lax.ppermute(x, "tensor", [(i, i ^ by) for i in range(size)])
+def flip(x, by, axis):
+    size = lax.axis_size(axis)
+    return lax.ppermute(x, axis, [(i, i ^ by) for i in range(size)])
 
 
 def exchange(x, axis):
     return lax.all_to_all(x, axis, 0, 0, tiled=True)
 
 
-def spread(x, axis):
-    size = lax.axis_size(axis)
-    return lax.all_to_all(
-        jnp.broadcast_to(x[None], (size,) + x.shape), axis, 0, 0, tiled=True
-    )
+def even_blocks(x):
+    size = lax.axis_size("expert")
+    return [x] + [flip(x, m, "expert") for m in range(2, size, 2)]
+
+
+def odd_blocks(evens):
+    return [flip(x, 1, "expert") for x in evens]
+
+
+def paired(evens, odds):
+    return [
+        (a.astype(F32) + flip(b, 1, "expert").astype(F32)).astype(BF) for a, b in zip(evens, odds)
+    ]
+
+
+def collected(sums):
+    return added([sums[0]] + [flip(sums[j], 2 * j, "expert") for j in range(1, len(sums))])
+
+
+def of_quarters(x):
+    quarters = lax.axis_size("tensor")
+    return [x] + [flip(x, k, "tensor") for k in range(1, quarters)]
+
+
+def in_order(parts, quarter):
+    out = jnp.zeros((len(parts),) + parts[0].shape, parts[0].dtype)
+    for k, p in enumerate(parts):
+        out = lax.dynamic_update_slice(out, p[None], (quarter ^ k,) + (0,) * p.ndim)
+    return out.reshape((-1,) + parts[0].shape[1:])
 
 
 def on_device(
@@ -548,20 +643,22 @@
     arrived = exchange(send, BOTH).reshape(blocks, quarters, 3 * hw, rows)
 
     def across(x):
-        return swapped(x, 2, quarters)
+        return flip(x, 2, "tensor")
 
     def beside(x):
-        return swapped(x, 1, quarters)
-
-    out_mine = output_weight.reshape(heads, hw, width)
-    out_far = across(after(out_mine, normed_one))
-    gate_far = across(after(routed_gate, normed_one))
-    up_far = across(after(routed_up, normed_one))
-    down_far = across(after(routed_down, out_far, arrived))
-    out_ws = (out_mine, beside(after(out_mine, normed_one)), out_far, beside(out_far))
-    gate_ws = (routed_gate, beside(after(routed_gate, normed_one)), gate_far, beside(gate_far))
-    up_ws = (routed_up, beside(after(routed_up, normed_one)), up_far, beside(up_far))
-    down_ws = (routed_down, beside(after(routed_down, arrived)), down_far, beside(down_far))
+        return flip(x, 1, "tensor")
+
+    def all_quarters(x, far):
+        return (x, beside(x), far, beside(far))
+
+    out_mine = after(output_weight.reshape(heads, hw, width), normed_one)
+    out_far = across(out_mine)
+    gate_mine = after(routed_gate, out_far)
+    gate_far = across(gate_mine)
+    arrived = after(arrived, out_far)
+    up_mine = after(routed_up, arrived)
+    up_far = across(up_mine)
+    out_ws = all_quarters(out_mine, out_far)
     out_full = jnp.zeros((heads, quarters, hw, width), BF)
     for k in range(quarters):
         out_full = lax.dynamic_update_slice(out_full, out_ws[k][:, None], (0, quarter ^ k, 0, 0))
@@ -575,27 +672,37 @@
     own_slots = jnp.sum(jnp.where(onehot, expert_slot[None, None, :], 0), axis=2)
     slot_hot = own_slots[:, :, None] == jnp.arange(experts_total, dtype=jnp.int32)
     dense_gates = jnp.sum(jnp.where(slot_hot, own_gates[:, :, None], 0.0), axis=1)
-    gate_send = after(dense_gates, normed_one).T.reshape(blocks, slots_local, own)
-    gates_in = exchange(gate_send, "expert").transpose(0, 2, 1).reshape(blocks * own, slots_local)
+    own_grads, dense_gates = lax.optimization_barrier((own_grads, dense_gates, arrived))[:2]
+    index = jnp.arange(blocks, dtype=jnp.int32)
+    half = blocks // 2
+    distance = jnp.where(index < half, 2 * index, 2 * (index - half) + 1)
+    gates_in = exchange(dense_gates.T.reshape(blocks, slots_local, own), "expert")
+    gates_in = gates_in[rank ^ distance].transpose(0, 2, 1).reshape(blocks * own, slots_local)
     gates_in = jnp.concatenate(
         [gates_in, jnp.zeros((blocks * own, 128 - slots_local), F32)], axis=1
     )
-    grads_in = spread(after(own_grads, arrived), "expert").reshape(blocks * own, width)
+    grads_even = even_blocks(own_grads)
 
     attended_units, lse = attend(bounds, arrived, seg_col, seg_row, most)
+    down_mine = after(routed_down, attended_units)
+    down_far = across(down_mine)
+    gate_ws = all_quarters(gate_mine, gate_far)
+    up_ws = all_quarters(up_mine, up_far)
+    down_ws = all_quarters(down_mine, down_far)
     back = exchange(attended_units.reshape(units, own, hd), BOTH)
+    back = after(back, out_full, gate_far, *grads_even)
+    grads_in = jnp.concatenate(grads_even + odd_blocks(grads_even), axis=0)
     attended_heads = lax.dynamic_slice_in_dim(back, block_group * heads, heads)
     attended = attended_heads.transpose(1, 0, 2).reshape(own, heads * hd)
     hidden_state = own_tokens + jnp.dot(attended, out_full, preferred_element_type=F32)
     second_scale = rms_scale(hidden_state)
     normed_two = (hidden_state * second_scale * second_gain).astype(BF)
 
-    rows_in = spread(normed_two, "expert").reshape(blocks * own, width)
-    shared_mine = [after(w, rows_in, down_far) for w in (shared_gate, shared_up, shared_down)]
-    shared_ws = []
-    for w in shared_mine:
-        far = across(w)
-        shared_ws.append((w, beside(w), far, beside(far)))
+    rows_even = even_blocks(normed_two)
+    rows_in = jnp.concatenate(rows_even + odd_blocks(rows_even), axis=0)
+    shared_mine = [after(w, rows_in) for w in (shared_gate, shared_up, shared_down)]
+    shared_far = [across(w) for w in shared_mine]
+    shared_ws = [all_quarters(w, far) for w, far in zip(shared_mine, shared_far)]
 
     total_rows = blocks * own
     step = min(total_rows, 512)
@@ -603,31 +710,36 @@
     firsts = []
     for c in spans:
         prod = down_products(grads_in[c], down_ws)
-        firsts.append(experts_first(rows_in[c], prod, gates_in[c], gate_ws, up_ws))
-    grad_rows = jnp.concatenate([f[4] for f in firsts], axis=0)
+        firsts.append(experts_first(rows_in[c], prod, gates_in[c], gate_ws, up_ws, own))
+    grad_rows = [x for f in firsts for x in f[4:]]
     gate_sums = jnp.concatenate([f[3] for f in firsts], axis=0)
-    grad_home = exchange(grad_rows.reshape(blocks, own, width), "expert")
+    grad_home = [grad_rows[0]]
+    for p in range(1, blocks):
+        m = 2 * p if p < half else 2 * (p - half) + 1
+        grad_home.append(flip(grad_rows[p], m, "expert"))
 
     rows_cut = lax.dynamic_slice_in_dim(rows_in, rank * cut, cut, axis=1)
     grads_cut = lax.dynamic_slice_in_dim(grads_in, rank * cut, cut, axis=1)
-    seconds = [
-        experts_second(rows_in[c], grads_in[c], f[0], f[1], f[2], down_ws)
-        for c, f in zip(spans, firsts)
+    seconds = []
+    for c, f in zip(spans, firsts):
+        act = after(f[0], shared_far[0])
+        seconds.append(experts_second(rows_in[c], grads_in[c], act, f[1], f[2], down_ws, own))
+    outs = step // own
+    out_parts = [x for s in seconds for x in s[:outs]]
+    if len(seconds) == 1:
+        parts = seconds[0][outs:]
+    else:
+        parts = [added([s[outs + i] for s in seconds]).astype(BF) for i in range(3 * quarters)]
+    to_far = [
+        (parts[6 + m].astype(F32) + beside(parts[9 + m]).astype(F32)).astype(BF) for m in range(3)
     ]
-    out_part = jnp.concatenate([s[0] for s in seconds], axis=0)
-    if len(seconds) == 1:
-        parts = seconds[0][1:]
-    else:
-        parts = [added([s[1 + i] for s in seconds]).astype(BF) for i in range(3 * quarters)]
-    grad_parts = [[parts[3 * k + m] for k in range(quarters)] for m in range(3)]
-    shared_out, shared_dx = shared_own(normed_two, own_grads, *shared_ws)
-    shared_parts = [
-        shared_grads(rows_in[c], grads_in[c], rows_cut[c], grads_cut[c], *shared_ws) for c in spans
-    ]
-    shared_parts = shared_parts[0] if len(spans) == 1 else added(shared_parts).astype(BF)
-
-    grad_home = after(grad_home, out_part, shared_dx, shared_parts)
-    grad_norm_two = jnp.sum(grad_home.astype(F32), axis=0) + shared_dx
+    near = [(parts[m], beside(parts[3 + m])) for m in range(3)]
+    shared_out, shared_dx = shared_own(
+        after(normed_two, out_parts[0]), own_grads, *shared_ws
+    )
+
+    grad_home = lax.optimization_barrier((tuple(grad_home), shared_dx, to_far[0], to_far[1]))[0]
+    grad_norm_two = added(grad_home) + shared_dx
     grad_full = own_grads.astype(F32)
     grad_second, second_gain_local = norm_backward(
         grad_norm_two, hidden_state, second_scale, second_gain
@@ -639,64 +751,80 @@
     ).astype(BF)
     do_send = jnp.concatenate([grad_attended] * groups + [grad_attended[: units - groups * heads]], axis=0)
     do_units = exchange(do_send, BOTH).reshape(blocks, rows, hd)
-    out_home = exchange(after(out_part, grad_home).reshape(blocks, own, width), "expert")
-
-    routed = []
+
+    out_pairs = paired(out_parts[:half], out_parts[half:])
+    place = jnp.stack([rank // 2, rank % 2, quarter])
+    out_low, out_high = output_grads(
+        place, of_quarters(grad_attn), of_quarters(attended), heads, hw, blocks
+    )
+    do_units = lax.optimization_barrier((do_units, to_far[2], tuple(out_pairs), out_low))[0]
+
+    grad_units = attend_back(bounds, arrived, seg_col, seg_row, lse, do_units, most)
+    routed_far = [across(g) for g in to_far]
+    out_home = collected(out_pairs)
+    out_grad_pairs = paired([out_low], [out_high])[0]
+    gate_send = gate_sums[:, :slots_local].reshape(blocks, own, slots_local).transpose(0, 2, 1)
+    away = rank ^ index
+    gate_send = after(gate_send, do_units)[away // 2 + (away % 2) * half]
+    gate_back = exchange(gate_send, "expert").reshape(experts_total, own)
+    grad_units = lax.optimization_barrier(
+        (grad_units, out_home, out_grad_pairs, routed_far[0], gate_back)
+    )[0]
+    back_grads = exchange(grad_units.reshape(units, 3 * hw, rows), BOTH)
+
+    shared_parts = [
+        shared_grads(
+            after(rows_in, grad_units)[c], grads_in[c], rows_cut[c], grads_cut[c], *shared_ws
+        )
+        for c in spans
+    ]
+    shared_parts = shared_parts[0] if len(spans) == 1 else added(shared_parts).astype(BF)
+    out_grad = collected([out_grad_pairs[j] for j in range(half)])
+    output = in_order(of_quarters((hidden_state + out_home + shared_out).astype(BF)), quarter)
+    gate_grad = jnp.sum(jnp.where(slot_hot, after(gate_back, grad_units).T[:, None, :], 0.0), axis=2)
+    gate_grad = in_order(of_quarters(gate_grad), quarter)
+    routed = [added([a, b, c]) for (a, b), c in zip(near, routed_far)]
+    back_grads = lax.optimization_barrier(
+        (back_grads, shared_parts, out_grad, routed_far[1], routed[0])
+    )[0]
+
+    back_out = project_back(
+        place,
+        back_grads,
+        cosine,
+        sine,
+        normed_one,
+        query_weight,
+        key_weight,
+        value_weight,
+        groups,
+        blocks,
+        quarters,
+    )
+    grad_one = added([back_out[0][0]] + [flip(back_out[0][k], k, "tensor") for k in range(1, quarters)])
+    qkv_grads = []
     for m in range(3):
-        g = grad_parts[m]
-        to_far = (g[2].astype(F32) + beside(g[3]).astype(F32)).astype(BF)
-        routed.append(added([g[0], beside(g[1]), across(to_far)]))
-    shared = added([shared_parts[0]] + [swapped(shared_parts[k], k, quarters) for k in range(1, quarters)])
-
-    grad_units = attend_back(bounds, arrived, seg_col, seg_row, lse, do_units, most)
-    back_grads = exchange(grad_units.reshape(units, 3 * hw, rows), BOTH)
-
-    att_t = after(attended, do_units).T.reshape(heads, quarters, hw, own).transpose(1, 0, 2, 3)
-    att_t = exchange(att_t, "tensor")
-    attn_all = spread(after(grad_attn, do_units), "tensor").reshape(quarters, own, width)
-    attn_all, att_t = lax.optimization_barrier((attn_all, att_t, grad_units))[:2]
-    out_grad_t = jnp.einsum(
-        "qtd,qhct->dhc", attn_all, att_t.reshape(quarters, heads, hw, own), preferred_element_type=F32
-    ).astype(BF)
-    out_grad = exchange(out_grad_t.reshape(blocks, cut, heads * hw), "expert")
-
-    qkv_grad_t, grad_one_part = project_back(
-        back_grads, cosine, sine, normed_one, query_weight, key_weight, value_weight, groups
-    )
-    grad_one = jnp.sum(
-        exchange(grad_one_part.reshape(quarters, own, width), "tensor").astype(F32), axis=0
-    )
-    qkv_grad = exchange(qkv_grad_t.reshape(blocks, cut, 3 * heads * hw), "expert")
+        sums = paired([back_out[1 + 2 * m]], [back_out[2 + 2 * m]])[0]
+        qkv_grads.append(collected([sums[j] for j in range(half)]))
     first_scale = rms_scale(own_tokens)
     grad_first, first_gain_local = norm_backward(grad_one, own_tokens, first_scale, first_gain)
-    input_grad = spread((grad_hidden + grad_first).astype(BF), "tensor").reshape(rows, width)
-
-    out_home = jnp.sum(after(out_home, qkv_grad_t).astype(F32), axis=0) + shared_out
-    output = spread((hidden_state + out_home).astype(BF), "tensor").reshape(rows, width)
-    gate_back = exchange(
-        after(gate_sums, do_units)[:, :slots_local].reshape(blocks, own, slots_local).transpose(0, 2, 1),
-        "expert",
-    ).reshape(experts_total, own)
-    gate_grad = jnp.sum(jnp.where(slot_hot, after(gate_back, grad_units).T[:, None, :], 0.0), axis=2)
-    gate_grad = spread(gate_grad, "tensor").reshape(rows, top)
+    input_grad = in_order(of_quarters((grad_hidden + grad_first).astype(BF)), quarter)
+    shared = added([shared_parts[0]] + [flip(shared_parts[k], k, "tensor") for k in range(1, quarters)])
 
     gains = jnp.stack([first_gain_local, second_gain_local]).reshape(2, blocks, cut).transpose(1, 0, 2)
     gains = jnp.broadcast_to(gains[:, None], (blocks, quarters, 2, cut)).reshape(units, 2, cut)
     gains = jnp.sum(exchange(gains, BOTH), axis=0)
 
-    out_grad = jnp.sum(out_grad.astype(F32), axis=0)
-    qkv_grad = jnp.sum(qkv_grad.astype(F32), axis=0)
     weight_shape = (heads, 2, pair_width, cut)
-    qkv_rows = qkv_grad.T.reshape(3, *weight_shape)
     return (
         output,
         input_grad,
         gate_grad,
         gains[0],
         gains[1],
-        qkv_rows[0],
-        qkv_rows[1],
-        qkv_rows[2],
+        qkv_grads[0].T.reshape(weight_shape),
+        qkv_grads[1].T.reshape(weight_shape),
+        qkv_grads[2].T.reshape(weight_shape),
         out_grad.T.reshape(weight_shape),
         shared[0],
         shared[1],

time: 637 us -> 535 us (0.84)
  waiting for transfers between devices: 301 us -> 182 us
  blocking collectives: 57.1 us -> 0 us
  starting transfers between devices: 86.2 us -> 139 us
  other arithmetic: 33.7 us -> 45.6 us
  local copies, waits for them, and re-layouts: 48.8 us -> 56.1 us
    ppermute x33 -> x95, starting transfers between devices: 16.3 us -> 98.4 us  [flip(): return lax.ppermute(x, axis, [(i, i ^ by) for i in range(size)])]
    all_to_all x11 -> x7, waiting for transfers between devices: 102 us -> 20.4 us  [exchange(): return lax.all_to_all(x, axis, 0, 0, tiled=True)]
    all_to_all x2 -> x0, blocking collectives: 57.1 us -> none  [exchange(): return lax.all_to_all(x, axis, 0, 0, tiled=True)]
    all_to_all x6 -> x0, waiting for transfers between devices: 54 us -> none  [spread(): lax.all_to_all(jnp.broadcast_to(x[None], (size,) + x.shape), axis, 0, 0,...]
    all_to_all x6 -> x0, starting transfers between devices: 23.8 us -> none  [spread(): lax.all_to_all(jnp.broadcast_to(x[None], (size,) + x.shape), axis, 0, 0,...]
    ppermute x33 -> x95, waiting for transfers between devices: 145 us -> 162 us  [flip(): return lax.ppermute(x, axis, [(i, i ^ by) for i in range(size)])]
    unnamed x93 -> x136, local copies, waits for them, and re-layouts: 10 us -> 20.8 us
    convert_element_type x6 -> x10, other arithmetic: 8.59 us -> 17.4 us  [the longest x7 9.13 us: paired(): (a.astype(F32) + flip(b, 1, 'expert').astype(F32)).astype(BF)]
  transfers between devices with their start and end apart: 50 -> 102, of which waited for: 19 -> 33; matrix products, arithmetic and copies ran while one was open for 11% -> 18% of each run, Pallas kernels for 11% -> 14%
where the time goes in v2:
time: 535 us; the launch traced here: 530 us
  waiting for transfers between devices  182 us (34%)
  starting transfers between devices  139 us (26%)
  Pallas kernels  101 us (19%)
  local copies, waits for them, and re-layouts  56.1 us (10%)
  other arithmetic  45.6 us (9%)
    ppermute x95, waiting for transfers between devices, flip(): return lax.ppermute(x, axis, [(i, i ^ by) for i in range(size)])  162 us
    ppermute x95, starting transfers between devices, flip(): return lax.ppermute(x, axis, [(i, i ^ by) for i in range(size)])  98.4 us
    all_to_all x7, starting transfers between devices, exchange(): return lax.all_to_all(x, axis, 0, 0, tiled=True)  40.1 us
    unnamed x136, local copies, waits for them, and re-layouts  20.8 us
    pallas_call x1, Pallas kernels, experts_first(): pl.pallas_call(body, grid=(slots,), in_specs=[whole(rows_in.shape), hid_s...  20.4 us
    all_to_all x7, waiting for transfers between devices, exchange(): return lax.all_to_all(x, axis, 0, 0, tiled=True)  20.4 us
    pallas_call x1, Pallas kernels, experts_second(): pl.pallas_call(body, grid=(slots,), in_specs=[whole(rows_in.shape), whole...  18.6 us
    pallas_call x1, Pallas kernels, shared_grads(): pl.pallas_call(body, out_shape=jax.ShapeDtypeStruct((parts, 3, hidden, cu...  12.5 us
  transfers between devices with their start and end apart: 102, of which 33 were waited for; matrix products, arithmetic and copies ran while one was open for 18% of the time, Pallas kernels for 14%

profile of v2, /device:TPU:0, one launch (start us, length us, event | category | flops | bytes accessed | tf_op | source)
XLA Modules:
  0.0 530.0 jit_solution(17495230236329497747)
XLA Ops:
  8.7 7.4 %all-to-all-start = ((bf16[32,96,256]{2,1,0:T(8,128)(2,1)}), bf16[32,96,256]{2,1,0:T(8,128)(2,1)}, u32[]{:S(2)}, u32[]{:S(2)}) async-start(bf16[32,96,256]{2,1,0:T(8,128)(2,1)} %get-tuple-element.89), calls=%async_computation | async-start | bytes 3145728 | tf_op jit(solution)/shard_map/all_to_all | solution.py:548
  25.7 27.6 %collective-permute-done = bf16[10,32,1280]{2,1,0:T(8,128)(2,1)} collective-permute-done((bf16[10,32,1280]{2,1,0:T(8,128)(2,1)}, bf16[10,32,1280]{2,1,0:T(8,128)(2,1)}, u32[]{:S(2)}, u32[]{:S(2)}) %collective-permute-start) | collective-permute-done | bytes 819232 | tf_op jit(solution)/shard_map/ppermute | solution.py:544
  55.7 5.4 %all-to-all-start.2 = ((f32[8,1,128]{2,1,0:T(1,128)}), f32[8,1,128]{2,1,0:T(1,128)S(1)}, u32[]{:S(2)}, u32[]{:S(2)}) async-start(f32[8,1,128]{2,1,0:T(1,128)} %reshape.344), calls=%async_computation.2 | async-start | bytes 8192 | tf_op jit(solution)/shard_map/all_to_all | solution.py:548
  63.7 9.1 %attend.1 = (bf16[8,256,128]{2,1,0:T(8,128)(2,1)}, f32[8,256,128]{2,1,0:T(8,128)}) custom-call(s32[2]{0:T(128)} %pad_add_fusion.bounds_ref, bf16[8,4,96,256]{3,2,1,0:T(8,128)(2,1)} %bitcast.3.arr_ref, s32[8,256,128]{2,1,0:T(8,128)} %broadcast_in_dim.127.col_ref, s32[8,1,256]{2,1,0:T(1,128)} %bitcast.203), custom_call_target="tpu_custom_call" | custom-call | tf_op jit(solution)/shard_map/attend/pallas_call | solution.py:146
  72.8 5.4 %all-to-all-start.1 = ((bf16[32,64,128]{2,1,0:T(8,128)(2,1)}), bf16[32,64,128]{2,1,0:T(8,128)(2,1)}, u32[]{:S(2)}, u32[]{:S(2)}) async-start(bf16[32,64,128]{2,1,0:T(8,128)(2,1)} %bitcast.197), calls=%async_computation.1 | async-start | bytes 1048576 | tf_op jit(solution)/shard_map/all_to_all | solution.py:548
  95.3 8.9 %collective-permute-done.5 = bf16[64,1280]{1,0:T(8,128)(2,1)} collective-permute-done((bf16[64,1280]{1,0:T(8,128)(2,1)S(1)}, bf16[64,1280]{1,0:T(8,128)(2,1)}, u32[]{:S(2)}, u32[]{:S(2)}) %collective-permute-start.5) | collective-permute-done | bytes 163872 | tf_op jit(solution)/shard_map/ppermute | solution.py:544
  121.1 7.4 %collective-permute-done.8 = bf16[64,1280]{1,0:T(8,128)(2,1)S(1)} collective-permute-done((bf16[64,1280]{1,0:T(8,128)(2,1)S(1)}, bf16[64,1280]{1,0:T(8,128)(2,1)S(1)}, u32[]{:S(2)}, u32[]{:S(2)}) %collective-permute-start.8) | collective-permute-done | bytes 163872 | tf_op jit(solution)/shard_map/ppermute | solution.py:544
  159.1 6.8 %down_products.1.da_ref = f32[2,4,512,224]{3,2,1,0:T(8,128)} custom-call(bf16[512,1280]{1,0:T(8,128)(2,1)} %constant_dynamic-update-slice_fusion.8.dy_ref, bf16[2,224,1280]{2,1,0:T(8,128)(2,1)} %refs_0_.2, bf16[2,224,1280]{2,1,0:T(8,128)(2,1)} %collective-permute-done.18.refs_1_, bf16[2,224,1280]{2,1,0:T(8,128)(2,1)} %collective-permute-done.19.refs_2_, ...), custom_call_target="tpu_custom_call" | custom-call | tf_op jit(solution)/shard_map/down_products/pallas_call | solution.py:251
  165.9 20.4 %experts_first.1 = (bf16[2,4,512,224]{3,2,1,0:T(8,128)(2,1)}, bf16[2,4,512,224]{3,2,1,0:T(8,128)(2,1)}, bf16[2,4,512,224]{3,2,1,0:T(8,128)(2,1)}, f32[512,128]{1...) custom-call(bf16[512,1280]{1,0:T(8,128)(2,1)} %constant_dynamic-upda, ...), custom_call_target="tpu_custom_call" | custom-call | tf_op jit(solution)/shard_map/experts_first/pallas_call | solution.py:308
  186.4 18.6 %experts_second.1 = (bf16[64,1280]{1,0:T(8,128)(2,1)}, bf16[64,1280]{1,0:T(8,128)(2,1)}, bf16[64,1280]{1,0:T(8,128)(2,1)}, bf16[64,1280]{1,0:T(8,128)(2,1)}, bf1...) custom-call(bf16[512,1280]{1,0:T(8,128)(2,1)} %constant_dynamic-upda, ...), custom_call_target="tpu_custom_call" | custom-call | tf_op jit(solution)/shard_map/experts_second/pallas_call | solution.py:359
  213.3 8.6 %collective-permute-done.37.refs_6_ = bf16[224,1280]{1,0:T(8,128)(2,1)S(1)} collective-permute-done((bf16[224,1280]{1,0:T(8,128)(2,1)}, bf16[224,1280]{1,0:T(8,128)(2,1)S(1)}, u32[]{:S(2)}, u32[]{:S(2)}) %collective-permute-start.37) | collective-permute-done | bytes 573472 | tf_op jit(solution)/shard_map/ppermute | solution.py:544
  221.9 11.9 %collective-permute-done.40.refs_10_ = bf16[224,1280]{1,0:T(8,128)(2,1)} collective-permute-done((bf16[224,1280]{1,0:T(8,128)(2,1)}, bf16[224,1280]{1,0:T(8,128)(2,1)}, u32[]{:S(2)}, u32[]{:S(2)}) %collective-permute-start.40) | collective-permute-done | bytes 573472 | tf_op jit(solution)/shard_map/ppermute | solution.py:544
  250.8 7.9 %shared_own.1 = (f32[64,1280]{1,0:T(8,128)}, f32[64,1280]{1,0:T(8,128)}) custom-call(bf16[64,1280]{1,0:T(8,128)(2,1)} %copy-done.29, bf16[64,1280]{1,0:T(8,128)(2,1)} %copy-done.7, bf16[224,1280]{1,0:T(8,128)(2,1)} %refs_0_.4, bf16[224,1280]{1,0:T(8,128)(2,1)} %collective-permute-done.34.refs_1_, bf16[224,1280]{1,0:T(8,128)(2,1)} %collective-permute-done.26.refs_2_, ...), custom_call_target="tpu_custom_call" | custom-call | tf_op jit(solution)/shard_map/shared_own/pallas_call | solution.py:394
  293.6 5.3 %collective-permute-done.50 = bf16[64,1280]{1,0:T(8,128)(2,1)S(1)} collective-permute-done((bf16[64,1280]{1,0:T(8,128)(2,1)S(1)}, bf16[64,1280]{1,0:T(8,128)(2,1)S(1)}, u32[]{:S(2)}, u32[]{:S(2)}) %collective-permute-start.50) | collective-permute-done | bytes 163872 | tf_op jit(solution)/shard_map/ppermute | solution.py:544
  325.1 8.2 %collective-permute-done.61 = bf16[4,160,320]{2,1,0:T(8,128)(2,1)} collective-permute-done((bf16[4,160,320]{2,1,0:T(8,128)(2,1)}, bf16[4,160,320]{2,1,0:T(8,128)(2,1)}, u32[]{:S(2)}, u32[]{:S(2)}) %collective-permute-start.61) | collective-permute-done | bytes 409632 | tf_op jit(solution)/shard_map/ppermute | solution.py:544
  344.3 5.5 %all-to-all-start.4 = ((f32[8,1,128]{2,1,0:T(1,128)}), f32[8,1,128]{2,1,0:T(1,128)S(1)}, u32[]{:S(2)}, u32[]{:S(2)}) async-start(f32[8,1,128]{2,1,0:T(1,128)} %reshape.346), calls=%async_computation.4 | async-start | bytes 8192 | tf_op jit(solution)/shard_map/all_to_all | solution.py:548
  352.1 11.5 %attend_back.1 = bf16[8,4,96,256]{3,2,1,0:T(8,128)(2,1)} custom-call(s32[2]{0:T(128)} %pad_add_fusion.bounds_ref, bf16[8,4,96,256]{3,2,1,0:T(8,128)(2,1)} %bitcast.3.arr_ref, s32[8,256,128]{2,1,0:T(8,128)} %broadcast_in_dim.127.col_ref, s32[8,1,256]{2,1,0:T(1,128)} %bitcast.204, f32[8,256,128]{2,1,0:T(8,128)} %get-tuple-element.138.lse_ref, ...), custom_call_target="tpu_custom_call" | custom-call | tf_op jit(solution)/shard_map/attend_back/pallas_call | solution.py:229
  375.1 12.5 %shared_grads.1 = bf16[4,3,224,160]{3,2,1,0:T(8,128)(2,1)} custom-call(bf16[512,1280]{1,0:T(8,128)(2,1)} %constant_dynamic-update-slice_fusion.x_ref, bf16[512,1280]{1,0:T(8,128)(2,1)} %constant_dynamic-update-slice_fusion.8.dy_ref, bf16[512,160]{1,0:T(8,128)(2,1)} %constant_dynamic-slice_fusion.1.xc_ref, ...), custom_call_target="tpu_custom_call" | custom-call | tf_op jit(solution)/shard_map/shared_grads/pallas_call | solution.py:419
  395.5 22.6 %collective-permute-done.66 = bf16[2,224,1280]{2,1,0:T(8,128)(2,1)} collective-permute-done((bf16[2,224,1280]{2,1,0:T(8,128)(2,1)S(1)}, bf16[2,224,1280]{2,1,0:T(8,128)(2,1)}, u32[]{:S(2)}, u32[]{:S(2)}) %collective-permute-start.66) | collective-permute-done | bytes 1146912 | tf_op jit(solution)/shard_map/ppermute | solution.py:544
  435.4 6.4 %project_back.1 = (bf16[4,64,1280]{2,1,0:T(8,128)(2,1)}, bf16[4,160,320]{2,1,0:T(8,128)(2,1)}, bf16[4,160,320]{2,1,0:T(8,128)(2,1)}, bf16[4,160,320]{2,1,0:T(8,1...) custom-call(s32[3]{0:T(128)} %pad_add_fusion.1.place_ref, ...), custom_call_target="tpu_custom_call" | custom-call | tf_op jit(solution)/shard_map/project_back/pallas_call | solution.py:507
  456.2 6.1 %all-to-all-start.6 = ((f32[32,2,160]{2,1,0:T(2,128)}), f32[32,2,160]{2,1,0:T(2,128)S(1)}, u32[]{:S(2)}, u32[]{:S(2)}) async-start(f32[32,2,160]{2,1,0:T(2,128)} %bitcast.59), calls=%async_computation.6 | async-start | bytes 131072 | tf_op jit(solution)/shard_map/all_to_all | solution.py:548
  465.8 19.2 %all-to-all-done.6 = f32[32,2,160]{2,1,0:T(2,128)S(1)} async-done(((f32[32,2,160]{2,1,0:T(2,128)}), f32[32,2,160]{2,1,0:T(2,128)S(1)}, u32[]{:S(2)}, u32[]{:S(2)}) %all-to-all-start.6) | async-done | bytes 40992 | tf_op jit(solution)/shard_map/all_to_all | solution.py:548
  486.6 5.4 %collective-permute-done.73 = bf16[64,1280]{1,0:T(8,128)(2,1)S(1)} collective-permute-done((bf16[64,1280]{1,0:T(8,128)(2,1)S(1)}, bf16[64,1280]{1,0:T(8,128)(2,1)S(1)}, u32[]{:S(2)}, u32[]{:S(2)}) %collective-permute-start.73) | collective-permute-done | bytes 163872 | tf_op jit(solution)/shard_map/ppermute | solution.py:544
  507.8 9.2 %collective-permute-start.79 = (bf16[160,320]{1,0:T(8,128)(2,1)S(1)}, bf16[160,320]{1,0:T(8,128)(2,1)S(1)}, u32[]{:S(2)}, u32[]{:S(2)}) collective-permute-start(bf16[160,320]{1,0:T(8,128)(2,1)S(1)} %get-tuple-element.283), channel_id=1, source_target_pairs={{0,16},{4,20},{8,24},{12,28},{16,0},{20,4},{24,8},{28,12},{1,17},{... | collective-permute-start | bytes 307208 | tf_op jit(solution)/shard_map/ppermute | solution.py:544
  (433 shorter events, 270.1 us)
Async XLA Ops:
  8.7 46.3 %all-to-all-start = ((bf16[32,96,256]{2,1,0:T(8,128)(2,1)}), bf16[32,96,256]{2,1,0:T(8,128)(2,1)}, u32[]{:S(2)}, u32[]{:S(2)}) async-start(bf16[32,96,256]{2,1,0:T(8,128)(2,1)} %get-tuple-element.89), calls=%async_computation | async-start | bytes 3145728 | tf_op jit(solution)/shard_map/all_to_all | solution.py:548
  16.1 37.2 %collective-permute-start = (bf16[10,32,1280]{2,1,0:T(8,128)(2,1)}, bf16[10,32,1280]{2,1,0:T(8,128)(2,1)}, u32[]{:S(2)}, u32[]{:S(2)}) collective-permute-start(bf16[10,32,1280]{2,1,0:T(8,128)(2,1)} %bitcast.4), channel_id=1, source_target_pairs={{0,2},{1,3},{2,0},{3,1},{4,6},{5,7},{6,4},{7,5},{8,10},{9,11},{10,... | collective-permute-start | bytes 2457608 | tf_op jit(solution)/shard_map/ppermute | solution.py:544
  17.9 35.9 %collective-permute-start.1 = (bf16[10,32,1280]{2,1,0:T(8,128)(2,1)}, bf16[10,32,1280]{2,1,0:T(8,128)(2,1)}, u32[]{:S(2)}, u32[]{:S(2)}) collective-permute-start(bf16[10,32,1280]{2,1,0:T(8,128)(2,1)} %bitcast.4), channel_id=1, source_target_pairs={{0,1},{1,0},{2,3},{3,2},{4,5},{5,4},{6,7},{7,6},{8,9},{9,8},{10,11... | collective-permute-start | bytes 2457608 | tf_op jit(solution)/shard_map/ppermute | solution.py:544
  53.4 55.6 %collective-permute-start.3 = (bf16[2,224,1280]{2,1,0:T(8,128)(2,1)}, bf16[2,224,1280]{2,1,0:T(8,128)(2,1)}, u32[]{:S(2)}, u32[]{:S(2)}) collective-permute-start(bf16[2,224,1280]{2,1,0:T(8,128)(2,1)} %refs_0_.1), channel_id=1, source_target_pairs={{0,2},{1,3},{2,0},{3,1},{4,6},{5,7},{6,4},{7,5},{8,10},{9,11},{10,... | collective-permute-start | bytes 3440648 | tf_op jit(solution)/shard_map/ppermute | solution.py:544
  72.8 37.7 %all-to-all-start.1 = ((bf16[32,64,128]{2,1,0:T(8,128)(2,1)}), bf16[32,64,128]{2,1,0:T(8,128)(2,1)}, u32[]{:S(2)}, u32[]{:S(2)}) async-start(bf16[32,64,128]{2,1,0:T(8,128)(2,1)} %bitcast.197), calls=%async_computation.1 | async-start | bytes 1048576 | tf_op jit(solution)/shard_map/all_to_all | solution.py:548
  92.6 38.6 %collective-permute-start.19 = (bf16[2,224,1280]{2,1,0:T(8,128)(2,1)}, bf16[2,224,1280]{2,1,0:T(8,128)(2,1)}, u32[]{:S(2)}, u32[]{:S(2)}) collective-permute-start(bf16[2,224,1280]{2,1,0:T(8,128)(2,1)} %refs_0_.2), channel_id=1, source_target_pairs={{0,2},{1,3},{2,0},{3,1},{4,6},{5,7},{6,4},{7,5},{8,10},{9,11},{10,... | collective-permute-start | bytes 3440648 | tf_op jit(solution)/shard_map/ppermute | solution.py:544
  104.3 45.7 %collective-permute-start.18 = (bf16[2,224,1280]{2,1,0:T(8,128)(2,1)}, bf16[2,224,1280]{2,1,0:T(8,128)(2,1)}, u32[]{:S(2)}, u32[]{:S(2)}) collective-permute-start(bf16[2,224,1280]{2,1,0:T(8,128)(2,1)} %refs_0_.2), channel_id=1, source_target_pairs={{0,1},{1,0},{2,3},{3,2},{4,5},{5,4},{6,7},{7,6},{8,9},{9,8},{10,11... | collective-permute-start | bytes 3440648 | tf_op jit(solution)/shard_map/ppermute | solution.py:544
  105.9 44.1 %collective-permute-start.24 = (bf16[2,224,1280]{2,1,0:T(8,128)(2,1)}, bf16[2,224,1280]{2,1,0:T(8,128)(2,1)}, u32[]{:S(2)}, u32[]{:S(2)}) collective-permute-start(bf16[2,224,1280]{2,1,0:T(8,128)(2,1)} %refs_4_), channel_id=1, source_target_pairs={{0,2},{1,3},{2,0},{3,1},{4,6},{5,7},{6,4},{7,5},{8,10},{9,11},{10,... | collective-permute-start | bytes 3440648 | tf_op jit(solution)/shard_map/ppermute | solution.py:544
  155.6 30.8 %collective-permute-start.26 = (bf16[224,1280]{1,0:T(8,128)(2,1)S(1)}, bf16[224,1280]{1,0:T(8,128)(2,1)}, u32[]{:S(2)}, u32[]{:S(2)}) collective-permute-start(bf16[224,1280]{1,0:T(8,128)(2,1)S(1)} %copy-done.12), channel_id=1, source_target_pairs={{0,2},{1,3},{2,0},{3,1},{4,6},{5,7},{6,4},{7,5},{8,10},{9,11},{10,... | collective-permute-start | bytes 1720328 | tf_op jit(solution)/shard_map/ppermute | solution.py:544
  208.4 33.8 %collective-permute-start.36 = (bf16[224,1280]{1,0:T(8,128)(2,1)}, bf16[224,1280]{1,0:T(8,128)(2,1)S(1)}, u32[]{:S(2)}, u32[]{:S(2)}) collective-permute-start(bf16[224,1280]{1,0:T(8,128)(2,1)} %refs_4_.2), channel_id=1, source_target_pairs={{0,1},{1,0},{2,3},{3,2},{4,5},{5,4},{6,7},{7,6},{8,9},{9,8},{10,11... | collective-permute-start | bytes 1720328 | tf_op jit(solution)/shard_map/ppermute | solution.py:544
  299.0 38.9 %collective-permute-start.54 = (bf16[2,224,1280]{2,1,0:T(8,128)(2,1)}, bf16[2,224,1280]{2,1,0:T(8,128)(2,1)}, u32[]{:S(2)}, u32[]{:S(2)}) collective-permute-start(bf16[2,224,1280]{2,1,0:T(8,128)(2,1)} %get-tuple-element.140), channel_id=1, source_target_pairs={{0,1},{1,0},{2,3},{3,2},{4,5},{5,4},{6,7},{7,6},{8,9},{9,8},{10,11... | collective-permute-start | bytes 3440648 | tf_op jit(solution)/shard_map/ppermute | solution.py:544
  308.0 63.0 %collective-permute-start.67 = (bf16[2,224,1280]{2,1,0:T(8,128)(2,1)}, bf16[2,224,1280]{2,1,0:T(8,128)(2,1)}, u32[]{:S(2)}, u32[]{:S(2)}) collective-permute-start(bf16[2,224,1280]{2,1,0:T(8,128)(2,1)} %get-tuple-element.149), channel_id=1, source_target_pairs={{0,1},{1,0},{2,3},{3,2},{4,5},{5,4},{6,7},{7,6},{8,9},{9,8},{10,11... | collective-permute-start | bytes 3440648 | tf_op jit(solution)/shard_map/ppermute | solution.py:544
  308.0 56.3 %collective-permute-start.62 = (bf16[2,224,1280]{2,1,0:T(8,128)(2,1)}, bf16[2,224,1280]{2,1,0:T(8,128)(2,1)}, u32[]{:S(2)}, u32[]{:S(2)}) collective-permute-start(bf16[2,224,1280]{2,1,0:T(8,128)(2,1)} %add_convert_fusion.2), channel_id=1, source_target_pairs={{0,2},{1,3},{2,0},{3,1},{4,6},{5,7},{6,4},{7,5},{8,10},{9,11},{10,... | collective-permute-start | bytes 3440648 | tf_op jit(solution)/shard_map/ppermute | solution.py:544
  349.8 40.0 %collective-permute-start.93 = (bf16[2,224,1280]{2,1,0:T(8,128)(2,1)}, bf16[2,224,1280]{2,1,0:T(8,128)(2,1)}, u32[]{:S(2)}, u32[]{:S(2)}) collective-permute-start(bf16[2,224,1280]{2,1,0:T(8,128)(2,1)} %get-tuple-element.162), channel_id=1, source_target_pairs={{0,1},{1,0},{2,3},{3,2},{4,5},{5,4},{6,7},{7,6},{8,9},{9,8},{10,11... | collective-permute-start | bytes 3440648 | tf_op jit(solution)/shard_map/ppermute | solution.py:544
  349.9 45.2 %collective-permute-start.92 = (bf16[2,224,1280]{2,1,0:T(8,128)(2,1)}, bf16[2,224,1280]{2,1,0:T(8,128)(2,1)}, u32[]{:S(2)}, u32[]{:S(2)}) collective-permute-start(bf16[2,224,1280]{2,1,0:T(8,128)(2,1)} %get-tuple-element.160), channel_id=1, source_target_pairs={{0,1},{1,0},{2,3},{3,2},{4,5},{5,4},{6,7},{7,6},{8,9},{9,8},{10,11... | collective-permute-start | bytes 3440648 | tf_op jit(solution)/shard_map/ppermute | solution.py:544
  350.4 41.1 %collective-permute-start.94 = (bf16[2,224,1280]{2,1,0:T(8,128)(2,1)}, bf16[2,224,1280]{2,1,0:T(8,128)(2,1)}, u32[]{:S(2)}, u32[]{:S(2)}) collective-permute-start(bf16[2,224,1280]{2,1,0:T(8,128)(2,1)} %add_convert_fusion), channel_id=1, source_target_pairs={{0,2},{1,3},{2,0},{3,1},{4,6},{5,7},{6,4},{7,5},{8,10},{9,11},{10,... | collective-permute-start | bytes 3440648 | tf_op jit(solution)/shard_map/ppermute | solution.py:544
  364.3 53.8 %collective-permute-start.66 = (bf16[2,224,1280]{2,1,0:T(8,128)(2,1)S(1)}, bf16[2,224,1280]{2,1,0:T(8,128)(2,1)}, u32[]{:S(2)}, u32[]{:S(2)}) collective-permute-start(bf16[2,224,1280]{2,1,0:T(8,128)(2,1)S(1)} %copy-done.21), channel_id=1, source_target_pairs={{0,2},{1,3},{2,0},{3,1},{4,6},{5,7},{6,4},{7,5},{8,10},{9,11},{10,... | collective-permute-start | bytes 3440648 | tf_op jit(solution)/shard_map/ppermute | solution.py:544
  365.6 68.6 %all-to-all-start.5 = ((bf16[32,96,256]{2,1,0:T(8,128)(2,1)}), bf16[32,96,256]{2,1,0:T(8,128)(2,1)S(1)}, u32[]{:S(2)}, u32[]{:S(2)}) async-start(bf16[32,96,256]{2,1,0:T(8,128)(2,1)} %bitcast.185), calls=%async_computation.5 | async-start | bytes 3145728 | tf_op jit(solution)/shard_map/all_to_all | solution.py:548
  371.0 51.4 %collective-permute-start.74 = (f32[64,7]{0,1:T(8,128)S(1)}, f32[64,7]{0,1:T(8,128)S(1)}, u32[]{:S(2)}, u32[]{:S(2)}) collective-permute-start(f32[64,7]{0,1:T(8,128)S(1)} %select_reduce_fusion), channel_id=1, source_target_pairs={{0,1},{1,0},{2,3},{3,2},{4,5},{5,4},{6,7},{7,6},{8,9},{9,8},{10,11... | collective-permute-start | bytes 5384 | tf_op jit(solution)/shard_map/ppermute | solution.py:544
  389.8 32.7 %collective-permute-start.75 = (f32[64,7]{0,1:T(8,128)S(1)}, f32[64,7]{0,1:T(8,128)S(1)}, u32[]{:S(2)}, u32[]{:S(2)}) collective-permute-start(f32[64,7]{0,1:T(8,128)S(1)} %select_reduce_fusion), channel_id=1, source_target_pairs={{0,2},{1,3},{2,0},{3,1},{4,6},{5,7},{6,4},{7,5},{8,10},{9,11},{10,... | collective-permute-start | bytes 5384 | tf_op jit(solution)/shard_map/ppermute | solution.py:544
  391.5 31.1 %collective-permute-start.76 = (f32[64,7]{0,1:T(8,128)S(1)}, f32[64,7]{0,1:T(8,128)S(1)}, u32[]{:S(2)}, u32[]{:S(2)}) collective-permute-start(f32[64,7]{0,1:T(8,128)S(1)} %select_reduce_fusion), channel_id=1, source_target_pairs={{0,3},{1,2},{2,1},{3,0},{4,7},{5,6},{6,5},{7,4},{8,11},{9,10},{10,... | collective-permute-start | bytes 5384 | tf_op jit(solution)/shard_map/ppermute | solution.py:544
  448.7 43.3 %collective-permute-start.85 = (bf16[4,160,320]{2,1,0:T(8,128)(2,1)}, bf16[4,160,320]{2,1,0:T(8,128)(2,1)}, u32[]{:S(2)}, u32[]{:S(2)}) collective-permute-start(bf16[4,160,320]{2,1,0:T(8,128)(2,1)} %get-tuple-element.158), channel_id=1, source_target_pairs={{0,4},{4,0},{8,12},{12,8},{16,20},{20,16},{24,28},{28,24},{1,5},{5... | collective-permute-start | bytes 1228808 | tf_op jit(solution)/shard_map/ppermute | solution.py:544
  450.7 47.2 %collective-permute-start.81 = (bf16[4,160,320]{2,1,0:T(8,128)(2,1)}, bf16[4,160,320]{2,1,0:T(8,128)(2,1)}, u32[]{:S(2)}, u32[]{:S(2)}) collective-permute-start(bf16[4,160,320]{2,1,0:T(8,128)(2,1)} %get-tuple-element.156), channel_id=1, source_target_pairs={{0,4},{4,0},{8,12},{12,8},{16,20},{20,16},{24,28},{28,24},{1,5},{5... | collective-permute-start | bytes 1228808 | tf_op jit(solution)/shard_map/ppermute | solution.py:544
  450.8 49.4 %collective-permute-start.77 = (bf16[4,160,320]{2,1,0:T(8,128)(2,1)}, bf16[4,160,320]{2,1,0:T(8,128)(2,1)}, u32[]{:S(2)}, u32[]{:S(2)}) collective-permute-start(bf16[4,160,320]{2,1,0:T(8,128)(2,1)} %get-tuple-element.154), channel_id=1, source_target_pairs={{0,4},{4,0},{8,12},{12,8},{16,20},{20,16},{24,28},{28,24},{1,5},{5... | collective-permute-start | bytes 1228808 | tf_op jit(solution)/shard_map/ppermute | solution.py:544
  (136 other events, 1800.1 us)

commit v3 on v2

--- a/solution.py
+++ b/solution.py
@@ -239,24 +239,56 @@
     return [pl.BlockSpec((1, hidden, width), lambda s, *_: (s, 0, 0))] * (parts * mats)
 
 
-def down_products(grads_in, downs):
-    count, width = grads_in.shape
+def down_products(place, even, odd, first, count, width, downs):
+    half, own, wide = even.shape
     parts = len(downs)
     slots, hidden, _ = downs[0].shape
-
-    def body(dy_ref, *refs):
+    lanes = wide - width
+
+    def body(place_ref, even_ref, odd_ref, *refs):
+        da_ref, dy_ref, gate_ref = refs[parts:]
+
+        @pl.when(pl.program_id(0) == 0)
+        def _():
+            for c in range(count // own // 2):
+                at = place_ref[0] ^ (first + c)
+                for parity in range(2):
+
+                    @pl.when(place_ref[1] == parity)
+                    def _():
+                        for b, ref in ((2 * c + parity, even_ref), (2 * c + 1 - parity, odd_ref)):
+                            dy_ref[b * own : (b + 1) * own] = ref[at, :, 0:width]
+                            gate_ref[b * own : (b + 1) * own] = ref[at, :, width:wide]
+
         for k in range(parts):
-            refs[parts][0, k] = dot(dy_ref[...], refs[k][0], 1, 1)
+            da_ref[0, k] = dot(dy_ref[...], refs[k][0], 1, 1)
 
     return pl.pallas_call(
         body,
-        grid=(slots,),
-        in_specs=[whole(grads_in.shape)] + weight_specs(parts, hidden, width, 1),
-        out_specs=pl.BlockSpec((1, parts, count, hidden), lambda s: (s, 0, 0, 0)),
-        out_shape=jax.ShapeDtypeStruct((slots, parts, count, hidden), F32),
+        grid_spec=pltpu.PrefetchScalarGridSpec(
+            num_scalar_prefetch=1,
+            grid=(slots,),
+            in_specs=[whole(even.shape), whole(odd.shape)] + weight_specs(parts, hidden, width, 1),
+            out_specs=[
+                pl.BlockSpec((1, parts, count, hidden), lambda s, *_: (s, 0, 0, 0)),
+                whole((count, width)),
+                whole((count, lanes)),
+            ],
+        ),
+        out_shape=(
+            jax.ShapeDtypeStruct((slots, parts, count, hidden), F32),
+            jax.ShapeDtypeStruct((count, width), BF),
+            jax.ShapeDtypeStruct((count, lanes), BF),
+        ),
         compiler_params=pltpu.CompilerParams(vmem_limit_bytes=VMEM_LIMIT),
         name="down_products",
-    )(grads_in, *downs)
+    )(place, even, odd, *downs)
+
+
+def pieces(x):
+    high = lax.reduce_precision(x, 8, 7)
+    middle = lax.reduce_precision(x - high, 8, 7)
+    return [high, middle, x - high - middle]
 
 
 def swish_parts(g, u, da):
@@ -265,25 +297,27 @@
     return swish * u, da * u * (sig * (1.0 + g * (1.0 - sig))), da * swish
 
 
-def experts_first(rows_in, down_prod, gates, gate_ws, up_ws, own):
+def experts_first(place, rows_in, down_prod, gates, gate_ws, up_ws, experts):
     count, width = rows_in.shape
     parts = len(gate_ws)
     slots, hidden, _ = gate_ws[0].shape
-
-    def body(x_ref, da_ref, gate_ref, *refs):
+    lanes = gates.shape[1]
+
+    def body(place_ref, x_ref, da_ref, gate_ref, *refs):
         gate_w, up_w = refs[:parts], refs[parts : 2 * parts]
-        act_ref, dg_ref, du_ref, gg_ref = refs[2 * parts : 2 * parts + 4]
-        dx_refs, acc_ref = refs[2 * parts + 4 : -1], refs[-1]
+        act_ref, dg_ref, du_ref, gg_ref, dx_ref, acc_ref, sum_ref = refs[2 * parts :]
         s = pl.program_id(0)
         x = x_ref[...]
-        lane = lax.broadcasted_iota(jnp.int32, (count, 128), 1)
-        gate = jnp.sum(jnp.where(lane == s, gate_ref[...], 0.0), axis=1, keepdims=True)
+        lane = lax.broadcasted_iota(jnp.int32, (count, lanes), 1)
+        slot = place_ref[3] * slots + s
+        mine = lane % experts == slot
+        gate = jnp.sum(jnp.where(mine, gate_ref[...].astype(F32), 0.0), axis=1, keepdims=True)
         total = jnp.zeros((count, 1), F32)
 
         @pl.when(s == 0)
         def _():
             acc_ref[...] = jnp.zeros(acc_ref.shape, F32)
-            gg_ref[...] = jnp.zeros(gg_ref.shape, F32)
+            sum_ref[...] = jnp.zeros(sum_ref.shape, F32)
 
         for k in range(parts):
             g = dot(x, gate_w[k][0], 1, 1)
@@ -296,45 +330,51 @@
             du_ref[0, k] = du.astype(BF)
             acc_ref[...] += dot(dg_ref[0, k], gate_w[k][0], 1, 0) + dot(du_ref[0, k], up_w[k][0], 1, 0)
 
-        gg_ref[...] += jnp.where(lane == s, total, 0.0)
+        high = total.astype(BF).astype(F32)
+        middle = (total - high).astype(BF).astype(F32)
+        for n, piece in enumerate((high, middle, total - high - middle)):
+            sum_ref[...] += jnp.where(lane == n * experts + slot, piece, 0.0)
 
         @pl.when(s == slots - 1)
         def _():
-            for b, dx_ref in enumerate(dx_refs):
-                dx_ref[...] = acc_ref[b * own : (b + 1) * own].astype(BF)
+            dx_ref[...] = acc_ref[...].astype(BF)
+            gg_ref[...] = sum_ref[...].astype(BF)
 
     hid = jax.ShapeDtypeStruct((slots, parts, count, hidden), BF)
-    hid_spec = pl.BlockSpec((1, parts, count, hidden), lambda s: (s, 0, 0, 0))
+    hid_spec = pl.BlockSpec((1, parts, count, hidden), lambda s, *_: (s, 0, 0, 0))
     return pl.pallas_call(
         body,
-        grid=(slots,),
-        in_specs=[whole(rows_in.shape), hid_spec, whole(gates.shape)]
-        + weight_specs(parts, hidden, width, 2),
-        out_specs=[hid_spec, hid_spec, hid_spec, whole((count, 128))]
-        + [whole((own, width))] * (count // own),
+        grid_spec=pltpu.PrefetchScalarGridSpec(
+            num_scalar_prefetch=1,
+            grid=(slots,),
+            in_specs=[whole(rows_in.shape), hid_spec, whole(gates.shape)]
+            + weight_specs(parts, hidden, width, 2),
+            out_specs=[hid_spec, hid_spec, hid_spec, whole((count, lanes)), whole((count, width))],
+            scratch_shapes=[pltpu.VMEM((count, width), F32), pltpu.VMEM((count, lanes), F32)],
+        ),
         out_shape=(
             hid,
             hid,
             hid,
-            jax.ShapeDtypeStruct((count, 128), F32),
-        )
-        + (jax.ShapeDtypeStruct((own, width), BF),) * (count // own),
-        scratch_shapes=[pltpu.VMEM((count, width), F32)],
+            jax.ShapeDtypeStruct((count, lanes), BF),
+            jax.ShapeDtypeStruct((count, width), BF),
+        ),
         compiler_params=pltpu.CompilerParams(vmem_limit_bytes=VMEM_LIMIT),
         name="experts_first",
-    )(rows_in, down_prod, gates, *gate_ws, *up_ws)
-
-
-def experts_second(rows_in, grads_in, act, dgate, dup, downs, own):
+    )(place, rows_in, down_prod, gates, *gate_ws, *up_ws)
+
+
+def experts_second(place, rows_in, grads_in, sums, act, dgate, dup, downs, own):
     count, width = rows_in.shape
     parts = len(downs)
     slots, hidden, _ = downs[0].shape
-    outs = count // own
-
-    def body(x_ref, dy_ref, act_ref, dg_ref, du_ref, *refs):
+    wide = width + sums.shape[1]
+    half = count // own // 2
+
+    def body(place_ref, x_ref, dy_ref, sum_ref, act_ref, dg_ref, du_ref, *refs):
         down_w = refs[:parts]
-        out_refs = refs[parts : parts + outs]
-        grads = refs[parts + outs : -1]
+        low_ref, high_ref = refs[parts : parts + 2]
+        grads = refs[parts + 2 : -1]
         acc_ref = refs[-1]
         s = pl.program_id(0)
 
@@ -344,45 +384,57 @@
 
         for k in range(parts):
             acc_ref[...] += dot(act_ref[0, k], down_w[k][0], 1, 0)
-            grads[3 * k][0] = dot(dg_ref[0, k], x_ref[...], 0, 0).astype(BF)
-            grads[3 * k + 1][0] = dot(du_ref[0, k], x_ref[...], 0, 0).astype(BF)
-            grads[3 * k + 2][0] = dot(act_ref[0, k], dy_ref[...], 0, 0).astype(BF)
+            grads[k][0, 0] = dot(dg_ref[0, k], x_ref[...], 0, 0).astype(BF)
+            grads[k][1, 0] = dot(du_ref[0, k], x_ref[...], 0, 0).astype(BF)
+            grads[k][2, 0] = dot(act_ref[0, k], dy_ref[...], 0, 0).astype(BF)
 
         @pl.when(s == slots - 1)
         def _():
-            for b, out_ref in enumerate(out_refs):
-                out_ref[...] = acc_ref[b * own : (b + 1) * own].astype(BF)
-
-    hid_spec = pl.BlockSpec((1, parts, count, hidden), lambda s: (s, 0, 0, 0))
-    grad_spec = pl.BlockSpec((1, hidden, width), lambda s: (s, 0, 0))
-    grad_shape = jax.ShapeDtypeStruct((slots, hidden, width), BF)
+            for c in range(half):
+                at = (place_ref[0] % half) ^ c
+                for parity in range(2):
+
+                    @pl.when(place_ref[1] == parity)
+                    def _():
+                        for b, ref in ((2 * c + parity, low_ref), (2 * c + 1 - parity, high_ref)):
+                            ref[at, :, 0:width] = acc_ref[b * own : (b + 1) * own].astype(BF)
+                            ref[at, :, width:wide] = sum_ref[b * own : (b + 1) * own]
+
+    hid_spec = pl.BlockSpec((1, parts, count, hidden), lambda s, *_: (s, 0, 0, 0))
+    out_shape = (half, own, wide)
     return pl.pallas_call(
         body,
-        grid=(slots,),
-        in_specs=[whole(rows_in.shape), whole(grads_in.shape), hid_spec, hid_spec, hid_spec]
-        + weight_specs(parts, hidden, width, 1),
-        out_specs=[whole((own, width))] * outs + [grad_spec] * (3 * parts),
-        out_shape=(jax.ShapeDtypeStruct((own, width), BF),) * outs + (grad_shape,) * (3 * parts),
-        scratch_shapes=[pltpu.VMEM((count, width), F32)],
+        grid_spec=pltpu.PrefetchScalarGridSpec(
+            num_scalar_prefetch=1,
+            grid=(slots,),
+            in_specs=[whole(rows_in.shape), whole(grads_in.shape), whole(sums.shape)]
+            + [hid_spec] * 3
+            + weight_specs(parts, hidden, width, 1),
+            out_specs=[whole(out_shape)] * 2
+            + [pl.BlockSpec((3, 1, hidden, width), lambda s, *_: (0, s, 0, 0))] * parts,
+            scratch_shapes=[pltpu.VMEM((count, width), F32)],
+        ),
+        out_shape=(jax.ShapeDtypeStruct(out_shape, BF),) * 2
+        + (jax.ShapeDtypeStruct((3, slots, hidden, width), BF),) * parts,
         compiler_params=pltpu.CompilerParams(vmem_limit_bytes=VMEM_LIMIT),
         name="experts_second",
-    )(rows_in, grads_in, act, dgate, dup, *downs)
-
-
-def shared_own(rows, grads, gate_ws, up_ws, down_ws):
-    parts = len(gate_ws)
+    )(place, rows_in, grads_in, sums, act, dgate, dup, *downs)
+
+
+def shared_own(rows, grads, weights):
+    parts = len(weights)
 
     def body(x_ref, dy_ref, *refs):
-        out_ref, dx_ref = refs[3 * parts :]
+        out_ref, dx_ref = refs[parts:]
         for k in range(parts):
-            gw, uw, dw = refs[k], refs[parts + k], refs[2 * parts + k]
+            gw, uw, dw = refs[k][0], refs[k][1], refs[k][2]
             act, dg, du = swish_parts(
-                dot(x_ref[...], gw[...], 1, 1),
-                dot(x_ref[...], uw[...], 1, 1),
-                dot(dy_ref[...], dw[...], 1, 1),
+                dot(x_ref[...], gw, 1, 1),
+                dot(x_ref[...], uw, 1, 1),
+                dot(dy_ref[...], dw, 1, 1),
             )
-            out = dot(act.astype(BF), dw[...], 1, 0)
-            dx = dot(dg.astype(BF), gw[...], 1, 0) + dot(du.astype(BF), uw[...], 1, 0)
+            out = dot(act.astype(BF), dw, 1, 0)
+            dx = dot(dg.astype(BF), gw, 1, 0) + dot(du.astype(BF), uw, 1, 0)
             if k == 0:
                 out_ref[...] = out
                 dx_ref[...] = dx
@@ -396,21 +448,21 @@
         out_shape=(shape, shape),
         compiler_params=pltpu.CompilerParams(vmem_limit_bytes=VMEM_LIMIT),
         name="shared_own",
-    )(rows, grads, *gate_ws, *up_ws, *down_ws)
-
-
-def shared_grads(rows_in, grads_in, rows_cut, grads_cut, gate_ws, up_ws, down_ws):
-    parts = len(gate_ws)
-    hidden = gate_ws[0].shape[0]
+    )(rows, grads, *weights)
+
+
+def shared_grads(rows_in, grads_in, rows_cut, grads_cut, weights):
+    parts = len(weights)
+    hidden = weights[0].shape[1]
     cut = rows_cut.shape[1]
 
     def body(x_ref, dy_ref, xc_ref, dyc_ref, *refs):
-        out_ref = refs[3 * parts]
+        out_ref = refs[parts]
         for k in range(parts):
             act, dg, du = swish_parts(
-                dot(x_ref[...], refs[k][...], 1, 1),
-                dot(x_ref[...], refs[parts + k][...], 1, 1),
-                dot(dy_ref[...], refs[2 * parts + k][...], 1, 1),
+                dot(x_ref[...], refs[k][0], 1, 1),
+                dot(x_ref[...], refs[k][1], 1, 1),
+                dot(dy_ref[...], refs[k][2], 1, 1),
             )
             out_ref[k, 0] = dot(dg.astype(BF), xc_ref[...], 0, 0).astype(BF)
             out_ref[k, 1] = dot(du.astype(BF), xc_ref[...], 0, 0).astype(BF)
@@ -421,7 +473,7 @@
         out_shape=jax.ShapeDtypeStruct((parts, 3, hidden, cut), BF),
         compiler_params=pltpu.CompilerParams(vmem_limit_bytes=VMEM_LIMIT),
         name="shared_grads",
-    )(rows_in, grads_in, rows_cut, grads_cut, *gate_ws, *up_ws, *down_ws)
+    )(rows_in, grads_in, rows_cut, grads_cut, *weights)
 
 
 def store_chunks(place_ref, value, low_ref, high_ref):
@@ -468,7 +520,7 @@
     )(place, *attn_parts, *att_parts)
 
 
-def project_back(place, back, cosine, sine, normed, wq, wk, wv, groups, blocks, quarters):
+def project_back(place, back, cosine, sine, tokens, normed, wq, wk, wv, groups, blocks, quarters):
     heads = wq.shape[0]
     pw = wq.shape[2]
     hw = 2 * pw
@@ -476,9 +528,9 @@
     own = rows // quarters
     span = heads * hw
 
-    def body(place_ref, back_ref, cos_ref, sin_ref, norm_ref, q_ref, k_ref, v_ref, *refs):
-        dx_ref = refs[0]
-        chunk_refs = refs[1:-1]
+    def body(place_ref, back_ref, cos_ref, sin_ref, tok_ref, norm_ref, q_ref, k_ref, v_ref, *refs):
+        dx_ref, gain_ref = refs[:2]
+        chunk_refs = refs[2:-1]
         grad_ref = refs[-1]
         cos = cos_ref[...]
         sin = sin_ref[...]
@@ -501,6 +553,8 @@
         dx = dx + dot(grad_ref[2 * span :], v_ref[...], 0, 0)
         for j in range(quarters):
             dx_ref[place_ref[2] ^ j] = dx[j * own : (j + 1) * own].astype(BF)
+        x = tok_ref[...].astype(F32)
+        gain_ref[...] = jnp.sum(dx * (x * rms_scale(x)), axis=0, keepdims=True)
 
     flat = (span, width)
     chunk = (blocks // 2, width // blocks, span)
@@ -513,19 +567,23 @@
                 whole(back.shape),
                 whole(cosine.shape),
                 whole(sine.shape),
+                whole(tokens.shape),
                 whole(normed.shape),
                 whole(flat),
                 whole(flat),
                 whole(flat),
             ],
-            out_specs=[whole((quarters, own, width))] + [whole(chunk)] * 6,
+            out_specs=[whole((quarters, own, width)), whole((1, width))] + [whole(chunk)] * 6,
             scratch_shapes=[pltpu.VMEM((3 * span, rows), BF)],
         ),
-        out_shape=(jax.ShapeDtypeStruct((quarters, own, width), BF),)
+        out_shape=(
+            jax.ShapeDtypeStruct((quarters, own, width), BF),
+            jax.ShapeDtypeStruct((1, width), F32),
+        )
         + (jax.ShapeDtypeStruct(chunk, BF),) * 6,
         compiler_params=pltpu.CompilerParams(vmem_limit_bytes=VMEM_LIMIT),
         name="project_back",
-    )(place, back, cosine, sine, normed, wq.reshape(flat), wk.reshape(flat), wv.reshape(flat))
+    )(place, back, cosine, sine, tokens, normed, wq.reshape(flat), wk.reshape(flat), wv.reshape(flat))
 
 
 def after(x, *others):
@@ -548,23 +606,26 @@
     return lax.all_to_all(x, axis, 0, 0, tiled=True)
 
 
+def spread(x, axis):
+    size = lax.axis_size(axis)
+    return exchange(jnp.broadcast_to(x[None], (size,) + x.shape), axis)
+
+
 def even_blocks(x):
     size = lax.axis_size("expert")
-    return [x] + [flip(x, m, "expert") for m in range(2, size, 2)]
+    return jnp.stack([x] + [flip(x, m, "expert") for m in range(2, size, 2)])
 
 
 def odd_blocks(evens):
-    return [flip(x, 1, "expert") for x in evens]
+    return flip(evens, 1, "expert")
 
 
 def paired(evens, odds):
-    return [
-        (a.astype(F32) + flip(b, 1, "expert").astype(F32)).astype(BF) for a, b in zip(evens, odds)
-    ]
+    return (evens.astype(F32) + flip(odds, 1, "expert").astype(F32)).astype(BF)
 
 
 def collected(sums):
-    return added([sums[0]] + [flip(sums[j], 2 * j, "expert") for j in range(1, len(sums))])
+    return added([sums[0]] + [flip(sums[j], 2 * j, "expert") for j in range(1, sums.shape[0])])
 
 
 def of_quarters(x):
@@ -664,6 +725,8 @@
         out_full = lax.dynamic_update_slice(out_full, out_ws[k][:, None], (0, quarter ^ k, 0, 0))
     out_full = out_full.reshape(heads * hd, width)
 
+    half = blocks // 2
+    place = jnp.stack([rank // 2, rank % 2, quarter, rank])
     own_tokens = lax.dynamic_slice_in_dim(tokens, quarter * own, own).astype(F32)
     own_grads = lax.dynamic_slice_in_dim(cotangent, quarter * own, own)
     own_ids = lax.dynamic_slice_in_dim(expert_ids, quarter * own, own)
@@ -672,16 +735,13 @@
     own_slots = jnp.sum(jnp.where(onehot, expert_slot[None, None, :], 0), axis=2)
     slot_hot = own_slots[:, :, None] == jnp.arange(experts_total, dtype=jnp.int32)
     dense_gates = jnp.sum(jnp.where(slot_hot, own_gates[:, :, None], 0.0), axis=1)
-    own_grads, dense_gates = lax.optimization_barrier((own_grads, dense_gates, arrived))[:2]
-    index = jnp.arange(blocks, dtype=jnp.int32)
-    half = blocks // 2
-    distance = jnp.where(index < half, 2 * index, 2 * (index - half) + 1)
-    gates_in = exchange(dense_gates.T.reshape(blocks, slots_local, own), "expert")
-    gates_in = gates_in[rank ^ distance].transpose(0, 2, 1).reshape(blocks * own, slots_local)
-    gates_in = jnp.concatenate(
-        [gates_in, jnp.zeros((blocks * own, 128 - slots_local), F32)], axis=1
-    )
-    grads_even = even_blocks(own_grads)
+    lanes = -(-3 * experts_total // 128) * 128
+    spare = jnp.zeros((own, lanes - 3 * experts_total), BF)
+    own_wide = jnp.concatenate(
+        [own_grads] + [p.astype(BF) for p in pieces(dense_gates)] + [spare], axis=1
+    )
+    grads_even = even_blocks(after(own_wide, arrived))
+    grads_odd = odd_blocks(grads_even)
 
     attended_units, lse = attend(bounds, arrived, seg_col, seg_row, most)
     down_mine = after(routed_down, attended_units)
@@ -690,56 +750,60 @@
     up_ws = all_quarters(up_mine, up_far)
     down_ws = all_quarters(down_mine, down_far)
     back = exchange(attended_units.reshape(units, own, hd), BOTH)
-    back = after(back, out_full, gate_far, *grads_even)
-    grads_in = jnp.concatenate(grads_even + odd_blocks(grads_even), axis=0)
+    back = after(back, out_full, gate_far, grads_even)
     attended_heads = lax.dynamic_slice_in_dim(back, block_group * heads, heads)
     attended = attended_heads.transpose(1, 0, 2).reshape(own, heads * hd)
     hidden_state = own_tokens + jnp.dot(attended, out_full, preferred_element_type=F32)
     second_scale = rms_scale(hidden_state)
     normed_two = (hidden_state * second_scale * second_gain).astype(BF)
 
-    rows_even = even_blocks(normed_two)
-    rows_in = jnp.concatenate(rows_even + odd_blocks(rows_even), axis=0)
-    shared_mine = [after(w, rows_in) for w in (shared_gate, shared_up, shared_down)]
-    shared_far = [across(w) for w in shared_mine]
-    shared_ws = [all_quarters(w, far) for w, far in zip(shared_mine, shared_far)]
+    rows_in = spread(normed_two, "expert").reshape(blocks * own, width)
+    shared_mine = after(jnp.stack([shared_gate, shared_up, shared_down]), normed_two)
+    shared_far = across(shared_mine)
+    shared_near = beside(shared_mine)
+    shared_ws = (shared_mine, shared_near, shared_far, beside(shared_far))
 
     total_rows = blocks * own
     step = min(total_rows, 512)
     spans = [slice(c, c + step) for c in range(0, total_rows, step)]
-    firsts = []
-    for c in spans:
-        prod = down_products(grads_in[c], down_ws)
-        firsts.append(experts_first(rows_in[c], prod, gates_in[c], gate_ws, up_ws, own))
-    grad_rows = [x for f in firsts for x in f[4:]]
-    gate_sums = jnp.concatenate([f[3] for f in firsts], axis=0)
-    grad_home = [grad_rows[0]]
-    for p in range(1, blocks):
-        m = 2 * p if p < half else 2 * (p - half) + 1
-        grad_home.append(flip(grad_rows[p], m, "expert"))
+    prods = [
+        down_products(place, grads_even, grads_odd, c.start // own // 2, step, width, down_ws)
+        for c in spans
+    ]
+    firsts = [
+        experts_first(place, rows_in[c], p[0], p[2], gate_ws, up_ws, experts_total)
+        for c, p in zip(spans, prods)
+    ]
+    grads_in = jnp.concatenate([p[1] for p in prods], axis=0)
+    grad_rows = jnp.concatenate([f[4] for f in firsts], axis=0)
+    grad_home = exchange(grad_rows.reshape(blocks, own, width), "expert")
 
     rows_cut = lax.dynamic_slice_in_dim(rows_in, rank * cut, cut, axis=1)
     grads_cut = lax.dynamic_slice_in_dim(grads_in, rank * cut, cut, axis=1)
     seconds = []
     for c, f in zip(spans, firsts):
-        act = after(f[0], shared_far[0])
-        seconds.append(experts_second(rows_in[c], grads_in[c], act, f[1], f[2], down_ws, own))
-    outs = step // own
-    out_parts = [x for s in seconds for x in s[:outs]]
+        act = lax.optimization_barrier((f[0], shared_far, shared_near))[0]
+        seconds.append(
+            experts_second(place, rows_in[c], grads_in[c], f[3], act, f[1], f[2], down_ws, own)
+        )
     if len(seconds) == 1:
-        parts = seconds[0][outs:]
+        out_low, out_high = seconds[0][:2]
+        parts = seconds[0][2:]
     else:
-        parts = [added([s[outs + i] for s in seconds]).astype(BF) for i in range(3 * quarters)]
-    to_far = [
-        (parts[6 + m].astype(F32) + beside(parts[9 + m]).astype(F32)).astype(BF) for m in range(3)
-    ]
-    near = [(parts[m], beside(parts[3 + m])) for m in range(3)]
-    shared_out, shared_dx = shared_own(
-        after(normed_two, out_parts[0]), own_grads, *shared_ws
-    )
-
-    grad_home = lax.optimization_barrier((tuple(grad_home), shared_dx, to_far[0], to_far[1]))[0]
-    grad_norm_two = added(grad_home) + shared_dx
+        order = (rank // (step // own)) ^ jnp.arange(len(seconds), dtype=jnp.int32)
+        out_low, out_high = (
+            jnp.stack([s[i] for s in seconds])[order].reshape(half, own, width + lanes)
+            for i in range(2)
+        )
+        parts = [added([s[2 + k] for s in seconds]).astype(BF) for k in range(quarters)]
+    shared_out, shared_dx = shared_own(after(normed_two, out_low), own_grads, shared_ws)
+    att_parts = of_quarters(after(attended, shared_far))
+
+    out_pairs = paired(out_low, out_high)
+    grad_home, out_pairs = lax.optimization_barrier(
+        (grad_home, out_pairs, shared_dx, tuple(att_parts))
+    )[:2]
+    grad_norm_two = jnp.sum(grad_home.astype(F32), axis=0) + shared_dx
     grad_full = own_grads.astype(F32)
     grad_second, second_gain_local = norm_backward(
         grad_norm_two, hidden_state, second_scale, second_gain
@@ -752,40 +816,39 @@
     do_send = jnp.concatenate([grad_attended] * groups + [grad_attended[: units - groups * heads]], axis=0)
     do_units = exchange(do_send, BOTH).reshape(blocks, rows, hd)
 
-    out_pairs = paired(out_parts[:half], out_parts[half:])
-    place = jnp.stack([rank // 2, rank % 2, quarter])
-    out_low, out_high = output_grads(
-        place, of_quarters(grad_attn), of_quarters(attended), heads, hw, blocks
-    )
-    do_units = lax.optimization_barrier((do_units, to_far[2], tuple(out_pairs), out_low))[0]
+    from_far = beside(after(parts[3], grad_home))
+    to_far = [(parts[2][m].astype(F32) + from_far[m].astype(F32)).astype(BF) for m in range(3)]
+    near = beside(after(parts[1], from_far))
+    routed_far = [across(to_far[0]), across(to_far[1])]
+    proj_low, proj_high = output_grads(
+        place, of_quarters(grad_attn), att_parts, heads, hw, blocks
+    )
+    do_units, to_far_last = lax.optimization_barrier(
+        (do_units, to_far[2], proj_low)
+    )[:2]
 
     grad_units = attend_back(bounds, arrived, seg_col, seg_row, lse, do_units, most)
-    routed_far = [across(g) for g in to_far]
+    routed_far.append(across(to_far_last))
     out_home = collected(out_pairs)
-    out_grad_pairs = paired([out_low], [out_high])[0]
-    gate_send = gate_sums[:, :slots_local].reshape(blocks, own, slots_local).transpose(0, 2, 1)
-    away = rank ^ index
-    gate_send = after(gate_send, do_units)[away // 2 + (away % 2) * half]
-    gate_back = exchange(gate_send, "expert").reshape(experts_total, own)
-    grad_units = lax.optimization_barrier(
-        (grad_units, out_home, out_grad_pairs, routed_far[0], gate_back)
-    )[0]
+    proj_pairs = paired(proj_low, proj_high)
+    grad_units = lax.optimization_barrier((grad_units, out_home, proj_pairs, routed_far[0]))[0]
     back_grads = exchange(grad_units.reshape(units, 3 * hw, rows), BOTH)
 
+    rows_late = after(rows_in, grad_units)
     shared_parts = [
-        shared_grads(
-            after(rows_in, grad_units)[c], grads_in[c], rows_cut[c], grads_cut[c], *shared_ws
-        )
-        for c in spans
+        shared_grads(rows_late[c], grads_in[c], rows_cut[c], grads_cut[c], shared_ws) for c in spans
     ]
     shared_parts = shared_parts[0] if len(spans) == 1 else added(shared_parts).astype(BF)
-    out_grad = collected([out_grad_pairs[j] for j in range(half)])
-    output = in_order(of_quarters((hidden_state + out_home + shared_out).astype(BF)), quarter)
-    gate_grad = jnp.sum(jnp.where(slot_hot, after(gate_back, grad_units).T[:, None, :], 0.0), axis=2)
+    out_grad = collected(proj_pairs)
+    moe_out = out_home[:, :width] + shared_out
+    output = in_order(of_quarters((hidden_state + moe_out).astype(BF)), quarter)
+    slot_sums = out_home[:, width : width + 3 * experts_total].reshape(own, 3, experts_total)
+    slot_sums = jnp.sum(slot_sums, axis=1)
+    gate_grad = jnp.sum(jnp.where(slot_hot, slot_sums[:, None, :], 0.0), axis=2)
     gate_grad = in_order(of_quarters(gate_grad), quarter)
-    routed = [added([a, b, c]) for (a, b), c in zip(near, routed_far)]
+    routed = [added([parts[0][m], near[m], routed_far[m]]) for m in range(2)]
     back_grads = lax.optimization_barrier(
-        (back_grads, shared_parts, out_grad, routed_far[1], routed[0])
+        (back_grads, shared_parts, out_grad, output, routed[0], routed_far[1])
     )[0]
 
     back_out = project_back(
@@ -793,6 +856,7 @@
         back_grads,
         cosine,
         sine,
+        tokens,
         normed_one,
         query_weight,
         key_weight,
@@ -801,19 +865,23 @@
         blocks,
         quarters,
     )
-    grad_one = added([back_out[0][0]] + [flip(back_out[0][k], k, "tensor") for k in range(1, quarters)])
-    qkv_grads = []
-    for m in range(3):
-        sums = paired([back_out[1 + 2 * m]], [back_out[2 + 2 * m]])[0]
-        qkv_grads.append(collected([sums[j] for j in range(half)]))
+    gains = jnp.stack([back_out[1][0], second_gain_local]).reshape(2, blocks, cut).transpose(1, 0, 2)
+    gains = jnp.broadcast_to(gains[:, None], (blocks, quarters, 2, cut)).reshape(units, 2, cut)
+    gains = exchange(gains, BOTH)
+    dx_parts = [back_out[0][0]] + [flip(back_out[0][k], k, "tensor") for k in range(1, quarters)]
+    pair_q = paired(back_out[2], back_out[3])
+    pair_k = paired(back_out[4], after(back_out[5], pair_q))
+    dx_parts, pair_q = lax.optimization_barrier((tuple(dx_parts), pair_q))
+    grad_one = added(dx_parts)
+    pair_v = paired(back_out[6], after(back_out[7], pair_k))
+    qkv_grads = [collected(p) for p in (pair_q, pair_k, pair_v)]
     first_scale = rms_scale(own_tokens)
-    grad_first, first_gain_local = norm_backward(grad_one, own_tokens, first_scale, first_gain)
-    input_grad = in_order(of_quarters((grad_hidden + grad_first).astype(BF)), quarter)
+    grad_first, _ = norm_backward(grad_one, own_tokens, first_scale, first_gain)
+    input_mine = after((grad_hidden + grad_first).astype(BF), pair_k)
+    input_grad = in_order(of_quarters(input_mine), quarter)
     shared = added([shared_parts[0]] + [flip(shared_parts[k], k, "tensor") for k in range(1, quarters)])
-
-    gains = jnp.stack([first_gain_local, second_gain_local]).reshape(2, blocks, cut).transpose(1, 0, 2)
-    gains = jnp.broadcast_to(gains[:, None], (blocks, quarters, 2, cut)).reshape(units, 2, cut)
-    gains = jnp.sum(exchange(gains, BOTH), axis=0)
+    gains = jnp.sum(after(gains, pair_v), axis=0)
+    routed.append(added([parts[0][2], near[2], after(routed_far[2], pair_q)]))
 
     weight_shape = (heads, 2, pair_width, cut)
     return (

time: 535 us -> 496 us (0.927)
  starting transfers between devices: 139 us -> 97.6 us
  waiting for transfers between devices: 182 us -> 205 us
  local copies, waits for them, and re-layouts: 56.1 us -> 38.4 us
  other arithmetic: 45.6 us -> 37.6 us
    ppermute x95 -> x65, waiting for transfers between devices: 162 us -> 205 us  [flip(): return lax.ppermute(x, axis, [(i, i ^ by) for i in range(size)])]
    ppermute x95 -> x65, starting transfers between devices: 98.4 us -> 59.5 us  [flip(): return lax.ppermute(x, axis, [(i, i ^ by) for i in range(size)])]
    all_to_all x7, waiting for transfers between devices: 20.4 us -> 0.02 us  [exchange(): return lax.all_to_all(x, axis, 0, 0, tiled=True)]
    unnamed x136 -> x81, local copies, waits for them, and re-layouts: 20.8 us -> 7.41 us
    convert_element_type x10 -> x9, other arithmetic: 17.4 us -> 9.49 us  [the longest x5 4.73 us: paired(): return (evens.astype(F32) + flip(odds, 1, 'expert').astype(F32)).astype(BF)]
  transfers between devices with their start and end apart: 102 -> 72, of which waited for: 33 -> 22; matrix products, arithmetic and copies ran while one was open for 18% -> 14% of each run, Pallas kernels for 14% -> 20%
where the time goes in v3:
time: 496 us; the launch traced here: 488 us
  waiting for transfers between devices  205 us (41%)
  Pallas kernels  103 us (21%)
  starting transfers between devices  97.6 us (20%)
  local copies, waits for them, and re-layouts  38.4 us (8%)
  other arithmetic  37.6 us (8%)
    ppermute x65, waiting for transfers between devices, flip(): return lax.ppermute(x, axis, [(i, i ^ by) for i in range(size)])  205 us
    ppermute x65, starting transfers between devices, flip(): return lax.ppermute(x, axis, [(i, i ^ by) for i in range(size)])  59.5 us
    all_to_all x7, starting transfers between devices, exchange(): return lax.all_to_all(x, axis, 0, 0, tiled=True)  38.1 us
    pallas_call x1, Pallas kernels, experts_first(): pl.pallas_call(body, grid_spec=pltpu.PrefetchScalarGridSpec(num_scalar_pr...  21.1 us
    pallas_call x1, Pallas kernels, experts_second(): pl.pallas_call(body, grid_spec=pltpu.PrefetchScalarGridSpec(num_scalar_pr...  18.6 us
    pallas_call x1, Pallas kernels, shared_grads(): pl.pallas_call(body, out_shape=jax.ShapeDtypeStruct((parts, 3, hidden, cu...  12.5 us
    add x5, other arithmetic, added(): total = total + p.astype(F32)  12.4 us
    pallas_call x1, Pallas kernels, attend_back(): pl.pallas_call(body, grid_spec=grid_spec, out_shape=jax.ShapeDtypeStruct(...  11.4 us
  transfers between devices with their start and end apart: 72, of which 22 were waited for; matrix products, arithmetic and copies ran while one was open for 14% of the time, Pallas kernels for 20%

profile of v3, /device:TPU:0, one launch (start us, length us, event | category | flops | bytes accessed | tf_op | source)
XLA Modules:
  0.0 487.6 jit_solution(10914539025460889316)
XLA Ops:
  8.6 7.4 %all-to-all-start = ((bf16[32,96,256]{2,1,0:T(8,128)(2,1)}), bf16[32,96,256]{2,1,0:T(8,128)(2,1)}, u32[]{:S(2)}, u32[]{:S(2)}) async-start(bf16[32,96,256]{2,1,0:T(8,128)(2,1)} %get-tuple-element.75), calls=%async_computation | async-start | bytes 3145728 | tf_op jit(solution)/shard_map/all_to_all | solution.py:606
  26.0 27.3 %collective-permute-done = bf16[10,32,1280]{2,1,0:T(8,128)(2,1)} collective-permute-done((bf16[10,32,1280]{2,1,0:T(8,128)(2,1)}, bf16[10,32,1280]{2,1,0:T(8,128)(2,1)}, u32[]{:S(2)}, u32[]{:S(2)}) %collective-permute-start) | collective-permute-done | bytes 819232 | tf_op jit(solution)/shard_map/ppermute | solution.py:602
  56.8 9.3 %attend.1 = (bf16[8,256,128]{2,1,0:T(8,128)(2,1)}, f32[8,256,128]{2,1,0:T(8,128)}) custom-call(s32[2]{0:T(128)} %pad_add_fusion.bounds_ref, bf16[8,4,96,256]{3,2,1,0:T(8,128)(2,1)} %bitcast.3.arr_ref, s32[8,256,128]{2,1,0:T(8,128)} %broadcast_in_dim.133.col_ref, s32[8,1,256]{2,1,0:T(1,128)} %bitcast.216), custom_call_target="tpu_custom_call" | custom-call | tf_op jit(solution)/shard_map/attend/pallas_call | solution.py:146
  77.7 9.7 %collective-permute-done.4 = bf16[64,1408]{1,0:T(8,128)(2,1)S(1)} collective-permute-done((bf16[64,1408]{1,0:T(8,128)(2,1)S(1)}, bf16[64,1408]{1,0:T(8,128)(2,1)S(1)}, u32[]{:S(2)}, u32[]{:S(2)}) %collective-permute-start.4) | collective-permute-done | bytes 180256 | tf_op jit(solution)/shard_map/ppermute | solution.py:602
  88.8 9.0 %collective-permute-done.5 = bf16[64,1408]{1,0:T(8,128)(2,1)S(1)} collective-permute-done((bf16[64,1408]{1,0:T(8,128)(2,1)S(1)}, bf16[64,1408]{1,0:T(8,128)(2,1)S(1)}, u32[]{:S(2)}, u32[]{:S(2)}) %collective-permute-start.5) | collective-permute-done | bytes 180256 | tf_op jit(solution)/shard_map/ppermute | solution.py:602
  104.1 6.3 %all-to-all-start.2 = ((bf16[8,64,1280]{2,1,0:T(8,128)(2,1)}), bf16[8,64,1280]{2,1,0:T(8,128)(2,1)}, u32[]{:S(2)}, u32[]{:S(2)}) async-start(bf16[8,64,1280]{2,1,0:T(8,128)(2,1)} %broadcast_in_dim.144), calls=%async_computation.2 | async-start | bytes 2621440 | tf_op jit(solution)/shard_map/all_to_all | solution.py:606
  119.1 23.0 %collective-permute-done.7.odd_ref = bf16[4,64,1408]{2,1,0:T(8,128)(2,1)} collective-permute-done((bf16[4,64,1408]{2,1,0:T(8,128)(2,1)}, bf16[4,64,1408]{2,1,0:T(8,128)(2,1)}, u32[]{:S(2)}, u32[]{:S(2)}) %collective-permute-start.7) | collective-permute-done | bytes 720928 | tf_op jit(solution)/shard_map/ppermute | solution.py:602
  143.8 7.5 %down_products.1 = (f32[2,4,512,224]{3,2,1,0:T(8,128)}, bf16[512,1280]{1,0:T(8,128)(2,1)}, bf16[512,128]{1,0:T(8,128)(2,1)}) custom-call(s32[4]{0:T(128)} %pad_add_fusion.1.place_ref, bf16[4,64,1408]{2,1,0:T(8,128)(2,1)} %pad_maximum_fusion.1.even_ref, bf16[4,64,1408]{2,1,0:T(8,128)(2,1)} %collective-permute-done.7.odd_ref, bf16[2,224,1280]{2,1,0:T(8,128)(2,1)} %refs_0_.2, ...), custom_call_target="tpu_custom_call" | custom-call | tf_op jit(solution)/shard_map/down_products/pallas_call | solution.py:266
  151.4 21.1 %experts_first.1 = (bf16[2,4,512,224]{3,2,1,0:T(8,128)(2,1)}, bf16[2,4,512,224]{3,2,1,0:T(8,128)(2,1)}, bf16[2,4,512,224]{3,2,1,0:T(8,128)(2,1)}, bf16[512,128]{1,0:T(8,128)(2,1)}, bf16[512,1280]{1,0:T(8,128)(2,1)}) custom-call(s32[4]{0:T(128)} %pad_add_fusion.1.place_ref, bf16[512,1280]{1,0:T(8,128)(2,1)} %bitcast.26.x_ref, ...), custom_call_target="tpu_custom_call" | custom-call | tf_op jit(solution)/shard_map/experts_first/pallas_call | solution.py:345
  182.5 18.6 %experts_second.1 = (bf16[4,64,1408]{2,1,0:T(8,128)(2,1)}, bf16[4,64,1408]{2,1,0:T(8,128)(2,1)}, bf16[3,2,224,1280]{3,2,1,0:T(8,128)(2,1)}, bf16[3,2,224,1280]{3...) custom-call(s32[4]{0:T(128)} %pad_add_fusion.1.place_ref, ...), custom_call_target="tpu_custom_call" | custom-call | tf_op jit(solution)/shard_map/experts_second/pallas_call | solution.py:405
  204.4 15.9 %collective-permute-done.18 = bf16[4,64,1408]{2,1,0:T(8,128)(2,1)S(1)} collective-permute-done((bf16[4,64,1408]{2,1,0:T(8,128)(2,1)}, bf16[4,64,1408]{2,1,0:T(8,128)(2,1)S(1)}, u32[]{:S(2)}, u32[]{:S(2)}) %collective-permute-start.18) | collective-permute-done | bytes 720928 | tf_op jit(solution)/shard_map/ppermute | solution.py:602
  222.5 7.9 %shared_own.1 = (f32[64,1280]{1,0:T(8,128)}, f32[64,1280]{1,0:T(8,128)}) custom-call(bf16[64,1280]{1,0:T(8,128)(2,1)} %copy-done.10, bf16[64,1280]{1,0:T(8,128)(2,1)} %copy-done.9, bf16[3,224,1280]{2,1,0:T(8,128)(2,1)} %pad_maximum_fusion.refs_0_, bf16[3,224,1280]{2,1,0:T(8,128)(2,1)} %collective-permute-done.17.refs_1_, ...), custom_call_target="tpu_custom_call" | custom-call | tf_op jit(solution)/shard_map/shared_own/pallas_call | solution.py:446
  275.0 25.3 %collective-permute-done.50 = f32[64,7]{0,1:T(8,128)S(1)} collective-permute-done((f32[64,7]{0,1:T(8,128)S(1)}, f32[64,7]{0,1:T(8,128)S(1)}, u32[]{:S(2)}, u32[]{:S(2)}) %collective-permute-start.50) | collective-permute-done | bytes 1824 | tf_op jit(solution)/shard_map/ppermute | solution.py:602
  303.9 11.4 %attend_back.1 = bf16[8,4,96,256]{3,2,1,0:T(8,128)(2,1)} custom-call(s32[2]{0:T(128)} %pad_add_fusion.bounds_ref, bf16[8,4,96,256]{3,2,1,0:T(8,128)(2,1)} %bitcast.3.arr_ref, s32[8,256,128]{2,1,0:T(8,128)} %broadcast_in_dim.133.col_ref, s32[8,1,256]{2,1,0:T(1,128)} %bitcast.217, f32[8,256,128]{2,1,0:T(8,128)} %get-tuple-element.103.lse_ref, ...), custom_call_target="tpu_custom_call" | custom-call | tf_op jit(solution)/shard_map/attend_back/pallas_call | solution.py:229
  316.3 8.3 %all-to-all-start.5 = ((bf16[32,96,256]{2,1,0:T(8,128)(2,1)}), bf16[32,96,256]{2,1,0:T(8,128)(2,1)S(1)}, u32[]{:S(2)}, u32[]{:S(2)}) async-start(bf16[32,96,256]{2,1,0:T(8,128)(2,1)} %bitcast.193), calls=%async_computation.5 | async-start | bytes 3145728 | tf_op jit(solution)/shard_map/all_to_all | solution.py:606
  331.1 12.5 %shared_grads.1 = bf16[4,3,224,160]{3,2,1,0:T(8,128)(2,1)} custom-call(bf16[512,1280]{1,0:T(8,128)(2,1)} %bitcast.26.x_ref, bf16[512,1280]{1,0:T(8,128)(2,1)} %get-tuple-element.88.dy_ref, bf16[512,160]{1,0:T(8,128)(2,1)} %constant_dynamic-slice_fusion.1.xc_ref, bf16[512,160]{1,0:T(8,128)(2,1)} %constant_dynamic-slice_fusion.dyc_ref, ...), custom_call_target="tpu_custom_call" | custom-call | tf_op jit(solution)/shard_map/shared_grads/pallas_call | solution.py:471
  345.9 7.8 %collective-permute-done.35 = bf16[160,320]{1,0:T(8,128)(2,1)S(1)} collective-permute-done((bf16[160,320]{1,0:T(8,128)(2,1)S(1)}, bf16[160,320]{1,0:T(8,128)(2,1)S(1)}, u32[]{:S(2)}, u32[]{:S(2)}) %collective-permute-start.35) | collective-permute-done | bytes 102432 | tf_op jit(solution)/shard_map/ppermute | solution.py:602
  355.6 14.9 %collective-permute-done.36 = bf16[160,320]{1,0:T(8,128)(2,1)S(1)} collective-permute-done((bf16[160,320]{1,0:T(8,128)(2,1)S(1)}, bf16[160,320]{1,0:T(8,128)(2,1)S(1)}, u32[]{:S(2)}, u32[]{:S(2)}) %collective-permute-start.36) | collective-permute-done | bytes 102432 | tf_op jit(solution)/shard_map/ppermute | solution.py:602
  373.6 7.5 %collective-permute-done.63 = bf16[3,224,160]{2,1,0:T(8,128)(2,1)} collective-permute-done((bf16[3,224,160]{2,1,0:T(8,128)(2,1)}, bf16[3,224,160]{2,1,0:T(8,128)(2,1)}, u32[]{:S(2)}, u32[]{:S(2)}) %collective-permute-start.63) | collective-permute-done | bytes 215072 | tf_op jit(solution)/shard_map/ppermute | solution.py:602
  388.6 17.2 %collective-permute-done.39 = bf16[2,224,1280]{2,1,0:T(8,128)(2,1)} collective-permute-done((bf16[2,224,1280]{2,1,0:T(8,128)(2,1)}, bf16[2,224,1280]{2,1,0:T(8,128)(2,1)}, u32[]{:S(2)}, u32[]{:S(2)}) %collective-permute-start.39) | collective-permute-done | bytes 1146912 | tf_op jit(solution)/shard_map/ppermute | solution.py:602
  407.0 6.7 %project_back.1 = (bf16[4,64,1280]{2,1,0:T(8,128)(2,1)}, f32[1,1280]{1,0:T(1,128)}, bf16[4,160,320]{2,1,0:T(8,128)(2,1)}, bf16[4,160,320]{2,1,0:T(8,128)(2,1)}, ...) custom-call(s32[4]{0:T(128)} %pad_add_fusion.1.place_ref, ...), custom_call_target="tpu_custom_call" | custom-call | tf_op jit(solution)/shard_map/project_back/pallas_call | solution.py:561
  428.4 6.0 %collective-permute-done.41 = bf16[64,1280]{1,0:T(8,128)(2,1)S(1)} collective-permute-done((bf16[64,1280]{1,0:T(8,128)(2,1)S(1)}, bf16[64,1280]{1,0:T(8,128)(2,1)S(1)}, u32[]{:S(2)}, u32[]{:S(2)}) %collective-permute-start.41) | collective-permute-done | bytes 163872 | tf_op jit(solution)/shard_map/ppermute | solution.py:602
  460.5 7.3 %collective-permute-done.56 = bf16[160,320]{1,0:T(8,128)(2,1)S(1)} collective-permute-done((bf16[160,320]{1,0:T(8,128)(2,1)S(1)}, bf16[160,320]{1,0:T(8,128)(2,1)S(1)}, u32[]{:S(2)}, u32[]{:S(2)}) %collective-permute-start.56) | collective-permute-done | bytes 102432 | tf_op jit(solution)/shard_map/ppermute | solution.py:602
  469.3 7.5 %collective-permute-done.51 = bf16[4,160,320]{2,1,0:T(8,128)(2,1)S(1)} collective-permute-done((bf16[4,160,320]{2,1,0:T(8,128)(2,1)}, bf16[4,160,320]{2,1,0:T(8,128)(2,1)S(1)}, u32[]{:S(2)}, u32[]{:S(2)}) %collective-permute-start.51) | collective-permute-done | bytes 409632 | tf_op jit(solution)/shard_map/ppermute | solution.py:602
  (317 shorter events, 189.9 us)
Async XLA Ops:
  8.6 46.8 %all-to-all-start = ((bf16[32,96,256]{2,1,0:T(8,128)(2,1)}), bf16[32,96,256]{2,1,0:T(8,128)(2,1)}, u32[]{:S(2)}, u32[]{:S(2)}) async-start(bf16[32,96,256]{2,1,0:T(8,128)(2,1)} %get-tuple-element.75), calls=%async_computation | async-start | bytes 3145728 | tf_op jit(solution)/shard_map/all_to_all | solution.py:606
  16.1 37.2 %collective-permute-start = (bf16[10,32,1280]{2,1,0:T(8,128)(2,1)}, bf16[10,32,1280]{2,1,0:T(8,128)(2,1)}, u32[]{:S(2)}, u32[]{:S(2)}) collective-permute-start(bf16[10,32,1280]{2,1,0:T(8,128)(2,1)} %bitcast.4), channel_id=1, source_target_pairs={{0,2},{1,3},{2,0},{3,1},{4,6},{5,7},{6,4},{7,5},{8,10},{9,11},{10,... | collective-permute-start | bytes 2457608 | tf_op jit(solution)/shard_map/ppermute | solution.py:602
  17.8 36.4 %collective-permute-start.1 = (bf16[10,32,1280]{2,1,0:T(8,128)(2,1)}, bf16[10,32,1280]{2,1,0:T(8,128)(2,1)}, u32[]{:S(2)}, u32[]{:S(2)}) collective-permute-start(bf16[10,32,1280]{2,1,0:T(8,128)(2,1)} %bitcast.4), channel_id=1, source_target_pairs={{0,1},{1,0},{2,3},{3,2},{4,5},{5,4},{6,7},{7,6},{8,9},{9,8},{10,11... | collective-permute-start | bytes 2457608 | tf_op jit(solution)/shard_map/ppermute | solution.py:602
  53.3 47.0 %collective-permute-start.3 = (bf16[2,224,1280]{2,1,0:T(8,128)(2,1)}, bf16[2,224,1280]{2,1,0:T(8,128)(2,1)}, u32[]{:S(2)}, u32[]{:S(2)}) collective-permute-start(bf16[2,224,1280]{2,1,0:T(8,128)(2,1)} %refs_0_.1), channel_id=1, source_target_pairs={{0,2},{1,3},{2,0},{3,1},{4,6},{5,7},{6,4},{7,5},{8,10},{9,11},{10,... | collective-permute-start | bytes 3440648 | tf_op jit(solution)/shard_map/ppermute | solution.py:602
  53.7 64.9 %collective-permute-start.11 = (bf16[2,224,1280]{2,1,0:T(8,128)(2,1)}, bf16[2,224,1280]{2,1,0:T(8,128)(2,1)}, u32[]{:S(2)}, u32[]{:S(2)}) collective-permute-start(bf16[2,224,1280]{2,1,0:T(8,128)(2,1)} %refs_0_.1), channel_id=1, source_target_pairs={{0,1},{1,0},{2,3},{3,2},{4,5},{5,4},{6,7},{7,6},{8,9},{9,8},{10,11... | collective-permute-start | bytes 3440648 | tf_op jit(solution)/shard_map/ppermute | solution.py:602
  97.8 44.8 %collective-permute-start.8 = (bf16[2,224,1280]{2,1,0:T(8,128)(2,1)}, bf16[2,224,1280]{2,1,0:T(8,128)(2,1)}, u32[]{:S(2)}, u32[]{:S(2)}) collective-permute-start(bf16[2,224,1280]{2,1,0:T(8,128)(2,1)} %refs_0_.2), channel_id=1, source_target_pairs={{0,1},{1,0},{2,3},{3,2},{4,5},{5,4},{6,7},{7,6},{8,9},{9,8},{10,11... | collective-permute-start | bytes 3440648 | tf_op jit(solution)/shard_map/ppermute | solution.py:602
  97.8 44.3 %collective-permute-start.14 = (bf16[2,224,1280]{2,1,0:T(8,128)(2,1)}, bf16[2,224,1280]{2,1,0:T(8,128)(2,1)}, u32[]{:S(2)}, u32[]{:S(2)}) collective-permute-start(bf16[2,224,1280]{2,1,0:T(8,128)(2,1)} %refs_4_), channel_id=1, source_target_pairs={{0,2},{1,3},{2,0},{3,1},{4,6},{5,7},{6,4},{7,5},{8,10},{9,11},{10,... | collective-permute-start | bytes 3440648 | tf_op jit(solution)/shard_map/ppermute | solution.py:602
  104.1 47.3 %all-to-all-start.2 = ((bf16[8,64,1280]{2,1,0:T(8,128)(2,1)}), bf16[8,64,1280]{2,1,0:T(8,128)(2,1)}, u32[]{:S(2)}, u32[]{:S(2)}) async-start(bf16[8,64,1280]{2,1,0:T(8,128)(2,1)} %broadcast_in_dim.144), calls=%async_computation.2 | async-start | bytes 2621440 | tf_op jit(solution)/shard_map/all_to_all | solution.py:606
  142.6 39.8 %collective-permute-start.16 = (bf16[3,224,1280]{2,1,0:T(8,128)(2,1)}, bf16[3,224,1280]{2,1,0:T(8,128)(2,1)}, u32[]{:S(2)}, u32[]{:S(2)}) collective-permute-start(bf16[3,224,1280]{2,1,0:T(8,128)(2,1)} %pad_maximum_fusion.refs_0_), channel_id=1, source_target_pairs={{0,2},{1,3},{2,0},{3,1},{4,6},{5,7},{6,4},{7,5},{8,10},{9,11},{10,... | collective-permute-start | bytes 5160968 | tf_op jit(solution)/shard_map/ppermute | solution.py:602
  143.2 39.3 %collective-permute-start.17 = (bf16[3,224,1280]{2,1,0:T(8,128)(2,1)}, bf16[3,224,1280]{2,1,0:T(8,128)(2,1)}, u32[]{:S(2)}, u32[]{:S(2)}) collective-permute-start(bf16[3,224,1280]{2,1,0:T(8,128)(2,1)} %pad_maximum_fusion.refs_0_), channel_id=1, source_target_pairs={{0,1},{1,0},{2,3},{3,2},{4,5},{5,4},{6,7},{7,6},{8,9},{9,8},{10,11... | collective-permute-start | bytes 5160968 | tf_op jit(solution)/shard_map/ppermute | solution.py:602
  172.5 59.3 %all-to-all-start.3 = ((bf16[8,64,1280]{2,1,0:T(8,128)(2,1)}), bf16[8,64,1280]{2,1,0:T(8,128)(2,1)}, u32[]{:S(2)}, u32[]{:S(2)}) async-start(bf16[8,64,1280]{2,1,0:T(8,128)(2,1)} %bitcast.200), calls=%async_computation.3 | async-start | bytes 2621440 | tf_op jit(solution)/shard_map/all_to_all | solution.py:606
  182.5 40.0 %collective-permute-start.19 = (bf16[3,224,1280]{2,1,0:T(8,128)(2,1)}, bf16[3,224,1280]{2,1,0:T(8,128)(2,1)}, u32[]{:S(2)}, u32[]{:S(2)}) collective-permute-start(bf16[3,224,1280]{2,1,0:T(8,128)(2,1)} %collective-permute-done.16.refs_2_), channel_id=1, source_target_pairs={{0,1},{1,0},{2,3},{3,2},{4,5},{5,4},{6,7},{7,6},{8,9},{9,8},{10,11... | collective-permute-start | bytes 5160968 | tf_op jit(solution)/shard_map/ppermute | solution.py:602
  231.8 36.2 %collective-permute-start.29 = (bf16[3,2,224,1280]{3,2,1,0:T(8,128)(2,1)}, bf16[3,2,224,1280]{3,2,1,0:T(8,128)(2,1)}, u32[]{:S(2)}, u32[]{:S(2)}) collective-permute-start(bf16[3,2,224,1280]{3,2,1,0:T(8,128)(2,1)} %get-tuple-element.106), channel_id=1, source_target_pairs={{0,1},{1,0},{2,3},{3,2},{4,5},{5,4},{6,7},{7,6},{8,9},{9,8},{10,11... | collective-permute-start | bytes 10321928 | tf_op jit(solution)/shard_map/ppermute | solution.py:602
  254.5 49.4 %all-to-all-start.4 = ((bf16[32,64,128]{2,1,0:T(8,128)(2,1)}), bf16[32,64,128]{2,1,0:T(8,128)(2,1)}, u32[]{:S(2)}, u32[]{:S(2)}) async-start(bf16[32,64,128]{2,1,0:T(8,128)(2,1)} %pad_maximum_fusion.2), calls=%async_computation.4 | async-start | bytes 1048576 | tf_op jit(solution)/shard_map/all_to_all | solution.py:606
  262.4 39.2 %collective-permute-start.33 = (bf16[4,160,320]{2,1,0:T(8,128)(2,1)}, bf16[4,160,320]{2,1,0:T(8,128)(2,1)}, u32[]{:S(2)}, u32[]{:S(2)}) collective-permute-start(bf16[4,160,320]{2,1,0:T(8,128)(2,1)} %get-tuple-element.109), channel_id=1, source_target_pairs={{0,4},{4,0},{8,12},{12,8},{16,20},{20,16},{24,28},{28,24},{1,5},{5... | collective-permute-start | bytes 1228808 | tf_op jit(solution)/shard_map/ppermute | solution.py:602
  272.5 42.8 %collective-permute-start.34 = (bf16[2,224,1280]{2,1,0:T(8,128)(2,1)}, bf16[2,224,1280]{2,1,0:T(8,128)(2,1)S(1)}, u32[]{:S(2)}, u32[]{:S(2)}) collective-permute-start(bf16[2,224,1280]{2,1,0:T(8,128)(2,1)} %get-tuple-element.219), channel_id=1, source_target_pairs={{0,2},{1,3},{2,0},{3,1},{4,6},{5,7},{6,4},{7,5},{8,10},{9,11},{10,... | collective-permute-start | bytes 3440648 | tf_op jit(solution)/shard_map/ppermute | solution.py:602
  273.2 111.8 %collective-permute-start.38 = (bf16[3,2,224,1280]{3,2,1,0:T(8,128)(2,1)}, bf16[3,2,224,1280]{3,2,1,0:T(8,128)(2,1)}, u32[]{:S(2)}, u32[]{:S(2)}) collective-permute-start(bf16[3,2,224,1280]{3,2,1,0:T(8,128)(2,1)} %get-tuple-element.114), channel_id=1, source_target_pairs={{0,1},{1,0},{2,3},{3,2},{4,5},{5,4},{6,7},{7,6},{8,9},{9,8},{10,11... | collective-permute-start | bytes 10321928 | tf_op jit(solution)/shard_map/ppermute | solution.py:602
  274.9 49.7 %collective-permute-start.26 = (bf16[64,1280]{1,0:T(8,128)(2,1)S(1)}, bf16[64,1280]{1,0:T(8,128)(2,1)S(1)}, u32[]{:S(2)}, u32[]{:S(2)}) collective-permute-start(bf16[64,1280]{1,0:T(8,128)(2,1)S(1)} %get-tuple-element.215), channel_id=1, source_target_pairs={{0,1},{1,0},{2,3},{3,2},{4,5},{5,4},{6,7},{7,6},{8,9},{9,8},{10,11... | collective-permute-start | bytes 491528 | tf_op jit(solution)/shard_map/ppermute | solution.py:602
  316.3 89.5 %all-to-all-start.5 = ((bf16[32,96,256]{2,1,0:T(8,128)(2,1)}), bf16[32,96,256]{2,1,0:T(8,128)(2,1)S(1)}, u32[]{:S(2)}, u32[]{:S(2)}) async-start(bf16[32,96,256]{2,1,0:T(8,128)(2,1)} %bitcast.193), calls=%async_computation.5 | async-start | bytes 3145728 | tf_op jit(solution)/shard_map/all_to_all | solution.py:606
  328.6 41.9 %collective-permute-start.36 = (bf16[160,320]{1,0:T(8,128)(2,1)S(1)}, bf16[160,320]{1,0:T(8,128)(2,1)S(1)}, u32[]{:S(2)}, u32[]{:S(2)}) collective-permute-start(bf16[160,320]{1,0:T(8,128)(2,1)S(1)} %get-tuple-element.245), channel_id=1, source_target_pairs={{0,16},{4,20},{8,24},{12,28},{16,0},{20,4},{24,8},{28,12},{1,17},{... | collective-permute-start | bytes 307208 | tf_op jit(solution)/shard_map/ppermute | solution.py:602
  330.8 39.8 %collective-permute-start.37 = (bf16[160,320]{1,0:T(8,128)(2,1)S(1)}, bf16[160,320]{1,0:T(8,128)(2,1)S(1)}, u32[]{:S(2)}, u32[]{:S(2)}) collective-permute-start(bf16[160,320]{1,0:T(8,128)(2,1)S(1)} %get-tuple-element.244), channel_id=1, source_target_pairs={{0,24},{4,28},{8,16},{12,20},{16,8},{20,12},{24,0},{28,4},{1,25},{... | collective-permute-start | bytes 307208 | tf_op jit(solution)/shard_map/ppermute | solution.py:602
  371.6 34.3 %collective-permute-start.39 = (bf16[2,224,1280]{2,1,0:T(8,128)(2,1)}, bf16[2,224,1280]{2,1,0:T(8,128)(2,1)}, u32[]{:S(2)}, u32[]{:S(2)}) collective-permute-start(bf16[2,224,1280]{2,1,0:T(8,128)(2,1)} %get-tuple-element.218), channel_id=1, source_target_pairs={{0,2},{1,3},{2,0},{3,1},{4,6},{5,7},{6,4},{7,5},{8,10},{9,11},{10,... | collective-permute-start | bytes 3440648 | tf_op jit(solution)/shard_map/ppermute | solution.py:602
  373.0 64.8 %collective-permute-start.64 = (bf16[2,224,1280]{2,1,0:T(8,128)(2,1)S(1)}, bf16[2,224,1280]{2,1,0:T(8,128)(2,1)}, u32[]{:S(2)}, u32[]{:S(2)}) collective-permute-start(bf16[2,224,1280]{2,1,0:T(8,128)(2,1)S(1)} %copy-done.15), channel_id=1, source_target_pairs={{0,2},{1,3},{2,0},{3,1},{4,6},{5,7},{6,4},{7,5},{8,10},{9,11},{10,... | collective-permute-start | bytes 3440648 | tf_op jit(solution)/shard_map/ppermute | solution.py:602
  420.4 61.0 %all-to-all-start.6 = ((f32[32,2,160]{2,1,0:T(2,128)}), f32[32,2,160]{2,1,0:T(2,128)S(1)}, u32[]{:S(2)}, u32[]{:S(2)}) async-start(f32[32,2,160]{2,1,0:T(2,128)} %bitcast.68), calls=%async_computation.6 | async-start | bytes 131072 | tf_op jit(solution)/shard_map/all_to_all | solution.py:606
  (87 other events, 1268.8 us)

commit v4 on v3

--- a/solution.py
+++ b/solution.py
@@ -620,8 +620,9 @@
     return flip(evens, 1, "expert")
 
 
-def paired(evens, odds):
-    return (evens.astype(F32) + flip(odds, 1, "expert").astype(F32)).astype(BF)
+def paired(evens, odds, *others):
+    got = after(flip(odds, 1, "expert"), *others) if others else flip(odds, 1, "expert")
+    return (evens.astype(F32) + got.astype(F32)).astype(BF)
 
 
 def collected(sums):
@@ -778,8 +779,6 @@
     grad_rows = jnp.concatenate([f[4] for f in firsts], axis=0)
     grad_home = exchange(grad_rows.reshape(blocks, own, width), "expert")
 
-    rows_cut = lax.dynamic_slice_in_dim(rows_in, rank * cut, cut, axis=1)
-    grads_cut = lax.dynamic_slice_in_dim(grads_in, rank * cut, cut, axis=1)
     seconds = []
     for c, f in zip(spans, firsts):
         act = lax.optimization_barrier((f[0], shared_far, shared_near))[0]
@@ -799,7 +798,7 @@
     shared_out, shared_dx = shared_own(after(normed_two, out_low), own_grads, shared_ws)
     att_parts = of_quarters(after(attended, shared_far))
 
-    out_pairs = paired(out_low, out_high)
+    out_pairs = paired(out_low, out_high, shared_dx)
     grad_home, out_pairs = lax.optimization_barrier(
         (grad_home, out_pairs, shared_dx, tuple(att_parts))
     )[:2]
@@ -816,40 +815,41 @@
     do_send = jnp.concatenate([grad_attended] * groups + [grad_attended[: units - groups * heads]], axis=0)
     do_units = exchange(do_send, BOTH).reshape(blocks, rows, hd)
 
-    from_far = beside(after(parts[3], grad_home))
+    grad_attn_sent, out_pairs = lax.optimization_barrier((grad_attn, out_pairs, do_send))[:2]
+    from_far = beside(after(parts[3], do_send))
     to_far = [(parts[2][m].astype(F32) + from_far[m].astype(F32)).astype(BF) for m in range(3)]
     near = beside(after(parts[1], from_far))
-    routed_far = [across(to_far[0]), across(to_far[1])]
+    routed_far = [across(to_far[0])]
     proj_low, proj_high = output_grads(
-        place, of_quarters(grad_attn), att_parts, heads, hw, blocks
-    )
-    do_units, to_far_last = lax.optimization_barrier(
-        (do_units, to_far[2], proj_low)
-    )[:2]
+        place, of_quarters(grad_attn_sent), att_parts, heads, hw, blocks
+    )
+    do_units, to_far = lax.optimization_barrier((do_units, to_far, proj_low))[:2]
 
     grad_units = attend_back(bounds, arrived, seg_col, seg_row, lse, do_units, most)
-    routed_far.append(across(to_far_last))
     out_home = collected(out_pairs)
     proj_pairs = paired(proj_low, proj_high)
     grad_units = lax.optimization_barrier((grad_units, out_home, proj_pairs, routed_far[0]))[0]
     back_grads = exchange(grad_units.reshape(units, 3 * hw, rows), BOTH)
 
-    rows_late = after(rows_in, grad_units)
+    rows_late, grads_late = lax.optimization_barrier((rows_in, grads_in, grad_units))[:2]
+    rows_cut = lax.dynamic_slice_in_dim(rows_late, rank * cut, cut, axis=1)
+    grads_cut = lax.dynamic_slice_in_dim(grads_late, rank * cut, cut, axis=1)
     shared_parts = [
-        shared_grads(rows_late[c], grads_in[c], rows_cut[c], grads_cut[c], shared_ws) for c in spans
+        shared_grads(rows_late[c], grads_late[c], rows_cut[c], grads_cut[c], shared_ws) for c in spans
     ]
     shared_parts = shared_parts[0] if len(spans) == 1 else added(shared_parts).astype(BF)
-    out_grad = collected(proj_pairs)
+    out_grad = collected(after(proj_pairs, grad_units))
     moe_out = out_home[:, :width] + shared_out
-    output = in_order(of_quarters((hidden_state + moe_out).astype(BF)), quarter)
     slot_sums = out_home[:, width : width + 3 * experts_total].reshape(own, 3, experts_total)
     slot_sums = jnp.sum(slot_sums, axis=1)
     gate_grad = jnp.sum(jnp.where(slot_hot, slot_sums[:, None, :], 0.0), axis=2)
-    gate_grad = in_order(of_quarters(gate_grad), quarter)
-    routed = [added([parts[0][m], near[m], routed_far[m]]) for m in range(2)]
-    back_grads = lax.optimization_barrier(
-        (back_grads, shared_parts, out_grad, output, routed[0], routed_far[1])
-    )[0]
+    final = [(hidden_state + moe_out).astype(BF)] + [p.astype(BF) for p in pieces(gate_grad)]
+    final = jnp.concatenate(final + [jnp.zeros((own, 128 - 3 * top), BF)], axis=1)
+    final = in_order(of_quarters(after(final, grad_units)), quarter)
+    output = final[:, :width]
+    gate_grad = jnp.sum(final[:, width : width + 3 * top].reshape(rows, 3, top).astype(F32), axis=1)
+    routed = [added([parts[0][0], near[0], routed_far[0]])]
+    back_grads = lax.optimization_barrier((back_grads, shared_parts, out_grad, output, routed[0]))[0]
 
     back_out = project_back(
         place,
@@ -871,17 +871,20 @@
     dx_parts = [back_out[0][0]] + [flip(back_out[0][k], k, "tensor") for k in range(1, quarters)]
     pair_q = paired(back_out[2], back_out[3])
     pair_k = paired(back_out[4], after(back_out[5], pair_q))
-    dx_parts, pair_q = lax.optimization_barrier((tuple(dx_parts), pair_q))
+    far_one = across(after(to_far[1], grad_units))
+    dx_parts, pair_q, far_one = lax.optimization_barrier((tuple(dx_parts), pair_q, far_one))
     grad_one = added(dx_parts)
     pair_v = paired(back_out[6], after(back_out[7], pair_k))
+    far_two = across(after(to_far[2], far_one))
     qkv_grads = [collected(p) for p in (pair_q, pair_k, pair_v)]
     first_scale = rms_scale(own_tokens)
     grad_first, _ = norm_backward(grad_one, own_tokens, first_scale, first_gain)
-    input_mine = after((grad_hidden + grad_first).astype(BF), pair_k)
+    input_mine = after((grad_hidden + grad_first).astype(BF), pair_v)
     input_grad = in_order(of_quarters(input_mine), quarter)
     shared = added([shared_parts[0]] + [flip(shared_parts[k], k, "tensor") for k in range(1, quarters)])
     gains = jnp.sum(after(gains, pair_v), axis=0)
-    routed.append(added([parts[0][2], near[2], after(routed_far[2], pair_q)]))
+    routed.append(added([parts[0][1], near[1], after(far_one, pair_v)]))
+    routed.append(added([parts[0][2], near[2], far_two]))
 
     weight_shape = (heads, 2, pair_width, cut)
     return (

time: 496 us -> 473 us (0.954)
  waiting for transfers between devices: 205 us -> 152 us
  starting transfers between devices: 97.6 us -> 115 us
  local copies, waits for them, and re-layouts: 38.4 us -> 49.6 us
    ppermute x65 -> x62, waiting for transfers between devices: 205 us -> 151 us  [flip(): return lax.ppermute(x, axis, [(i, i ^ by) for i in range(size)])]
    ppermute x65 -> x62, starting transfers between devices: 59.5 us -> 76.3 us  [flip(): return lax.ppermute(x, axis, [(i, i ^ by) for i in range(size)])]
    dynamic_update_slice x12 -> x8, local copies, waits for them, and re-layouts: 2.01 us -> 8.3 us  [in_order(): out = lax.dynamic_update_slice(out, p[None], (quarter ^ k,) + (0,) * p.ndim)]
  transfers between devices with their start and end apart: 72 -> 69, of which waited for: 22 -> 18; matrix products, arithmetic and copies ran while one was open for 14% -> 15% of each run, Pallas kernels for 20% -> 21%
where the time goes in v4:
time: 473 us; the launch traced here: 467 us
  waiting for transfers between devices  152 us (32%)
  starting transfers between devices  115 us (24%)
  Pallas kernels  103 us (22%)
  local copies, waits for them, and re-layouts  49.6 us (10%)
  other arithmetic  42.3 us (9%)
    ppermute x62, waiting for transfers between devices, flip(): return lax.ppermute(x, axis, [(i, i ^ by) for i in range(size)])  151 us
    ppermute x62, starting transfers between devices, flip(): return lax.ppermute(x, axis, [(i, i ^ by) for i in range(size)])  76.3 us
    all_to_all x7, starting transfers between devices, exchange(): return lax.all_to_all(x, axis, 0, 0, tiled=True)  38.3 us
    pallas_call x1, Pallas kernels, experts_first(): pl.pallas_call(body, grid_spec=pltpu.PrefetchScalarGridSpec(num_scalar_pr...  21.1 us
    pallas_call x1, Pallas kernels, experts_second(): pl.pallas_call(body, grid_spec=pltpu.PrefetchScalarGridSpec(num_scalar_pr...  18.6 us
    add x5, other arithmetic, added(): total = total + p.astype(F32)  12.6 us
    pallas_call x1, Pallas kernels, shared_grads(): pl.pallas_call(body, out_shape=jax.ShapeDtypeStruct((parts, 3, hidden, cu...  12.5 us
    pallas_call x1, Pallas kernels, attend_back(): pl.pallas_call(body, grid_spec=grid_spec, out_shape=jax.ShapeDtypeStruct(...  11.4 us
  transfers between devices with their start and end apart: 69, of which 18 were waited for; matrix products, arithmetic and copies ran while one was open for 15% of the time, Pallas kernels for 21%

profile of v4, /device:TPU:0, one launch (start us, length us, event | category | flops | bytes accessed | tf_op | source)
XLA Modules:
  0.0 466.5 jit_solution(5579092356152692017)
XLA Ops:
  8.6 7.4 %all-to-all-start = ((bf16[32,96,256]{2,1,0:T(8,128)(2,1)}), bf16[32,96,256]{2,1,0:T(8,128)(2,1)}, u32[]{:S(2)}, u32[]{:S(2)}) async-start(bf16[32,96,256]{2,1,0:T(8,128)(2,1)} %get-tuple-element.85), calls=%async_computation | async-start | bytes 3145728 | tf_op jit(solution)/shard_map/all_to_all | solution.py:606
  26.0 27.3 %collective-permute-done = bf16[10,32,1280]{2,1,0:T(8,128)(2,1)} collective-permute-done((bf16[10,32,1280]{2,1,0:T(8,128)(2,1)}, bf16[10,32,1280]{2,1,0:T(8,128)(2,1)}, u32[]{:S(2)}, u32[]{:S(2)}) %collective-permute-start) | collective-permute-done | bytes 819232 | tf_op jit(solution)/shard_map/ppermute | solution.py:602
  56.8 9.3 %attend.1 = (bf16[8,256,128]{2,1,0:T(8,128)(2,1)}, f32[8,256,128]{2,1,0:T(8,128)}) custom-call(s32[2]{0:T(128)} %pad_add_fusion.bounds_ref, bf16[8,4,96,256]{3,2,1,0:T(8,128)(2,1)} %bitcast.3.arr_ref, s32[8,256,128]{2,1,0:T(8,128)} %broadcast_in_dim.128.col_ref, s32[8,1,256]{2,1,0:T(1,128)} %bitcast.207), custom_call_target="tpu_custom_call" | custom-call | tf_op jit(solution)/shard_map/attend/pallas_call | solution.py:146
  77.7 9.7 %collective-permute-done.4 = bf16[64,1408]{1,0:T(8,128)(2,1)S(1)} collective-permute-done((bf16[64,1408]{1,0:T(8,128)(2,1)S(1)}, bf16[64,1408]{1,0:T(8,128)(2,1)S(1)}, u32[]{:S(2)}, u32[]{:S(2)}) %collective-permute-start.4) | collective-permute-done | bytes 180256 | tf_op jit(solution)/shard_map/ppermute | solution.py:602
  88.9 9.0 %collective-permute-done.5 = bf16[64,1408]{1,0:T(8,128)(2,1)S(1)} collective-permute-done((bf16[64,1408]{1,0:T(8,128)(2,1)S(1)}, bf16[64,1408]{1,0:T(8,128)(2,1)S(1)}, u32[]{:S(2)}, u32[]{:S(2)}) %collective-permute-start.5) | collective-permute-done | bytes 180256 | tf_op jit(solution)/shard_map/ppermute | solution.py:602
  104.1 6.3 %all-to-all-start.2 = ((bf16[8,64,1280]{2,1,0:T(8,128)(2,1)}), bf16[8,64,1280]{2,1,0:T(8,128)(2,1)}, u32[]{:S(2)}, u32[]{:S(2)}) async-start(bf16[8,64,1280]{2,1,0:T(8,128)(2,1)} %broadcast_in_dim.139), calls=%async_computation.2 | async-start | bytes 2621440 | tf_op jit(solution)/shard_map/all_to_all | solution.py:606
  120.1 22.0 %collective-permute-done.7.odd_ref = bf16[4,64,1408]{2,1,0:T(8,128)(2,1)} collective-permute-done((bf16[4,64,1408]{2,1,0:T(8,128)(2,1)}, bf16[4,64,1408]{2,1,0:T(8,128)(2,1)}, u32[]{:S(2)}, u32[]{:S(2)}) %collective-permute-start.7) | collective-permute-done | bytes 720928 | tf_op jit(solution)/shard_map/ppermute | solution.py:602
  143.8 7.5 %down_products.1 = (f32[2,4,512,224]{3,2,1,0:T(8,128)}, bf16[512,1280]{1,0:T(8,128)(2,1)}, bf16[512,128]{1,0:T(8,128)(2,1)}) custom-call(s32[4]{0:T(128)} %pad_add_fusion.1.place_ref, bf16[4,64,1408]{2,1,0:T(8,128)(2,1)} %pad_maximum_fusion.1.even_ref, bf16[4,64,1408]{2,1,0:T(8,128)(2,1)} %collective-permute-done.7.odd_ref, bf16[2,224,1280]{2,1,0:T(8,128)(2,1)} %refs_0_.2, ...), custom_call_target="tpu_custom_call" | custom-call | tf_op jit(solution)/shard_map/down_products/pallas_call | solution.py:266
  151.3 21.1 %experts_first.1 = (bf16[2,4,512,224]{3,2,1,0:T(8,128)(2,1)}, bf16[2,4,512,224]{3,2,1,0:T(8,128)(2,1)}, bf16[2,4,512,224]{3,2,1,0:T(8,128)(2,1)}, bf16[512,128]{1,0:T(8,128)(2,1)}, bf16[512,1280]{1,0:T(8,128)(2,1)}) custom-call(s32[4]{0:T(128)} %pad_add_fusion.1.place_ref, bf16[512,1280]{1,0:T(8,128)(2,1)} %bitcast.26.x_ref, ...), custom_call_target="tpu_custom_call" | custom-call | tf_op jit(solution)/shard_map/experts_first/pallas_call | solution.py:345
  177.4 18.6 %experts_second.1 = (bf16[4,64,1408]{2,1,0:T(8,128)(2,1)}, bf16[4,64,1408]{2,1,0:T(8,128)(2,1)}, bf16[3,2,224,1280]{3,2,1,0:T(8,128)(2,1)}, bf16[3,2,224,1280]{3...) custom-call(s32[4]{0:T(128)} %pad_add_fusion.1.place_ref, ...), custom_call_target="tpu_custom_call" | custom-call | tf_op jit(solution)/shard_map/experts_second/pallas_call | solution.py:405
  201.0 7.9 %shared_own.1 = (f32[64,1280]{1,0:T(8,128)}, f32[64,1280]{1,0:T(8,128)}) custom-call(bf16[64,1280]{1,0:T(8,128)(2,1)} %copy-done.12, bf16[64,1280]{1,0:T(8,128)(2,1)} %copy-done.11, bf16[3,224,1280]{2,1,0:T(8,128)(2,1)} %pad_maximum_fusion.refs_0_, bf16[3,224,1280]{2,1,0:T(8,128)(2,1)} %collective-permute-done.17.refs_1_, ...), custom_call_target="tpu_custom_call" | custom-call | tf_op jit(solution)/shard_map/shared_own/pallas_call | solution.py:446
  208.9 8.0 %collective-permute-done.18 = bf16[4,64,1408]{2,1,0:T(8,128)(2,1)} collective-permute-done((bf16[4,64,1408]{2,1,0:T(8,128)(2,1)}, bf16[4,64,1408]{2,1,0:T(8,128)(2,1)}, u32[]{:S(2)}, u32[]{:S(2)}) %collective-permute-start.18) | collective-permute-done | bytes 720928 | tf_op jit(solution)/shard_map/ppermute | solution.py:602
  256.1 5.2 %fusion.2 = (bf16[2,224,1280]{2,1,0:T(8,128)(2,1)}, bf16[2,224,1280]{2,1,0:T(8,128)(2,1)}, bf16[2,224,1280]{2,1,0:T(8,128)(2,1)S(1)}) fusion(bf16[3,2,224,1280]{3,2,1,0:T(8,128)(2,1)} %copy-done.7, bf16[3,2,224,1280]{3,2,1,0:T(8,128)(2,1)} %get-tuple-element.116), kind=kLoop, calls=%fused_computation.14 | loop fusion | flops 6881280 | bytes 10321920 | tf_op jit(solution)/shard_map/convert_element_type | solution.py:820
  266.4 11.4 %attend_back.1 = bf16[8,4,96,256]{3,2,1,0:T(8,128)(2,1)} custom-call(s32[2]{0:T(128)} %pad_add_fusion.bounds_ref, bf16[8,4,96,256]{3,2,1,0:T(8,128)(2,1)} %bitcast.3.arr_ref, s32[8,256,128]{2,1,0:T(8,128)} %broadcast_in_dim.128.col_ref, s32[8,1,256]{2,1,0:T(1,128)} %bitcast.208, f32[8,256,128]{2,1,0:T(8,128)} %get-tuple-element.115.lse_ref, ...), custom_call_target="tpu_custom_call" | custom-call | tf_op jit(solution)/shard_map/attend_back/pallas_call | solution.py:229
  277.8 10.7 %collective-permute-done.31 = bf16[2,224,1280]{2,1,0:T(8,128)(2,1)} collective-permute-done((bf16[2,224,1280]{2,1,0:T(8,128)(2,1)S(1)}, bf16[2,224,1280]{2,1,0:T(8,128)(2,1)}, u32[]{:S(2)}, u32[]{:S(2)}) %collective-permute-start.31) | collective-permute-done | bytes 1146912 | tf_op jit(solution)/shard_map/ppermute | solution.py:602
  289.2 9.0 %collective-permute-start.35 = (bf16[160,320]{1,0:T(8,128)(2,1)}, bf16[160,320]{1,0:T(8,128)(2,1)S(1)}, u32[]{:S(2)}, u32[]{:S(2)}) collective-permute-start(bf16[160,320]{1,0:T(8,128)(2,1)} %get-tuple-element.276), channel_id=1, source_target_pairs={{0,8},{4,12},{8,0},{12,4},{16,24},{20,28},{24,16},{28,20},{1,9},{5... | collective-permute-start | bytes 307208 | tf_op jit(solution)/shard_map/ppermute | solution.py:602
  300.7 5.5 %all-to-all-start.5 = ((bf16[32,96,256]{2,1,0:T(8,128)(2,1)}), bf16[32,96,256]{2,1,0:T(8,128)(2,1)S(1)}, u32[]{:S(2)}, u32[]{:S(2)}) async-start(bf16[32,96,256]{2,1,0:T(8,128)(2,1)} %bitcast.184), calls=%async_computation.5 | async-start | bytes 3145728 | tf_op jit(solution)/shard_map/all_to_all | solution.py:606
  308.4 12.5 %shared_grads.1 = bf16[4,3,224,160]{3,2,1,0:T(8,128)(2,1)} custom-call(bf16[512,1280]{1,0:T(8,128)(2,1)} %bitcast.26.x_ref, bf16[512,1280]{1,0:T(8,128)(2,1)} %get-tuple-element.126.dy_ref, bf16[512,160]{1,0:T(8,128)(2,1)} %get-tuple-element.293.xc_ref, bf16[512,160]{1,0:T(8,128)(2,1)} %get-tuple-element.292.dyc_ref, ...), custom_call_target="tpu_custom_call" | custom-call | tf_op jit(solution)/shard_map/shared_grads/pallas_call | solution.py:471
  340.5 29.8 %collective-permute-done.59 = bf16[3,224,160]{2,1,0:T(8,128)(2,1)S(1)} collective-permute-done((bf16[3,224,160]{2,1,0:T(8,128)(2,1)}, bf16[3,224,160]{2,1,0:T(8,128)(2,1)S(1)}, u32[]{:S(2)}, u32[]{:S(2)}) %collective-permute-start.59) | collective-permute-done | bytes 215072 | tf_op jit(solution)/shard_map/ppermute | solution.py:602
  370.3 7.3 %collective-permute-done.60 = bf16[3,224,160]{2,1,0:T(8,128)(2,1)S(1)} collective-permute-done((bf16[3,224,160]{2,1,0:T(8,128)(2,1)}, bf16[3,224,160]{2,1,0:T(8,128)(2,1)S(1)}, u32[]{:S(2)}, u32[]{:S(2)}) %collective-permute-start.60) | collective-permute-done | bytes 215072 | tf_op jit(solution)/shard_map/ppermute | solution.py:602
  386.0 6.7 %project_back.1 = (bf16[4,64,1280]{2,1,0:T(8,128)(2,1)}, f32[1,1280]{1,0:T(1,128)}, bf16[4,160,320]{2,1,0:T(8,128)(2,1)}, bf16[4,160,320]{2,1,0:T(8,128)(2,1)}, ...) custom-call(s32[4]{0:T(128)} %pad_add_fusion.1.place_ref, ...), custom_call_target="tpu_custom_call" | custom-call | tf_op jit(solution)/shard_map/project_back/pallas_call | solution.py:561
  398.1 6.2 %all-to-all-start.6 = ((f32[32,2,160]{2,1,0:T(2,128)}), f32[32,2,160]{2,1,0:T(2,128)S(1)}, u32[]{:S(2)}, u32[]{:S(2)}) async-start(f32[32,2,160]{2,1,0:T(2,128)} %bitcast.64), calls=%async_computation.6 | async-start | bytes 131072 | tf_op jit(solution)/shard_map/all_to_all | solution.py:606
  428.9 7.2 %collective-permute-done.53 = bf16[160,320]{1,0:T(8,128)(2,1)S(1)} collective-permute-done((bf16[160,320]{1,0:T(8,128)(2,1)S(1)}, bf16[160,320]{1,0:T(8,128)(2,1)S(1)}, u32[]{:S(2)}, u32[]{:S(2)}) %collective-permute-start.53) | collective-permute-done | bytes 102432 | tf_op jit(solution)/shard_map/ppermute | solution.py:602
  460.9 5.4 %bitcast_add_fusion = (f32[2,224,1280]{2,1,0:T(8,128)}, f32[2,224,1280]{2,1,0:T(8,128)}) fusion(bf16[2,224,1280]{2,1,0:T(8,128)(2,1)} %collective-permute-done.61, bf16[3,2,224,1280]{3,2,1,0:T(8,128)(2,1)} %collective-permute-done.38, bf16[3,2,224,1280]{3,2,1,0:T(8,128)(2,1)S(1)} %copy-done.8, bf16[2,224,1280]{2,1,0:T(8,128)(2,1)} %collective-permute-done.43), kind=kLoop, calls=%fused_computation.2 | loop fusion | flops 5734400 | bytes 11468800 | tf_op jit(solution)/shard_map/add | solution.py:596
  (307 shorter events, 193.3 us)
Async XLA Ops:
  8.6 46.8 %all-to-all-start = ((bf16[32,96,256]{2,1,0:T(8,128)(2,1)}), bf16[32,96,256]{2,1,0:T(8,128)(2,1)}, u32[]{:S(2)}, u32[]{:S(2)}) async-start(bf16[32,96,256]{2,1,0:T(8,128)(2,1)} %get-tuple-element.85), calls=%async_computation | async-start | bytes 3145728 | tf_op jit(solution)/shard_map/all_to_all | solution.py:606
  16.1 37.2 %collective-permute-start = (bf16[10,32,1280]{2,1,0:T(8,128)(2,1)}, bf16[10,32,1280]{2,1,0:T(8,128)(2,1)}, u32[]{:S(2)}, u32[]{:S(2)}) collective-permute-start(bf16[10,32,1280]{2,1,0:T(8,128)(2,1)} %bitcast.4), channel_id=1, source_target_pairs={{0,2},{1,3},{2,0},{3,1},{4,6},{5,7},{6,4},{7,5},{8,10},{9,11},{10,... | collective-permute-start | bytes 2457608 | tf_op jit(solution)/shard_map/ppermute | solution.py:602
  17.8 36.4 %collective-permute-start.1 = (bf16[10,32,1280]{2,1,0:T(8,128)(2,1)}, bf16[10,32,1280]{2,1,0:T(8,128)(2,1)}, u32[]{:S(2)}, u32[]{:S(2)}) collective-permute-start(bf16[10,32,1280]{2,1,0:T(8,128)(2,1)} %bitcast.4), channel_id=1, source_target_pairs={{0,1},{1,0},{2,3},{3,2},{4,5},{5,4},{6,7},{7,6},{8,9},{9,8},{10,11... | collective-permute-start | bytes 2457608 | tf_op jit(solution)/shard_map/ppermute | solution.py:602
  53.3 47.0 %collective-permute-start.3 = (bf16[2,224,1280]{2,1,0:T(8,128)(2,1)}, bf16[2,224,1280]{2,1,0:T(8,128)(2,1)}, u32[]{:S(2)}, u32[]{:S(2)}) collective-permute-start(bf16[2,224,1280]{2,1,0:T(8,128)(2,1)} %refs_0_.1), channel_id=1, source_target_pairs={{0,2},{1,3},{2,0},{3,1},{4,6},{5,7},{6,4},{7,5},{8,10},{9,11},{10,... | collective-permute-start | bytes 3440648 | tf_op jit(solution)/shard_map/ppermute | solution.py:602
  53.7 64.9 %collective-permute-start.11 = (bf16[2,224,1280]{2,1,0:T(8,128)(2,1)}, bf16[2,224,1280]{2,1,0:T(8,128)(2,1)}, u32[]{:S(2)}, u32[]{:S(2)}) collective-permute-start(bf16[2,224,1280]{2,1,0:T(8,128)(2,1)} %refs_0_.1), channel_id=1, source_target_pairs={{0,1},{1,0},{2,3},{3,2},{4,5},{5,4},{6,7},{7,6},{8,9},{9,8},{10,11... | collective-permute-start | bytes 3440648 | tf_op jit(solution)/shard_map/ppermute | solution.py:602
  66.1 34.2 %all-to-all-start.1 = ((bf16[32,64,128]{2,1,0:T(8,128)(2,1)}), bf16[32,64,128]{2,1,0:T(8,128)(2,1)}, u32[]{:S(2)}, u32[]{:S(2)}) async-start(bf16[32,64,128]{2,1,0:T(8,128)(2,1)} %bitcast.199), calls=%async_computation.1 | async-start | bytes 1048576 | tf_op jit(solution)/shard_map/all_to_all | solution.py:606
  87.4 28.5 %collective-permute-start.9 = (bf16[2,224,1280]{2,1,0:T(8,128)(2,1)}, bf16[2,224,1280]{2,1,0:T(8,128)(2,1)}, u32[]{:S(2)}, u32[]{:S(2)}) collective-permute-start(bf16[2,224,1280]{2,1,0:T(8,128)(2,1)} %refs_0_.2), channel_id=1, source_target_pairs={{0,2},{1,3},{2,0},{3,1},{4,6},{5,7},{6,4},{7,5},{8,10},{9,11},{10,... | collective-permute-start | bytes 3440648 | tf_op jit(solution)/shard_map/ppermute | solution.py:602
  97.8 44.3 %collective-permute-start.8 = (bf16[2,224,1280]{2,1,0:T(8,128)(2,1)}, bf16[2,224,1280]{2,1,0:T(8,128)(2,1)}, u32[]{:S(2)}, u32[]{:S(2)}) collective-permute-start(bf16[2,224,1280]{2,1,0:T(8,128)(2,1)} %refs_0_.2), channel_id=1, source_target_pairs={{0,1},{1,0},{2,3},{3,2},{4,5},{5,4},{6,7},{7,6},{8,9},{9,8},{10,11... | collective-permute-start | bytes 3440648 | tf_op jit(solution)/shard_map/ppermute | solution.py:602
  97.8 44.8 %collective-permute-start.14 = (bf16[2,224,1280]{2,1,0:T(8,128)(2,1)}, bf16[2,224,1280]{2,1,0:T(8,128)(2,1)}, u32[]{:S(2)}, u32[]{:S(2)}) collective-permute-start(bf16[2,224,1280]{2,1,0:T(8,128)(2,1)} %refs_4_), channel_id=1, source_target_pairs={{0,2},{1,3},{2,0},{3,1},{4,6},{5,7},{6,4},{7,5},{8,10},{9,11},{10,... | collective-permute-start | bytes 3440648 | tf_op jit(solution)/shard_map/ppermute | solution.py:602
  104.1 47.2 %all-to-all-start.2 = ((bf16[8,64,1280]{2,1,0:T(8,128)(2,1)}), bf16[8,64,1280]{2,1,0:T(8,128)(2,1)}, u32[]{:S(2)}, u32[]{:S(2)}) async-start(bf16[8,64,1280]{2,1,0:T(8,128)(2,1)} %broadcast_in_dim.139), calls=%async_computation.2 | async-start | bytes 2621440 | tf_op jit(solution)/shard_map/all_to_all | solution.py:606
  110.4 31.8 %collective-permute-start.7 = (bf16[4,64,1408]{2,1,0:T(8,128)(2,1)}, bf16[4,64,1408]{2,1,0:T(8,128)(2,1)}, u32[]{:S(2)}, u32[]{:S(2)}) collective-permute-start(bf16[4,64,1408]{2,1,0:T(8,128)(2,1)} %pad_maximum_fusion.1.even_ref), channel_id=1, source_target_pairs={{0,4},{4,0},{8,12},{12,8},{16,20},{20,16},{24,28},{28,24},{1,5},{5... | collective-permute-start | bytes 2162696 | tf_op jit(solution)/shard_map/ppermute | solution.py:602
  118.6 58.7 %collective-permute-start.16 = (bf16[3,224,1280]{2,1,0:T(8,128)(2,1)}, bf16[3,224,1280]{2,1,0:T(8,128)(2,1)}, u32[]{:S(2)}, u32[]{:S(2)}) collective-permute-start(bf16[3,224,1280]{2,1,0:T(8,128)(2,1)} %pad_maximum_fusion.refs_0_), channel_id=1, source_target_pairs={{0,2},{1,3},{2,0},{3,1},{4,6},{5,7},{6,4},{7,5},{8,10},{9,11},{10,... | collective-permute-start | bytes 5160968 | tf_op jit(solution)/shard_map/ppermute | solution.py:602
  142.7 34.7 %collective-permute-start.17 = (bf16[3,224,1280]{2,1,0:T(8,128)(2,1)}, bf16[3,224,1280]{2,1,0:T(8,128)(2,1)}, u32[]{:S(2)}, u32[]{:S(2)}) collective-permute-start(bf16[3,224,1280]{2,1,0:T(8,128)(2,1)} %pad_maximum_fusion.refs_0_), channel_id=1, source_target_pairs={{0,1},{1,0},{2,3},{3,2},{4,5},{5,4},{6,7},{7,6},{8,9},{9,8},{10,11... | collective-permute-start | bytes 5160968 | tf_op jit(solution)/shard_map/ppermute | solution.py:602
  172.5 48.1 %all-to-all-start.3 = ((bf16[8,64,1280]{2,1,0:T(8,128)(2,1)}), bf16[8,64,1280]{2,1,0:T(8,128)(2,1)}, u32[]{:S(2)}, u32[]{:S(2)}) async-start(bf16[8,64,1280]{2,1,0:T(8,128)(2,1)} %bitcast.193), calls=%async_computation.3 | async-start | bytes 2621440 | tf_op jit(solution)/shard_map/all_to_all | solution.py:606
  261.4 27.1 %collective-permute-start.31 = (bf16[2,224,1280]{2,1,0:T(8,128)(2,1)S(1)}, bf16[2,224,1280]{2,1,0:T(8,128)(2,1)}, u32[]{:S(2)}, u32[]{:S(2)}) collective-permute-start(bf16[2,224,1280]{2,1,0:T(8,128)(2,1)S(1)} %get-tuple-element.253), channel_id=1, source_target_pairs={{0,2},{1,3},{2,0},{3,1},{4,6},{5,7},{6,4},{7,5},{8,10},{9,11},{10,... | collective-permute-start | bytes 3440648 | tf_op jit(solution)/shard_map/ppermute | solution.py:602
  263.0 118.1 %collective-permute-start.38 = (bf16[3,2,224,1280]{3,2,1,0:T(8,128)(2,1)}, bf16[3,2,224,1280]{3,2,1,0:T(8,128)(2,1)}, u32[]{:S(2)}, u32[]{:S(2)}) collective-permute-start(bf16[3,2,224,1280]{3,2,1,0:T(8,128)(2,1)} %get-tuple-element.130), channel_id=1, source_target_pairs={{0,1},{1,0},{2,3},{3,2},{4,5},{5,4},{6,7},{7,6},{8,9},{9,8},{10,11... | collective-permute-start | bytes 10321928 | tf_op jit(solution)/shard_map/ppermute | solution.py:602
  289.2 33.9 %collective-permute-start.35 = (bf16[160,320]{1,0:T(8,128)(2,1)}, bf16[160,320]{1,0:T(8,128)(2,1)S(1)}, u32[]{:S(2)}, u32[]{:S(2)}) collective-permute-start(bf16[160,320]{1,0:T(8,128)(2,1)} %get-tuple-element.276), channel_id=1, source_target_pairs={{0,8},{4,12},{8,0},{12,4},{16,24},{20,28},{24,16},{28,20},{1,9},{5... | collective-permute-start | bytes 307208 | tf_op jit(solution)/shard_map/ppermute | solution.py:602
  300.7 27.7 %collective-permute-start.32 = (bf16[64,1408]{1,0:T(8,128)(2,1)S(1)}, bf16[64,1408]{1,0:T(8,128)(2,1)S(1)}, u32[]{:S(2)}, u32[]{:S(2)}) collective-permute-start(bf16[64,1408]{1,0:T(8,128)(2,1)S(1)} %concatenate.12), channel_id=1, source_target_pairs={{0,1},{1,0},{2,3},{3,2},{4,5},{5,4},{6,7},{7,6},{8,9},{9,8},{10,11... | collective-permute-start | bytes 540680 | tf_op jit(solution)/shard_map/ppermute | solution.py:602
  300.7 84.1 %all-to-all-start.5 = ((bf16[32,96,256]{2,1,0:T(8,128)(2,1)}), bf16[32,96,256]{2,1,0:T(8,128)(2,1)S(1)}, u32[]{:S(2)}, u32[]{:S(2)}) async-start(bf16[32,96,256]{2,1,0:T(8,128)(2,1)} %bitcast.184), calls=%async_computation.5 | async-start | bytes 3145728 | tf_op jit(solution)/shard_map/all_to_all | solution.py:606
  325.7 82.9 %collective-permute-start.43 = (bf16[2,224,1280]{2,1,0:T(8,128)(2,1)}, bf16[2,224,1280]{2,1,0:T(8,128)(2,1)}, u32[]{:S(2)}, u32[]{:S(2)}) collective-permute-start(bf16[2,224,1280]{2,1,0:T(8,128)(2,1)} %get-tuple-element.136), channel_id=1, source_target_pairs={{0,2},{1,3},{2,0},{3,1},{4,6},{5,7},{6,4},{7,5},{8,10},{9,11},{10,... | collective-permute-start | bytes 3440648 | tf_op jit(solution)/shard_map/ppermute | solution.py:602
  332.0 38.3 %collective-permute-start.59 = (bf16[3,224,160]{2,1,0:T(8,128)(2,1)}, bf16[3,224,160]{2,1,0:T(8,128)(2,1)S(1)}, u32[]{:S(2)}, u32[]{:S(2)}) collective-permute-start(bf16[3,224,160]{2,1,0:T(8,128)(2,1)} %get-tuple-element.256), channel_id=1, source_target_pairs={{0,2},{1,3},{2,0},{3,1},{4,6},{5,7},{6,4},{7,5},{8,10},{9,11},{10,... | collective-permute-start | bytes 645128 | tf_op jit(solution)/shard_map/ppermute | solution.py:602
  335.8 41.8 %collective-permute-start.60 = (bf16[3,224,160]{2,1,0:T(8,128)(2,1)}, bf16[3,224,160]{2,1,0:T(8,128)(2,1)S(1)}, u32[]{:S(2)}, u32[]{:S(2)}) collective-permute-start(bf16[3,224,160]{2,1,0:T(8,128)(2,1)} %get-tuple-element.255), channel_id=1, source_target_pairs={{0,3},{1,2},{2,1},{3,0},{4,7},{5,6},{6,5},{7,4},{8,11},{9,10},{10,... | collective-permute-start | bytes 645128 | tf_op jit(solution)/shard_map/ppermute | solution.py:602
  398.1 45.0 %all-to-all-start.6 = ((f32[32,2,160]{2,1,0:T(2,128)}), f32[32,2,160]{2,1,0:T(2,128)S(1)}, u32[]{:S(2)}, u32[]{:S(2)}) async-start(f32[32,2,160]{2,1,0:T(2,128)} %bitcast.64), calls=%async_computation.6 | async-start | bytes 131072 | tf_op jit(solution)/shard_map/all_to_all | solution.py:606
  408.6 52.3 %collective-permute-start.61 = (bf16[2,224,1280]{2,1,0:T(8,128)(2,1)}, bf16[2,224,1280]{2,1,0:T(8,128)(2,1)}, u32[]{:S(2)}, u32[]{:S(2)}) collective-permute-start(bf16[2,224,1280]{2,1,0:T(8,128)(2,1)} %get-tuple-element.154), channel_id=1, source_target_pairs={{0,2},{1,3},{2,0},{3,1},{4,6},{5,7},{6,4},{7,5},{8,10},{9,11},{10,... | collective-permute-start | bytes 3440648 | tf_op jit(solution)/shard_map/ppermute | solution.py:602
  (80 other events, 981.7 us)

commit v5 on v4

--- a/solution.py
+++ b/solution.py
@@ -384,9 +384,12 @@
 
         for k in range(parts):
             acc_ref[...] += dot(act_ref[0, k], down_w[k][0], 1, 0)
-            grads[k][0, 0] = dot(dg_ref[0, k], x_ref[...], 0, 0).astype(BF)
-            grads[k][1, 0] = dot(du_ref[0, k], x_ref[...], 0, 0).astype(BF)
-            grads[k][2, 0] = dot(act_ref[0, k], dy_ref[...], 0, 0).astype(BF)
+            for m, (left, right) in enumerate(((dg_ref, x_ref), (du_ref, x_ref), (act_ref, dy_ref))):
+                grad = dot(left[0, k], right[...], 0, 0).astype(BF)
+                if k < parts - 1:
+                    grads[k][m, 0] = grad
+                else:
+                    grads[k + m][0] = grad
 
         @pl.when(s == slots - 1)
         def _():
@@ -411,11 +414,13 @@
             + [hid_spec] * 3
             + weight_specs(parts, hidden, width, 1),
             out_specs=[whole(out_shape)] * 2
-            + [pl.BlockSpec((3, 1, hidden, width), lambda s, *_: (0, s, 0, 0))] * parts,
+            + [pl.BlockSpec((3, 1, hidden, width), lambda s, *_: (0, s, 0, 0))] * (parts - 1)
+            + [pl.BlockSpec((1, hidden, width), lambda s, *_: (s, 0, 0))] * 3,
             scratch_shapes=[pltpu.VMEM((count, width), F32)],
         ),
         out_shape=(jax.ShapeDtypeStruct(out_shape, BF),) * 2
-        + (jax.ShapeDtypeStruct((3, slots, hidden, width), BF),) * parts,
+        + (jax.ShapeDtypeStruct((3, slots, hidden, width), BF),) * (parts - 1)
+        + (jax.ShapeDtypeStruct((slots, hidden, width), BF),) * 3,
         compiler_params=pltpu.CompilerParams(vmem_limit_bytes=VMEM_LIMIT),
         name="experts_second",
     )(place, rows_in, grads_in, sums, act, dgate, dup, *downs)
@@ -613,16 +618,15 @@
 
 def even_blocks(x):
     size = lax.axis_size("expert")
-    return jnp.stack([x] + [flip(x, m, "expert") for m in range(2, size, 2)])
+    return [x] + [flip(x, m, "expert") for m in range(2, size, 2)]
 
 
 def odd_blocks(evens):
     return flip(evens, 1, "expert")
 
 
-def paired(evens, odds, *others):
-    got = after(flip(odds, 1, "expert"), *others) if others else flip(odds, 1, "expert")
-    return (evens.astype(F32) + got.astype(F32)).astype(BF)
+def paired(evens, odds):
+    return added([evens, flip(odds, 1, "expert")]).astype(BF)
 
 
 def collected(sums):
@@ -742,16 +746,18 @@
         [own_grads] + [p.astype(BF) for p in pieces(dense_gates)] + [spare], axis=1
     )
     grads_even = even_blocks(after(own_wide, arrived))
+
+    attended_units, lse = attend(bounds, arrived, seg_col, seg_row, most)
+    attended_units, grads_even = lax.optimization_barrier((attended_units, tuple(grads_even)))
+    grads_even = jnp.stack(grads_even)
     grads_odd = odd_blocks(grads_even)
-
-    attended_units, lse = attend(bounds, arrived, seg_col, seg_row, most)
     down_mine = after(routed_down, attended_units)
     down_far = across(down_mine)
     gate_ws = all_quarters(gate_mine, gate_far)
     up_ws = all_quarters(up_mine, up_far)
     down_ws = all_quarters(down_mine, down_far)
     back = exchange(attended_units.reshape(units, own, hd), BOTH)
-    back = after(back, out_full, gate_far, grads_even)
+    back, grads_odd = lax.optimization_barrier((back, grads_odd, out_full, gate_far))[:2]
     attended_heads = lax.dynamic_slice_in_dim(back, block_group * heads, heads)
     attended = attended_heads.transpose(1, 0, 2).reshape(own, heads * hd)
     hidden_state = own_tokens + jnp.dot(attended, out_full, preferred_element_type=F32)
@@ -794,14 +800,14 @@
             jnp.stack([s[i] for s in seconds])[order].reshape(half, own, width + lanes)
             for i in range(2)
         )
-        parts = [added([s[2 + k] for s in seconds]).astype(BF) for k in range(quarters)]
+        parts = [added([s[2 + k] for s in seconds]).astype(BF) for k in range(quarters + 2)]
     shared_out, shared_dx = shared_own(after(normed_two, out_low), own_grads, shared_ws)
     att_parts = of_quarters(after(attended, shared_far))
 
-    out_pairs = paired(out_low, out_high, shared_dx)
-    grad_home, out_pairs = lax.optimization_barrier(
-        (grad_home, out_pairs, shared_dx, tuple(att_parts))
-    )[:2]
+    to_far = [added([parts[2][0], beside(parts[3])]).astype(BF)]
+    grad_home, to_far[0], att_parts = lax.optimization_barrier(
+        (grad_home, to_far[0], tuple(att_parts), shared_dx)
+    )[:3]
     grad_norm_two = jnp.sum(grad_home.astype(F32), axis=0) + shared_dx
     grad_full = own_grads.astype(F32)
     grad_second, second_gain_local = norm_backward(
@@ -812,18 +818,23 @@
     grad_attended = jnp.einsum(
         "td,hcd->htc", grad_attn, out_full.reshape(heads, hd, width), preferred_element_type=F32
     ).astype(BF)
+    out_got = flip(out_high, 1, "expert")
+    grad_attended, out_got = lax.optimization_barrier((grad_attended, out_got))
     do_send = jnp.concatenate([grad_attended] * groups + [grad_attended[: units - groups * heads]], axis=0)
     do_units = exchange(do_send, BOTH).reshape(blocks, rows, hd)
 
-    grad_attn_sent, out_pairs = lax.optimization_barrier((grad_attn, out_pairs, do_send))[:2]
-    from_far = beside(after(parts[3], do_send))
-    to_far = [(parts[2][m].astype(F32) + from_far[m].astype(F32)).astype(BF) for m in range(3)]
-    near = beside(after(parts[1], from_far))
+    grad_attn_sent = after(grad_attn, do_send)
     routed_far = [across(to_far[0])]
+    from_far = [beside(after(parts[3 + m], do_send)) for m in (1, 2)]
+    routed_far[0], att_parts = lax.optimization_barrier((routed_far[0], att_parts))
     proj_low, proj_high = output_grads(
         place, of_quarters(grad_attn_sent), att_parts, heads, hw, blocks
     )
-    do_units, to_far = lax.optimization_barrier((do_units, to_far, proj_low))[:2]
+    from_far = lax.optimization_barrier((tuple(from_far), proj_low))[0]
+    to_far += [added([parts[2][m], from_far[m - 1]]).astype(BF) for m in (1, 2)]
+    near = beside(after(parts[1], from_far[1]))
+    out_pairs = added([out_low, after(out_got, proj_low)]).astype(BF)
+    do_units, out_pairs = lax.optimization_barrier((do_units, out_pairs, proj_low))[:2]
 
     grad_units = attend_back(bounds, arrived, seg_col, seg_row, lse, do_units, most)
     out_home = collected(out_pairs)
@@ -838,6 +849,7 @@
         shared_grads(rows_late[c], grads_late[c], rows_cut[c], grads_cut[c], shared_ws) for c in spans
     ]
     shared_parts = shared_parts[0] if len(spans) == 1 else added(shared_parts).astype(BF)
+    shared_gots = [flip(shared_parts[k], k, "tensor") for k in range(1, quarters)]
     out_grad = collected(after(proj_pairs, grad_units))
     moe_out = out_home[:, :width] + shared_out
     slot_sums = out_home[:, width : width + 3 * experts_total].reshape(own, 3, experts_total)
@@ -871,7 +883,7 @@
     dx_parts = [back_out[0][0]] + [flip(back_out[0][k], k, "tensor") for k in range(1, quarters)]
     pair_q = paired(back_out[2], back_out[3])
     pair_k = paired(back_out[4], after(back_out[5], pair_q))
-    far_one = across(after(to_far[1], grad_units))
+    far_one = across(lax.optimization_barrier((to_far[1], tuple(shared_gots)))[0])
     dx_parts, pair_q, far_one = lax.optimization_barrier((tuple(dx_parts), pair_q, far_one))
     grad_one = added(dx_parts)
     pair_v = paired(back_out[6], after(back_out[7], pair_k))
@@ -881,7 +893,7 @@
     grad_first, _ = norm_backward(grad_one, own_tokens, first_scale, first_gain)
     input_mine = after((grad_hidden + grad_first).astype(BF), pair_v)
     input_grad = in_order(of_quarters(input_mine), quarter)
-    shared = added([shared_parts[0]] + [flip(shared_parts[k], k, "tensor") for k in range(1, quarters)])
+    shared = added([shared_parts[0]] + shared_gots)
     gains = jnp.sum(after(gains, pair_v), axis=0)
     routed.append(added([parts[0][1], near[1], after(far_one, pair_v)]))
     routed.append(added([parts[0][2], near[2], far_two]))

time: 473 us -> 445 us (0.941)
  starting transfers between devices: 115 us -> 98.7 us
  waiting for transfers between devices: 152 us -> 138 us
    ppermute x62 -> x64, waiting for transfers between devices: 151 us -> 131 us  [flip(): return lax.ppermute(x, axis, [(i, i ^ by) for i in range(size)])]
    ppermute x62 -> x64, starting transfers between devices: 76.3 us -> 60.1 us  [flip(): return lax.ppermute(x, axis, [(i, i ^ by) for i in range(size)])]
    all_to_all x7, waiting for transfers between devices: 0.29 us -> 6.91 us  [exchange(): return lax.all_to_all(x, axis, 0, 0, tiled=True)]
    unnamed x74 -> x78, local copies, waits for them, and re-layouts: 9.68 us -> 7.18 us
    convert_element_type x6 -> x7, other arithmetic: 10.3 us -> 11.2 us  [the longest x1 3.7 us: on_device(): to_far += [added([parts[2][m], from_far[m - 1]]).astype(BF) for m in (1, 2)]]
  transfers between devices with their start and end apart: 69 -> 71, of which waited for: 18 -> 21; matrix products, arithmetic and copies ran while one was open for 15% -> 19% of each run, Pallas kernels for 21% -> 23%
where the time goes in v5:
time: 445 us; the launch traced here: 439 us
  waiting for transfers between devices  138 us (31%)
  Pallas kernels  104 us (23%)
  starting transfers between devices  98.7 us (22%)
  local copies, waits for them, and re-layouts  50.7 us (11%)
  other arithmetic  42.1 us (9%)
    ppermute x64, waiting for transfers between devices, flip(): return lax.ppermute(x, axis, [(i, i ^ by) for i in range(size)])  131 us
    ppermute x64, starting transfers between devices, flip(): return lax.ppermute(x, axis, [(i, i ^ by) for i in range(size)])  60.1 us
    all_to_all x7, starting transfers between devices, exchange(): return lax.all_to_all(x, axis, 0, 0, tiled=True)  38.6 us
    pallas_call x1, Pallas kernels, experts_first(): pl.pallas_call(body, grid_spec=pltpu.PrefetchScalarGridSpec(num_scalar_pr...  21.1 us
    pallas_call x1, Pallas kernels, experts_second(): pl.pallas_call(body, grid_spec=pltpu.PrefetchScalarGridSpec(num_scalar_pr...  18.8 us
    pallas_call x1, Pallas kernels, shared_grads(): pl.pallas_call(body, out_shape=jax.ShapeDtypeStruct((parts, 3, hidden, cu...  12.5 us
    add x5, other arithmetic, added(): total = total + p.astype(F32)  12.5 us
    pallas_call x1, Pallas kernels, attend_back(): pl.pallas_call(body, grid_spec=grid_spec, out_shape=jax.ShapeDtypeStruct(...  11.5 us
  transfers between devices with their start and end apart: 71, of which 21 were waited for; matrix products, arithmetic and copies ran while one was open for 19% of the time, Pallas kernels for 23%

profile of v5, /device:TPU:0, one launch (start us, length us, event | category | flops | bytes accessed | tf_op | source)
XLA Modules:
  0.0 438.6 jit_solution(1495292873956614849)
XLA Ops:
  8.6 7.4 %all-to-all-start = ((bf16[32,96,256]{2,1,0:T(8,128)(2,1)}), bf16[32,96,256]{2,1,0:T(8,128)(2,1)}, u32[]{:S(2)}, u32[]{:S(2)}) async-start(bf16[32,96,256]{2,1,0:T(8,128)(2,1)} %get-tuple-element.105), calls=%async_computation | async-start | bytes 3145728 | tf_op jit(solution)/shard_map/all_to_all | solution.py:611
  26.0 27.3 %collective-permute-done = bf16[10,32,1280]{2,1,0:T(8,128)(2,1)} collective-permute-done((bf16[10,32,1280]{2,1,0:T(8,128)(2,1)}, bf16[10,32,1280]{2,1,0:T(8,128)(2,1)}, u32[]{:S(2)}, u32[]{:S(2)}) %collective-permute-start) | collective-permute-done | bytes 819232 | tf_op jit(solution)/shard_map/ppermute | solution.py:607
  60.7 9.2 %attend.1 = (bf16[8,256,128]{2,1,0:T(8,128)(2,1)}, f32[8,256,128]{2,1,0:T(8,128)}) custom-call(s32[2]{0:T(128)} %pad_add_fusion.bounds_ref, bf16[8,4,96,256]{3,2,1,0:T(8,128)(2,1)} %bitcast.3.arr_ref, s32[8,256,128]{2,1,0:T(8,128)} %broadcast_in_dim.128.col_ref, s32[8,1,256]{2,1,0:T(1,128)} %bitcast.209), custom_call_target="tpu_custom_call" | custom-call | tf_op jit(solution)/shard_map/attend/pallas_call | solution.py:146
  74.1 6.0 %all-to-all-start.1 = ((bf16[32,64,128]{2,1,0:T(8,128)(2,1)}), bf16[32,64,128]{2,1,0:T(8,128)(2,1)}, u32[]{:S(2)}, u32[]{:S(2)}) async-start(bf16[32,64,128]{2,1,0:T(8,128)(2,1)} %bitcast.201), calls=%async_computation.1 | async-start | bytes 1048576 | tf_op jit(solution)/shard_map/all_to_all | solution.py:611
  84.7 9.7 %collective-permute-done.4.odd_ref = bf16[4,64,1408]{2,1,0:T(8,128)(2,1)} collective-permute-done((bf16[4,64,1408]{2,1,0:T(8,128)(2,1)}, bf16[4,64,1408]{2,1,0:T(8,128)(2,1)}, u32[]{:S(2)}, u32[]{:S(2)}) %collective-permute-start.4) | collective-permute-done | bytes 720928 | tf_op jit(solution)/shard_map/ppermute | solution.py:607
  98.9 15.7 %collective-permute-done.9.refs_2_ = bf16[2,224,1280]{2,1,0:T(8,128)(2,1)} collective-permute-done((bf16[2,224,1280]{2,1,0:T(8,128)(2,1)}, bf16[2,224,1280]{2,1,0:T(8,128)(2,1)}, u32[]{:S(2)}, u32[]{:S(2)}) %collective-permute-start.9) | collective-permute-done | bytes 1146912 | tf_op jit(solution)/shard_map/ppermute | solution.py:607
  115.7 5.2 %all-to-all-start.2 = ((bf16[8,64,1280]{2,1,0:T(8,128)(2,1)}), bf16[8,64,1280]{2,1,0:T(8,128)(2,1)}, u32[]{:S(2)}, u32[]{:S(2)}) async-start(bf16[8,64,1280]{2,1,0:T(8,128)(2,1)} %broadcast_in_dim.139), calls=%async_computation.2 | async-start | bytes 2621440 | tf_op jit(solution)/shard_map/all_to_all | solution.py:611
  124.4 14.8 %collective-permute-done.14.refs_6_ = bf16[2,224,1280]{2,1,0:T(8,128)(2,1)} collective-permute-done((bf16[2,224,1280]{2,1,0:T(8,128)(2,1)}, bf16[2,224,1280]{2,1,0:T(8,128)(2,1)}, u32[]{:S(2)}, u32[]{:S(2)}) %collective-permute-start.14) | collective-permute-done | bytes 1146912 | tf_op jit(solution)/shard_map/ppermute | solution.py:607
  140.4 7.5 %down_products.1 = (f32[2,4,512,224]{3,2,1,0:T(8,128)}, bf16[512,1280]{1,0:T(8,128)(2,1)}, bf16[512,128]{1,0:T(8,128)(2,1)}) custom-call(s32[4]{0:T(128)} %pad_add_fusion.1.place_ref, bf16[4,64,1408]{2,1,0:T(8,128)(2,1)} %pad_maximum_fusion.1.even_ref, bf16[4,64,1408]{2,1,0:T(8,128)(2,1)} %collective-permute-done.4.odd_ref, bf16[2,224,1280]{2,1,0:T(8,128)(2,1)} %refs_0_.2, ...), custom_call_target="tpu_custom_call" | custom-call | tf_op jit(solution)/shard_map/down_products/pallas_call | solution.py:266
  147.9 5.1 %all-to-all-done.2 = bf16[8,64,1280]{2,1,0:T(8,128)(2,1)} async-done(((bf16[8,64,1280]{2,1,0:T(8,128)(2,1)}), bf16[8,64,1280]{2,1,0:T(8,128)(2,1)}, u32[]{:S(2)}, u32[]{:S(2)}) %all-to-all-start.2) | async-done | bytes 1310752 | tf_op jit(solution)/shard_map/all_to_all | solution.py:611
  153.0 21.1 %experts_first.1 = (bf16[2,4,512,224]{3,2,1,0:T(8,128)(2,1)}, bf16[2,4,512,224]{3,2,1,0:T(8,128)(2,1)}, bf16[2,4,512,224]{3,2,1,0:T(8,128)(2,1)}, bf16[512,128]{1,0:T(8,128)(2,1)}, bf16[512,1280]{1,0:T(8,128)(2,1)}) custom-call(s32[4]{0:T(128)} %pad_add_fusion.1.place_ref, bf16[512,1280]{1,0:T(8,128)(2,1)} %bitcast.27.x_ref, ...), custom_call_target="tpu_custom_call" | custom-call | tf_op jit(solution)/shard_map/experts_first/pallas_call | solution.py:345
  178.6 18.8 %experts_second.1 = (bf16[4,64,1408]{2,1,0:T(8,128)(2,1)}, bf16[4,64,1408]{2,1,0:T(8,128)(2,1)}, bf16[3,2,224,1280]{3,2,1,0:T(8,128)(2,1)}, bf16[3,2,224,1280]{3...) custom-call(s32[4]{0:T(128)} %pad_add_fusion.1.place_ref, ...), custom_call_target="tpu_custom_call" | custom-call | tf_op jit(solution)/shard_map/experts_second/pallas_call | solution.py:408
  205.5 7.9 %shared_own.1 = (f32[64,1280]{1,0:T(8,128)}, f32[64,1280]{1,0:T(8,128)}) custom-call(bf16[64,1280]{1,0:T(8,128)(2,1)} %copy-done.12, bf16[64,1280]{1,0:T(8,128)(2,1)} %copy-done.11, bf16[3,224,1280]{2,1,0:T(8,128)(2,1)} %pad_maximum_fusion.refs_0_, bf16[3,224,1280]{2,1,0:T(8,128)(2,1)} %collective-permute-done.17.refs_1_, ...), custom_call_target="tpu_custom_call" | custom-call | tf_op jit(solution)/shard_map/shared_own/pallas_call | solution.py:451
  229.5 20.6 %collective-permute-done.27 = bf16[2,224,1280]{2,1,0:T(8,128)(2,1)} collective-permute-done((bf16[2,224,1280]{2,1,0:T(8,128)(2,1)}, bf16[2,224,1280]{2,1,0:T(8,128)(2,1)}, u32[]{:S(2)}, u32[]{:S(2)}) %collective-permute-start.27) | collective-permute-done | bytes 1146912 | tf_op jit(solution)/shard_map/ppermute | solution.py:607
  273.7 11.5 %attend_back.1 = bf16[8,4,96,256]{3,2,1,0:T(8,128)(2,1)} custom-call(s32[2]{0:T(128)} %pad_add_fusion.bounds_ref, bf16[8,4,96,256]{3,2,1,0:T(8,128)(2,1)} %bitcast.3.arr_ref, s32[8,256,128]{2,1,0:T(8,128)} %broadcast_in_dim.128.col_ref, s32[8,1,256]{2,1,0:T(1,128)} %bitcast.210, f32[8,256,128]{2,1,0:T(8,128)} %get-tuple-element.155.lse_ref, ...), custom_call_target="tpu_custom_call" | custom-call | tf_op jit(solution)/shard_map/attend_back/pallas_call | solution.py:229
  293.4 5.3 %all-to-all-start.5 = ((bf16[32,96,256]{2,1,0:T(8,128)(2,1)}), bf16[32,96,256]{2,1,0:T(8,128)(2,1)S(1)}, u32[]{:S(2)}, u32[]{:S(2)}) async-start(bf16[32,96,256]{2,1,0:T(8,128)(2,1)} %bitcast.46), calls=%async_computation.5 | async-start | bytes 3145728 | tf_op jit(solution)/shard_map/all_to_all | solution.py:611
  300.9 12.5 %shared_grads.1 = bf16[4,3,224,160]{3,2,1,0:T(8,128)(2,1)} custom-call(bf16[512,1280]{1,0:T(8,128)(2,1)} %bitcast.27.x_ref, bf16[512,1280]{1,0:T(8,128)(2,1)} %get-tuple-element.162.dy_ref, bf16[512,160]{1,0:T(8,128)(2,1)} %get-tuple-element.332.xc_ref, bf16[512,160]{1,0:T(8,128)(2,1)} %get-tuple-element.331.dyc_ref, ...), custom_call_target="tpu_custom_call" | custom-call | tf_op jit(solution)/shard_map/shared_grads/pallas_call | solution.py:476
  330.9 8.0 %collective-permute-done.46 = bf16[3,224,160]{2,1,0:T(8,128)(2,1)} collective-permute-done((bf16[3,224,160]{2,1,0:T(8,128)(2,1)}, bf16[3,224,160]{2,1,0:T(8,128)(2,1)}, u32[]{:S(2)}, u32[]{:S(2)}) %collective-permute-start.46) | collective-permute-done | bytes 215072 | tf_op jit(solution)/shard_map/ppermute | solution.py:607
  338.9 6.8 %collective-permute-done.47 = bf16[3,224,160]{2,1,0:T(8,128)(2,1)} collective-permute-done((bf16[3,224,160]{2,1,0:T(8,128)(2,1)}, bf16[3,224,160]{2,1,0:T(8,128)(2,1)}, u32[]{:S(2)}, u32[]{:S(2)}) %collective-permute-start.47) | collective-permute-done | bytes 215072 | tf_op jit(solution)/shard_map/ppermute | solution.py:607
  356.2 6.7 %project_back.1 = (bf16[4,64,1280]{2,1,0:T(8,128)(2,1)}, f32[1,1280]{1,0:T(1,128)}, bf16[4,160,320]{2,1,0:T(8,128)(2,1)}, bf16[4,160,320]{2,1,0:T(8,128)(2,1)}, ...) custom-call(s32[4]{0:T(128)} %pad_add_fusion.1.place_ref, ...), custom_call_target="tpu_custom_call" | custom-call | tf_op jit(solution)/shard_map/project_back/pallas_call | solution.py:566
  369.1 5.6 %all-to-all-start.6 = ((f32[32,2,160]{2,1,0:T(2,128)}), f32[32,2,160]{2,1,0:T(2,128)S(1)}, u32[]{:S(2)}, u32[]{:S(2)}) async-start(f32[32,2,160]{2,1,0:T(2,128)} %bitcast.66), calls=%async_computation.6 | async-start | bytes 131072 | tf_op jit(solution)/shard_map/all_to_all | solution.py:611
  401.5 6.0 %collective-permute-done.58 = bf16[160,320]{1,0:T(8,128)(2,1)S(1)} collective-permute-done((bf16[160,320]{1,0:T(8,128)(2,1)S(1)}, bf16[160,320]{1,0:T(8,128)(2,1)S(1)}, u32[]{:S(2)}, u32[]{:S(2)}) %collective-permute-start.58) | collective-permute-done | bytes 102432 | tf_op jit(solution)/shard_map/ppermute | solution.py:607
  418.8 5.8 %collective-permute-done.61 = bf16[160,320]{1,0:T(8,128)(2,1)} collective-permute-done((bf16[160,320]{1,0:T(8,128)(2,1)}, bf16[160,320]{1,0:T(8,128)(2,1)}, u32[]{:S(2)}, u32[]{:S(2)}) %collective-permute-start.61) | collective-permute-done | bytes 102432 | tf_op jit(solution)/shard_map/ppermute | solution.py:607
  433.0 5.4 %bitcast_add_fusion = (f32[2,224,1280]{2,1,0:T(8,128)}, f32[2,224,1280]{2,1,0:T(8,128)}) fusion(bf16[2,224,1280]{2,1,0:T(8,128)(2,1)} %collective-permute-done.63, bf16[3,2,224,1280]{3,2,1,0:T(8,128)(2,1)} %collective-permute-done.40, bf16[3,2,224,1280]{3,2,1,0:T(8,128)(2,1)S(1)} %copy-done.8, bf16[2,224,1280]{2,1,0:T(8,128)(2,1)} %collective-permute-done.48), kind=kLoop, calls=%fused_computation.8 | loop fusion | flops 5734400 | bytes 11468800 | tf_op jit(solution)/shard_map/add | solution.py:601
  (316 shorter events, 186.4 us)
Async XLA Ops:
  8.6 45.1 %all-to-all-start = ((bf16[32,96,256]{2,1,0:T(8,128)(2,1)}), bf16[32,96,256]{2,1,0:T(8,128)(2,1)}, u32[]{:S(2)}, u32[]{:S(2)}) async-start(bf16[32,96,256]{2,1,0:T(8,128)(2,1)} %get-tuple-element.105), calls=%async_computation | async-start | bytes 3145728 | tf_op jit(solution)/shard_map/all_to_all | solution.py:611
  16.1 37.2 %collective-permute-start = (bf16[10,32,1280]{2,1,0:T(8,128)(2,1)}, bf16[10,32,1280]{2,1,0:T(8,128)(2,1)}, u32[]{:S(2)}, u32[]{:S(2)}) collective-permute-start(bf16[10,32,1280]{2,1,0:T(8,128)(2,1)} %bitcast.4), channel_id=1, source_target_pairs={{0,2},{1,3},{2,0},{3,1},{4,6},{5,7},{6,4},{7,5},{8,10},{9,11},{10,... | collective-permute-start | bytes 2457608 | tf_op jit(solution)/shard_map/ppermute | solution.py:607
  17.8 39.9 %collective-permute-start.5 = (bf16[10,32,1280]{2,1,0:T(8,128)(2,1)}, bf16[10,32,1280]{2,1,0:T(8,128)(2,1)}, u32[]{:S(2)}, u32[]{:S(2)}) collective-permute-start(bf16[10,32,1280]{2,1,0:T(8,128)(2,1)} %bitcast.4), channel_id=1, source_target_pairs={{0,1},{1,0},{2,3},{3,2},{4,5},{5,4},{6,7},{7,6},{8,9},{9,8},{10,11... | collective-permute-start | bytes 2457608 | tf_op jit(solution)/shard_map/ppermute | solution.py:607
  53.3 31.4 %collective-permute-start.7 = (bf16[2,224,1280]{2,1,0:T(8,128)(2,1)}, bf16[2,224,1280]{2,1,0:T(8,128)(2,1)}, u32[]{:S(2)}, u32[]{:S(2)}) collective-permute-start(bf16[2,224,1280]{2,1,0:T(8,128)(2,1)} %refs_0_.1), channel_id=1, source_target_pairs={{0,2},{1,3},{2,0},{3,1},{4,6},{5,7},{6,4},{7,5},{8,10},{9,11},{10,... | collective-permute-start | bytes 3440648 | tf_op jit(solution)/shard_map/ppermute | solution.py:607
  53.7 29.4 %collective-permute-start.6 = (bf16[10,32,1280]{2,1,0:T(8,128)(2,1)}, bf16[10,32,1280]{2,1,0:T(8,128)(2,1)}, u32[]{:S(2)}, u32[]{:S(2)}) collective-permute-start(bf16[10,32,1280]{2,1,0:T(8,128)(2,1)} %collective-permute-done), channel_id=1, source_target_pairs={{0,1},{1,0},{2,3},{3,2},{4,5},{5,4},{6,7},{7,6},{8,9},{9,8},{10,11... | collective-permute-start | bytes 2457608 | tf_op jit(solution)/shard_map/ppermute | solution.py:607
  69.9 54.3 %collective-permute-start.11 = (bf16[2,224,1280]{2,1,0:T(8,128)(2,1)}, bf16[2,224,1280]{2,1,0:T(8,128)(2,1)}, u32[]{:S(2)}, u32[]{:S(2)}) collective-permute-start(bf16[2,224,1280]{2,1,0:T(8,128)(2,1)} %refs_0_.1), channel_id=1, source_target_pairs={{0,1},{1,0},{2,3},{3,2},{4,5},{5,4},{6,7},{7,6},{8,9},{9,8},{10,11... | collective-permute-start | bytes 3440648 | tf_op jit(solution)/shard_map/ppermute | solution.py:607
  81.3 33.2 %collective-permute-start.9 = (bf16[2,224,1280]{2,1,0:T(8,128)(2,1)}, bf16[2,224,1280]{2,1,0:T(8,128)(2,1)}, u32[]{:S(2)}, u32[]{:S(2)}) collective-permute-start(bf16[2,224,1280]{2,1,0:T(8,128)(2,1)} %refs_0_.2), channel_id=1, source_target_pairs={{0,2},{1,3},{2,0},{3,1},{4,6},{5,7},{6,4},{7,5},{8,10},{9,11},{10,... | collective-permute-start | bytes 3440648 | tf_op jit(solution)/shard_map/ppermute | solution.py:607
  84.3 54.8 %collective-permute-start.14 = (bf16[2,224,1280]{2,1,0:T(8,128)(2,1)}, bf16[2,224,1280]{2,1,0:T(8,128)(2,1)}, u32[]{:S(2)}, u32[]{:S(2)}) collective-permute-start(bf16[2,224,1280]{2,1,0:T(8,128)(2,1)} %refs_4_), channel_id=1, source_target_pairs={{0,2},{1,3},{2,0},{3,1},{4,6},{5,7},{6,4},{7,5},{8,10},{9,11},{10,... | collective-permute-start | bytes 3440648 | tf_op jit(solution)/shard_map/ppermute | solution.py:607
  84.7 54.5 %collective-permute-start.8 = (bf16[2,224,1280]{2,1,0:T(8,128)(2,1)}, bf16[2,224,1280]{2,1,0:T(8,128)(2,1)}, u32[]{:S(2)}, u32[]{:S(2)}) collective-permute-start(bf16[2,224,1280]{2,1,0:T(8,128)(2,1)} %refs_0_.2), channel_id=1, source_target_pairs={{0,1},{1,0},{2,3},{3,2},{4,5},{5,4},{6,7},{7,6},{8,9},{9,8},{10,11... | collective-permute-start | bytes 3440648 | tf_op jit(solution)/shard_map/ppermute | solution.py:607
  115.7 37.3 %all-to-all-start.2 = ((bf16[8,64,1280]{2,1,0:T(8,128)(2,1)}), bf16[8,64,1280]{2,1,0:T(8,128)(2,1)}, u32[]{:S(2)}, u32[]{:S(2)}) async-start(bf16[8,64,1280]{2,1,0:T(8,128)(2,1)} %broadcast_in_dim.139), calls=%async_computation.2 | async-start | bytes 2621440 | tf_op jit(solution)/shard_map/all_to_all | solution.py:611
  123.7 54.9 %collective-permute-start.16 = (bf16[3,224,1280]{2,1,0:T(8,128)(2,1)}, bf16[3,224,1280]{2,1,0:T(8,128)(2,1)}, u32[]{:S(2)}, u32[]{:S(2)}) collective-permute-start(bf16[3,224,1280]{2,1,0:T(8,128)(2,1)} %pad_maximum_fusion.refs_0_), channel_id=1, source_target_pairs={{0,2},{1,3},{2,0},{3,1},{4,6},{5,7},{6,4},{7,5},{8,10},{9,11},{10,... | collective-permute-start | bytes 5160968 | tf_op jit(solution)/shard_map/ppermute | solution.py:607
  124.1 54.5 %collective-permute-start.17 = (bf16[3,224,1280]{2,1,0:T(8,128)(2,1)}, bf16[3,224,1280]{2,1,0:T(8,128)(2,1)}, u32[]{:S(2)}, u32[]{:S(2)}) collective-permute-start(bf16[3,224,1280]{2,1,0:T(8,128)(2,1)} %pad_maximum_fusion.refs_0_), channel_id=1, source_target_pairs={{0,1},{1,0},{2,3},{3,2},{4,5},{5,4},{6,7},{7,6},{8,9},{9,8},{10,11... | collective-permute-start | bytes 5160968 | tf_op jit(solution)/shard_map/ppermute | solution.py:607
  174.1 40.6 %all-to-all-start.3 = ((bf16[8,64,1280]{2,1,0:T(8,128)(2,1)}), bf16[8,64,1280]{2,1,0:T(8,128)(2,1)}, u32[]{:S(2)}, u32[]{:S(2)}) async-start(bf16[8,64,1280]{2,1,0:T(8,128)(2,1)} %bitcast.195), calls=%async_computation.3 | async-start | bytes 2621440 | tf_op jit(solution)/shard_map/all_to_all | solution.py:611
  216.7 33.4 %collective-permute-start.27 = (bf16[2,224,1280]{2,1,0:T(8,128)(2,1)}, bf16[2,224,1280]{2,1,0:T(8,128)(2,1)}, u32[]{:S(2)}, u32[]{:S(2)}) collective-permute-start(bf16[2,224,1280]{2,1,0:T(8,128)(2,1)} %fusion.2), channel_id=1, source_target_pairs={{0,2},{1,3},{2,0},{3,1},{4,6},{5,7},{6,4},{7,5},{8,10},{9,11},{10,... | collective-permute-start | bytes 3440648 | tf_op jit(solution)/shard_map/ppermute | solution.py:607
  221.6 39.4 %collective-permute-start.39 = (bf16[2,224,1280]{2,1,0:T(8,128)(2,1)}, bf16[2,224,1280]{2,1,0:T(8,128)(2,1)}, u32[]{:S(2)}, u32[]{:S(2)}) collective-permute-start(bf16[2,224,1280]{2,1,0:T(8,128)(2,1)} %get-tuple-element.169), channel_id=1, source_target_pairs={{0,1},{1,0},{2,3},{3,2},{4,5},{5,4},{6,7},{7,6},{8,9},{9,8},{10,11... | collective-permute-start | bytes 3440648 | tf_op jit(solution)/shard_map/ppermute | solution.py:607
  221.6 39.4 %collective-permute-start.38 = (bf16[2,224,1280]{2,1,0:T(8,128)(2,1)}, bf16[2,224,1280]{2,1,0:T(8,128)(2,1)}, u32[]{:S(2)}, u32[]{:S(2)}) collective-permute-start(bf16[2,224,1280]{2,1,0:T(8,128)(2,1)} %get-tuple-element.167), channel_id=1, source_target_pairs={{0,1},{1,0},{2,3},{3,2},{4,5},{5,4},{6,7},{7,6},{8,9},{9,8},{10,11... | collective-permute-start | bytes 3440648 | tf_op jit(solution)/shard_map/ppermute | solution.py:607
  222.1 41.7 %all-to-all-start.4 = ((bf16[32,64,128]{2,1,0:T(8,128)(2,1)}), bf16[32,64,128]{2,1,0:T(8,128)(2,1)}, u32[]{:S(2)}, u32[]{:S(2)}) async-start(bf16[32,64,128]{2,1,0:T(8,128)(2,1)} %pad_maximum_fusion.2), calls=%async_computation.4 | async-start | bytes 1048576 | tf_op jit(solution)/shard_map/all_to_all | solution.py:611
  261.0 90.3 %collective-permute-start.40 = (bf16[3,2,224,1280]{3,2,1,0:T(8,128)(2,1)}, bf16[3,2,224,1280]{3,2,1,0:T(8,128)(2,1)}, u32[]{:S(2)}, u32[]{:S(2)}) collective-permute-start(bf16[3,2,224,1280]{3,2,1,0:T(8,128)(2,1)} %get-tuple-element.171), channel_id=1, source_target_pairs={{0,1},{1,0},{2,3},{3,2},{4,5},{5,4},{6,7},{7,6},{8,9},{9,8},{10,11... | collective-permute-start | bytes 10321928 | tf_op jit(solution)/shard_map/ppermute | solution.py:607
  289.0 27.7 %collective-permute-start.35 = (bf16[160,320]{1,0:T(8,128)(2,1)S(1)}, bf16[160,320]{1,0:T(8,128)(2,1)S(1)}, u32[]{:S(2)}, u32[]{:S(2)}) collective-permute-start(bf16[160,320]{1,0:T(8,128)(2,1)S(1)} %get-tuple-element.315), channel_id=1, source_target_pairs={{0,8},{4,12},{8,0},{12,4},{16,24},{20,28},{24,16},{28,20},{1,9},{5... | collective-permute-start | bytes 307208 | tf_op jit(solution)/shard_map/ppermute | solution.py:607
  293.4 28.0 %collective-permute-start.32 = (bf16[64,1408]{1,0:T(8,128)(2,1)}, bf16[64,1408]{1,0:T(8,128)(2,1)}, u32[]{:S(2)}, u32[]{:S(2)}) collective-permute-start(bf16[64,1408]{1,0:T(8,128)(2,1)} %concatenate.12), channel_id=1, source_target_pairs={{0,1},{1,0},{2,3},{3,2},{4,5},{5,4},{6,7},{7,6},{8,9},{9,8},{10,11... | collective-permute-start | bytes 540680 | tf_op jit(solution)/shard_map/ppermute | solution.py:607
  293.4 61.6 %all-to-all-start.5 = ((bf16[32,96,256]{2,1,0:T(8,128)(2,1)}), bf16[32,96,256]{2,1,0:T(8,128)(2,1)S(1)}, u32[]{:S(2)}, u32[]{:S(2)}) async-start(bf16[32,96,256]{2,1,0:T(8,128)(2,1)} %bitcast.46), calls=%async_computation.5 | async-start | bytes 3145728 | tf_op jit(solution)/shard_map/all_to_all | solution.py:611
  345.7 32.8 %collective-permute-start.48 = (bf16[2,224,1280]{2,1,0:T(8,128)(2,1)S(1)}, bf16[2,224,1280]{2,1,0:T(8,128)(2,1)}, u32[]{:S(2)}, u32[]{:S(2)}) collective-permute-start(bf16[2,224,1280]{2,1,0:T(8,128)(2,1)S(1)} %copy-done.15), channel_id=1, source_target_pairs={{0,2},{1,3},{2,0},{3,1},{4,6},{5,7},{6,4},{7,5},{8,10},{9,11},{10,... | collective-permute-start | bytes 3440648 | tf_op jit(solution)/shard_map/ppermute | solution.py:607
  369.1 45.9 %all-to-all-start.6 = ((f32[32,2,160]{2,1,0:T(2,128)}), f32[32,2,160]{2,1,0:T(2,128)S(1)}, u32[]{:S(2)}, u32[]{:S(2)}) async-start(f32[32,2,160]{2,1,0:T(2,128)} %bitcast.66), calls=%async_computation.6 | async-start | bytes 131072 | tf_op jit(solution)/shard_map/all_to_all | solution.py:611
  380.0 53.0 %collective-permute-start.63 = (bf16[2,224,1280]{2,1,0:T(8,128)(2,1)}, bf16[2,224,1280]{2,1,0:T(8,128)(2,1)}, u32[]{:S(2)}, u32[]{:S(2)}) collective-permute-start(bf16[2,224,1280]{2,1,0:T(8,128)(2,1)} %get-tuple-element.194), channel_id=1, source_target_pairs={{0,2},{1,3},{2,0},{3,1},{4,6},{5,7},{6,4},{7,5},{8,10},{9,11},{10,... | collective-permute-start | bytes 3440648 | tf_op jit(solution)/shard_map/ppermute | solution.py:607
  (84 other events, 1056.9 us)

commit v6 on v5

--- a/solution.py
+++ b/solution.py
@@ -638,11 +638,26 @@
     return [x] + [flip(x, k, "tensor") for k in range(1, quarters)]
 
 
-def in_order(parts, quarter):
-    out = jnp.zeros((len(parts),) + parts[0].shape, parts[0].dtype)
-    for k, p in enumerate(parts):
-        out = lax.dynamic_update_slice(out, p[None], (quarter ^ k,) + (0,) * p.ndim)
-    return out.reshape((-1,) + parts[0].shape[1:])
+def in_order(place, parts):
+    count = len(parts)
+    rows, width = parts[0].shape
+
+    def body(place_ref, *refs):
+        for k in range(count):
+            refs[count][place_ref[2] ^ k] = refs[k][...]
+
+    return pl.pallas_call(
+        body,
+        grid_spec=pltpu.PrefetchScalarGridSpec(
+            num_scalar_prefetch=1,
+            grid=(1,),
+            in_specs=[whole((rows, width))] * count,
+            out_specs=whole((count, rows, width)),
+        ),
+        out_shape=jax.ShapeDtypeStruct((count, rows, width), parts[0].dtype),
+        compiler_params=pltpu.CompilerParams(vmem_limit_bytes=VMEM_LIMIT),
+        name="in_order",
+    )(place, *parts).reshape(count * rows, width)
 
 
 def on_device(
@@ -825,16 +840,13 @@
 
     grad_attn_sent = after(grad_attn, do_send)
     routed_far = [across(to_far[0])]
-    from_far = [beside(after(parts[3 + m], do_send)) for m in (1, 2)]
-    routed_far[0], att_parts = lax.optimization_barrier((routed_far[0], att_parts))
     proj_low, proj_high = output_grads(
         place, of_quarters(grad_attn_sent), att_parts, heads, hw, blocks
     )
-    from_far = lax.optimization_barrier((tuple(from_far), proj_low))[0]
-    to_far += [added([parts[2][m], from_far[m - 1]]).astype(BF) for m in (1, 2)]
-    near = beside(after(parts[1], from_far[1]))
     out_pairs = added([out_low, after(out_got, proj_low)]).astype(BF)
-    do_units, out_pairs = lax.optimization_barrier((do_units, out_pairs, proj_low))[:2]
+    do_units, out_pairs = lax.optimization_barrier(
+        (do_units, out_pairs, proj_low, routed_far[0])
+    )[:2]
 
     grad_units = attend_back(bounds, arrived, seg_col, seg_row, lse, do_units, most)
     out_home = collected(out_pairs)
@@ -842,6 +854,8 @@
     grad_units = lax.optimization_barrier((grad_units, out_home, proj_pairs, routed_far[0]))[0]
     back_grads = exchange(grad_units.reshape(units, 3 * hw, rows), BOTH)
 
+    from_far = [beside(after(parts[3 + m], grad_units)) for m in (1, 2)]
+    to_far += [added([parts[2][m], from_far[m - 1]]).astype(BF) for m in (1, 2)]
     rows_late, grads_late = lax.optimization_barrier((rows_in, grads_in, grad_units))[:2]
     rows_cut = lax.dynamic_slice_in_dim(rows_late, rank * cut, cut, axis=1)
     grads_cut = lax.dynamic_slice_in_dim(grads_late, rank * cut, cut, axis=1)
@@ -850,6 +864,7 @@
     ]
     shared_parts = shared_parts[0] if len(spans) == 1 else added(shared_parts).astype(BF)
     shared_gots = [flip(shared_parts[k], k, "tensor") for k in range(1, quarters)]
+    near = beside(after(parts[1], grad_units))
     out_grad = collected(after(proj_pairs, grad_units))
     moe_out = out_home[:, :width] + shared_out
     slot_sums = out_home[:, width : width + 3 * experts_total].reshape(own, 3, experts_total)
@@ -857,11 +872,10 @@
     gate_grad = jnp.sum(jnp.where(slot_hot, slot_sums[:, None, :], 0.0), axis=2)
     final = [(hidden_state + moe_out).astype(BF)] + [p.astype(BF) for p in pieces(gate_grad)]
     final = jnp.concatenate(final + [jnp.zeros((own, 128 - 3 * top), BF)], axis=1)
-    final = in_order(of_quarters(after(final, grad_units)), quarter)
+    final = in_order(place, of_quarters(after(final, grad_units)))
     output = final[:, :width]
     gate_grad = jnp.sum(final[:, width : width + 3 * top].reshape(rows, 3, top).astype(F32), axis=1)
-    routed = [added([parts[0][0], near[0], routed_far[0]])]
-    back_grads = lax.optimization_barrier((back_grads, shared_parts, out_grad, output, routed[0]))[0]
+    back_grads, near = lax.optimization_barrier((back_grads, near, shared_parts, out_grad, output))[:2]
 
     back_out = project_back(
         place,
@@ -883,20 +897,24 @@
     dx_parts = [back_out[0][0]] + [flip(back_out[0][k], k, "tensor") for k in range(1, quarters)]
     pair_q = paired(back_out[2], back_out[3])
     pair_k = paired(back_out[4], after(back_out[5], pair_q))
-    far_one = across(lax.optimization_barrier((to_far[1], tuple(shared_gots)))[0])
-    dx_parts, pair_q, far_one = lax.optimization_barrier((tuple(dx_parts), pair_q, far_one))
+    far_one = across(lax.optimization_barrier((to_far[1], output, tuple(shared_gots)))[0])
+    dx_parts, pair_q = lax.optimization_barrier((tuple(dx_parts), pair_q))
     grad_one = added(dx_parts)
+    far_two = across(after(to_far[2], far_one))
+    routed = [added([parts[0][0], near[0], after(routed_far[0], pair_q)])]
+    shared_gots = lax.optimization_barrier((tuple(shared_gots), pair_q))[0]
+    shared = added([shared_parts[0], *shared_gots])
     pair_v = paired(back_out[6], after(back_out[7], pair_k))
-    far_two = across(after(to_far[2], far_one))
+    routed.append(added([parts[0][1], near[1], after(far_one, pair_k)]))
+    pair_v, routed, shared = lax.optimization_barrier((pair_v, routed, shared))
+    routed.append(added([parts[0][2], near[2], after(far_two, pair_v)]))
     qkv_grads = [collected(p) for p in (pair_q, pair_k, pair_v)]
     first_scale = rms_scale(own_tokens)
     grad_first, _ = norm_backward(grad_one, own_tokens, first_scale, first_gain)
-    input_mine = after((grad_hidden + grad_first).astype(BF), pair_v)
-    input_grad = in_order(of_quarters(input_mine), quarter)
-    shared = added([shared_parts[0]] + shared_gots)
+    input_mine = after((grad_hidden + grad_first).astype(BF), pair_k)
+    input_parts, routed[2] = lax.optimization_barrier((tuple(of_quarters(input_mine)), routed[2]))
+    input_grad = in_order(place, input_parts)
     gains = jnp.sum(after(gains, pair_v), axis=0)
-    routed.append(added([parts[0][1], near[1], after(far_one, pair_v)]))
-    routed.append(added([parts[0][2], near[2], far_two]))
 
     weight_shape = (heads, 2, pair_width, cut)
     return (

time: 445 us -> 461 us (1.036)
  waiting for transfers between devices: 138 us -> 168 us
  local copies, waits for them, and re-layouts: 50.7 us -> 39.6 us
  starting transfers between devices: 98.7 us -> 91.2 us
    ppermute x64, waiting for transfers between devices: 131 us -> 161 us  [flip(): return lax.ppermute(x, axis, [(i, i ^ by) for i in range(size)])]
    dynamic_update_slice x8 -> x0, local copies, waits for them, and re-layouts: 10.1 us -> none  [in_order(): out = lax.dynamic_update_slice(out, p[None], (quarter ^ k,) + (0,) * p.ndim)]
    ppermute x64, starting transfers between devices: 60.1 us -> 54.1 us  [flip(): return lax.ppermute(x, axis, [(i, i ^ by) for i in range(size)])]
    pallas_call x0 -> x2, Pallas kernels: none -> 5.46 us  [in_order(): pl.pallas_call(body, grid_spec=pltpu.PrefetchScalarGridSpec(num_scalar_pr...]
  transfers between devices with their start and end apart: 71 -> 71, of which waited for: 21 -> 23; matrix products, arithmetic and copies ran while one was open for 19% -> 16% of each run, Pallas kernels for 23% -> 23%
where the time goes in v6:
time: 461 us; the launch traced here: 455 us
  waiting for transfers between devices  168 us (36%)
  Pallas kernels  108 us (23%)
  starting transfers between devices  91.2 us (20%)
  other arithmetic  42.3 us (9%)
  local copies, waits for them, and re-layouts  39.6 us (9%)
    ppermute x64, waiting for transfers between devices, flip(): return lax.ppermute(x, axis, [(i, i ^ by) for i in range(size)])  161 us
    ppermute x64, starting transfers between devices, flip(): return lax.ppermute(x, axis, [(i, i ^ by) for i in range(size)])  54.1 us
    all_to_all x7, starting transfers between devices, exchange(): return lax.all_to_all(x, axis, 0, 0, tiled=True)  37.1 us
    pallas_call x1, Pallas kernels, experts_first(): pl.pallas_call(body, grid_spec=pltpu.PrefetchScalarGridSpec(num_scalar_pr...  21.1 us
    pallas_call x1, Pallas kernels, experts_second(): pl.pallas_call(body, grid_spec=pltpu.PrefetchScalarGridSpec(num_scalar_pr...  18.7 us
    pallas_call x1, Pallas kernels, shared_grads(): pl.pallas_call(body, out_shape=jax.ShapeDtypeStruct((parts, 3, hidden, cu...  12.5 us
    add x5, other arithmetic, added(): total = total + p.astype(F32)  12.2 us
    pallas_call x1, Pallas kernels, attend_back(): pl.pallas_call(body, grid_spec=grid_spec, out_shape=jax.ShapeDtypeStruct(...  11.4 us
  transfers between devices with their start and end apart: 71, of which 23 were waited for; matrix products, arithmetic and copies ran while one was open for 16% of the time, Pallas kernels for 23%

profile of v6, /device:TPU:0, one launch (start us, length us, event | category | flops | bytes accessed | tf_op | source)
XLA Modules:
  0.0 455.0 jit_solution(8460197793594108025)
XLA Ops:
  8.6 7.4 %all-to-all-start = ((bf16[32,96,256]{2,1,0:T(8,128)(2,1)}), bf16[32,96,256]{2,1,0:T(8,128)(2,1)}, u32[]{:S(2)}, u32[]{:S(2)}) async-start(bf16[32,96,256]{2,1,0:T(8,128)(2,1)} %get-tuple-element.112), calls=%async_computation | async-start | bytes 3145728 | tf_op jit(solution)/shard_map/all_to_all | solution.py:611
  26.0 27.3 %collective-permute-done = bf16[10,32,1280]{2,1,0:T(8,128)(2,1)} collective-permute-done((bf16[10,32,1280]{2,1,0:T(8,128)(2,1)}, bf16[10,32,1280]{2,1,0:T(8,128)(2,1)}, u32[]{:S(2)}, u32[]{:S(2)}) %collective-permute-start) | collective-permute-done | bytes 819232 | tf_op jit(solution)/shard_map/ppermute | solution.py:607
  60.6 9.2 %attend.1 = (bf16[8,256,128]{2,1,0:T(8,128)(2,1)}, f32[8,256,128]{2,1,0:T(8,128)}) custom-call(s32[2]{0:T(128)} %pad_add_fusion.1.bounds_ref, bf16[8,4,96,256]{3,2,1,0:T(8,128)(2,1)} %bitcast.7.arr_ref, s32[8,256,128]{2,1,0:T(8,128)} %broadcast_in_dim.60.col_ref, s32[8,1,256]{2,1,0:T(1,128)} %bitcast.194), custom_call_target="tpu_custom_call" | custom-call | tf_op jit(solution)/shard_map/attend/pallas_call | solution.py:146
  74.1 6.0 %all-to-all-start.1 = ((bf16[32,64,128]{2,1,0:T(8,128)(2,1)}), bf16[32,64,128]{2,1,0:T(8,128)(2,1)}, u32[]{:S(2)}, u32[]{:S(2)}) async-start(bf16[32,64,128]{2,1,0:T(8,128)(2,1)} %bitcast.186), calls=%async_computation.1 | async-start | bytes 1048576 | tf_op jit(solution)/shard_map/all_to_all | solution.py:611
  84.7 9.6 %collective-permute-done.4.odd_ref = bf16[4,64,1408]{2,1,0:T(8,128)(2,1)} collective-permute-done((bf16[4,64,1408]{2,1,0:T(8,128)(2,1)}, bf16[4,64,1408]{2,1,0:T(8,128)(2,1)}, u32[]{:S(2)}, u32[]{:S(2)}) %collective-permute-start.4) | collective-permute-done | bytes 720928 | tf_op jit(solution)/shard_map/ppermute | solution.py:607
  98.8 15.7 %collective-permute-done.9.refs_2_ = bf16[2,224,1280]{2,1,0:T(8,128)(2,1)} collective-permute-done((bf16[2,224,1280]{2,1,0:T(8,128)(2,1)}, bf16[2,224,1280]{2,1,0:T(8,128)(2,1)}, u32[]{:S(2)}, u32[]{:S(2)}) %collective-permute-start.9) | collective-permute-done | bytes 1146912 | tf_op jit(solution)/shard_map/ppermute | solution.py:607
  115.7 5.2 %all-to-all-start.2 = ((bf16[8,64,1280]{2,1,0:T(8,128)(2,1)}), bf16[8,64,1280]{2,1,0:T(8,128)(2,1)}, u32[]{:S(2)}, u32[]{:S(2)}) async-start(bf16[8,64,1280]{2,1,0:T(8,128)(2,1)} %broadcast_in_dim.108), calls=%async_computation.2 | async-start | bytes 2621440 | tf_op jit(solution)/shard_map/all_to_all | solution.py:611
  124.4 14.8 %collective-permute-done.14.refs_6_ = bf16[2,224,1280]{2,1,0:T(8,128)(2,1)} collective-permute-done((bf16[2,224,1280]{2,1,0:T(8,128)(2,1)}, bf16[2,224,1280]{2,1,0:T(8,128)(2,1)}, u32[]{:S(2)}, u32[]{:S(2)}) %collective-permute-start.14) | collective-permute-done | bytes 1146912 | tf_op jit(solution)/shard_map/ppermute | solution.py:607
  140.3 7.5 %down_products.1 = (f32[2,4,512,224]{3,2,1,0:T(8,128)}, bf16[512,1280]{1,0:T(8,128)(2,1)}, bf16[512,128]{1,0:T(8,128)(2,1)}) custom-call(s32[4]{0:T(128)} %pad_add_fusion.place_ref, bf16[4,64,1408]{2,1,0:T(8,128)(2,1)} %pad_maximum_fusion.1.even_ref, bf16[4,64,1408]{2,1,0:T(8,128)(2,1)} %collective-permute-done.4.odd_ref, bf16[2,224,1280]{2,1,0:T(8,128)(2,1)} %refs_0_.2, ...), custom_call_target="tpu_custom_call" | custom-call | tf_op jit(solution)/shard_map/down_products/pallas_call | solution.py:266
  153.0 21.1 %experts_first.1 = (bf16[2,4,512,224]{3,2,1,0:T(8,128)(2,1)}, bf16[2,4,512,224]{3,2,1,0:T(8,128)(2,1)}, bf16[2,4,512,224]{3,2,1,0:T(8,128)(2,1)}, bf16[512,128]{1,0:T(8,128)(2,1)}, bf16[512,1280]{1,0:T(8,128)(2,1)}) custom-call(s32[4]{0:T(128)} %pad_add_fusion.place_ref, bf16[512,1280]{1,0:T(8,128)(2,1)} %bitcast.27.x_ref, ...), custom_call_target="tpu_custom_call" | custom-call | tf_op jit(solution)/shard_map/experts_first/pallas_call | solution.py:345
  178.6 18.7 %experts_second.1 = (bf16[4,64,1408]{2,1,0:T(8,128)(2,1)}, bf16[4,64,1408]{2,1,0:T(8,128)(2,1)}, bf16[3,2,224,1280]{3,2,1,0:T(8,128)(2,1)}, bf16[3,2,224,1280]{3...) custom-call(s32[4]{0:T(128)} %pad_add_fusion.place_ref, ...), custom_call_target="tpu_custom_call" | custom-call | tf_op jit(solution)/shard_map/experts_second/pallas_call | solution.py:408
  205.3 7.9 %shared_own.1 = (f32[64,1280]{1,0:T(8,128)}, f32[64,1280]{1,0:T(8,128)}) custom-call(bf16[64,1280]{1,0:T(8,128)(2,1)} %copy-done.13, bf16[64,1280]{1,0:T(8,128)(2,1)} %copy-done.12, bf16[3,224,1280]{2,1,0:T(8,128)(2,1)} %pad_maximum_fusion.refs_0_, bf16[3,224,1280]{2,1,0:T(8,128)(2,1)} %collective-permute-done.17.refs_1_, ...), custom_call_target="tpu_custom_call" | custom-call | tf_op jit(solution)/shard_map/shared_own/pallas_call | solution.py:451
  227.9 26.1 %collective-permute-done.25.refs_2_ = bf16[64,1280]{1,0:T(8,128)(2,1)S(1)} collective-permute-done((bf16[64,1280]{1,0:T(8,128)(2,1)S(1)}, bf16[64,1280]{1,0:T(8,128)(2,1)S(1)}, u32[]{:S(2)}, u32[]{:S(2)}) %collective-permute-start.25) | collective-permute-done | bytes 163872 | tf_op jit(solution)/shard_map/ppermute | solution.py:607
  266.8 7.7 %collective-permute-done.31 = bf16[4,160,320]{2,1,0:T(8,128)(2,1)S(1)} collective-permute-done((bf16[4,160,320]{2,1,0:T(8,128)(2,1)}, bf16[4,160,320]{2,1,0:T(8,128)(2,1)S(1)}, u32[]{:S(2)}, u32[]{:S(2)}) %collective-permute-start.31) | collective-permute-done | bytes 409632 | tf_op jit(solution)/shard_map/ppermute | solution.py:607
  274.6 11.4 %attend_back.1 = bf16[8,4,96,256]{3,2,1,0:T(8,128)(2,1)} custom-call(s32[2]{0:T(128)} %pad_add_fusion.1.bounds_ref, bf16[8,4,96,256]{3,2,1,0:T(8,128)(2,1)} %bitcast.7.arr_ref, s32[8,256,128]{2,1,0:T(8,128)} %broadcast_in_dim.60.col_ref, s32[8,1,256]{2,1,0:T(1,128)} %bitcast.195, f32[8,256,128]{2,1,0:T(8,128)} %get-tuple-element.158.lse_ref, ...), custom_call_target="tpu_custom_call" | custom-call | tf_op jit(solution)/shard_map/attend_back/pallas_call | solution.py:229
  295.8 12.5 %shared_grads.1 = bf16[4,3,224,160]{3,2,1,0:T(8,128)(2,1)} custom-call(bf16[512,1280]{1,0:T(8,128)(2,1)} %bitcast.27.x_ref, bf16[512,1280]{1,0:T(8,128)(2,1)} %get-tuple-element.166.dy_ref, bf16[512,160]{1,0:T(8,128)(2,1)} %get-tuple-element.331.xc_ref, bf16[512,160]{1,0:T(8,128)(2,1)} %get-tuple-element.330.dyc_ref, ...), custom_call_target="tpu_custom_call" | custom-call | tf_op jit(solution)/shard_map/shared_grads/pallas_call | solution.py:476
  330.0 5.9 %collective-permute-done.51 = bf16[3,224,160]{2,1,0:T(8,128)(2,1)S(1)} collective-permute-done((bf16[3,224,160]{2,1,0:T(8,128)(2,1)}, bf16[3,224,160]{2,1,0:T(8,128)(2,1)S(1)}, u32[]{:S(2)}, u32[]{:S(2)}) %collective-permute-start.51) | collective-permute-done | bytes 215072 | tf_op jit(solution)/shard_map/ppermute | solution.py:607
  345.6 7.6 %collective-permute-done.37 = bf16[160,320]{1,0:T(8,128)(2,1)} collective-permute-done((bf16[160,320]{1,0:T(8,128)(2,1)}, bf16[160,320]{1,0:T(8,128)(2,1)}, u32[]{:S(2)}, u32[]{:S(2)}) %collective-permute-start.37) | collective-permute-done | bytes 102432 | tf_op jit(solution)/shard_map/ppermute | solution.py:607
  356.7 6.9 %collective-permute-done.52 = bf16[2,224,1280]{2,1,0:T(8,128)(2,1)} collective-permute-done((bf16[2,224,1280]{2,1,0:T(8,128)(2,1)S(1)}, bf16[2,224,1280]{2,1,0:T(8,128)(2,1)}, u32[]{:S(2)}, u32[]{:S(2)}) %collective-permute-start.52) | collective-permute-done | bytes 1146912 | tf_op jit(solution)/shard_map/ppermute | solution.py:607
  365.3 6.7 %project_back.1 = (bf16[4,64,1280]{2,1,0:T(8,128)(2,1)}, f32[1,1280]{1,0:T(1,128)}, bf16[4,160,320]{2,1,0:T(8,128)(2,1)}, bf16[4,160,320]{2,1,0:T(8,128)(2,1)}, ...) custom-call(s32[4]{0:T(128)} %pad_add_fusion.place_ref, ...), custom_call_target="tpu_custom_call" | custom-call | tf_op jit(solution)/shard_map/project_back/pallas_call | solution.py:566
  377.9 5.5 %all-to-all-start.6 = ((f32[32,2,160]{2,1,0:T(2,128)}), f32[32,2,160]{2,1,0:T(2,128)S(1)}, u32[]{:S(2)}, u32[]{:S(2)}) async-start(f32[32,2,160]{2,1,0:T(2,128)} %bitcast.62), calls=%async_computation.6 | async-start | bytes 131072 | tf_op jit(solution)/shard_map/all_to_all | solution.py:611
  385.0 11.1 %collective-permute-done.40 = bf16[64,1280]{1,0:T(8,128)(2,1)S(1)} collective-permute-done((bf16[64,1280]{1,0:T(8,128)(2,1)S(1)}, bf16[64,1280]{1,0:T(8,128)(2,1)S(1)}, u32[]{:S(2)}, u32[]{:S(2)}) %collective-permute-start.40) | collective-permute-done | bytes 163872 | tf_op jit(solution)/shard_map/ppermute | solution.py:607
  407.1 6.7 %collective-permute-done.56 = bf16[160,320]{1,0:T(8,128)(2,1)S(1)} collective-permute-done((bf16[160,320]{1,0:T(8,128)(2,1)S(1)}, bf16[160,320]{1,0:T(8,128)(2,1)S(1)}, u32[]{:S(2)}, u32[]{:S(2)}) %collective-permute-start.56) | collective-permute-done | bytes 102432 | tf_op jit(solution)/shard_map/ppermute | solution.py:607
  423.2 5.4 %bitcast_add_fusion = (f32[2,224,1280]{2,1,0:T(8,128)}, f32[2,224,1280]{2,1,0:T(8,128)}) fusion(bf16[2,224,1280]{2,1,0:T(8,128)(2,1)} %collective-permute-done.52, bf16[3,2,224,1280]{3,2,1,0:T(8,128)(2,1)} %collective-permute-done.35, bf16[3,2,224,1280]{3,2,1,0:T(8,128)(2,1)S(1)} %copy-done.7, bf16[2,224,1280]{2,1,0:T(8,128)(2,1)} %collective-permute-done.27), kind=kLoop, calls=%fused_computation.8 | loop fusion | flops 5734400 | bytes 11468800 | tf_op jit(solution)/shard_map/add | solution.py:601
  (328 shorter events, 188.5 us)
Async XLA Ops:
  8.6 45.1 %all-to-all-start = ((bf16[32,96,256]{2,1,0:T(8,128)(2,1)}), bf16[32,96,256]{2,1,0:T(8,128)(2,1)}, u32[]{:S(2)}, u32[]{:S(2)}) async-start(bf16[32,96,256]{2,1,0:T(8,128)(2,1)} %get-tuple-element.112), calls=%async_computation | async-start | bytes 3145728 | tf_op jit(solution)/shard_map/all_to_all | solution.py:611
  16.1 37.2 %collective-permute-start = (bf16[10,32,1280]{2,1,0:T(8,128)(2,1)}, bf16[10,32,1280]{2,1,0:T(8,128)(2,1)}, u32[]{:S(2)}, u32[]{:S(2)}) collective-permute-start(bf16[10,32,1280]{2,1,0:T(8,128)(2,1)} %bitcast.8), channel_id=1, source_target_pairs={{0,2},{1,3},{2,0},{3,1},{4,6},{5,7},{6,4},{7,5},{8,10},{9,11},{10,... | collective-permute-start | bytes 2457608 | tf_op jit(solution)/shard_map/ppermute | solution.py:607
  17.8 39.9 %collective-permute-start.5 = (bf16[10,32,1280]{2,1,0:T(8,128)(2,1)}, bf16[10,32,1280]{2,1,0:T(8,128)(2,1)}, u32[]{:S(2)}, u32[]{:S(2)}) collective-permute-start(bf16[10,32,1280]{2,1,0:T(8,128)(2,1)} %bitcast.8), channel_id=1, source_target_pairs={{0,1},{1,0},{2,3},{3,2},{4,5},{5,4},{6,7},{7,6},{8,9},{9,8},{10,11... | collective-permute-start | bytes 2457608 | tf_op jit(solution)/shard_map/ppermute | solution.py:607
  53.3 31.4 %collective-permute-start.7 = (bf16[2,224,1280]{2,1,0:T(8,128)(2,1)}, bf16[2,224,1280]{2,1,0:T(8,128)(2,1)}, u32[]{:S(2)}, u32[]{:S(2)}) collective-permute-start(bf16[2,224,1280]{2,1,0:T(8,128)(2,1)} %refs_0_.1), channel_id=1, source_target_pairs={{0,2},{1,3},{2,0},{3,1},{4,6},{5,7},{6,4},{7,5},{8,10},{9,11},{10,... | collective-permute-start | bytes 3440648 | tf_op jit(solution)/shard_map/ppermute | solution.py:607
  53.7 29.4 %collective-permute-start.6 = (bf16[10,32,1280]{2,1,0:T(8,128)(2,1)}, bf16[10,32,1280]{2,1,0:T(8,128)(2,1)}, u32[]{:S(2)}, u32[]{:S(2)}) collective-permute-start(bf16[10,32,1280]{2,1,0:T(8,128)(2,1)} %collective-permute-done), channel_id=1, source_target_pairs={{0,1},{1,0},{2,3},{3,2},{4,5},{5,4},{6,7},{7,6},{8,9},{9,8},{10,11... | collective-permute-start | bytes 2457608 | tf_op jit(solution)/shard_map/ppermute | solution.py:607
  69.8 54.3 %collective-permute-start.11 = (bf16[2,224,1280]{2,1,0:T(8,128)(2,1)}, bf16[2,224,1280]{2,1,0:T(8,128)(2,1)}, u32[]{:S(2)}, u32[]{:S(2)}) collective-permute-start(bf16[2,224,1280]{2,1,0:T(8,128)(2,1)} %refs_0_.1), channel_id=1, source_target_pairs={{0,1},{1,0},{2,3},{3,2},{4,5},{5,4},{6,7},{7,6},{8,9},{9,8},{10,11... | collective-permute-start | bytes 3440648 | tf_op jit(solution)/shard_map/ppermute | solution.py:607
  81.3 33.2 %collective-permute-start.9 = (bf16[2,224,1280]{2,1,0:T(8,128)(2,1)}, bf16[2,224,1280]{2,1,0:T(8,128)(2,1)}, u32[]{:S(2)}, u32[]{:S(2)}) collective-permute-start(bf16[2,224,1280]{2,1,0:T(8,128)(2,1)} %refs_0_.2), channel_id=1, source_target_pairs={{0,2},{1,3},{2,0},{3,1},{4,6},{5,7},{6,4},{7,5},{8,10},{9,11},{10,... | collective-permute-start | bytes 3440648 | tf_op jit(solution)/shard_map/ppermute | solution.py:607
  84.3 54.8 %collective-permute-start.14 = (bf16[2,224,1280]{2,1,0:T(8,128)(2,1)}, bf16[2,224,1280]{2,1,0:T(8,128)(2,1)}, u32[]{:S(2)}, u32[]{:S(2)}) collective-permute-start(bf16[2,224,1280]{2,1,0:T(8,128)(2,1)} %refs_4_), channel_id=1, source_target_pairs={{0,2},{1,3},{2,0},{3,1},{4,6},{5,7},{6,4},{7,5},{8,10},{9,11},{10,... | collective-permute-start | bytes 3440648 | tf_op jit(solution)/shard_map/ppermute | solution.py:607
  84.7 54.5 %collective-permute-start.8 = (bf16[2,224,1280]{2,1,0:T(8,128)(2,1)}, bf16[2,224,1280]{2,1,0:T(8,128)(2,1)}, u32[]{:S(2)}, u32[]{:S(2)}) collective-permute-start(bf16[2,224,1280]{2,1,0:T(8,128)(2,1)} %refs_0_.2), channel_id=1, source_target_pairs={{0,1},{1,0},{2,3},{3,2},{4,5},{5,4},{6,7},{7,6},{8,9},{9,8},{10,11... | collective-permute-start | bytes 3440648 | tf_op jit(solution)/shard_map/ppermute | solution.py:607
  115.7 37.3 %all-to-all-start.2 = ((bf16[8,64,1280]{2,1,0:T(8,128)(2,1)}), bf16[8,64,1280]{2,1,0:T(8,128)(2,1)}, u32[]{:S(2)}, u32[]{:S(2)}) async-start(bf16[8,64,1280]{2,1,0:T(8,128)(2,1)} %broadcast_in_dim.108), calls=%async_computation.2 | async-start | bytes 2621440 | tf_op jit(solution)/shard_map/all_to_all | solution.py:611
  123.7 54.9 %collective-permute-start.16 = (bf16[3,224,1280]{2,1,0:T(8,128)(2,1)}, bf16[3,224,1280]{2,1,0:T(8,128)(2,1)}, u32[]{:S(2)}, u32[]{:S(2)}) collective-permute-start(bf16[3,224,1280]{2,1,0:T(8,128)(2,1)} %pad_maximum_fusion.refs_0_), channel_id=1, source_target_pairs={{0,2},{1,3},{2,0},{3,1},{4,6},{5,7},{6,4},{7,5},{8,10},{9,11},{10,... | collective-permute-start | bytes 5160968 | tf_op jit(solution)/shard_map/ppermute | solution.py:607
  124.1 54.5 %collective-permute-start.17 = (bf16[3,224,1280]{2,1,0:T(8,128)(2,1)}, bf16[3,224,1280]{2,1,0:T(8,128)(2,1)}, u32[]{:S(2)}, u32[]{:S(2)}) collective-permute-start(bf16[3,224,1280]{2,1,0:T(8,128)(2,1)} %pad_maximum_fusion.refs_0_), channel_id=1, source_target_pairs={{0,1},{1,0},{2,3},{3,2},{4,5},{5,4},{6,7},{7,6},{8,9},{9,8},{10,11... | collective-permute-start | bytes 5160968 | tf_op jit(solution)/shard_map/ppermute | solution.py:607
  174.1 40.5 %all-to-all-start.3 = ((bf16[8,64,1280]{2,1,0:T(8,128)(2,1)}), bf16[8,64,1280]{2,1,0:T(8,128)(2,1)}, u32[]{:S(2)}, u32[]{:S(2)}) async-start(bf16[8,64,1280]{2,1,0:T(8,128)(2,1)} %bitcast.179), calls=%async_computation.3 | async-start | bytes 2621440 | tf_op jit(solution)/shard_map/all_to_all | solution.py:611
  216.5 45.8 %collective-permute-start.27 = (bf16[2,224,1280]{2,1,0:T(8,128)(2,1)}, bf16[2,224,1280]{2,1,0:T(8,128)(2,1)}, u32[]{:S(2)}, u32[]{:S(2)}) collective-permute-start(bf16[2,224,1280]{2,1,0:T(8,128)(2,1)} %fusion.2), channel_id=1, source_target_pairs={{0,2},{1,3},{2,0},{3,1},{4,6},{5,7},{6,4},{7,5},{8,10},{9,11},{10,... | collective-permute-start | bytes 3440648 | tf_op jit(solution)/shard_map/ppermute | solution.py:607
  221.6 40.7 %all-to-all-start.4 = ((bf16[32,64,128]{2,1,0:T(8,128)(2,1)}), bf16[32,64,128]{2,1,0:T(8,128)(2,1)S(1)}, u32[]{:S(2)}, u32[]{:S(2)}) async-start(bf16[32,64,128]{2,1,0:T(8,128)(2,1)} %pad_maximum_fusion.2), calls=%async_computation.4 | async-start | bytes 1048576 | tf_op jit(solution)/shard_map/all_to_all | solution.py:611
  226.3 27.8 %collective-permute-start.25 = (bf16[64,1280]{1,0:T(8,128)(2,1)S(1)}, bf16[64,1280]{1,0:T(8,128)(2,1)S(1)}, u32[]{:S(2)}, u32[]{:S(2)}) collective-permute-start(bf16[64,1280]{1,0:T(8,128)(2,1)S(1)} %get-tuple-element.148.refs_0_), channel_id=1, source_target_pairs={{0,2},{1,3},{2,0},{3,1},{4,6},{5,7},{6,4},{7,5},{8,10},{9,11},{10,... | collective-permute-start | bytes 491528 | tf_op jit(solution)/shard_map/ppermute | solution.py:607
  227.9 27.9 %collective-permute-start.26 = (bf16[64,1280]{1,0:T(8,128)(2,1)S(1)}, bf16[64,1280]{1,0:T(8,128)(2,1)S(1)}, u32[]{:S(2)}, u32[]{:S(2)}) collective-permute-start(bf16[64,1280]{1,0:T(8,128)(2,1)S(1)} %get-tuple-element.148.refs_0_), channel_id=1, source_target_pairs={{0,3},{1,2},{2,1},{3,0},{4,7},{5,6},{6,5},{7,4},{8,11},{9,10},{10,... | collective-permute-start | bytes 491528 | tf_op jit(solution)/shard_map/ppermute | solution.py:607
  286.1 78.1 %collective-permute-start.35 = (bf16[3,2,224,1280]{3,2,1,0:T(8,128)(2,1)}, bf16[3,2,224,1280]{3,2,1,0:T(8,128)(2,1)}, u32[]{:S(2)}, u32[]{:S(2)}) collective-permute-start(bf16[3,2,224,1280]{3,2,1,0:T(8,128)(2,1)} %get-tuple-element.164), channel_id=1, source_target_pairs={{0,1},{1,0},{2,3},{3,2},{4,5},{5,4},{6,7},{7,6},{8,9},{9,8},{10,11... | collective-permute-start | bytes 10321928 | tf_op jit(solution)/shard_map/ppermute | solution.py:607
  286.3 77.9 %all-to-all-start.5 = ((bf16[32,96,256]{2,1,0:T(8,128)(2,1)}), bf16[32,96,256]{2,1,0:T(8,128)(2,1)S(1)}, u32[]{:S(2)}, u32[]{:S(2)}) async-start(bf16[32,96,256]{2,1,0:T(8,128)(2,1)} %bitcast.169), calls=%async_computation.5 | async-start | bytes 3145728 | tf_op jit(solution)/shard_map/all_to_all | solution.py:611
  290.8 31.1 %collective-permute-start.47 = (bf16[2,224,1280]{2,1,0:T(8,128)(2,1)}, bf16[2,224,1280]{2,1,0:T(8,128)(2,1)}, u32[]{:S(2)}, u32[]{:S(2)}) collective-permute-start(bf16[2,224,1280]{2,1,0:T(8,128)(2,1)} %get-tuple-element.183), channel_id=1, source_target_pairs={{0,1},{1,0},{2,3},{3,2},{4,5},{5,4},{6,7},{7,6},{8,9},{9,8},{10,11... | collective-permute-start | bytes 3440648 | tf_op jit(solution)/shard_map/ppermute | solution.py:607
  291.2 31.2 %collective-permute-start.48 = (bf16[2,224,1280]{2,1,0:T(8,128)(2,1)}, bf16[2,224,1280]{2,1,0:T(8,128)(2,1)}, u32[]{:S(2)}, u32[]{:S(2)}) collective-permute-start(bf16[2,224,1280]{2,1,0:T(8,128)(2,1)} %get-tuple-element.185), channel_id=1, source_target_pairs={{0,1},{1,0},{2,3},{3,2},{4,5},{5,4},{6,7},{7,6},{8,9},{9,8},{10,11... | collective-permute-start | bytes 3440648 | tf_op jit(solution)/shard_map/ppermute | solution.py:607
  335.8 27.8 %collective-permute-start.52 = (bf16[2,224,1280]{2,1,0:T(8,128)(2,1)S(1)}, bf16[2,224,1280]{2,1,0:T(8,128)(2,1)}, u32[]{:S(2)}, u32[]{:S(2)}) collective-permute-start(bf16[2,224,1280]{2,1,0:T(8,128)(2,1)S(1)} %get-tuple-element.186), channel_id=1, source_target_pairs={{0,2},{1,3},{2,0},{3,1},{4,6},{5,7},{6,4},{7,5},{8,10},{9,11},{10,... | collective-permute-start | bytes 3440648 | tf_op jit(solution)/shard_map/ppermute | solution.py:607
  363.6 76.4 %collective-permute-start.53 = (bf16[2,224,1280]{2,1,0:T(8,128)(2,1)}, bf16[2,224,1280]{2,1,0:T(8,128)(2,1)}, u32[]{:S(2)}, u32[]{:S(2)}) collective-permute-start(bf16[2,224,1280]{2,1,0:T(8,128)(2,1)} %get-tuple-element.187), channel_id=1, source_target_pairs={{0,2},{1,3},{2,0},{3,1},{4,6},{5,7},{6,4},{7,5},{8,10},{9,11},{10,... | collective-permute-start | bytes 3440648 | tf_op jit(solution)/shard_map/ppermute | solution.py:607
  377.9 62.0 %all-to-all-start.6 = ((f32[32,2,160]{2,1,0:T(2,128)}), f32[32,2,160]{2,1,0:T(2,128)S(1)}, u32[]{:S(2)}, u32[]{:S(2)}) async-start(f32[32,2,160]{2,1,0:T(2,128)} %bitcast.62), calls=%async_computation.6 | async-start | bytes 131072 | tf_op jit(solution)/shard_map/all_to_all | solution.py:611
  (94 other events, 1176.2 us)

commit v7 on v6

--- a/solution.py
+++ b/solution.py
@@ -839,23 +839,28 @@
     do_units = exchange(do_send, BOTH).reshape(blocks, rows, hd)
 
     grad_attn_sent = after(grad_attn, do_send)
-    routed_far = [across(to_far[0])]
+    attn_parts = of_quarters(grad_attn_sent)
+    from_near = beside(after(parts[4], do_send))
     proj_low, proj_high = output_grads(
-        place, of_quarters(grad_attn_sent), att_parts, heads, hw, blocks
+        place, attn_parts, att_parts, heads, hw, blocks
     )
     out_pairs = added([out_low, after(out_got, proj_low)]).astype(BF)
-    do_units, out_pairs = lax.optimization_barrier(
-        (do_units, out_pairs, proj_low, routed_far[0])
-    )[:2]
+    routed_far = [across(lax.optimization_barrier((to_far[0], tuple(attn_parts)))[0])]
+    to_far.append(added([parts[2][1], after(from_near, proj_low)]).astype(BF))
+    do_units, out_pairs, to_far[1] = lax.optimization_barrier(
+        (do_units, out_pairs, to_far[1], proj_low)
+    )[:3]
 
     grad_units = attend_back(bounds, arrived, seg_col, seg_row, lse, do_units, most)
     out_home = collected(out_pairs)
     proj_pairs = paired(proj_low, proj_high)
-    grad_units = lax.optimization_barrier((grad_units, out_home, proj_pairs, routed_far[0]))[0]
+    grad_units, routed_far[0] = lax.optimization_barrier(
+        (grad_units, routed_far[0], out_home, proj_pairs)
+    )[:2]
+    far_one = across(after(to_far[1], routed_far[0]))
     back_grads = exchange(grad_units.reshape(units, 3 * hw, rows), BOTH)
 
-    from_far = [beside(after(parts[3 + m], grad_units)) for m in (1, 2)]
-    to_far += [added([parts[2][m], from_far[m - 1]]).astype(BF) for m in (1, 2)]
+    to_far.append(added([parts[2][2], beside(after(parts[5], grad_units))]).astype(BF))
     rows_late, grads_late = lax.optimization_barrier((rows_in, grads_in, grad_units))[:2]
     rows_cut = lax.dynamic_slice_in_dim(rows_late, rank * cut, cut, axis=1)
     grads_cut = lax.dynamic_slice_in_dim(grads_late, rank * cut, cut, axis=1)
@@ -863,7 +868,8 @@
         shared_grads(rows_late[c], grads_late[c], rows_cut[c], grads_cut[c], shared_ws) for c in spans
     ]
     shared_parts = shared_parts[0] if len(spans) == 1 else added(shared_parts).astype(BF)
-    shared_gots = [flip(shared_parts[k], k, "tensor") for k in range(1, quarters)]
+    shared_sent, far_one = lax.optimization_barrier((shared_parts, far_one))
+    shared_gots = [flip(shared_sent[k], k, "tensor") for k in range(1, quarters)]
     near = beside(after(parts[1], grad_units))
     out_grad = collected(after(proj_pairs, grad_units))
     moe_out = out_home[:, :width] + shared_out
@@ -897,12 +903,11 @@
     dx_parts = [back_out[0][0]] + [flip(back_out[0][k], k, "tensor") for k in range(1, quarters)]
     pair_q = paired(back_out[2], back_out[3])
     pair_k = paired(back_out[4], after(back_out[5], pair_q))
-    far_one = across(lax.optimization_barrier((to_far[1], output, tuple(shared_gots)))[0])
     dx_parts, pair_q = lax.optimization_barrier((tuple(dx_parts), pair_q))
     grad_one = added(dx_parts)
-    far_two = across(after(to_far[2], far_one))
+    far_two = across(after(to_far[2], dx_parts[1]))
     routed = [added([parts[0][0], near[0], after(routed_far[0], pair_q)])]
-    shared_gots = lax.optimization_barrier((tuple(shared_gots), pair_q))[0]
+    shared_gots = lax.optimization_barrier((tuple(shared_gots), pair_k))[0]
     shared = added([shared_parts[0], *shared_gots])
     pair_v = paired(back_out[6], after(back_out[7], pair_k))
     routed.append(added([parts[0][1], near[1], after(far_one, pair_k)]))

time: 461 us -> 445 us (0.965)
  waiting for transfers between devices: 168 us -> 142 us
  starting transfers between devices: 91.2 us -> 97.2 us
    ppermute x64, waiting for transfers between devices: 161 us -> 135 us  [flip(): return lax.ppermute(x, axis, [(i, i ^ by) for i in range(size)])]
    ppermute x64, starting transfers between devices: 54.1 us -> 62.5 us  [flip(): return lax.ppermute(x, axis, [(i, i ^ by) for i in range(size)])]
  transfers between devices with their start and end apart: 71 -> 71, of which waited for: 23 -> 24; matrix products, arithmetic and copies ran while one was open for 16% -> 18% of each run, Pallas kernels for 23% -> 23%
where the time goes in v7:
time: 445 us; the launch traced here: 438 us
  waiting for transfers between devices  142 us (32%)
  Pallas kernels  109 us (24%)
  starting transfers between devices  97.2 us (22%)
  other arithmetic  45.9 us (10%)
  local copies, waits for them, and re-layouts  39.1 us (9%)
    ppermute x64, waiting for transfers between devices, flip(): return lax.ppermute(x, axis, [(i, i ^ by) for i in range(size)])  135 us
    ppermute x64, starting transfers between devices, flip(): return lax.ppermute(x, axis, [(i, i ^ by) for i in range(size)])  62.5 us
    all_to_all x7, starting transfers between devices, exchange(): return lax.all_to_all(x, axis, 0, 0, tiled=True)  34.7 us
    pallas_call x1, Pallas kernels, experts_first(): pl.pallas_call(body, grid_spec=pltpu.PrefetchScalarGridSpec(num_scalar_pr...  21.2 us
    pallas_call x1, Pallas kernels, experts_second(): pl.pallas_call(body, grid_spec=pltpu.PrefetchScalarGridSpec(num_scalar_pr...  18.8 us
    add x5, other arithmetic, added(): total = total + p.astype(F32)  13.4 us
    pallas_call x1, Pallas kernels, shared_grads(): pl.pallas_call(body, out_shape=jax.ShapeDtypeStruct((parts, 3, hidden, cu...  12.5 us
    pallas_call x1, Pallas kernels, attend_back(): pl.pallas_call(body, grid_spec=grid_spec, out_shape=jax.ShapeDtypeStruct(...  11.4 us
  transfers between devices with their start and end apart: 71, of which 24 were waited for; matrix products, arithmetic and copies ran while one was open for 18% of the time, Pallas kernels for 23%

profile of v7, /device:TPU:0, one launch (start us, length us, event | category | flops | bytes accessed | tf_op | source)
XLA Modules:
  0.0 437.7 jit_solution(15717455091903751608)
XLA Ops:
  8.6 7.4 %all-to-all-start = ((bf16[32,96,256]{2,1,0:T(8,128)(2,1)}), bf16[32,96,256]{2,1,0:T(8,128)(2,1)}, u32[]{:S(2)}, u32[]{:S(2)}) async-start(bf16[32,96,256]{2,1,0:T(8,128)(2,1)} %get-tuple-element.118), calls=%async_computation | async-start | bytes 3145728 | tf_op jit(solution)/shard_map/all_to_all | solution.py:611
  26.1 27.3 %collective-permute-done = bf16[10,32,1280]{2,1,0:T(8,128)(2,1)} collective-permute-done((bf16[10,32,1280]{2,1,0:T(8,128)(2,1)}, bf16[10,32,1280]{2,1,0:T(8,128)(2,1)}, u32[]{:S(2)}, u32[]{:S(2)}) %collective-permute-start) | collective-permute-done | bytes 819232 | tf_op jit(solution)/shard_map/ppermute | solution.py:607
  60.6 9.3 %attend.1 = (bf16[8,256,128]{2,1,0:T(8,128)(2,1)}, f32[8,256,128]{2,1,0:T(8,128)}) custom-call(s32[2]{0:T(128)} %pad_add_fusion.1.bounds_ref, bf16[8,4,96,256]{3,2,1,0:T(8,128)(2,1)} %bitcast.7.arr_ref, s32[8,256,128]{2,1,0:T(8,128)} %broadcast_in_dim.60.col_ref, s32[8,1,256]{2,1,0:T(1,128)} %bitcast.195), custom_call_target="tpu_custom_call" | custom-call | tf_op jit(solution)/shard_map/attend/pallas_call | solution.py:146
  74.1 6.0 %all-to-all-start.1 = ((bf16[32,64,128]{2,1,0:T(8,128)(2,1)}), bf16[32,64,128]{2,1,0:T(8,128)(2,1)}, u32[]{:S(2)}, u32[]{:S(2)}) async-start(bf16[32,64,128]{2,1,0:T(8,128)(2,1)} %bitcast.186), calls=%async_computation.1 | async-start | bytes 1048576 | tf_op jit(solution)/shard_map/all_to_all | solution.py:611
  84.7 9.8 %collective-permute-done.4.odd_ref = bf16[4,64,1408]{2,1,0:T(8,128)(2,1)} collective-permute-done((bf16[4,64,1408]{2,1,0:T(8,128)(2,1)}, bf16[4,64,1408]{2,1,0:T(8,128)(2,1)}, u32[]{:S(2)}, u32[]{:S(2)}) %collective-permute-start.4) | collective-permute-done | bytes 720928 | tf_op jit(solution)/shard_map/ppermute | solution.py:607
  98.9 15.6 %collective-permute-done.9.refs_2_ = bf16[2,224,1280]{2,1,0:T(8,128)(2,1)} collective-permute-done((bf16[2,224,1280]{2,1,0:T(8,128)(2,1)}, bf16[2,224,1280]{2,1,0:T(8,128)(2,1)}, u32[]{:S(2)}, u32[]{:S(2)}) %collective-permute-start.9) | collective-permute-done | bytes 1146912 | tf_op jit(solution)/shard_map/ppermute | solution.py:607
  115.7 5.2 %all-to-all-start.2 = ((bf16[8,64,1280]{2,1,0:T(8,128)(2,1)}), bf16[8,64,1280]{2,1,0:T(8,128)(2,1)}, u32[]{:S(2)}, u32[]{:S(2)}) async-start(bf16[8,64,1280]{2,1,0:T(8,128)(2,1)} %broadcast_in_dim.108), calls=%async_computation.2 | async-start | bytes 2621440 | tf_op jit(solution)/shard_map/all_to_all | solution.py:611
  124.4 14.8 %collective-permute-done.14.refs_6_ = bf16[2,224,1280]{2,1,0:T(8,128)(2,1)} collective-permute-done((bf16[2,224,1280]{2,1,0:T(8,128)(2,1)}, bf16[2,224,1280]{2,1,0:T(8,128)(2,1)}, u32[]{:S(2)}, u32[]{:S(2)}) %collective-permute-start.14) | collective-permute-done | bytes 1146912 | tf_op jit(solution)/shard_map/ppermute | solution.py:607
  140.4 7.5 %down_products.1 = (f32[2,4,512,224]{3,2,1,0:T(8,128)}, bf16[512,1280]{1,0:T(8,128)(2,1)}, bf16[512,128]{1,0:T(8,128)(2,1)}) custom-call(s32[4]{0:T(128)} %pad_add_fusion.place_ref, bf16[4,64,1408]{2,1,0:T(8,128)(2,1)} %pad_maximum_fusion.1.even_ref, bf16[4,64,1408]{2,1,0:T(8,128)(2,1)} %collective-permute-done.4.odd_ref, bf16[2,224,1280]{2,1,0:T(8,128)(2,1)} %refs_0_.2, ...), custom_call_target="tpu_custom_call" | custom-call | tf_op jit(solution)/shard_map/down_products/pallas_call | solution.py:266
  147.9 5.2 %all-to-all-done.2 = bf16[8,64,1280]{2,1,0:T(8,128)(2,1)} async-done(((bf16[8,64,1280]{2,1,0:T(8,128)(2,1)}), bf16[8,64,1280]{2,1,0:T(8,128)(2,1)}, u32[]{:S(2)}, u32[]{:S(2)}) %all-to-all-start.2) | async-done | bytes 1310752 | tf_op jit(solution)/shard_map/all_to_all | solution.py:611
  153.0 21.2 %experts_first.1 = (bf16[2,4,512,224]{3,2,1,0:T(8,128)(2,1)}, bf16[2,4,512,224]{3,2,1,0:T(8,128)(2,1)}, bf16[2,4,512,224]{3,2,1,0:T(8,128)(2,1)}, bf16[512,128]{1,0:T(8,128)(2,1)}, bf16[512,1280]{1,0:T(8,128)(2,1)}) custom-call(s32[4]{0:T(128)} %pad_add_fusion.place_ref, bf16[512,1280]{1,0:T(8,128)(2,1)} %bitcast.27.x_ref, ...), custom_call_target="tpu_custom_call" | custom-call | tf_op jit(solution)/shard_map/experts_first/pallas_call | solution.py:345
  174.2 4.5 %all-to-all-start.3 = ((bf16[8,64,1280]{2,1,0:T(8,128)(2,1)}), bf16[8,64,1280]{2,1,0:T(8,128)(2,1)}, u32[]{:S(2)}, u32[]{:S(2)}) async-start(bf16[8,64,1280]{2,1,0:T(8,128)(2,1)} %bitcast.179), calls=%async_computation.3 | async-start | bytes 2621440 | tf_op jit(solution)/shard_map/all_to_all | solution.py:611
  178.7 18.8 %experts_second.1 = (bf16[4,64,1408]{2,1,0:T(8,128)(2,1)}, bf16[4,64,1408]{2,1,0:T(8,128)(2,1)}, bf16[3,2,224,1280]{3,2,1,0:T(8,128)(2,1)}, bf16[3,2,224,1280]{3...) custom-call(s32[4]{0:T(128)} %pad_add_fusion.place_ref, ...), custom_call_target="tpu_custom_call" | custom-call | tf_op jit(solution)/shard_map/experts_second/pallas_call | solution.py:408
  205.5 7.9 %shared_own.1 = (f32[64,1280]{1,0:T(8,128)}, f32[64,1280]{1,0:T(8,128)}) custom-call(bf16[64,1280]{1,0:T(8,128)(2,1)} %copy-done.11, bf16[64,1280]{1,0:T(8,128)(2,1)} %copy-done.10, bf16[3,224,1280]{2,1,0:T(8,128)(2,1)} %pad_maximum_fusion.refs_0_, bf16[3,224,1280]{2,1,0:T(8,128)(2,1)} %collective-permute-done.17.refs_1_, ...), custom_call_target="tpu_custom_call" | custom-call | tf_op jit(solution)/shard_map/shared_own/pallas_call | solution.py:451
  223.5 4.8 %all-to-all-start.4 = ((bf16[32,64,128]{2,1,0:T(8,128)(2,1)}), bf16[32,64,128]{2,1,0:T(8,128)(2,1)S(1)}, u32[]{:S(2)}, u32[]{:S(2)}) async-start(bf16[32,64,128]{2,1,0:T(8,128)(2,1)} %pad_maximum_fusion.2), calls=%async_computation.4 | async-start | bytes 1048576 | tf_op jit(solution)/shard_map/all_to_all | solution.py:611
  235.6 5.6 %collective-permute-start.32 = (bf16[4,160,320]{2,1,0:T(8,128)(2,1)}, bf16[4,160,320]{2,1,0:T(8,128)(2,1)}, u32[]{:S(2)}, u32[]{:S(2)}) collective-permute-start(bf16[4,160,320]{2,1,0:T(8,128)(2,1)} %get-tuple-element.170), channel_id=1, source_target_pairs={{0,4},{4,0},{8,12},{12,8},{16,20},{20,16},{24,28},{28,24},{1,5},{5... | collective-permute-start | bytes 1228808 | tf_op jit(solution)/shard_map/ppermute | solution.py:607
  254.1 11.4 %attend_back.1 = bf16[8,4,96,256]{3,2,1,0:T(8,128)(2,1)} custom-call(s32[2]{0:T(128)} %pad_add_fusion.1.bounds_ref, bf16[8,4,96,256]{3,2,1,0:T(8,128)(2,1)} %bitcast.7.arr_ref, s32[8,256,128]{2,1,0:T(8,128)} %broadcast_in_dim.60.col_ref, s32[8,1,256]{2,1,0:T(1,128)} %bitcast.196, f32[8,256,128]{2,1,0:T(8,128)} %get-tuple-element.166.lse_ref, ...), custom_call_target="tpu_custom_call" | custom-call | tf_op jit(solution)/shard_map/attend_back/pallas_call | solution.py:229
  281.5 20.1 %collective-permute-done.37 = bf16[160,320]{1,0:T(8,128)(2,1)} collective-permute-done((bf16[160,320]{1,0:T(8,128)(2,1)}, bf16[160,320]{1,0:T(8,128)(2,1)}, u32[]{:S(2)}, u32[]{:S(2)}) %collective-permute-start.37) | collective-permute-done | bytes 102432 | tf_op jit(solution)/shard_map/ppermute | solution.py:607
  301.7 13.6 %collective-permute-done.38 = bf16[160,320]{1,0:T(8,128)(2,1)} collective-permute-done((bf16[160,320]{1,0:T(8,128)(2,1)}, bf16[160,320]{1,0:T(8,128)(2,1)}, u32[]{:S(2)}, u32[]{:S(2)}) %collective-permute-start.38) | collective-permute-done | bytes 102432 | tf_op jit(solution)/shard_map/ppermute | solution.py:607
  318.7 12.5 %shared_grads.1 = bf16[4,3,224,160]{3,2,1,0:T(8,128)(2,1)} custom-call(bf16[512,1280]{1,0:T(8,128)(2,1)} %bitcast.27.x_ref, bf16[512,1280]{1,0:T(8,128)(2,1)} %get-tuple-element.176.dy_ref, bf16[512,160]{1,0:T(8,128)(2,1)} %get-tuple-element.341.xc_ref, bf16[512,160]{1,0:T(8,128)(2,1)} %get-tuple-element.340.dyc_ref, ...), custom_call_target="tpu_custom_call" | custom-call | tf_op jit(solution)/shard_map/shared_grads/pallas_call | solution.py:476
  352.8 6.7 %project_back.1 = (bf16[4,64,1280]{2,1,0:T(8,128)(2,1)}, f32[1,1280]{1,0:T(1,128)}, bf16[4,160,320]{2,1,0:T(8,128)(2,1)}, bf16[4,160,320]{2,1,0:T(8,128)(2,1)}, ...) custom-call(s32[4]{0:T(128)} %pad_add_fusion.place_ref, ...), custom_call_target="tpu_custom_call" | custom-call | tf_op jit(solution)/shard_map/project_back/pallas_call | solution.py:566
  383.2 4.5 %collective-permute-done.56 = bf16[160,320]{1,0:T(8,128)(2,1)S(1)} collective-permute-done((bf16[160,320]{1,0:T(8,128)(2,1)S(1)}, bf16[160,320]{1,0:T(8,128)(2,1)S(1)}, u32[]{:S(2)}, u32[]{:S(2)}) %collective-permute-start.56) | collective-permute-done | bytes 102432 | tf_op jit(solution)/shard_map/ppermute | solution.py:607
  391.6 6.7 %collective-permute-done.54 = bf16[3,224,160]{2,1,0:T(8,128)(2,1)} collective-permute-done((bf16[3,224,160]{2,1,0:T(8,128)(2,1)}, bf16[3,224,160]{2,1,0:T(8,128)(2,1)}, u32[]{:S(2)}, u32[]{:S(2)}) %collective-permute-start.54) | collective-permute-done | bytes 215072 | tf_op jit(solution)/shard_map/ppermute | solution.py:607
  402.8 5.9 %bitcast_add_fusion = (f32[2,224,1280]{2,1,0:T(8,128)}, f32[2,224,1280]{2,1,0:T(8,128)}) fusion(bf16[2,224,1280]{2,1,0:T(8,128)(2,1)} %collective-permute-done.51, bf16[3,2,224,1280]{3,2,1,0:T(8,128)(2,1)} %collective-permute-done.36, bf16[3,2,224,1280]{3,2,1,0:T(8,128)(2,1)} %get-tuple-element.190, bf16[2,224,1280]{2,1,0:T(8,128)(2,1)} %collective-permute-done.31), kind=kLoop, calls=%fused_computation.8 | loop fusion | flops 5734400 | bytes 11468800 | tf_op jit(solution)/shard_map/add | solution.py:601
  (317 shorter events, 183.5 us)
Async XLA Ops:
  8.6 45.1 %all-to-all-start = ((bf16[32,96,256]{2,1,0:T(8,128)(2,1)}), bf16[32,96,256]{2,1,0:T(8,128)(2,1)}, u32[]{:S(2)}, u32[]{:S(2)}) async-start(bf16[32,96,256]{2,1,0:T(8,128)(2,1)} %get-tuple-element.118), calls=%async_computation | async-start | bytes 3145728 | tf_op jit(solution)/shard_map/all_to_all | solution.py:611
  16.1 37.2 %collective-permute-start = (bf16[10,32,1280]{2,1,0:T(8,128)(2,1)}, bf16[10,32,1280]{2,1,0:T(8,128)(2,1)}, u32[]{:S(2)}, u32[]{:S(2)}) collective-permute-start(bf16[10,32,1280]{2,1,0:T(8,128)(2,1)} %bitcast.8), channel_id=1, source_target_pairs={{0,2},{1,3},{2,0},{3,1},{4,6},{5,7},{6,4},{7,5},{8,10},{9,11},{10,... | collective-permute-start | bytes 2457608 | tf_op jit(solution)/shard_map/ppermute | solution.py:607
  17.8 39.9 %collective-permute-start.5 = (bf16[10,32,1280]{2,1,0:T(8,128)(2,1)}, bf16[10,32,1280]{2,1,0:T(8,128)(2,1)}, u32[]{:S(2)}, u32[]{:S(2)}) collective-permute-start(bf16[10,32,1280]{2,1,0:T(8,128)(2,1)} %bitcast.8), channel_id=1, source_target_pairs={{0,1},{1,0},{2,3},{3,2},{4,5},{5,4},{6,7},{7,6},{8,9},{9,8},{10,11... | collective-permute-start | bytes 2457608 | tf_op jit(solution)/shard_map/ppermute | solution.py:607
  53.3 31.4 %collective-permute-start.7 = (bf16[2,224,1280]{2,1,0:T(8,128)(2,1)}, bf16[2,224,1280]{2,1,0:T(8,128)(2,1)}, u32[]{:S(2)}, u32[]{:S(2)}) collective-permute-start(bf16[2,224,1280]{2,1,0:T(8,128)(2,1)} %refs_0_.1), channel_id=1, source_target_pairs={{0,2},{1,3},{2,0},{3,1},{4,6},{5,7},{6,4},{7,5},{8,10},{9,11},{10,... | collective-permute-start | bytes 3440648 | tf_op jit(solution)/shard_map/ppermute | solution.py:607
  53.7 29.4 %collective-permute-start.6 = (bf16[10,32,1280]{2,1,0:T(8,128)(2,1)}, bf16[10,32,1280]{2,1,0:T(8,128)(2,1)}, u32[]{:S(2)}, u32[]{:S(2)}) collective-permute-start(bf16[10,32,1280]{2,1,0:T(8,128)(2,1)} %collective-permute-done), channel_id=1, source_target_pairs={{0,1},{1,0},{2,3},{3,2},{4,5},{5,4},{6,7},{7,6},{8,9},{9,8},{10,11... | collective-permute-start | bytes 2457608 | tf_op jit(solution)/shard_map/ppermute | solution.py:607
  69.9 54.3 %collective-permute-start.11 = (bf16[2,224,1280]{2,1,0:T(8,128)(2,1)}, bf16[2,224,1280]{2,1,0:T(8,128)(2,1)}, u32[]{:S(2)}, u32[]{:S(2)}) collective-permute-start(bf16[2,224,1280]{2,1,0:T(8,128)(2,1)} %refs_0_.1), channel_id=1, source_target_pairs={{0,1},{1,0},{2,3},{3,2},{4,5},{5,4},{6,7},{7,6},{8,9},{9,8},{10,11... | collective-permute-start | bytes 3440648 | tf_op jit(solution)/shard_map/ppermute | solution.py:607
  81.3 33.2 %collective-permute-start.9 = (bf16[2,224,1280]{2,1,0:T(8,128)(2,1)}, bf16[2,224,1280]{2,1,0:T(8,128)(2,1)}, u32[]{:S(2)}, u32[]{:S(2)}) collective-permute-start(bf16[2,224,1280]{2,1,0:T(8,128)(2,1)} %refs_0_.2), channel_id=1, source_target_pairs={{0,2},{1,3},{2,0},{3,1},{4,6},{5,7},{6,4},{7,5},{8,10},{9,11},{10,... | collective-permute-start | bytes 3440648 | tf_op jit(solution)/shard_map/ppermute | solution.py:607
  84.3 54.8 %collective-permute-start.14 = (bf16[2,224,1280]{2,1,0:T(8,128)(2,1)}, bf16[2,224,1280]{2,1,0:T(8,128)(2,1)}, u32[]{:S(2)}, u32[]{:S(2)}) collective-permute-start(bf16[2,224,1280]{2,1,0:T(8,128)(2,1)} %refs_4_), channel_id=1, source_target_pairs={{0,2},{1,3},{2,0},{3,1},{4,6},{5,7},{6,4},{7,5},{8,10},{9,11},{10,... | collective-permute-start | bytes 3440648 | tf_op jit(solution)/shard_map/ppermute | solution.py:607
  84.7 54.5 %collective-permute-start.8 = (bf16[2,224,1280]{2,1,0:T(8,128)(2,1)}, bf16[2,224,1280]{2,1,0:T(8,128)(2,1)}, u32[]{:S(2)}, u32[]{:S(2)}) collective-permute-start(bf16[2,224,1280]{2,1,0:T(8,128)(2,1)} %refs_0_.2), channel_id=1, source_target_pairs={{0,1},{1,0},{2,3},{3,2},{4,5},{5,4},{6,7},{7,6},{8,9},{9,8},{10,11... | collective-permute-start | bytes 3440648 | tf_op jit(solution)/shard_map/ppermute | solution.py:607
  115.7 37.3 %all-to-all-start.2 = ((bf16[8,64,1280]{2,1,0:T(8,128)(2,1)}), bf16[8,64,1280]{2,1,0:T(8,128)(2,1)}, u32[]{:S(2)}, u32[]{:S(2)}) async-start(bf16[8,64,1280]{2,1,0:T(8,128)(2,1)} %broadcast_in_dim.108), calls=%async_computation.2 | async-start | bytes 2621440 | tf_op jit(solution)/shard_map/all_to_all | solution.py:611
  123.7 55.0 %collective-permute-start.16 = (bf16[3,224,1280]{2,1,0:T(8,128)(2,1)}, bf16[3,224,1280]{2,1,0:T(8,128)(2,1)}, u32[]{:S(2)}, u32[]{:S(2)}) collective-permute-start(bf16[3,224,1280]{2,1,0:T(8,128)(2,1)} %pad_maximum_fusion.refs_0_), channel_id=1, source_target_pairs={{0,2},{1,3},{2,0},{3,1},{4,6},{5,7},{6,4},{7,5},{8,10},{9,11},{10,... | collective-permute-start | bytes 5160968 | tf_op jit(solution)/shard_map/ppermute | solution.py:607
  124.2 54.6 %collective-permute-start.17 = (bf16[3,224,1280]{2,1,0:T(8,128)(2,1)}, bf16[3,224,1280]{2,1,0:T(8,128)(2,1)}, u32[]{:S(2)}, u32[]{:S(2)}) collective-permute-start(bf16[3,224,1280]{2,1,0:T(8,128)(2,1)} %pad_maximum_fusion.refs_0_), channel_id=1, source_target_pairs={{0,1},{1,0},{2,3},{3,2},{4,5},{5,4},{6,7},{7,6},{8,9},{9,8},{10,11... | collective-permute-start | bytes 5160968 | tf_op jit(solution)/shard_map/ppermute | solution.py:607
  174.2 40.6 %all-to-all-start.3 = ((bf16[8,64,1280]{2,1,0:T(8,128)(2,1)}), bf16[8,64,1280]{2,1,0:T(8,128)(2,1)}, u32[]{:S(2)}, u32[]{:S(2)}) async-start(bf16[8,64,1280]{2,1,0:T(8,128)(2,1)} %bitcast.179), calls=%async_computation.3 | async-start | bytes 2621440 | tf_op jit(solution)/shard_map/all_to_all | solution.py:611
  241.2 27.8 %collective-permute-start.31 = (bf16[2,224,1280]{2,1,0:T(8,128)(2,1)S(1)}, bf16[2,224,1280]{2,1,0:T(8,128)(2,1)}, u32[]{:S(2)}, u32[]{:S(2)}) collective-permute-start(bf16[2,224,1280]{2,1,0:T(8,128)(2,1)S(1)} %copy-done.14), channel_id=1, source_target_pairs={{0,2},{1,3},{2,0},{3,1},{4,6},{5,7},{6,4},{7,5},{8,10},{9,11},{10,... | collective-permute-start | bytes 3440648 | tf_op jit(solution)/shard_map/ppermute | solution.py:607
  269.0 82.6 %collective-permute-start.36 = (bf16[3,2,224,1280]{3,2,1,0:T(8,128)(2,1)}, bf16[3,2,224,1280]{3,2,1,0:T(8,128)(2,1)}, u32[]{:S(2)}, u32[]{:S(2)}) collective-permute-start(bf16[3,2,224,1280]{3,2,1,0:T(8,128)(2,1)} %get-tuple-element.174), channel_id=1, source_target_pairs={{0,1},{1,0},{2,3},{3,2},{4,5},{5,4},{6,7},{7,6},{8,9},{9,8},{10,11... | collective-permute-start | bytes 10321928 | tf_op jit(solution)/shard_map/ppermute | solution.py:607
  269.3 82.4 %all-to-all-start.5 = ((bf16[32,96,256]{2,1,0:T(8,128)(2,1)}), bf16[32,96,256]{2,1,0:T(8,128)(2,1)S(1)}, u32[]{:S(2)}, u32[]{:S(2)}) async-start(bf16[32,96,256]{2,1,0:T(8,128)(2,1)} %bitcast.169), calls=%async_computation.5 | async-start | bytes 3145728 | tf_op jit(solution)/shard_map/all_to_all | solution.py:611
  273.6 73.1 %collective-permute-start.51 = (bf16[2,224,1280]{2,1,0:T(8,128)(2,1)}, bf16[2,224,1280]{2,1,0:T(8,128)(2,1)}, u32[]{:S(2)}, u32[]{:S(2)}) collective-permute-start(bf16[2,224,1280]{2,1,0:T(8,128)(2,1)} %fusion.1), channel_id=1, source_target_pairs={{0,2},{1,3},{2,0},{3,1},{4,6},{5,7},{6,4},{7,5},{8,10},{9,11},{10,... | collective-permute-start | bytes 3440648 | tf_op jit(solution)/shard_map/ppermute | solution.py:607
  276.1 25.5 %collective-permute-start.37 = (bf16[160,320]{1,0:T(8,128)(2,1)}, bf16[160,320]{1,0:T(8,128)(2,1)}, u32[]{:S(2)}, u32[]{:S(2)}) collective-permute-start(bf16[160,320]{1,0:T(8,128)(2,1)} %get-tuple-element.324), channel_id=1, source_target_pairs={{0,8},{4,12},{8,0},{12,4},{16,24},{20,28},{24,16},{28,20},{1,9},{5... | collective-permute-start | bytes 307208 | tf_op jit(solution)/shard_map/ppermute | solution.py:607
  277.7 37.6 %collective-permute-start.38 = (bf16[160,320]{1,0:T(8,128)(2,1)}, bf16[160,320]{1,0:T(8,128)(2,1)}, u32[]{:S(2)}, u32[]{:S(2)}) collective-permute-start(bf16[160,320]{1,0:T(8,128)(2,1)} %get-tuple-element.326), channel_id=1, source_target_pairs={{0,16},{4,20},{8,24},{12,28},{16,0},{20,4},{24,8},{28,12},{1,17},{... | collective-permute-start | bytes 307208 | tf_op jit(solution)/shard_map/ppermute | solution.py:607
  280.2 68.5 %collective-permute-start.48 = (bf16[2,224,1280]{2,1,0:T(8,128)(2,1)}, bf16[2,224,1280]{2,1,0:T(8,128)(2,1)}, u32[]{:S(2)}, u32[]{:S(2)}) collective-permute-start(bf16[2,224,1280]{2,1,0:T(8,128)(2,1)} %get-tuple-element.193), channel_id=1, source_target_pairs={{0,1},{1,0},{2,3},{3,2},{4,5},{5,4},{6,7},{7,6},{8,9},{9,8},{10,11... | collective-permute-start | bytes 3440648 | tf_op jit(solution)/shard_map/ppermute | solution.py:607
  301.6 31.2 %collective-permute-start.33 = (bf16[64,1408]{1,0:T(8,128)(2,1)}, bf16[64,1408]{1,0:T(8,128)(2,1)S(1)}, u32[]{:S(2)}, u32[]{:S(2)}) collective-permute-start(bf16[64,1408]{1,0:T(8,128)(2,1)} %concatenate.12.refs_0_), channel_id=1, source_target_pairs={{0,1},{1,0},{2,3},{3,2},{4,5},{5,4},{6,7},{7,6},{8,9},{9,8},{10,11... | collective-permute-start | bytes 540680 | tf_op jit(solution)/shard_map/ppermute | solution.py:607
  347.7 43.9 %collective-permute-start.52 = (bf16[3,224,160]{2,1,0:T(8,128)(2,1)}, bf16[3,224,160]{2,1,0:T(8,128)(2,1)}, u32[]{:S(2)}, u32[]{:S(2)}) collective-permute-start(bf16[3,224,160]{2,1,0:T(8,128)(2,1)} %get-tuple-element.304), channel_id=1, source_target_pairs={{0,1},{1,0},{2,3},{3,2},{4,5},{5,4},{6,7},{7,6},{8,9},{9,8},{10,11... | collective-permute-start | bytes 645128 | tf_op jit(solution)/shard_map/ppermute | solution.py:607
  366.5 52.1 %all-to-all-start.6 = ((f32[32,2,160]{2,1,0:T(2,128)}), f32[32,2,160]{2,1,0:T(2,128)}, u32[]{:S(2)}, u32[]{:S(2)}) async-start(f32[32,2,160]{2,1,0:T(2,128)} %bitcast.191), calls=%async_computation.6 | async-start | bytes 131072 | tf_op jit(solution)/shard_map/all_to_all | solution.py:611
  387.7 42.0 %collective-permute-start.49 = (bf16[2,224,1280]{2,1,0:T(8,128)(2,1)}, bf16[2,224,1280]{2,1,0:T(8,128)(2,1)S(1)}, u32[]{:S(2)}, u32[]{:S(2)}) collective-permute-start(bf16[2,224,1280]{2,1,0:T(8,128)(2,1)} %fusion), channel_id=1, source_target_pairs={{0,2},{1,3},{2,0},{3,1},{4,6},{5,7},{6,4},{7,5},{8,10},{9,11},{10,... | collective-permute-start | bytes 3440648 | tf_op jit(solution)/shard_map/ppermute | solution.py:607
  (88 other events, 989.9 us)

commit v8 on v7

--- a/solution.py
+++ b/solution.py
@@ -871,7 +871,7 @@
     shared_sent, far_one = lax.optimization_barrier((shared_parts, far_one))
     shared_gots = [flip(shared_sent[k], k, "tensor") for k in range(1, quarters)]
     near = beside(after(parts[1], grad_units))
-    out_grad = collected(after(proj_pairs, grad_units))
+    out_parts = [flip(after(proj_pairs[j], shared_parts), 2 * j, "expert") for j in range(1, half)]
     moe_out = out_home[:, :width] + shared_out
     slot_sums = out_home[:, width : width + 3 * experts_total].reshape(own, 3, experts_total)
     slot_sums = jnp.sum(slot_sums, axis=1)
@@ -881,7 +881,7 @@
     final = in_order(place, of_quarters(after(final, grad_units)))
     output = final[:, :width]
     gate_grad = jnp.sum(final[:, width : width + 3 * top].reshape(rows, 3, top).astype(F32), axis=1)
-    back_grads, near = lax.optimization_barrier((back_grads, near, shared_parts, out_grad, output))[:2]
+    back_grads, near, out_parts = lax.optimization_barrier((back_grads, near, tuple(out_parts), shared_parts, output))[:3]
 
     back_out = project_back(
         place,
@@ -906,6 +906,7 @@
     dx_parts, pair_q = lax.optimization_barrier((tuple(dx_parts), pair_q))
     grad_one = added(dx_parts)
     far_two = across(after(to_far[2], dx_parts[1]))
+    out_grad = added([proj_pairs[0], *lax.optimization_barrier((out_parts, pair_q))[0]])
     routed = [added([parts[0][0], near[0], after(routed_far[0], pair_q)])]
     shared_gots = lax.optimization_barrier((tuple(shared_gots), pair_k))[0]
     shared = added([shared_parts[0], *shared_gots])

time: 445 us -> 436 us (0.980)
  waiting for transfers between devices: 142 us -> 136 us
    ppermute x64, waiting for transfers between devices: 135 us -> 129 us  [flip(): return lax.ppermute(x, axis, [(i, i ^ by) for i in range(size)])]
    add x5 -> x4, other arithmetic: 13.4 us -> 12 us  [added(): total = total + p.astype(F32)]
  transfers between devices with their start and end apart: 71 -> 71, of which waited for: 24 -> 22; matrix products, arithmetic and copies ran while one was open for 18% -> 18% of each run, Pallas kernels for 23% -> 24%
where the time goes in v8:
time: 436 us; the launch traced here: 429 us
  waiting for transfers between devices  136 us (31%)
  Pallas kernels  108 us (25%)
  starting transfers between devices  94.1 us (22%)
  other arithmetic  45.9 us (11%)
  local copies, waits for them, and re-layouts  39.7 us (9%)
    ppermute x64, waiting for transfers between devices, flip(): return lax.ppermute(x, axis, [(i, i ^ by) for i in range(size)])  129 us
    ppermute x64, starting transfers between devices, flip(): return lax.ppermute(x, axis, [(i, i ^ by) for i in range(size)])  60.2 us
    all_to_all x7, starting transfers between devices, exchange(): return lax.all_to_all(x, axis, 0, 0, tiled=True)  33.9 us
    pallas_call x1, Pallas kernels, experts_first(): pl.pallas_call(body, grid_spec=pltpu.PrefetchScalarGridSpec(num_scalar_pr...  21.2 us
    pallas_call x1, Pallas kernels, experts_second(): pl.pallas_call(body, grid_spec=pltpu.PrefetchScalarGridSpec(num_scalar_pr...  18.7 us
    pallas_call x1, Pallas kernels, shared_grads(): pl.pallas_call(body, out_shape=jax.ShapeDtypeStruct((parts, 3, hidden, cu...  12.5 us
    add x4, other arithmetic, added(): total = total + p.astype(F32)  12 us
    pallas_call x1, Pallas kernels, attend_back(): pl.pallas_call(body, grid_spec=grid_spec, out_shape=jax.ShapeDtypeStruct(...  11.4 us
  transfers between devices with their start and end apart: 71, of which 22 were waited for; matrix products, arithmetic and copies ran while one was open for 18% of the time, Pallas kernels for 24%

profile of v8, /device:TPU:0, one launch (start us, length us, event | category | flops | bytes accessed | tf_op | source)
XLA Modules:
  0.0 429.4 jit_solution(15084193594792361679)
XLA Ops:
  8.6 7.4 %all-to-all-start = ((bf16[32,96,256]{2,1,0:T(8,128)(2,1)}), bf16[32,96,256]{2,1,0:T(8,128)(2,1)}, u32[]{:S(2)}, u32[]{:S(2)}) async-start(bf16[32,96,256]{2,1,0:T(8,128)(2,1)} %get-tuple-element.126), calls=%async_computation | async-start | bytes 3145728 | tf_op jit(solution)/shard_map/all_to_all | solution.py:611
  26.0 27.3 %collective-permute-done = bf16[10,32,1280]{2,1,0:T(8,128)(2,1)} collective-permute-done((bf16[10,32,1280]{2,1,0:T(8,128)(2,1)}, bf16[10,32,1280]{2,1,0:T(8,128)(2,1)}, u32[]{:S(2)}, u32[]{:S(2)}) %collective-permute-start) | collective-permute-done | bytes 819232 | tf_op jit(solution)/shard_map/ppermute | solution.py:607
  60.7 9.2 %attend.1 = (bf16[8,256,128]{2,1,0:T(8,128)(2,1)}, f32[8,256,128]{2,1,0:T(8,128)}) custom-call(s32[2]{0:T(128)} %pad_add_fusion.1.bounds_ref, bf16[8,4,96,256]{3,2,1,0:T(8,128)(2,1)} %bitcast.7.arr_ref, s32[8,256,128]{2,1,0:T(8,128)} %broadcast_in_dim.60.col_ref, s32[8,1,256]{2,1,0:T(1,128)} %bitcast.196), custom_call_target="tpu_custom_call" | custom-call | tf_op jit(solution)/shard_map/attend/pallas_call | solution.py:146
  74.1 6.0 %all-to-all-start.1 = ((bf16[32,64,128]{2,1,0:T(8,128)(2,1)}), bf16[32,64,128]{2,1,0:T(8,128)(2,1)}, u32[]{:S(2)}, u32[]{:S(2)}) async-start(bf16[32,64,128]{2,1,0:T(8,128)(2,1)} %bitcast.188), calls=%async_computation.1 | async-start | bytes 1048576 | tf_op jit(solution)/shard_map/all_to_all | solution.py:611
  84.7 9.7 %collective-permute-done.4.odd_ref = bf16[4,64,1408]{2,1,0:T(8,128)(2,1)} collective-permute-done((bf16[4,64,1408]{2,1,0:T(8,128)(2,1)}, bf16[4,64,1408]{2,1,0:T(8,128)(2,1)}, u32[]{:S(2)}, u32[]{:S(2)}) %collective-permute-start.4) | collective-permute-done | bytes 720928 | tf_op jit(solution)/shard_map/ppermute | solution.py:607
  98.9 15.7 %collective-permute-done.9.refs_2_ = bf16[2,224,1280]{2,1,0:T(8,128)(2,1)} collective-permute-done((bf16[2,224,1280]{2,1,0:T(8,128)(2,1)}, bf16[2,224,1280]{2,1,0:T(8,128)(2,1)}, u32[]{:S(2)}, u32[]{:S(2)}) %collective-permute-start.9) | collective-permute-done | bytes 1146912 | tf_op jit(solution)/shard_map/ppermute | solution.py:607
  115.7 5.2 %all-to-all-start.2 = ((bf16[8,64,1280]{2,1,0:T(8,128)(2,1)}), bf16[8,64,1280]{2,1,0:T(8,128)(2,1)}, u32[]{:S(2)}, u32[]{:S(2)}) async-start(bf16[8,64,1280]{2,1,0:T(8,128)(2,1)} %broadcast_in_dim.108), calls=%async_computation.2 | async-start | bytes 2621440 | tf_op jit(solution)/shard_map/all_to_all | solution.py:611
  124.4 14.8 %collective-permute-done.14.refs_6_ = bf16[2,224,1280]{2,1,0:T(8,128)(2,1)} collective-permute-done((bf16[2,224,1280]{2,1,0:T(8,128)(2,1)}, bf16[2,224,1280]{2,1,0:T(8,128)(2,1)}, u32[]{:S(2)}, u32[]{:S(2)}) %collective-permute-start.14) | collective-permute-done | bytes 1146912 | tf_op jit(solution)/shard_map/ppermute | solution.py:607
  140.4 7.5 %down_products.1 = (f32[2,4,512,224]{3,2,1,0:T(8,128)}, bf16[512,1280]{1,0:T(8,128)(2,1)}, bf16[512,128]{1,0:T(8,128)(2,1)}) custom-call(s32[4]{0:T(128)} %pad_add_fusion.place_ref, bf16[4,64,1408]{2,1,0:T(8,128)(2,1)} %pad_maximum_fusion.1.even_ref, bf16[4,64,1408]{2,1,0:T(8,128)(2,1)} %collective-permute-done.4.odd_ref, bf16[2,224,1280]{2,1,0:T(8,128)(2,1)} %refs_0_.2, ...), custom_call_target="tpu_custom_call" | custom-call | tf_op jit(solution)/shard_map/down_products/pallas_call | solution.py:266
  147.9 5.1 %all-to-all-done.2 = bf16[8,64,1280]{2,1,0:T(8,128)(2,1)} async-done(((bf16[8,64,1280]{2,1,0:T(8,128)(2,1)}), bf16[8,64,1280]{2,1,0:T(8,128)(2,1)}, u32[]{:S(2)}, u32[]{:S(2)}) %all-to-all-start.2) | async-done | bytes 1310752 | tf_op jit(solution)/shard_map/all_to_all | solution.py:611
  153.0 21.2 %experts_first.1 = (bf16[2,4,512,224]{3,2,1,0:T(8,128)(2,1)}, bf16[2,4,512,224]{3,2,1,0:T(8,128)(2,1)}, bf16[2,4,512,224]{3,2,1,0:T(8,128)(2,1)}, bf16[512,128]{1,0:T(8,128)(2,1)}, bf16[512,1280]{1,0:T(8,128)(2,1)}) custom-call(s32[4]{0:T(128)} %pad_add_fusion.place_ref, bf16[512,1280]{1,0:T(8,128)(2,1)} %bitcast.27.x_ref, ...), custom_call_target="tpu_custom_call" | custom-call | tf_op jit(solution)/shard_map/experts_first/pallas_call | solution.py:345
  174.2 4.5 %all-to-all-start.3 = ((bf16[8,64,1280]{2,1,0:T(8,128)(2,1)}), bf16[8,64,1280]{2,1,0:T(8,128)(2,1)}, u32[]{:S(2)}, u32[]{:S(2)}) async-start(bf16[8,64,1280]{2,1,0:T(8,128)(2,1)} %bitcast.182), calls=%async_computation.3 | async-start | bytes 2621440 | tf_op jit(solution)/shard_map/all_to_all | solution.py:611
  178.7 18.7 %experts_second.1 = (bf16[4,64,1408]{2,1,0:T(8,128)(2,1)}, bf16[4,64,1408]{2,1,0:T(8,128)(2,1)}, bf16[3,2,224,1280]{3,2,1,0:T(8,128)(2,1)}, bf16[3,2,224,1280]{3...) custom-call(s32[4]{0:T(128)} %pad_add_fusion.place_ref, ...), custom_call_target="tpu_custom_call" | custom-call | tf_op jit(solution)/shard_map/experts_second/pallas_call | solution.py:408
  205.4 7.9 %shared_own.1 = (f32[64,1280]{1,0:T(8,128)}, f32[64,1280]{1,0:T(8,128)}) custom-call(bf16[64,1280]{1,0:T(8,128)(2,1)} %copy-done.11, bf16[64,1280]{1,0:T(8,128)(2,1)} %copy-done.10, bf16[3,224,1280]{2,1,0:T(8,128)(2,1)} %pad_maximum_fusion.refs_0_, bf16[3,224,1280]{2,1,0:T(8,128)(2,1)} %collective-permute-done.17.refs_1_, ...), custom_call_target="tpu_custom_call" | custom-call | tf_op jit(solution)/shard_map/shared_own/pallas_call | solution.py:451
  223.5 4.8 %all-to-all-start.4 = ((bf16[32,64,128]{2,1,0:T(8,128)(2,1)}), bf16[32,64,128]{2,1,0:T(8,128)(2,1)S(1)}, u32[]{:S(2)}, u32[]{:S(2)}) async-start(bf16[32,64,128]{2,1,0:T(8,128)(2,1)} %pad_maximum_fusion.2), calls=%async_computation.4 | async-start | bytes 1048576 | tf_op jit(solution)/shard_map/all_to_all | solution.py:611
  235.7 5.6 %collective-permute-start.32 = (bf16[4,160,320]{2,1,0:T(8,128)(2,1)}, bf16[4,160,320]{2,1,0:T(8,128)(2,1)}, u32[]{:S(2)}, u32[]{:S(2)}) collective-permute-start(bf16[4,160,320]{2,1,0:T(8,128)(2,1)} %get-tuple-element.178), channel_id=1, source_target_pairs={{0,4},{4,0},{8,12},{12,8},{16,20},{20,16},{24,28},{28,24},{1,5},{5... | collective-permute-start | bytes 1228808 | tf_op jit(solution)/shard_map/ppermute | solution.py:607
  247.3 4.4 %collective-permute-start.30 = (bf16[64,1408]{1,0:T(8,128)(2,1)S(1)}, bf16[64,1408]{1,0:T(8,128)(2,1)}, u32[]{:S(2)}, u32[]{:S(2)}) collective-permute-start(bf16[64,1408]{1,0:T(8,128)(2,1)S(1)} %get-tuple-element.322), channel_id=1, source_target_pairs={{0,24},{4,28},{8,16},{12,20},{16,8},{20,12},{24,0},{28,4},{1,25},{... | collective-permute-start | bytes 540680 | tf_op jit(solution)/shard_map/ppermute | solution.py:607
  254.2 11.4 %attend_back.1 = bf16[8,4,96,256]{3,2,1,0:T(8,128)(2,1)} custom-call(s32[2]{0:T(128)} %pad_add_fusion.1.bounds_ref, bf16[8,4,96,256]{3,2,1,0:T(8,128)(2,1)} %bitcast.7.arr_ref, s32[8,256,128]{2,1,0:T(8,128)} %broadcast_in_dim.60.col_ref, s32[8,1,256]{2,1,0:T(1,128)} %bitcast.197, f32[8,256,128]{2,1,0:T(8,128)} %get-tuple-element.174.lse_ref, ...), custom_call_target="tpu_custom_call" | custom-call | tf_op jit(solution)/shard_map/attend_back/pallas_call | solution.py:229
  281.7 12.5 %shared_grads.1 = bf16[4,3,224,160]{3,2,1,0:T(8,128)(2,1)} custom-call(bf16[512,1280]{1,0:T(8,128)(2,1)} %bitcast.27.x_ref, bf16[512,1280]{1,0:T(8,128)(2,1)} %get-tuple-element.184.dy_ref, bf16[512,160]{1,0:T(8,128)(2,1)} %get-tuple-element.357.xc_ref, bf16[512,160]{1,0:T(8,128)(2,1)} %get-tuple-element.356.dyc_ref, ...), custom_call_target="tpu_custom_call" | custom-call | tf_op jit(solution)/shard_map/shared_grads/pallas_call | solution.py:476
  294.2 27.0 %collective-permute-done.34.refs_2_ = bf16[64,1408]{1,0:T(8,128)(2,1)S(1)} collective-permute-done((bf16[64,1408]{1,0:T(8,128)(2,1)}, bf16[64,1408]{1,0:T(8,128)(2,1)S(1)}, u32[]{:S(2)}, u32[]{:S(2)}) %collective-permute-start.34) | collective-permute-done | bytes 180256 | tf_op jit(solution)/shard_map/ppermute | solution.py:607
  339.5 6.7 %project_back.1 = (bf16[4,64,1280]{2,1,0:T(8,128)(2,1)}, f32[1,1280]{1,0:T(1,128)}, bf16[4,160,320]{2,1,0:T(8,128)(2,1)}, bf16[4,160,320]{2,1,0:T(8,128)(2,1)}, ...) custom-call(s32[4]{0:T(128)} %pad_add_fusion.place_ref, ...), custom_call_target="tpu_custom_call" | custom-call | tf_op jit(solution)/shard_map/project_back/pallas_call | solution.py:566
  384.9 5.5 %collective-permute-done.54 = bf16[3,224,160]{2,1,0:T(8,128)(2,1)S(1)} collective-permute-done((bf16[3,224,160]{2,1,0:T(8,128)(2,1)}, bf16[3,224,160]{2,1,0:T(8,128)(2,1)S(1)}, u32[]{:S(2)}, u32[]{:S(2)}) %collective-permute-start.54) | collective-permute-done | bytes 215072 | tf_op jit(solution)/shard_map/ppermute | solution.py:607
  395.7 5.9 %bitcast_add_fusion = (f32[2,224,1280]{2,1,0:T(8,128)}, f32[2,224,1280]{2,1,0:T(8,128)}) fusion(bf16[2,224,1280]{2,1,0:T(8,128)(2,1)} %collective-permute-done.51, bf16[3,2,224,1280]{3,2,1,0:T(8,128)(2,1)} %collective-permute-done.36, bf16[3,2,224,1280]{3,2,1,0:T(8,128)(2,1)} %get-tuple-element.200, bf16[2,224,1280]{2,1,0:T(8,128)(2,1)} %collective-permute-done.31), kind=kLoop, calls=%fused_computation.8 | loop fusion | flops 5734400 | bytes 11468800 | tf_op jit(solution)/shard_map/add | solution.py:601
  414.6 5.4 %collective-permute-done.62 = bf16[160,320]{1,0:T(8,128)(2,1)S(1)} collective-permute-done((bf16[160,320]{1,0:T(8,128)(2,1)S(1)}, bf16[160,320]{1,0:T(8,128)(2,1)S(1)}, u32[]{:S(2)}, u32[]{:S(2)}) %collective-permute-start.62) | collective-permute-done | bytes 102432 | tf_op jit(solution)/shard_map/ppermute | solution.py:607
  (327 shorter events, 177.9 us)
Async XLA Ops:
  8.6 45.1 %all-to-all-start = ((bf16[32,96,256]{2,1,0:T(8,128)(2,1)}), bf16[32,96,256]{2,1,0:T(8,128)(2,1)}, u32[]{:S(2)}, u32[]{:S(2)}) async-start(bf16[32,96,256]{2,1,0:T(8,128)(2,1)} %get-tuple-element.126), calls=%async_computation | async-start | bytes 3145728 | tf_op jit(solution)/shard_map/all_to_all | solution.py:611
  16.1 37.2 %collective-permute-start = (bf16[10,32,1280]{2,1,0:T(8,128)(2,1)}, bf16[10,32,1280]{2,1,0:T(8,128)(2,1)}, u32[]{:S(2)}, u32[]{:S(2)}) collective-permute-start(bf16[10,32,1280]{2,1,0:T(8,128)(2,1)} %bitcast.8), channel_id=1, source_target_pairs={{0,2},{1,3},{2,0},{3,1},{4,6},{5,7},{6,4},{7,5},{8,10},{9,11},{10,... | collective-permute-start | bytes 2457608 | tf_op jit(solution)/shard_map/ppermute | solution.py:607
  17.9 39.9 %collective-permute-start.5 = (bf16[10,32,1280]{2,1,0:T(8,128)(2,1)}, bf16[10,32,1280]{2,1,0:T(8,128)(2,1)}, u32[]{:S(2)}, u32[]{:S(2)}) collective-permute-start(bf16[10,32,1280]{2,1,0:T(8,128)(2,1)} %bitcast.8), channel_id=1, source_target_pairs={{0,1},{1,0},{2,3},{3,2},{4,5},{5,4},{6,7},{7,6},{8,9},{9,8},{10,11... | collective-permute-start | bytes 2457608 | tf_op jit(solution)/shard_map/ppermute | solution.py:607
  53.3 31.4 %collective-permute-start.7 = (bf16[2,224,1280]{2,1,0:T(8,128)(2,1)}, bf16[2,224,1280]{2,1,0:T(8,128)(2,1)}, u32[]{:S(2)}, u32[]{:S(2)}) collective-permute-start(bf16[2,224,1280]{2,1,0:T(8,128)(2,1)} %refs_0_.1), channel_id=1, source_target_pairs={{0,2},{1,3},{2,0},{3,1},{4,6},{5,7},{6,4},{7,5},{8,10},{9,11},{10,... | collective-permute-start | bytes 3440648 | tf_op jit(solution)/shard_map/ppermute | solution.py:607
  53.7 29.4 %collective-permute-start.6 = (bf16[10,32,1280]{2,1,0:T(8,128)(2,1)}, bf16[10,32,1280]{2,1,0:T(8,128)(2,1)}, u32[]{:S(2)}, u32[]{:S(2)}) collective-permute-start(bf16[10,32,1280]{2,1,0:T(8,128)(2,1)} %collective-permute-done), channel_id=1, source_target_pairs={{0,1},{1,0},{2,3},{3,2},{4,5},{5,4},{6,7},{7,6},{8,9},{9,8},{10,11... | collective-permute-start | bytes 2457608 | tf_op jit(solution)/shard_map/ppermute | solution.py:607
  69.8 54.3 %collective-permute-start.11 = (bf16[2,224,1280]{2,1,0:T(8,128)(2,1)}, bf16[2,224,1280]{2,1,0:T(8,128)(2,1)}, u32[]{:S(2)}, u32[]{:S(2)}) collective-permute-start(bf16[2,224,1280]{2,1,0:T(8,128)(2,1)} %refs_0_.1), channel_id=1, source_target_pairs={{0,1},{1,0},{2,3},{3,2},{4,5},{5,4},{6,7},{7,6},{8,9},{9,8},{10,11... | collective-permute-start | bytes 3440648 | tf_op jit(solution)/shard_map/ppermute | solution.py:607
  81.3 33.2 %collective-permute-start.9 = (bf16[2,224,1280]{2,1,0:T(8,128)(2,1)}, bf16[2,224,1280]{2,1,0:T(8,128)(2,1)}, u32[]{:S(2)}, u32[]{:S(2)}) collective-permute-start(bf16[2,224,1280]{2,1,0:T(8,128)(2,1)} %refs_0_.2), channel_id=1, source_target_pairs={{0,2},{1,3},{2,0},{3,1},{4,6},{5,7},{6,4},{7,5},{8,10},{9,11},{10,... | collective-permute-start | bytes 3440648 | tf_op jit(solution)/shard_map/ppermute | solution.py:607
  84.3 54.8 %collective-permute-start.14 = (bf16[2,224,1280]{2,1,0:T(8,128)(2,1)}, bf16[2,224,1280]{2,1,0:T(8,128)(2,1)}, u32[]{:S(2)}, u32[]{:S(2)}) collective-permute-start(bf16[2,224,1280]{2,1,0:T(8,128)(2,1)} %refs_4_), channel_id=1, source_target_pairs={{0,2},{1,3},{2,0},{3,1},{4,6},{5,7},{6,4},{7,5},{8,10},{9,11},{10,... | collective-permute-start | bytes 3440648 | tf_op jit(solution)/shard_map/ppermute | solution.py:607
  84.7 54.5 %collective-permute-start.8 = (bf16[2,224,1280]{2,1,0:T(8,128)(2,1)}, bf16[2,224,1280]{2,1,0:T(8,128)(2,1)}, u32[]{:S(2)}, u32[]{:S(2)}) collective-permute-start(bf16[2,224,1280]{2,1,0:T(8,128)(2,1)} %refs_0_.2), channel_id=1, source_target_pairs={{0,1},{1,0},{2,3},{3,2},{4,5},{5,4},{6,7},{7,6},{8,9},{9,8},{10,11... | collective-permute-start | bytes 3440648 | tf_op jit(solution)/shard_map/ppermute | solution.py:607
  114.6 25.1 %collective-permute-start.10 = (bf16[2,224,1280]{2,1,0:T(8,128)(2,1)}, bf16[2,224,1280]{2,1,0:T(8,128)(2,1)}, u32[]{:S(2)}, u32[]{:S(2)}) collective-permute-start(bf16[2,224,1280]{2,1,0:T(8,128)(2,1)} %collective-permute-done.9.refs_2_), channel_id=1, source_target_pairs={{0,1},{1,0},{2,3},{3,2},{4,5},{5,4},{6,7},{7,6},{8,9},{9,8},{10,11... | collective-permute-start | bytes 3440648 | tf_op jit(solution)/shard_map/ppermute | solution.py:607
  115.7 37.3 %all-to-all-start.2 = ((bf16[8,64,1280]{2,1,0:T(8,128)(2,1)}), bf16[8,64,1280]{2,1,0:T(8,128)(2,1)}, u32[]{:S(2)}, u32[]{:S(2)}) async-start(bf16[8,64,1280]{2,1,0:T(8,128)(2,1)} %broadcast_in_dim.108), calls=%async_computation.2 | async-start | bytes 2621440 | tf_op jit(solution)/shard_map/all_to_all | solution.py:611
  123.7 55.0 %collective-permute-start.16 = (bf16[3,224,1280]{2,1,0:T(8,128)(2,1)}, bf16[3,224,1280]{2,1,0:T(8,128)(2,1)}, u32[]{:S(2)}, u32[]{:S(2)}) collective-permute-start(bf16[3,224,1280]{2,1,0:T(8,128)(2,1)} %pad_maximum_fusion.refs_0_), channel_id=1, source_target_pairs={{0,2},{1,3},{2,0},{3,1},{4,6},{5,7},{6,4},{7,5},{8,10},{9,11},{10,... | collective-permute-start | bytes 5160968 | tf_op jit(solution)/shard_map/ppermute | solution.py:607
  124.2 54.6 %collective-permute-start.17 = (bf16[3,224,1280]{2,1,0:T(8,128)(2,1)}, bf16[3,224,1280]{2,1,0:T(8,128)(2,1)}, u32[]{:S(2)}, u32[]{:S(2)}) collective-permute-start(bf16[3,224,1280]{2,1,0:T(8,128)(2,1)} %pad_maximum_fusion.refs_0_), channel_id=1, source_target_pairs={{0,1},{1,0},{2,3},{3,2},{4,5},{5,4},{6,7},{7,6},{8,9},{9,8},{10,11... | collective-permute-start | bytes 5160968 | tf_op jit(solution)/shard_map/ppermute | solution.py:607
  174.2 40.5 %all-to-all-start.3 = ((bf16[8,64,1280]{2,1,0:T(8,128)(2,1)}), bf16[8,64,1280]{2,1,0:T(8,128)(2,1)}, u32[]{:S(2)}, u32[]{:S(2)}) async-start(bf16[8,64,1280]{2,1,0:T(8,128)(2,1)} %bitcast.182), calls=%async_computation.3 | async-start | bytes 2621440 | tf_op jit(solution)/shard_map/all_to_all | solution.py:611
  241.2 27.9 %collective-permute-start.31 = (bf16[2,224,1280]{2,1,0:T(8,128)(2,1)S(1)}, bf16[2,224,1280]{2,1,0:T(8,128)(2,1)}, u32[]{:S(2)}, u32[]{:S(2)}) collective-permute-start(bf16[2,224,1280]{2,1,0:T(8,128)(2,1)S(1)} %copy-done.13), channel_id=1, source_target_pairs={{0,2},{1,3},{2,0},{3,1},{4,6},{5,7},{6,4},{7,5},{8,10},{9,11},{10,... | collective-permute-start | bytes 3440648 | tf_op jit(solution)/shard_map/ppermute | solution.py:607
  269.1 69.2 %collective-permute-start.36 = (bf16[3,2,224,1280]{3,2,1,0:T(8,128)(2,1)}, bf16[3,2,224,1280]{3,2,1,0:T(8,128)(2,1)}, u32[]{:S(2)}, u32[]{:S(2)}) collective-permute-start(bf16[3,2,224,1280]{3,2,1,0:T(8,128)(2,1)} %get-tuple-element.182), channel_id=1, source_target_pairs={{0,1},{1,0},{2,3},{3,2},{4,5},{5,4},{6,7},{7,6},{8,9},{9,8},{10,11... | collective-permute-start | bytes 10321928 | tf_op jit(solution)/shard_map/ppermute | solution.py:607
  269.3 69.0 %all-to-all-start.5 = ((bf16[32,96,256]{2,1,0:T(8,128)(2,1)}), bf16[32,96,256]{2,1,0:T(8,128)(2,1)S(1)}, u32[]{:S(2)}, u32[]{:S(2)}) async-start(bf16[32,96,256]{2,1,0:T(8,128)(2,1)} %bitcast.172), calls=%async_computation.5 | async-start | bytes 3145728 | tf_op jit(solution)/shard_map/all_to_all | solution.py:611
  273.7 58.9 %collective-permute-start.51 = (bf16[2,224,1280]{2,1,0:T(8,128)(2,1)}, bf16[2,224,1280]{2,1,0:T(8,128)(2,1)}, u32[]{:S(2)}, u32[]{:S(2)}) collective-permute-start(bf16[2,224,1280]{2,1,0:T(8,128)(2,1)} %fusion.1), channel_id=1, source_target_pairs={{0,2},{1,3},{2,0},{3,1},{4,6},{5,7},{6,4},{7,5},{8,10},{9,11},{10,... | collective-permute-start | bytes 3440648 | tf_op jit(solution)/shard_map/ppermute | solution.py:607
  275.5 59.8 %collective-permute-start.48 = (bf16[2,224,1280]{2,1,0:T(8,128)(2,1)}, bf16[2,224,1280]{2,1,0:T(8,128)(2,1)}, u32[]{:S(2)}, u32[]{:S(2)}) collective-permute-start(bf16[2,224,1280]{2,1,0:T(8,128)(2,1)} %get-tuple-element.203), channel_id=1, source_target_pairs={{0,1},{1,0},{2,3},{3,2},{4,5},{5,4},{6,7},{7,6},{8,9},{9,8},{10,11... | collective-permute-start | bytes 3440648 | tf_op jit(solution)/shard_map/ppermute | solution.py:607
  277.3 43.9 %collective-permute-start.34 = (bf16[64,1408]{1,0:T(8,128)(2,1)}, bf16[64,1408]{1,0:T(8,128)(2,1)S(1)}, u32[]{:S(2)}, u32[]{:S(2)}) collective-permute-start(bf16[64,1408]{1,0:T(8,128)(2,1)} %concatenate.12.refs_0_), channel_id=1, source_target_pairs={{0,2},{1,3},{2,0},{3,1},{4,6},{5,7},{6,4},{7,5},{8,10},{9,11},{10,... | collective-permute-start | bytes 540680 | tf_op jit(solution)/shard_map/ppermute | solution.py:607
  278.7 45.8 %collective-permute-start.35 = (bf16[64,1408]{1,0:T(8,128)(2,1)}, bf16[64,1408]{1,0:T(8,128)(2,1)S(1)}, u32[]{:S(2)}, u32[]{:S(2)}) collective-permute-start(bf16[64,1408]{1,0:T(8,128)(2,1)} %concatenate.12.refs_0_), channel_id=1, source_target_pairs={{0,3},{1,2},{2,1},{3,0},{4,7},{5,6},{6,5},{7,4},{8,11},{9,10},{10,... | collective-permute-start | bytes 540680 | tf_op jit(solution)/shard_map/ppermute | solution.py:607
  335.3 45.5 %collective-permute-start.52 = (bf16[3,224,160]{2,1,0:T(8,128)(2,1)}, bf16[3,224,160]{2,1,0:T(8,128)(2,1)}, u32[]{:S(2)}, u32[]{:S(2)}) collective-permute-start(bf16[3,224,160]{2,1,0:T(8,128)(2,1)} %get-tuple-element.320), channel_id=1, source_target_pairs={{0,1},{1,0},{2,3},{3,2},{4,5},{5,4},{6,7},{7,6},{8,9},{9,8},{10,11... | collective-permute-start | bytes 645128 | tf_op jit(solution)/shard_map/ppermute | solution.py:607
  353.3 56.8 %all-to-all-start.6 = ((f32[32,2,160]{2,1,0:T(2,128)}), f32[32,2,160]{2,1,0:T(2,128)S(1)}, u32[]{:S(2)}, u32[]{:S(2)}) async-start(f32[32,2,160]{2,1,0:T(2,128)} %bitcast.61), calls=%async_computation.6 | async-start | bytes 131072 | tf_op jit(solution)/shard_map/all_to_all | solution.py:611
  377.4 43.5 %collective-permute-start.49 = (bf16[2,224,1280]{2,1,0:T(8,128)(2,1)}, bf16[2,224,1280]{2,1,0:T(8,128)(2,1)}, u32[]{:S(2)}, u32[]{:S(2)}) collective-permute-start(bf16[2,224,1280]{2,1,0:T(8,128)(2,1)} %fusion), channel_id=1, source_target_pairs={{0,2},{1,3},{2,0},{3,1},{4,6},{5,7},{6,4},{7,5},{8,10},{9,11},{10,... | collective-permute-start | bytes 3440648 | tf_op jit(solution)/shard_map/ppermute | solution.py:607
  (93 other events, 1005.2 us)
